TPU v7x, 32 devices: a whole 2x2x4 slice. The times are simulated.
32 devices in a mesh: ctx: 8 (over z, y), head: 4 (over x, core).
Axes of the slice: x: 2, y: 2, z: 4, core: 2. Of those that a mesh axis runs over, the one named last changes fastest.
Arguments:
- q_first: bfloat16 [768, 4096], P('head'), may hold values from -24 to 24
- q_second: bfloat16 [768, 4096], P('head'), may hold values from -24 to 24
- k_cache: bfloat16 [32768, 16, 128], P('ctx', 'head'), may hold values from -8 to 8
- v_cache: bfloat16 [32768, 16, 128], P('ctx', 'head'), may hold values from -6 to 6
- kept_blocks: int32 [8, 8], P('ctx'), may hold values from 0 to 31, as said below
- kept_count: int32 [8], P('ctx'), may hold values from 1 to 8, 16 in all
Outputs:
- out_first: bfloat16 [768, 4096], P('ctx', 'head')
- out_second: bfloat16 [768, 4096], P('ctx', 'head')
Inputs may be any that keep to these rules, and one draw needn't show every extreme that they name: `kept_blocks`: row s lists distinct block numbers of shard s; only its first kept_count[s] entries are kept. `kept_count`: the counts sum to 16; the largest is 8.
All inputs are finite; a program needn't handle non-finite values. No bound on the sum of `kept_count` on one device may be relied on, other than what follows from the above.
Results may differ from a plain program's by a relative error of at most 0.022.
Values may be sent and summed in bfloat16 or wider, within the bound.
No kernel may reach another device: no remote copies, remote signals or barrier semaphores. Data moves between devices by JAX's collectives and lax.ppermute only.
A program may use at most 128 MiB of HBM per device.

v0:
```python
import functools
import math

import jax
import jax.numpy as jnp
from jax import lax
from jax.experimental import pallas as pl
from jax.experimental.pallas import tpu as pltpu
from jax.sharding import PartitionSpec as P


HD = 128
QPS = 168
BLK = 128
LANES = 128
SCALE = QPS ** (-0.5) * math.log2(math.e)
AXES = ("ctx", "head")
ATTEND_BYTES = 24 << 20
MERGE_BYTES = 8 << 20


def with_ones(values):
    return jnp.concatenate([values, jnp.ones_like(values)], axis=1)


def stacked_queries(query_refs, group_size):
    parts = []
    for head in range(group_size):
        for ref in query_refs:
            for item in range(ref.shape[0]):
                parts.append(ref[item, 0, :, head * HD : (head + 1) * HD])
    return jnp.concatenate(parts, axis=0)


def raw_scores(queries, keys):
    return SCALE * lax.dot_general(
        queries, keys, (((1,), (1,)), ((), ())), preferred_element_type=jnp.float32
    )


def chain_rows(total):
    return math.gcd(total, 384)


def in_terms(level):
    high = level.astype(jnp.bfloat16).astype(jnp.float32)
    rest = level - high
    middle = rest.astype(jnp.bfloat16).astype(jnp.float32)
    return high, middle, rest - middle


def write_partial(out_refs, held_ref, stat_ref, place_ref, chains, group_size, group, rows):
    values, levels = [], []
    for top, summed in chains:
        total = summed[:, HD:]
        values.append((summed[:, :HD] / total).astype(jnp.bfloat16))
        levels.append(in_terms(top + jnp.log2(total)))
    value = jnp.concatenate(values, axis=0)
    terms = [jnp.concatenate(term, axis=0) for term in zip(*levels)]
    kv_local = pl.num_programs(0)
    count = held_ref.shape[0]
    heads = (held_ref.shape[2] - LANES) // HD
    lane = lax.broadcasted_iota(jnp.int32, (rows, LANES), 1)
    for item in range(count):
        place = place_ref[item]
        stat = stat_ref[place]
        for head in range(group_size):
            column = group * group_size + head
            at = (head * count + item) * rows
            start = pl.multiple_of(column * HD, HD)
            held_ref[place, :, pl.ds(start, HD)] = value[at : at + rows]
            for order, term in enumerate(terms):
                stat = jnp.where(lane == order * heads + column, term[at : at + rows], stat)
        stat_ref[place] = stat

    @pl.when(group == kv_local - 1)
    def _():
        held_ref[:, :, heads * HD :] = stat_ref[...].astype(jnp.bfloat16)
        share = count // len(out_refs)
        for index, out_ref in enumerate(out_refs):
            out_ref[...] = held_ref[index * share : (index + 1) * share]


def dense_kernel(place_ref, column_ref, *refs, pieces, outs, group_size, block_keys):
    query_refs = refs[:pieces]
    key_ref, value_ref, _ = refs[pieces : pieces + 3]
    out_refs = refs[pieces + 3 : pieces + 3 + outs]
    held_ref, stat_ref = refs[pieces + 3 + outs :]
    group = pl.program_id(0)
    rows = query_refs[0].shape[2]

    @pl.when(group == 0)
    def _():
        stat_ref[...] = jnp.zeros_like(stat_ref)

    queries = stacked_queries(query_refs, group_size)
    size = chain_rows(queries.shape[0])
    starts = range(0, queries.shape[0], size)
    chains = [None for _ in starts]
    for step in range(key_ref.shape[1] // block_keys):
        span = pl.ds(step * block_keys, block_keys)
        keys, values = key_ref[0, span, :], with_ones(value_ref[0, span, :])
        for index, start in enumerate(starts):
            scores = raw_scores(queries[start : start + size], keys)
            newtop = jnp.max(scores, axis=1, keepdims=True)
            if chains[index] is not None:
                newtop = jnp.maximum(chains[index][0], newtop)
            weights = jnp.exp2(scores - newtop).astype(jnp.bfloat16)
            summed = jnp.dot(weights, values, preferred_element_type=jnp.float32)
            if chains[index] is not None:
                top, before = chains[index]
                summed = before * jnp.exp2(top - newtop) + summed
            chains[index] = (newtop, summed)
    write_partial(out_refs, held_ref, stat_ref, place_ref, chains, group_size, group, rows)


def kept_kernel(place_ref, column_ref, list_ref, count_ref, *refs, pieces, outs, group_size):
    query_refs = refs[:pieces]
    key_ref, value_ref, _ = refs[pieces : pieces + 3]
    out_refs = refs[pieces + 3 : pieces + 3 + outs]
    held_ref, stat_ref, top_ref, sum_ref, keys_ref, values_ref, sems = refs[pieces + 3 + outs :]
    group = pl.program_id(0)
    rows = query_refs[0].shape[2]
    kept = count_ref[0]
    few, many = 2, 4
    loaded = jnp.where(kept <= few, few, pl.cdiv(kept, many) * many)

    def copies(slot):
        block = list_ref[jnp.minimum(slot, kept - 1)]
        span = pl.ds(pl.multiple_of(block * BLK, BLK), BLK)
        return [
            pltpu.make_async_copy(source.at[:, span, :], held.at[slot], sems.at[which, slot])
            for which, (source, held) in enumerate(
                ((key_ref, keys_ref), (value_ref, values_ref))
            )
        ]

    @pl.when(group == 0)
    def _():
        stat_ref[...] = jnp.zeros_like(stat_ref)

        @pl.loop(0, loaded)
        def _(slot):
            for copy in copies(slot):
                copy.start()

        @pl.loop(0, loaded)
        def _(slot):
            for copy in copies(slot):
                copy.wait()

    queries = stacked_queries(query_refs, group_size)
    size = chain_rows(queries.shape[0])
    starts = range(0, queries.shape[0], size)

    def absorb(first, length, fresh):
        keys = jnp.concatenate([keys_ref[first + i, group] for i in range(length)], axis=0)
        values = jnp.concatenate([values_ref[first + i, group] for i in range(length)], axis=0)
        values = with_ones(values)
        slot = lax.broadcasted_iota(jnp.int32, (1, length * BLK), 1) // BLK + first
        for start in starts:
            span = pl.ds(start, size)
            scores = raw_scores(queries[start : start + size], keys)
            scores = jnp.where(slot < kept, scores, -jnp.inf)
            newtop = jnp.max(scores, axis=1, keepdims=True)
            if not fresh:
                top = top_ref[span, :1]
                newtop = jnp.maximum(top, newtop)
            weights = jnp.exp2(scores - newtop).astype(jnp.bfloat16)
            summed = jnp.dot(weights, values, preferred_element_type=jnp.float32)
            if not fresh:
                summed = sum_ref[span, :] * jnp.exp2(top - newtop) + summed
            sum_ref[span, :] = summed
            top_ref[span, :] = jnp.broadcast_to(newtop, (size, LANES))

    @pl.when(kept <= few)
    def _():
        absorb(0, few, True)

    @pl.when(kept > few)
    def _():
        absorb(0, many, True)

    @pl.loop(1, jnp.maximum(loaded // many, 1))
    def _(step):
        absorb(step * many, many, False)

    chains = [(top_ref[pl.ds(s, size), :1], sum_ref[pl.ds(s, size), :]) for s in starts]
    write_partial(out_refs, held_ref, stat_ref, place_ref, chains, group_size, group, rows)


def query_spec(piece, own, group_size, kept, half):
    block = (piece.shape[0], 1, piece.shape[2], group_size * HD)

    def index(group, *rest):
        column = group + rest[-3 if kept else -1][0] if own else group
        return (0, half, 0, column)

    return pl.BlockSpec(block, index)


def partial_call(pieces, places, column, keys, values, half, outs, after, kept=None):
    kv_local, length, _ = keys.shape
    heads = pieces[-1].shape[3] // HD
    group_size = heads // kv_local
    rows = pieces[0].shape[2]
    count = sum(piece.shape[0] for piece in pieces)
    width = heads * HD + LANES
    stacked = count * rows * group_size
    specs = [
        query_spec(piece, piece.shape[3] > heads * HD, group_size, kept is not None, half)
        for piece in pieces
    ]
    anywhere = pl.BlockSpec(memory_space=pl.ANY)
    out_shape = [jax.ShapeDtypeStruct((count // outs, rows, width), jnp.bfloat16)] * outs
    out_specs = [pl.BlockSpec((count // outs, rows, width), lambda *_: (0, 0, 0))] * outs
    scratch = [
        pltpu.VMEM((count, rows, width), jnp.bfloat16),
        pltpu.VMEM((count, rows, LANES), jnp.float32),
    ]
    if kept is None:
        whole = pl.BlockSpec((1, length, HD), lambda group, *_: (group, 0, 0))
        kernel = functools.partial(dense_kernel, block_keys=math.gcd(length, 512))
        operands, cache_specs, reads = (places, column), [whole, whole], length
    else:
        slots = pl.cdiv(kept[0].shape[0], 4) * 4
        kernel = kept_kernel
        operands, cache_specs, reads = (places, column, *kept), [anywhere, anywhere], 4 * BLK
        scratch += [
            pltpu.VMEM((stacked, LANES), jnp.float32),
            pltpu.VMEM((stacked, 2 * HD), jnp.float32),
            pltpu.VMEM((slots, kv_local, BLK, HD), jnp.bfloat16),
            pltpu.VMEM((slots, kv_local, BLK, HD), jnp.bfloat16),
            pltpu.SemaphoreType.DMA((2, slots)),
        ]
    return pl.pallas_call(
        functools.partial(kernel, pieces=len(pieces), outs=outs, group_size=group_size),
        grid_spec=pltpu.PrefetchScalarGridSpec(
            num_scalar_prefetch=len(operands),
            grid=(kv_local,),
            in_specs=specs + cache_specs + [anywhere],
            out_specs=out_specs,
            scratch_shapes=scratch,
        ),
        out_shape=out_shape,
        compiler_params=pltpu.CompilerParams(vmem_limit_bytes=ATTEND_BYTES),
        cost_estimate=pl.CostEstimate(
            flops=8 * stacked * reads * HD * kv_local,
            bytes_accessed=4 * reads * HD * kv_local,
            transcendentals=stacked * reads * kv_local,
        ),
    )(*operands, *pieces, keys, values, after)


def shares_of(parts, heads):
    levels = []
    for part in parts:
        terms = part[:, heads * HD :].astype(jnp.float32)
        level = terms + pltpu.roll(terms, LANES - heads, 1)
        levels.append(level + pltpu.roll(terms, LANES - 2 * heads, 1))
    best = functools.reduce(jnp.maximum, levels)
    shares = [jnp.exp2(level - best) for level in levels]
    total = functools.reduce(jnp.add, shares)
    return [share / total for share in shares], best + jnp.log2(total)


def weighted(parts, shares, head):
    columns = slice(head * HD, (head + 1) * HD)
    terms = [
        share[:, head : head + 1] * part[:, columns].astype(jnp.float32)
        for part, share in zip(parts, shares)
    ]
    return functools.reduce(jnp.add, terms).astype(jnp.bfloat16)


def merge_kernel(*refs, onto):
    out_ref = refs[-1]
    parts = []
    for ref in refs[: len(refs) - 1 - onto]:
        parts += [ref.at[index] for index in range(ref.shape[0])]
    heads = (parts[0].shape[1] - LANES) // HD
    shares, _ = shares_of(parts, heads)
    for head in range(heads):
        out_ref[0, :, head * HD : (head + 1) * HD] = weighted(parts, shares, head)


def merge(parts, half=0, halves=1, onto=None):
    _, rows, width = parts[0].shape
    sources = sum(part.shape[0] for part in parts)
    columns = width - LANES
    in_specs = [pl.BlockSpec(part.shape, lambda i: (0, 0, 0)) for part in parts]
    operands = list(parts)
    if onto is not None:
        in_specs.append(pl.BlockSpec(memory_space=pl.ANY))
        operands.append(onto)
    return pl.pallas_call(
        functools.partial(merge_kernel, onto=onto is not None),
        grid=(1,),
        in_specs=in_specs,
        out_specs=pl.BlockSpec((1, rows, columns), lambda i: (half, 0, 0)),
        out_shape=jax.ShapeDtypeStruct((halves, rows, columns), jnp.bfloat16),
        input_output_aliases={} if onto is None else {len(parts): 0},
        compiler_params=pltpu.CompilerParams(vmem_limit_bytes=MERGE_BYTES),
        cost_estimate=pl.CostEstimate(
            flops=4 * sources * rows * columns,
            bytes_accessed=2 * sources * rows * width,
            transcendentals=0,
        ),
    )(*operands)


def pair_kernel(spot_ref, mine_ref, theirs_ref, _, *out_refs):
    heads = (mine_ref.shape[2] - LANES) // HD
    lane = lax.broadcasted_iota(jnp.int32, (mine_ref.shape[1], LANES), 1)
    for offset, out_ref in enumerate(out_refs):
        spot = spot_ref[0] ^ offset
        parts = [mine_ref.at[spot], theirs_ref.at[spot]]
        shares, level = shares_of(parts, heads)
        for head in range(heads):
            out_ref[0, :, head * HD : (head + 1) * HD] = weighted(parts, shares, head)
        high, middle, low = in_terms(level)
        stat = jnp.where(lane < 2 * heads, pltpu.roll(middle, heads, 1), pltpu.roll(low, 2 * heads, 1))
        out_ref[0, :, heads * HD :] = jnp.where(lane < heads, high, stat).astype(jnp.bfloat16)


def merge_pair(mine, theirs, spot, after):
    owners, rows, width = mine.shape
    whole = pl.BlockSpec(mine.shape, lambda *_: (0, 0, 0))
    return pl.pallas_call(
        pair_kernel,
        grid_spec=pltpu.PrefetchScalarGridSpec(
            num_scalar_prefetch=1,
            grid=(1,),
            in_specs=[whole, whole, pl.BlockSpec(memory_space=pl.ANY)],
            out_specs=[pl.BlockSpec((1, rows, width), lambda *_: (0, 0, 0))] * owners,
        ),
        out_shape=[jax.ShapeDtypeStruct((1, rows, width), jnp.bfloat16)] * owners,
        compiler_params=pltpu.CompilerParams(vmem_limit_bytes=MERGE_BYTES),
        cost_estimate=pl.CostEstimate(
            flops=8 * owners * rows * width,
            bytes_accessed=6 * owners * rows * width,
            transcendentals=0,
        ),
    )(spot, mine, theirs, after)


def to_owners(part):
    return lax.all_to_all(part, "ctx", split_axis=0, concat_axis=0, tiled=True)


def swapped(shape, ctx_bit, head_bit):
    head = shape["head"]
    spots = [(c, h) for c in range(shape["ctx"]) for h in range(head)]
    return [(c * head + h, (c ^ ctx_bit) * head + (h ^ head_bit)) for c, h in spots]


def relayed(shape, q_first, q_second, k_cache):
    head = shape["head"]
    me = lax.axis_index("head")
    spot = lax.axis_index("ctx")
    low = spot % 2
    rows, wide = q_first.shape
    mine = wide // head
    half = rows // 2

    def columns_of(block, other, start, count):
        return lax.dynamic_slice(block, (start, other * mine), (count, mine))

    near = jnp.stack([columns_of(block, me ^ 1, 0, rows) for block in (q_second, q_first)])
    got = []
    for block in (q_second, q_first):
        pair = [columns_of(block, me ^ bit, low * half, half) for bit in (2, 3)]
        got.append([lax.ppermute(x, AXES, swapped(shape, 0, b)) for x, b in zip(pair, (2, 3))])
    near = lax.ppermute(near, AXES, swapped(shape, 0, 1))
    pieces = []
    for at, block in enumerate((q_second, q_first)):
        same, cross = got[at]
        other = lax.ppermute(jnp.stack([same, cross]), AXES, swapped(shape, 1, 0))
        pieces.append(
            [
                block.reshape(2, half, wide),
                near[at].reshape(2, half, mine),
                same.reshape(1, half, mine),
                cross.reshape(1, half, mine),
                other,
            ]
        )
    owners = []
    for bit in (0, 1):
        owners += [2 * (me ^ bit), 2 * (me ^ bit) + 1]
    owners += [2 * (me ^ 2) + low, 2 * (me ^ 3) + low]
    owners += [2 * (me ^ 2) + 1 - low, 2 * (me ^ 3) + 1 - low]
    places = [
        owner // 2 + jnp.where(owner % 2 == low, len(owners) // 2, 0) for owner in owners
    ]
    places = jnp.stack(places).astype(jnp.int32)
    column = jnp.reshape(me * k_cache.shape[1], (1,)).astype(jnp.int32)
    return pieces[0], pieces[1], places, column


def in_halves(pieces, halves):
    return [x.reshape(x.shape[0], halves, x.shape[1] // halves, x.shape[2]) for x in pieces]


def shards(shape, q_first, q_second, k_cache, v_cache, kept_blocks, kept_count):
    ctx, head = shape["ctx"], shape["head"]
    keys, values = jnp.swapaxes(k_cache, 0, 1), jnp.swapaxes(v_cache, 0, 1)
    owned = q_first.shape[0] * head // ctx
    kept = (kept_blocks[0], kept_count)
    if head == 4 and ctx == 2 * head and owned % 32 == 0:
        second, first, places, column = relayed(shape, q_first, q_second, k_cache)
        first, second = in_halves(first, 2), in_halves(second, 1)
        spot = jnp.reshape(lax.axis_index("ctx") // 2, (1,)).astype(jnp.int32)

        def across_pair(send):
            return lax.ppermute(send, AXES, swapped(shape, 1, 0))

        def across_owners(parts):
            moved = []
            for offset, part in enumerate(parts):
                if offset:
                    part = lax.ppermute(part, AXES, swapped(shape, 2 * offset, 0))
                moved.append(part)
            return moved

        def attend(pieces, half, after, kept=None):
            return partial_call(pieces, places, column, keys, values, half, 2, after, kept)

        send_s, keep_s = attend(second, 0, spot, kept)
        got_s = across_pair(send_s)
        send_a, keep_a = attend(first, 0, send_s)
        got_a = across_pair(send_a)
        pair_s = merge_pair(keep_s, got_s, spot, send_a)
        final_s = across_owners(pair_s)
        send_b, keep_b = attend(first, 1, pair_s[0])
        got_b = across_pair(send_b)
        pair_a = merge_pair(keep_a, got_a, spot, send_b)
        final_a = across_owners(pair_a)
        pair_b = merge_pair(keep_b, got_b, spot, pair_a[0])
        final_b = across_owners(pair_b)
        out_second = merge(final_s)[0]
        out_first = merge(final_b, 1, 2, merge(final_a, 0, 2))
        return (out_first.reshape(owned, -1), out_second)
    second, first = (
        [lax.all_to_all(block, "head", split_axis=1, concat_axis=0, tiled=True)[None, None]]
        for block in (q_second, q_first)
    )
    nothing = jnp.zeros((1,), jnp.int32)
    outs = []
    for pieces, which in ((first, None), (second, kept)):
        (part,) = partial_call(pieces, nothing, nothing, keys, values, 0, 1, nothing, which)
        outs.append(merge([to_owners(part.reshape(ctx, owned, part.shape[2]))])[0])
    return tuple(outs)


def layered(body, *operands):
    return body(*operands)


def solution(mesh):
    placed = (
        P("head", None),
        P("head", None),
        P("ctx", "head", None),
        P("ctx", "head", None),
        P("ctx", None),
        P("ctx"),
    )
    return jax.shard_map(
        functools.partial(layered, functools.partial(shards, dict(mesh.shape))),
        mesh=mesh,
        in_specs=placed,
        out_specs=(P("ctx", "head"), P("ctx", "head")),
        check_vma=False,
    )
```

profile of v0, /device:TPU:0, one launch (start us, length us, event | category | flops | bytes accessed | tf_op | source)
XLA Modules:
  0.0 137.4 jit_solution(5359515459595329294)
XLA Ops:
  0.7 1.2 fusion
  1.8 3.0 %collective-permute-start.4 = (bf16[96,1024]{1,0:T(8,128)(2,1)S(1)}, bf16[96,1024]{1,0:T(8,128)(2,1)S(1)}, u32[]{:S(2)}, u32[]{:S(2)}) collective-permute-start(bf16[96,1024]{1,0:T(8,128)(2,1)S(1)} %get-tuple-element.39), channel_id=1, source_target_pairs={{0,2},{1,3},{2,0},{3,1},{4,6},{5,7},{6,4},{7,5},{8,10},{9,11},{10,... | collective-permute-start | bytes 589832 | tf_op jit(solution)/shard_map/ppermute | solution.py:373
  4.9 1.0 dynamic-slice_bitcast_fusion.1
  5.9 1.0 dynamic-slice_bitcast_fusion
  6.9 1.0 pad_maximum_fusion
  8.9 1.9 %collective-permute-start.1 = (bf16[96,1024]{1,0:T(8,128)(2,1)}, bf16[96,1024]{1,0:T(8,128)(2,1)S(1)}, u32[]{:S(2)}, u32[]{:S(2)}) collective-permute-start(bf16[96,1024]{1,0:T(8,128)(2,1)} %get-tuple-element.41), channel_id=1, source_target_pairs={{0,2},{1,3},{2,0},{3,1},{4,6},{5,7},{6,4},{7,5},{8,10},{9,11},{10,... | collective-permute-start | bytes 589832 | tf_op jit(solution)/shard_map/ppermute | solution.py:373
  10.9 3.5 %collective-permute-done.5 = bf16[96,1024]{1,0:T(8,128)(2,1)S(1)} collective-permute-done((bf16[96,1024]{1,0:T(8,128)(2,1)S(1)}, bf16[96,1024]{1,0:T(8,128)(2,1)S(1)}, u32[]{:S(2)}, u32[]{:S(2)}) %collective-permute-start.5) | collective-permute-done | bytes 196640 | tf_op jit(solution)/shard_map/ppermute | solution.py:373
  15.9 1.5 %collective-permute-start.6 = (bf16[2,96,1024]{2,1,0:T(8,128)(2,1)}, bf16[2,96,1024]{2,1,0:T(8,128)(2,1)}, u32[]{:S(2)}, u32[]{:S(2)}) collective-permute-start(bf16[2,96,1024]{2,1,0:T(8,128)(2,1)} %pad_maximum_fusion.2), channel_id=1, source_target_pairs={{0,4},{1,5},{2,6},{3,7},{4,0},{5,1},{6,2},{7,3},{8,12},{9,13},{10,... | collective-permute-start | bytes 1179656 | tf_op jit(solution)/shard_map/ppermute | solution.py:378
  17.4 6.6 %copy_bitcast_fusion = (bf16[4,4096,128]{2,1,0:T(8,128)(2,1)}, bf16[4,4096,128]{2,1,0:T(8,128)(2,1)}) fusion(bf16[4096,4,128]{2,1,0:T(4,128)(2,1)} %param.9, bf16[4096,4,128]{2,1,0:T(4,128)(2,1)} %param.8), kind=kLoop, calls=%fused_computation | loop fusion | bytes 16777216 | tf_op jit(solution)/shard_map/transpose | solution.py:407
  26.3 1.2 fusion.2
  27.8 2.2 %copy-done = bf16[4,4096,128]{2,1,0:T(8,128)(2,1)S(1)} copy-done((bf16[4,4096,128]{2,1,0:T(8,128)(2,1)S(1)}, bf16[4,4096,128]{2,1,0:T(8,128)(2,1)}, u32[]{:S(2)}) %copy-start) | copy-done | bytes 4194328
  30.0 2.2 %copy-done.2 = bf16[4,4096,128]{2,1,0:T(8,128)(2,1)S(1)} copy-done((bf16[4,4096,128]{2,1,0:T(8,128)(2,1)S(1)}, bf16[4,4096,128]{2,1,0:T(8,128)(2,1)}, u32[]{:S(2)}) %copy-start.2) | copy-done | bytes 4194328
  33.1 7.6 %shard_map.77 = (bf16[4,96,1152]{2,1,0:T(8,128)(2,1)S(1)}, bf16[4,96,1152]{2,1,0:T(8,128)(2,1)S(1)}) custom-call(s32[8]{0:T(128)S(1)} %stack.62.place_ref, s32[1]{0:T(128)} %bitcast.9.column_ref, s32[8]{0:T(128)S(1)} %bitcast.50, s32[1]{0:T(128)S(6)} %copy.14.count_ref, bf16[2,1,96,4096]{3,2,1,0:T(8,128)(2,1)S(1)} %bitcast.35, ...), custom_call_target="tpu_custom_call" | custom-call | flops 3221225472 | bytes 1048576 | tf_op jit(solution)/shard_map/pallas_call | solution.py:236
  40.7 1.9 %collective-permute-start.7 = (bf16[4,96,1152]{2,1,0:T(8,128)(2,1)S(1)}, bf16[4,96,1152]{2,1,0:T(8,128)(2,1)S(1)}, u32[]{:S(2)}, u32[]{:S(2)}) collective-permute-start(bf16[4,96,1152]{2,1,0:T(8,128)(2,1)S(1)} %get-tuple-element.21.refs_7_), channel_id=1, source_target_pairs={{0,4},{1,5},{2,6},{3,7},{4,0},{5,1},{6,2},{7,3},{8,12},{9,13},{10,... | collective-permute-start | bytes 2654216 | tf_op jit(solution)/shard_map/ppermute | solution.py:416
  42.6 17.7 %shard_map.78 = (bf16[4,48,1152]{2,1,0:T(8,128)(2,1)S(1)}, bf16[4,48,1152]{2,1,0:T(8,128)(2,1)S(1)}) custom-call(s32[8]{0:T(128)S(1)} %stack.62.place_ref, s32[1]{0:T(128)} %bitcast.9.column_ref, bf16[2,2,48,4096]{3,2,1,0:T(8,128)(2,1)S(1)} %bitcast.36, bf16[2,2,48,1024]{3,2,1,0:T(8,128)(2,1)S(1)} %bitcast.38, bf16[1,2,48,1024]{3,2,1,0:T(8,128)(2,1)S(1)} %bitcast.42, ...), custom_call_target="tpu_custom_call" | custom-call | flops 12884901888 | bytes 8388608 | tf_op jit(solution)/shard_map/pallas_call | solution.py:236
  60.6 2.0 %collective-permute-done.7.theirs_ref = bf16[4,96,1152]{2,1,0:T(8,128)(2,1)S(1)} collective-permute-done((bf16[4,96,1152]{2,1,0:T(8,128)(2,1)S(1)}, bf16[4,96,1152]{2,1,0:T(8,128)(2,1)S(1)}, u32[]{:S(2)}, u32[]{:S(2)}) %collective-permute-start.7) | collective-permute-done | bytes 884768 | tf_op jit(solution)/shard_map/ppermute | solution.py:416
  62.6 1.9 %shard_map.79 = (bf16[1,96,1152]{2,1,0:T(8,128)(2,1)S(1)}, bf16[1,96,1152]{2,1,0:T(8,128)(2,1)S(1)}, bf16[1,96,1152]{2,1,0:T(8,128)(2,1)S(1)}, bf16[1,96,1152]{2,1,0:T(8,128)(2,1)S(1)}) custom-call(s32[1]{0:T(128)} %bitcast.refs_7_.spot_ref, bf16[4,96,1152]{2,1,0:T(8,128)(2,1)S(1)} %get-tuple-element.20.mine_ref, ...), custom_call_target="tpu_custom_call" | custom-call | flops 3538944 | bytes 2654208 | tf_op jit(solution)/shard_map/pallas_call | solution.py:329
  64.5 17.9 %shard_map.80 = (bf16[4,48,1152]{2,1,0:T(8,128)(2,1)S(1)}, bf16[4,48,1152]{2,1,0:T(8,128)(2,1)S(1)}) custom-call(s32[8]{0:T(128)S(1)} %stack.62.place_ref, s32[1]{0:T(128)} %bitcast.9.column_ref, bf16[2,2,48,4096]{3,2,1,0:T(8,128)(2,1)S(1)} %bitcast.37, bf16[2,2,48,1024]{3,2,1,0:T(8,128)(2,1)S(1)} %bitcast.39, bf16[1,2,48,1024]{3,2,1,0:T(8,128)(2,1)S(1)} %bitcast.43, ...), custom_call_target="tpu_custom_call" | custom-call | flops 12884901888 | bytes 8388608 | tf_op jit(solution)/shard_map/pallas_call | solution.py:236
  82.4 2.5 %collective-permute-start.8 = (bf16[4,48,1152]{2,1,0:T(8,128)(2,1)S(1)}, bf16[4,48,1152]{2,1,0:T(8,128)(2,1)S(1)}, u32[]{:S(2)}, u32[]{:S(2)}) collective-permute-start(bf16[4,48,1152]{2,1,0:T(8,128)(2,1)S(1)} %get-tuple-element.25._), channel_id=1, source_target_pairs={{0,4},{1,5},{2,6},{3,7},{4,0},{5,1},{6,2},{7,3},{8,12},{9,13},{10,... | collective-permute-start | bytes 1327112 | tf_op jit(solution)/shard_map/ppermute | solution.py:416
  85.0 1.2 shard_map.81
  86.1 1.5 %collective-permute-start.13 = (bf16[1,48,1152]{2,1,0:T(8,128)(2,1)S(1)}, bf16[1,48,1152]{2,1,0:T(8,128)(2,1)S(1)}, u32[]{:S(2)}, u32[]{:S(2)}) collective-permute-start(bf16[1,48,1152]{2,1,0:T(8,128)(2,1)S(1)} %get-tuple-element.32), channel_id=1, source_target_pairs={{0,8},{1,9},{2,10},{3,11},{4,12},{5,13},{6,14},{7,15},{8,0},{9,1},... | collective-permute-start | bytes 331784 | tf_op jit(solution)/shard_map/ppermute | solution.py:422
  88.2 11.3 %collective-permute-start.14 = (bf16[1,48,1152]{2,1,0:T(8,128)(2,1)S(1)}, bf16[1,48,1152]{2,1,0:T(8,128)(2,1)S(1)}, u32[]{:S(2)}, u32[]{:S(2)}) collective-permute-start(bf16[1,48,1152]{2,1,0:T(8,128)(2,1)S(1)} %get-tuple-element.33), channel_id=1, source_target_pairs={{0,16},{1,17},{2,18},{3,19},{4,20},{5,21},{6,22},{7,23},{8,24},{9,... | collective-permute-start | bytes 331784 | tf_op jit(solution)/shard_map/ppermute | solution.py:422
  99.6 4.5 %collective-permute-start.18 = (bf16[1,96,1152]{2,1,0:T(8,128)(2,1)S(1)}, bf16[1,96,1152]{2,1,0:T(8,128)(2,1)S(1)}, u32[]{:S(2)}, u32[]{:S(2)}) collective-permute-start(bf16[1,96,1152]{2,1,0:T(8,128)(2,1)S(1)} %get-tuple-element.37), channel_id=1, source_target_pairs={{0,24},{1,25},{2,26},{3,27},{4,28},{5,29},{6,30},{7,31},{8,16},{9,... | collective-permute-start | bytes 663560 | tf_op jit(solution)/shard_map/ppermute | solution.py:422
  104.1 1.2 shard_map.82
  105.3 10.4 %collective-permute-start.10 = (bf16[1,48,1152]{2,1,0:T(8,128)(2,1)S(1)}, bf16[1,48,1152]{2,1,0:T(8,128)(2,1)S(1)}, u32[]{:S(2)}, u32[]{:S(2)}) collective-permute-start(bf16[1,48,1152]{2,1,0:T(8,128)(2,1)S(1)} %get-tuple-element.29), channel_id=1, source_target_pairs={{0,8},{1,9},{2,10},{3,11},{4,12},{5,13},{6,14},{7,15},{8,0},{9,1},... | collective-permute-start | bytes 331784 | tf_op jit(solution)/shard_map/ppermute | solution.py:422
  115.7 4.8 %collective-permute-done.15.refs_3_ = bf16[1,48,1152]{2,1,0:T(8,128)(2,1)S(1)} collective-permute-done((bf16[1,48,1152]{2,1,0:T(8,128)(2,1)S(1)}, bf16[1,48,1152]{2,1,0:T(8,128)(2,1)S(1)}, u32[]{:S(2)}, u32[]{:S(2)}) %collective-permute-start.15) | collective-permute-done | bytes 110624 | tf_op jit(solution)/shard_map/ppermute | solution.py:422
  120.5 7.8 %collective-permute-start.11 = (bf16[1,48,1152]{2,1,0:T(8,128)(2,1)S(1)}, bf16[1,48,1152]{2,1,0:T(8,128)(2,1)S(1)}, u32[]{:S(2)}, u32[]{:S(2)}) collective-permute-start(bf16[1,48,1152]{2,1,0:T(8,128)(2,1)S(1)} %get-tuple-element.30), channel_id=1, source_target_pairs={{0,16},{1,17},{2,18},{3,19},{4,20},{5,21},{6,22},{7,23},{8,24},{9,... | collective-permute-start | bytes 331784 | tf_op jit(solution)/shard_map/ppermute | solution.py:422
  128.3 2.5 %collective-permute-start.12 = (bf16[1,48,1152]{2,1,0:T(8,128)(2,1)S(1)}, bf16[1,48,1152]{2,1,0:T(8,128)(2,1)S(1)}, u32[]{:S(2)}, u32[]{:S(2)}) collective-permute-start(bf16[1,48,1152]{2,1,0:T(8,128)(2,1)S(1)} %get-tuple-element.31), channel_id=1, source_target_pairs={{0,24},{1,25},{2,26},{3,27},{4,28},{5,29},{6,30},{7,31},{8,16},{9,... | collective-permute-start | bytes 331784 | tf_op jit(solution)/shard_map/ppermute | solution.py:422
  130.8 1.0 shard_map.83.refs_4_
  131.8 1.3 shard_map.85
  133.1 3.2 %collective-permute-done.11.refs_2_ = bf16[1,48,1152]{2,1,0:T(8,128)(2,1)S(1)} collective-permute-done((bf16[1,48,1152]{2,1,0:T(8,128)(2,1)S(1)}, bf16[1,48,1152]{2,1,0:T(8,128)(2,1)S(1)}, u32[]{:S(2)}, u32[]{:S(2)}) %collective-permute-start.11) | collective-permute-done | bytes 110624 | tf_op jit(solution)/shard_map/ppermute | solution.py:422
  136.4 1.0 shard_map.84
  (41 shorter events, 6.2 us)
Async XLA Ops:
  0.6 7.5 %copy-start.4 = (bf16[192,4096]{1,0:T(8,128)(2,1)S(1)}, bf16[192,4096]{1,0:T(8,128)(2,1)}, u32[]{:S(2)}) copy-start(bf16[192,4096]{1,0:T(8,128)(2,1)} %param.6) | copy-start | bytes 4718596
  1.8 9.0 %collective-permute-start.4 = (bf16[96,1024]{1,0:T(8,128)(2,1)S(1)}, bf16[96,1024]{1,0:T(8,128)(2,1)S(1)}, u32[]{:S(2)}, u32[]{:S(2)}) collective-permute-start(bf16[96,1024]{1,0:T(8,128)(2,1)S(1)} %get-tuple-element.39), channel_id=1, source_target_pairs={{0,2},{1,3},{2,0},{3,1},{4,6},{5,7},{6,4},{7,5},{8,10},{9,11},{10,... | collective-permute-start | bytes 589832 | tf_op jit(solution)/shard_map/ppermute | solution.py:373
  4.9 9.5 %collective-permute-start.5 = (bf16[96,1024]{1,0:T(8,128)(2,1)S(1)}, bf16[96,1024]{1,0:T(8,128)(2,1)S(1)}, u32[]{:S(2)}, u32[]{:S(2)}) collective-permute-start(bf16[96,1024]{1,0:T(8,128)(2,1)S(1)} %get-tuple-element.38), channel_id=1, source_target_pairs={{0,3},{1,2},{2,1},{3,0},{4,7},{5,6},{6,5},{7,4},{8,11},{9,10},{10,... | collective-permute-start | bytes 589832 | tf_op jit(solution)/shard_map/ppermute | solution.py:373
  7.9 18.4 %collective-permute-start = (bf16[2,192,1024]{2,1,0:T(8,128)(2,1)}, bf16[2,192,1024]{2,1,0:T(8,128)(2,1)}, u32[]{:S(2)}, u32[]{:S(2)}) collective-permute-start(bf16[2,192,1024]{2,1,0:T(8,128)(2,1)} %pad_maximum_fusion), channel_id=1, source_target_pairs={{0,1},{1,0},{2,3},{3,2},{4,5},{5,4},{6,7},{7,6},{8,9},{9,8},{10,11... | collective-permute-start | bytes 2359304 | tf_op jit(solution)/shard_map/ppermute | solution.py:374
  8.9 15.8 %collective-permute-start.1 = (bf16[96,1024]{1,0:T(8,128)(2,1)}, bf16[96,1024]{1,0:T(8,128)(2,1)S(1)}, u32[]{:S(2)}, u32[]{:S(2)}) collective-permute-start(bf16[96,1024]{1,0:T(8,128)(2,1)} %get-tuple-element.41), channel_id=1, source_target_pairs={{0,2},{1,3},{2,0},{3,1},{4,6},{5,7},{6,4},{7,5},{8,10},{9,11},{10,... | collective-permute-start | bytes 589832 | tf_op jit(solution)/shard_map/ppermute | solution.py:373
  10.9 13.9 %collective-permute-start.2 = (bf16[96,1024]{1,0:T(8,128)(2,1)}, bf16[96,1024]{1,0:T(8,128)(2,1)}, u32[]{:S(2)}, u32[]{:S(2)}) collective-permute-start(bf16[96,1024]{1,0:T(8,128)(2,1)} %get-tuple-element.40), channel_id=1, source_target_pairs={{0,3},{1,2},{2,1},{3,0},{4,7},{5,6},{6,5},{7,4},{8,11},{9,10},{10,... | collective-permute-start | bytes 589832 | tf_op jit(solution)/shard_map/ppermute | solution.py:373
  15.2 0.7 copy-start.5
  15.9 11.9 %copy-start.3 = (bf16[192,4096]{1,0:T(8,128)(2,1)S(1)}, bf16[192,4096]{1,0:T(8,128)(2,1)}, u32[]{:S(2)}) copy-start(bf16[192,4096]{1,0:T(8,128)(2,1)} %param.7) | copy-start | bytes 4718596
  15.9 11.9 %copy-start.7 = (s32[1,8]{1,0:T(1,128)S(1)}, s32[1,8]{1,0:T(1,128)}, u32[]{:S(2)}) copy-start(s32[1,8]{1,0:T(1,128)} %param.10) | copy-start | bytes 100
  15.9 11.9 %collective-permute-start.6 = (bf16[2,96,1024]{2,1,0:T(8,128)(2,1)}, bf16[2,96,1024]{2,1,0:T(8,128)(2,1)}, u32[]{:S(2)}, u32[]{:S(2)}) collective-permute-start(bf16[2,96,1024]{2,1,0:T(8,128)(2,1)} %pad_maximum_fusion.2), channel_id=1, source_target_pairs={{0,4},{1,5},{2,6},{3,7},{4,0},{5,1},{6,2},{7,3},{8,12},{9,13},{10,... | collective-permute-start | bytes 1179656 | tf_op jit(solution)/shard_map/ppermute | solution.py:378
  25.7 16.8 %collective-permute-start.3 = (bf16[2,96,1024]{2,1,0:T(8,128)(2,1)S(1)}, bf16[2,96,1024]{2,1,0:T(8,128)(2,1)S(1)}, u32[]{:S(2)}, u32[]{:S(2)}) collective-permute-start(bf16[2,96,1024]{2,1,0:T(8,128)(2,1)S(1)} %pad_maximum_fusion.1), channel_id=1, source_target_pairs={{0,4},{1,5},{2,6},{3,7},{4,0},{5,1},{6,2},{7,3},{8,12},{9,13},{10,... | collective-permute-start | bytes 1179656 | tf_op jit(solution)/shard_map/ppermute | solution.py:378
  27.8 2.2 %copy-start = (bf16[4,4096,128]{2,1,0:T(8,128)(2,1)S(1)}, bf16[4,4096,128]{2,1,0:T(8,128)(2,1)}, u32[]{:S(2)}) copy-start(bf16[4,4096,128]{2,1,0:T(8,128)(2,1)} %get-tuple-element.44.refs_6_) | copy-start | bytes 12582916
  30.0 2.2 %copy-start.2 = (bf16[4,4096,128]{2,1,0:T(8,128)(2,1)S(1)}, bf16[4,4096,128]{2,1,0:T(8,128)(2,1)}, u32[]{:S(2)}) copy-start(bf16[4,4096,128]{2,1,0:T(8,128)(2,1)} %get-tuple-element.45.refs_5_) | copy-start | bytes 12582916
  32.2 0.9 copy-start.6
  33.1 9.5 %copy-start.1 = (bf16[4,4096,128]{2,1,0:T(8,128)(2,1)S(1)}, bf16[4,4096,128]{2,1,0:T(8,128)(2,1)}, u32[]{:S(2)}) copy-start(bf16[4,4096,128]{2,1,0:T(8,128)(2,1)} %get-tuple-element.44.refs_6_) | copy-start | bytes 12582916
  40.7 21.9 %collective-permute-start.7 = (bf16[4,96,1152]{2,1,0:T(8,128)(2,1)S(1)}, bf16[4,96,1152]{2,1,0:T(8,128)(2,1)S(1)}, u32[]{:S(2)}, u32[]{:S(2)}) collective-permute-start(bf16[4,96,1152]{2,1,0:T(8,128)(2,1)S(1)} %get-tuple-element.21.refs_7_), channel_id=1, source_target_pairs={{0,4},{1,5},{2,6},{3,7},{4,0},{5,1},{6,2},{7,3},{8,12},{9,13},{10,... | collective-permute-start | bytes 2654216 | tf_op jit(solution)/shard_map/ppermute | solution.py:416
  60.3 24.7 %collective-permute-start.9 = (bf16[4,48,1152]{2,1,0:T(8,128)(2,1)S(1)}, bf16[4,48,1152]{2,1,0:T(8,128)(2,1)S(1)}, u32[]{:S(2)}, u32[]{:S(2)}) collective-permute-start(bf16[4,48,1152]{2,1,0:T(8,128)(2,1)S(1)} %get-tuple-element.22._), channel_id=1, source_target_pairs={{0,4},{1,5},{2,6},{3,7},{4,0},{5,1},{6,2},{7,3},{8,12},{9,13},{10,... | collective-permute-start | bytes 1327112 | tf_op jit(solution)/shard_map/ppermute | solution.py:416
  82.4 21.7 %collective-permute-start.8 = (bf16[4,48,1152]{2,1,0:T(8,128)(2,1)S(1)}, bf16[4,48,1152]{2,1,0:T(8,128)(2,1)S(1)}, u32[]{:S(2)}, u32[]{:S(2)}) collective-permute-start(bf16[4,48,1152]{2,1,0:T(8,128)(2,1)S(1)} %get-tuple-element.25._), channel_id=1, source_target_pairs={{0,4},{1,5},{2,6},{3,7},{4,0},{5,1},{6,2},{7,3},{8,12},{9,13},{10,... | collective-permute-start | bytes 1327112 | tf_op jit(solution)/shard_map/ppermute | solution.py:416
  86.1 13.5 %collective-permute-start.13 = (bf16[1,48,1152]{2,1,0:T(8,128)(2,1)S(1)}, bf16[1,48,1152]{2,1,0:T(8,128)(2,1)S(1)}, u32[]{:S(2)}, u32[]{:S(2)}) collective-permute-start(bf16[1,48,1152]{2,1,0:T(8,128)(2,1)S(1)} %get-tuple-element.32), channel_id=1, source_target_pairs={{0,8},{1,9},{2,10},{3,11},{4,12},{5,13},{6,14},{7,15},{8,0},{9,1},... | collective-permute-start | bytes 331784 | tf_op jit(solution)/shard_map/ppermute | solution.py:422
  87.6 40.7 %collective-permute-start.16 = (bf16[1,96,1152]{2,1,0:T(8,128)(2,1)S(1)}, bf16[1,96,1152]{2,1,0:T(8,128)(2,1)S(1)}, u32[]{:S(2)}, u32[]{:S(2)}) collective-permute-start(bf16[1,96,1152]{2,1,0:T(8,128)(2,1)S(1)} %get-tuple-element.35), channel_id=1, source_target_pairs={{0,8},{1,9},{2,10},{3,11},{4,12},{5,13},{6,14},{7,15},{8,0},{9,1},... | collective-permute-start | bytes 663560 | tf_op jit(solution)/shard_map/ppermute | solution.py:422
  88.2 17.0 %collective-permute-start.14 = (bf16[1,48,1152]{2,1,0:T(8,128)(2,1)S(1)}, bf16[1,48,1152]{2,1,0:T(8,128)(2,1)S(1)}, u32[]{:S(2)}, u32[]{:S(2)}) collective-permute-start(bf16[1,48,1152]{2,1,0:T(8,128)(2,1)S(1)} %get-tuple-element.33), channel_id=1, source_target_pairs={{0,16},{1,17},{2,18},{3,19},{4,20},{5,21},{6,22},{7,23},{8,24},{9,... | collective-permute-start | bytes 331784 | tf_op jit(solution)/shard_map/ppermute | solution.py:422
  99.6 32.2 %collective-permute-start.17 = (bf16[1,96,1152]{2,1,0:T(8,128)(2,1)S(1)}, bf16[1,96,1152]{2,1,0:T(8,128)(2,1)S(1)}, u32[]{:S(2)}, u32[]{:S(2)}) collective-permute-start(bf16[1,96,1152]{2,1,0:T(8,128)(2,1)S(1)} %get-tuple-element.36), channel_id=1, source_target_pairs={{0,16},{1,17},{2,18},{3,19},{4,20},{5,21},{6,22},{7,23},{8,24},{9,... | collective-permute-start | bytes 663560 | tf_op jit(solution)/shard_map/ppermute | solution.py:422
  99.6 32.2 %collective-permute-start.18 = (bf16[1,96,1152]{2,1,0:T(8,128)(2,1)S(1)}, bf16[1,96,1152]{2,1,0:T(8,128)(2,1)S(1)}, u32[]{:S(2)}, u32[]{:S(2)}) collective-permute-start(bf16[1,96,1152]{2,1,0:T(8,128)(2,1)S(1)} %get-tuple-element.37), channel_id=1, source_target_pairs={{0,24},{1,25},{2,26},{3,27},{4,28},{5,29},{6,30},{7,31},{8,16},{9,... | collective-permute-start | bytes 663560 | tf_op jit(solution)/shard_map/ppermute | solution.py:422
  104.1 16.4 %collective-permute-start.15 = (bf16[1,48,1152]{2,1,0:T(8,128)(2,1)S(1)}, bf16[1,48,1152]{2,1,0:T(8,128)(2,1)S(1)}, u32[]{:S(2)}, u32[]{:S(2)}) collective-permute-start(bf16[1,48,1152]{2,1,0:T(8,128)(2,1)S(1)} %get-tuple-element.34), channel_id=1, source_target_pairs={{0,24},{1,25},{2,26},{3,27},{4,28},{5,29},{6,30},{7,31},{8,16},{9,... | collective-permute-start | bytes 331784 | tf_op jit(solution)/shard_map/ppermute | solution.py:422
  105.3 27.9 %collective-permute-start.10 = (bf16[1,48,1152]{2,1,0:T(8,128)(2,1)S(1)}, bf16[1,48,1152]{2,1,0:T(8,128)(2,1)S(1)}, u32[]{:S(2)}, u32[]{:S(2)}) collective-permute-start(bf16[1,48,1152]{2,1,0:T(8,128)(2,1)S(1)} %get-tuple-element.29), channel_id=1, source_target_pairs={{0,8},{1,9},{2,10},{3,11},{4,12},{5,13},{6,14},{7,15},{8,0},{9,1},... | collective-permute-start | bytes 331784 | tf_op jit(solution)/shard_map/ppermute | solution.py:422
  120.5 15.9 %collective-permute-start.11 = (bf16[1,48,1152]{2,1,0:T(8,128)(2,1)S(1)}, bf16[1,48,1152]{2,1,0:T(8,128)(2,1)S(1)}, u32[]{:S(2)}, u32[]{:S(2)}) collective-permute-start(bf16[1,48,1152]{2,1,0:T(8,128)(2,1)S(1)} %get-tuple-element.30), channel_id=1, source_target_pairs={{0,16},{1,17},{2,18},{3,19},{4,20},{5,21},{6,22},{7,23},{8,24},{9,... | collective-permute-start | bytes 331784 | tf_op jit(solution)/shard_map/ppermute | solution.py:422
  128.3 8.1 %collective-permute-start.12 = (bf16[1,48,1152]{2,1,0:T(8,128)(2,1)S(1)}, bf16[1,48,1152]{2,1,0:T(8,128)(2,1)S(1)}, u32[]{:S(2)}, u32[]{:S(2)}) collective-permute-start(bf16[1,48,1152]{2,1,0:T(8,128)(2,1)S(1)} %get-tuple-element.31), channel_id=1, source_target_pairs={{0,24},{1,25},{2,26},{3,27},{4,28},{5,29},{6,30},{7,31},{8,16},{9,... | collective-permute-start | bytes 331784 | tf_op jit(solution)/shard_map/ppermute | solution.py:422
where the time goes:
time: 138 us; the launch traced here: 137 us
  Pallas kernels  50.8 us (37%)
  starting transfers between devices  50.6 us (37%)
  local copies, waits for them, and re-layouts  17.8 us (13%)
  waiting for transfers between devices  14 us (10%)
  other arithmetic  2.77 us (2%)
  between operations  1.46 us (1%)
    pallas_call x3, Pallas kernels, partial_call(): pl.pallas_call(functools.partial(kernel, pieces=len(pieces), outs=outs, g...  43.2 us
    ppermute x9, starting transfers between devices, across_owners(): part = lax.ppermute(part, AXES, swapped(shape, 2 * offset, 0))  38.6 us
    ppermute x9, waiting for transfers between devices, across_owners(): part = lax.ppermute(part, AXES, swapped(shape, 2 * offset, 0))  8.08 us
    transpose x1, local copies, waits for them, and re-layouts, shards(): keys, values = (jnp.swapaxes(k_cache, 0, 1), jnp.swapaxes(v_cache, 0, 1))  6.61 us
    unnamed x16, local copies, waits for them, and re-layouts  6 us
    ppermute x4, starting transfers between devices, relayed(): lax.ppermute(x, AXES, swapped(shape, 0, b))  4.98 us
    ppermute x3, starting transfers between devices, across_pair(): return lax.ppermute(send, AXES, swapped(shape, 1, 0))  4.7 us
    pallas_call x3, Pallas kernels, merge_pair(): pl.pallas_call(pair_kernel, grid_spec=pltpu.PrefetchScalarGridSpec(num_sc...  4.22 us
  transfers between devices with their start and end apart: 19, of which 5 were waited for; matrix products, arithmetic and copies ran while one was open for 10% of the time, Pallas kernels for 36%

commit v1 on v0

--- a/solution.py
+++ b/solution.py
@@ -49,17 +49,22 @@
     return high, middle, rest - middle
 
 
-def write_partial(out_refs, held_ref, stat_ref, place_ref, chains, group_size, group, rows):
+def term_lanes(level, heads):
+    lane = lax.broadcasted_iota(jnp.int32, level.shape, 1)
+    high, middle, low = in_terms(level)
+    rest = jnp.where(lane < 2 * heads, pltpu.roll(middle, heads, 1), pltpu.roll(low, 2 * heads, 1))
+    return jnp.where(lane < heads, high, rest).astype(jnp.bfloat16)
+
+
+def write_partial(held_ref, stat_ref, place_ref, chains, group_size, group, rows):
     values, levels = [], []
     for top, summed in chains:
         total = summed[:, HD:]
         values.append((summed[:, :HD] / total).astype(jnp.bfloat16))
-        levels.append(in_terms(top + jnp.log2(total)))
+        levels.append(top + jnp.log2(total))
     value = jnp.concatenate(values, axis=0)
-    terms = [jnp.concatenate(term, axis=0) for term in zip(*levels)]
-    kv_local = pl.num_programs(0)
+    level = jnp.concatenate(levels, axis=0)
     count = held_ref.shape[0]
-    heads = (held_ref.shape[2] - LANES) // HD
     lane = lax.broadcasted_iota(jnp.int32, (rows, LANES), 1)
     for item in range(count):
         place = place_ref[item]
@@ -69,16 +74,19 @@
             at = (head * count + item) * rows
             start = pl.multiple_of(column * HD, HD)
             held_ref[place, :, pl.ds(start, HD)] = value[at : at + rows]
-            for order, term in enumerate(terms):
-                stat = jnp.where(lane == order * heads + column, term[at : at + rows], stat)
+            stat = jnp.where(lane == column, level[at : at + rows], stat)
         stat_ref[place] = stat
 
-    @pl.when(group == kv_local - 1)
-    def _():
-        held_ref[:, :, heads * HD :] = stat_ref[...].astype(jnp.bfloat16)
-        share = count // len(out_refs)
-        for index, out_ref in enumerate(out_refs):
-            out_ref[...] = held_ref[index * share : (index + 1) * share]
+
+def hand_out(out_refs, held_ref, stat_ref):
+    count = held_ref.shape[0]
+    heads = (held_ref.shape[2] - LANES) // HD
+    share = count // len(out_refs)
+    for index, out_ref in enumerate(out_refs):
+        for item in range(share):
+            at = index * share + item
+            out_ref[item, :, : heads * HD] = held_ref[at, :, : heads * HD]
+            out_ref[item, :, heads * HD :] = term_lanes(stat_ref[at], heads)
 
 
 def dense_kernel(place_ref, column_ref, *refs, pieces, outs, group_size, block_keys):
@@ -111,7 +119,11 @@
                 top, before = chains[index]
                 summed = before * jnp.exp2(top - newtop) + summed
             chains[index] = (newtop, summed)
-    write_partial(out_refs, held_ref, stat_ref, place_ref, chains, group_size, group, rows)
+    write_partial(held_ref, stat_ref, place_ref, chains, group_size, group, rows)
+
+    @pl.when(group == pl.num_programs(0) - 1)
+    def _():
+        hand_out(out_refs, held_ref, stat_ref)
 
 
 def kept_kernel(place_ref, column_ref, list_ref, count_ref, *refs, pieces, outs, group_size):
@@ -122,8 +134,12 @@
     group = pl.program_id(0)
     rows = query_refs[0].shape[2]
     kept = count_ref[0]
-    few, many = 2, 4
-    loaded = jnp.where(kept <= few, few, pl.cdiv(kept, many) * many)
+    slots = keys_ref.shape[0]
+    sizes = [size for size in (2, 4) if size < slots] + [min(8, slots)]
+    most = sizes[-1]
+    loaded = pl.cdiv(kept, most) * most
+    for size in reversed(sizes[:-1]):
+        loaded = jnp.where(kept <= size, size, loaded)
 
     def copies(slot):
         block = list_ref[jnp.minimum(slot, kept - 1)]
@@ -158,6 +174,7 @@
         values = jnp.concatenate([values_ref[first + i, group] for i in range(length)], axis=0)
         values = with_ones(values)
         slot = lax.broadcasted_iota(jnp.int32, (1, length * BLK), 1) // BLK + first
+        chains = []
         for start in starts:
             span = pl.ds(start, size)
             scores = raw_scores(queries[start : start + size], keys)
@@ -170,23 +187,43 @@
             summed = jnp.dot(weights, values, preferred_element_type=jnp.float32)
             if not fresh:
                 summed = sum_ref[span, :] * jnp.exp2(top - newtop) + summed
-            sum_ref[span, :] = summed
-            top_ref[span, :] = jnp.broadcast_to(newtop, (size, LANES))
-
-    @pl.when(kept <= few)
+            chains.append((newtop, summed))
+        return chains
+
+    def finish(chains):
+        write_partial(held_ref, stat_ref, place_ref, chains, group_size, group, rows)
+
+    least = 0
+    for length in sizes:
+
+        @pl.when((kept > least) & (kept <= length))
+        def _(length=length):
+            finish(absorb(0, length, True))
+
+        least = length
+
+    if slots > most:
+
+        def hold(chains):
+            for start, (top, summed) in zip(starts, chains):
+                span = pl.ds(start, size)
+                sum_ref[span, :] = summed
+                top_ref[span, :] = jnp.broadcast_to(top, (size, LANES))
+
+        @pl.when(kept > most)
+        def _():
+            hold(absorb(0, most, True))
+
+            @pl.loop(1, loaded // most)
+            def _(step):
+                hold(absorb(step * most, most, False))
+
+            spans = [pl.ds(start, size) for start in starts]
+            finish([(top_ref[span, :1], sum_ref[span, :]) for span in spans])
+
+    @pl.when(group == pl.num_programs(0) - 1)
     def _():
-        absorb(0, few, True)
-
-    @pl.when(kept > few)
-    def _():
-        absorb(0, many, True)
-
-    @pl.loop(1, jnp.maximum(loaded // many, 1))
-    def _(step):
-        absorb(step * many, many, False)
-
-    chains = [(top_ref[pl.ds(s, size), :1], sum_ref[pl.ds(s, size), :]) for s in starts]
-    write_partial(out_refs, held_ref, stat_ref, place_ref, chains, group_size, group, rows)
+        hand_out(out_refs, held_ref, stat_ref)
 
 
 def query_spec(piece, own, group_size, kept, half):
@@ -213,7 +250,7 @@
     ]
     anywhere = pl.BlockSpec(memory_space=pl.ANY)
     out_shape = [jax.ShapeDtypeStruct((count // outs, rows, width), jnp.bfloat16)] * outs
-    out_specs = [pl.BlockSpec((count // outs, rows, width), lambda *_: (0, 0, 0))] * outs
+    out_specs = [pl.BlockSpec(memory_space=pltpu.VMEM)] * outs
     scratch = [
         pltpu.VMEM((count, rows, width), jnp.bfloat16),
         pltpu.VMEM((count, rows, LANES), jnp.float32),
@@ -223,12 +260,15 @@
         kernel = functools.partial(dense_kernel, block_keys=math.gcd(length, 512))
         operands, cache_specs, reads = (places, column), [whole, whole], length
     else:
-        slots = pl.cdiv(kept[0].shape[0], 4) * 4
+        slots = kept[0].shape[0]
+        slots = slots if slots <= 8 else pl.cdiv(slots, 8) * 8
         kernel = kept_kernel
-        operands, cache_specs, reads = (places, column, *kept), [anywhere, anywhere], 4 * BLK
+        operands, reads = (places, column, *kept), 4 * BLK
+        cache_specs = [anywhere] * 2
+        held = stacked if slots > 8 else 8
         scratch += [
-            pltpu.VMEM((stacked, LANES), jnp.float32),
-            pltpu.VMEM((stacked, 2 * HD), jnp.float32),
+            pltpu.VMEM((held, LANES), jnp.float32),
+            pltpu.VMEM((held, 2 * HD), jnp.float32),
             pltpu.VMEM((slots, kv_local, BLK, HD), jnp.bfloat16),
             pltpu.VMEM((slots, kv_local, BLK, HD), jnp.bfloat16),
             pltpu.SemaphoreType.DMA((2, slots)),
@@ -288,7 +328,7 @@
     _, rows, width = parts[0].shape
     sources = sum(part.shape[0] for part in parts)
     columns = width - LANES
-    in_specs = [pl.BlockSpec(part.shape, lambda i: (0, 0, 0)) for part in parts]
+    in_specs = [pl.BlockSpec(memory_space=pltpu.VMEM) for part in parts]
     operands = list(parts)
     if onto is not None:
         in_specs.append(pl.BlockSpec(memory_space=pl.ANY))
@@ -311,29 +351,27 @@
 
 def pair_kernel(spot_ref, mine_ref, theirs_ref, _, *out_refs):
     heads = (mine_ref.shape[2] - LANES) // HD
-    lane = lax.broadcasted_iota(jnp.int32, (mine_ref.shape[1], LANES), 1)
     for offset, out_ref in enumerate(out_refs):
         spot = spot_ref[0] ^ offset
         parts = [mine_ref.at[spot], theirs_ref.at[spot]]
         shares, level = shares_of(parts, heads)
         for head in range(heads):
             out_ref[0, :, head * HD : (head + 1) * HD] = weighted(parts, shares, head)
-        high, middle, low = in_terms(level)
-        stat = jnp.where(lane < 2 * heads, pltpu.roll(middle, heads, 1), pltpu.roll(low, 2 * heads, 1))
-        out_ref[0, :, heads * HD :] = jnp.where(lane < heads, high, stat).astype(jnp.bfloat16)
+        out_ref[0, :, heads * HD :] = term_lanes(level, heads)
 
 
 def merge_pair(mine, theirs, spot, after):
     owners, rows, width = mine.shape
-    whole = pl.BlockSpec(mine.shape, lambda *_: (0, 0, 0))
+    vmem = pl.BlockSpec(memory_space=pltpu.VMEM)
     return pl.pallas_call(
         pair_kernel,
-        grid_spec=pltpu.PrefetchScalarGridSpec(
-            num_scalar_prefetch=1,
-            grid=(1,),
-            in_specs=[whole, whole, pl.BlockSpec(memory_space=pl.ANY)],
-            out_specs=[pl.BlockSpec((1, rows, width), lambda *_: (0, 0, 0))] * owners,
-        ),
+        in_specs=[
+            pl.BlockSpec(memory_space=pltpu.SMEM),
+            vmem,
+            vmem,
+            pl.BlockSpec(memory_space=pl.ANY),
+        ],
+        out_specs=[vmem] * owners,
         out_shape=[jax.ShapeDtypeStruct((1, rows, width), jnp.bfloat16)] * owners,
         compiler_params=pltpu.CompilerParams(vmem_limit_bytes=MERGE_BYTES),
         cost_estimate=pl.CostEstimate(
@@ -344,6 +382,21 @@
     )(spot, mine, theirs, after)
 
 
+def settle_kernel(key_ref, value_ref, out_ref):
+    out_ref[...] = jnp.zeros_like(out_ref)
+
+
+def settle(keys, values):
+    anywhere = pl.BlockSpec(memory_space=pl.ANY)
+    return pl.pallas_call(
+        settle_kernel,
+        in_specs=[anywhere, anywhere],
+        out_specs=pl.BlockSpec(memory_space=pltpu.VMEM),
+        out_shape=jax.ShapeDtypeStruct((8, LANES), jnp.float32),
+        compiler_params=pltpu.CompilerParams(vmem_limit_bytes=MERGE_BYTES),
+    )(keys, values)
+
+
 def to_owners(part):
     return lax.all_to_all(part, "ctx", split_axis=0, concat_axis=0, tiled=True)
 
@@ -366,24 +419,21 @@
     def columns_of(block, other, start, count):
         return lax.dynamic_slice(block, (start, other * mine), (count, mine))
 
-    near = jnp.stack([columns_of(block, me ^ 1, 0, rows) for block in (q_second, q_first)])
-    got = []
-    for block in (q_second, q_first):
-        pair = [columns_of(block, me ^ bit, low * half, half) for bit in (2, 3)]
-        got.append([lax.ppermute(x, AXES, swapped(shape, 0, b)) for x, b in zip(pair, (2, 3))])
-    near = lax.ppermute(near, AXES, swapped(shape, 0, 1))
+    blocks = (q_second, q_first)
+
+    def sent(block, bit, start, count):
+        return lax.ppermute(columns_of(block, me ^ bit, start, count), AXES, swapped(shape, 0, bit))
+
+    got = [[sent(block, bit, low * half, half) for bit in (2, 3)] for block in blocks]
+    near = [sent(block, 1, 0, rows) for block in blocks]
     pieces = []
-    for at, block in enumerate((q_second, q_first)):
-        same, cross = got[at]
-        other = lax.ppermute(jnp.stack([same, cross]), AXES, swapped(shape, 1, 0))
+    for block, beside, remote in zip(blocks, near, got):
+        others = []
+        for x in remote:
+            others.append(lax.ppermute(x, AXES, swapped(shape, 1, 0)))
         pieces.append(
-            [
-                block.reshape(2, half, wide),
-                near[at].reshape(2, half, mine),
-                same.reshape(1, half, mine),
-                cross.reshape(1, half, mine),
-                other,
-            ]
+            [block.reshape(2, half, wide), beside.reshape(2, half, mine)]
+            + [x.reshape(1, half, mine) for x in remote + others]
         )
     owners = []
     for bit in (0, 1):
@@ -426,7 +476,8 @@
         def attend(pieces, half, after, kept=None):
             return partial_call(pieces, places, column, keys, values, half, 2, after, kept)
 
-        send_s, keep_s = attend(second, 0, spot, kept)
+        settled = settle(keys, values)
+        send_s, keep_s = attend(second, 0, settled, kept)
         got_s = across_pair(send_s)
         send_a, keep_a = attend(first, 0, send_s)
         got_a = across_pair(send_a)

time: 138 us -> 137 us (level)
  Pallas kernels: 50.8 us -> 45.7 us
  local copies, waits for them, and re-layouts: 17.8 us -> 21.8 us
  other arithmetic: 2.77 us -> 0 us
  waiting for transfers between devices: 14 us -> 16.5 us
    pallas_call x3, Pallas kernels: 43.2 us -> 38.1 us  [partial_call(): pl.pallas_call(functools.partial(kernel, pieces=len(pieces), outs=outs, g...]
    dynamic_slice x2 -> x4, local copies, waits for them, and re-layouts: 1.94 us -> 6.37 us  [columns_of(): return lax.dynamic_slice(block, (start, other * mine), (count, mine))]
    ppermute x7 -> x10, starting transfers between devices: 7.27 us -> 11 us  [the longest x4 5.66 us: relayed(): others.append(lax.ppermute(x, AXES, swapped(shape, 1, 0)))]
    another operation x3 -> x0, other arithmetic: 2.77 us -> none  [the longest x2 1.75 us: relayed(): other = lax.ppermute(jnp.stack([same, cross]), AXES, swapped(shape, 1, 0))]
    unnamed x16 -> x14, local copies, waits for them, and re-layouts: 6 us -> 8.75 us
    another operation x2 -> x0, local copies, waits for them, and re-layouts: 2.05 us -> none  [relayed(): jnp.stack([columns_of(block, me ^ 1, 0, rows) for block in (q_second, q_f...]
    ppermute x3, starting transfers between devices: 4.7 us -> 2.69 us  [across_pair(): return lax.ppermute(send, AXES, swapped(shape, 1, 0))]
    ppermute x3, waiting for transfers between devices: 2.05 us -> 3.72 us  [across_pair(): return lax.ppermute(send, AXES, swapped(shape, 1, 0))]
  transfers between devices with their start and end apart: 19 -> 22, of which waited for: 5 -> 5; matrix products, arithmetic and copies ran while one was open for 10% -> 8% of each run, Pallas kernels for 36% -> 33%
where the time goes in v1:
time: 137 us
  starting transfers between devices  51.5 us (38%)
  Pallas kernels  45.7 us (33%)
  local copies, waits for them, and re-layouts  21.8 us (16%)
  waiting for transfers between devices  16.5 us (12%)
  between operations  1.48 us (1%)
    pallas_call x3, Pallas kernels, partial_call(): pl.pallas_call(functools.partial(kernel, pieces=len(pieces), outs=outs, g...  38.1 us
    ppermute x9, starting transfers between devices, across_owners(): part = lax.ppermute(part, AXES, swapped(shape, 2 * offset, 0))  37.7 us
    unnamed x14, local copies, waits for them, and re-layouts  8.75 us
    ppermute x9, waiting for transfers between devices, across_owners(): part = lax.ppermute(part, AXES, swapped(shape, 2 * offset, 0))  8.17 us
    transpose x1, local copies, waits for them, and re-layouts, shards(): keys, values = (jnp.swapaxes(k_cache, 0, 1), jnp.swapaxes(v_cache, 0, 1))  6.57 us
    dynamic_slice x4, local copies, waits for them, and re-layouts, columns_of(): return lax.dynamic_slice(block, (start, other * mine), (count, mine))  6.37 us
    ppermute x4, starting transfers between devices, relayed(): others.append(lax.ppermute(x, AXES, swapped(shape, 1, 0)))  5.66 us
    ppermute x6, starting transfers between devices, sent(): lax.ppermute(columns_of(block, me ^ bit, start, count), AXES, swapped(sha...  5.36 us
  transfers between devices with their start and end apart: 22, of which 5 were waited for; matrix products, arithmetic and copies ran while one was open for 8% of the time, Pallas kernels for 33%

profile of v1, /device:TPU:0, one launch (start us, length us, event | category | flops | bytes accessed | tf_op | source)
XLA Modules:
  0.0 136.9 jit_solution(7081133111586602109)
XLA Ops:
  0.7 1.7 %fusion.1 = (bf16[96,1024]{1,0:T(8,128)(2,1)}, bf16[96,1024]{1,0:T(8,128)(2,1)S(1)}) fusion(bf16[192,4096]{1,0:T(8,128)(2,1)} %param.6, s32[]{:T(128)S(6)} %select_n.137, s32[]{:T(128)S(6)} %select_n.139, s32[]{:T(128)S(6)} %select_n.138), kind=kLoop, calls=%fused_computation.5 | loop fusion | bytes 786444 | tf_op jit(solution)/shard_map/dynamic_slice | solution.py:420
  2.4 3.0 %collective-permute-start.1 = (bf16[96,1024]{1,0:T(8,128)(2,1)S(1)}, bf16[96,1024]{1,0:T(8,128)(2,1)S(1)}, u32[]{:S(2)}, u32[]{:S(2)}) collective-permute-start(bf16[96,1024]{1,0:T(8,128)(2,1)S(1)} %get-tuple-element.41), channel_id=1, source_target_pairs={{0,2},{1,3},{2,0},{3,1},{4,6},{5,7},{6,4},{7,5},{8,10},{9,11},{10,... | collective-permute-start | bytes 589832 | tf_op jit(solution)/shard_map/ppermute | solution.py:425
  7.4 1.8 %constant_dynamic-slice_fusion.1 = bf16[192,1024]{1,0:T(8,128)(2,1)} fusion(bf16[192,4096]{1,0:T(8,128)(2,1)} %param.6, s32[]{:T(128)S(6)} %select_n.136), kind=kLoop, calls=%fused_computation.3 | loop fusion | bytes 786436 | tf_op jit(solution)/shard_map/dynamic_slice | solution.py:420
  9.2 1.2 collective-permute-start
  10.4 1.8 %constant_dynamic-slice_fusion = bf16[192,1024]{1,0:T(8,128)(2,1)} fusion(bf16[192,4096]{1,0:T(8,128)(2,1)} %param.7, s32[]{:T(128)S(6)} %select_n.136), kind=kLoop, calls=%fused_computation.2 | loop fusion | bytes 786436 | tf_op jit(solution)/shard_map/dynamic_slice | solution.py:420
  12.4 2.9 %collective-permute-done.6 = bf16[96,1024]{1,0:T(8,128)(2,1)S(1)} collective-permute-done((bf16[96,1024]{1,0:T(8,128)(2,1)S(1)}, bf16[96,1024]{1,0:T(8,128)(2,1)S(1)}, u32[]{:S(2)}, u32[]{:S(2)}) %collective-permute-start.6) | collective-permute-done | bytes 196640 | tf_op jit(solution)/shard_map/ppermute | solution.py:425
  15.3 2.1 %collective-permute-start.8 = (bf16[96,1024]{1,0:T(8,128)(2,1)S(1)}, bf16[96,1024]{1,0:T(8,128)(2,1)S(1)}, u32[]{:S(2)}, u32[]{:S(2)}) collective-permute-start(bf16[96,1024]{1,0:T(8,128)(2,1)S(1)} %collective-permute-done.6), channel_id=1, source_target_pairs={{0,4},{1,5},{2,6},{3,7},{4,0},{5,1},{6,2},{7,3},{8,12},{9,13},{10,... | collective-permute-start | bytes 589832 | tf_op jit(solution)/shard_map/ppermute | solution.py:433
  17.4 1.7 %collective-permute-done.7 = bf16[96,1024]{1,0:T(8,128)(2,1)S(1)} collective-permute-done((bf16[96,1024]{1,0:T(8,128)(2,1)S(1)}, bf16[96,1024]{1,0:T(8,128)(2,1)S(1)}, u32[]{:S(2)}, u32[]{:S(2)}) %collective-permute-start.7) | collective-permute-done | bytes 196640 | tf_op jit(solution)/shard_map/ppermute | solution.py:425
  19.1 1.5 %collective-permute-start.9 = (bf16[96,1024]{1,0:T(8,128)(2,1)S(1)}, bf16[96,1024]{1,0:T(8,128)(2,1)S(1)}, u32[]{:S(2)}, u32[]{:S(2)}) collective-permute-start(bf16[96,1024]{1,0:T(8,128)(2,1)S(1)} %collective-permute-done.7), channel_id=1, source_target_pairs={{0,4},{1,5},{2,6},{3,7},{4,0},{5,1},{6,2},{7,3},{8,12},{9,13},{10,... | collective-permute-start | bytes 589832 | tf_op jit(solution)/shard_map/ppermute | solution.py:433
  20.6 6.6 %copy_bitcast_fusion = (bf16[4,4096,128]{2,1,0:T(8,128)(2,1)}, bf16[4,4096,128]{2,1,0:T(8,128)(2,1)}) fusion(bf16[4096,4,128]{2,1,0:T(4,128)(2,1)} %param.9, bf16[4096,4,128]{2,1,0:T(4,128)(2,1)} %param.8), kind=kLoop, calls=%fused_computation | loop fusion | bytes 16777216 | tf_op jit(solution)/shard_map/transpose | solution.py:457
  27.9 2.2 %copy-done = bf16[4,4096,128]{2,1,0:T(8,128)(2,1)S(1)} copy-done((bf16[4,4096,128]{2,1,0:T(8,128)(2,1)S(1)}, bf16[4,4096,128]{2,1,0:T(8,128)(2,1)}, u32[]{:S(2)}) %copy-start) | copy-done | bytes 4194328
  30.1 2.2 %copy-done.2 = bf16[4,4096,128]{2,1,0:T(8,128)(2,1)S(1)} copy-done((bf16[4,4096,128]{2,1,0:T(8,128)(2,1)S(1)}, bf16[4,4096,128]{2,1,0:T(8,128)(2,1)}, u32[]{:S(2)}) %copy-start.2) | copy-done | bytes 4194328
  32.9 1.5 %collective-permute-start.4 = (bf16[96,1024]{1,0:T(8,128)(2,1)S(1)}, bf16[96,1024]{1,0:T(8,128)(2,1)S(1)}, u32[]{:S(2)}, u32[]{:S(2)}) collective-permute-start(bf16[96,1024]{1,0:T(8,128)(2,1)S(1)} %collective-permute-done.2), channel_id=1, source_target_pairs={{0,4},{1,5},{2,6},{3,7},{4,0},{5,1},{6,2},{7,3},{8,12},{9,13},{10,... | collective-permute-start | bytes 589832 | tf_op jit(solution)/shard_map/ppermute | solution.py:433
  34.5 2.2 %copy-done.1 = bf16[4,4096,128]{2,1,0:T(8,128)(2,1)S(1)} copy-done((bf16[4,4096,128]{2,1,0:T(8,128)(2,1)S(1)}, bf16[4,4096,128]{2,1,0:T(8,128)(2,1)}, u32[]{:S(2)}) %copy-start.1) | copy-done | bytes 4194328
  36.6 2.2 %copy-done.3 = bf16[4,4096,128]{2,1,0:T(8,128)(2,1)S(1)} copy-done((bf16[4,4096,128]{2,1,0:T(8,128)(2,1)S(1)}, bf16[4,4096,128]{2,1,0:T(8,128)(2,1)}, u32[]{:S(2)}) %copy-start.3) | copy-done | bytes 4194328
  38.8 4.9 %shard_map.78 = (bf16[4,96,1152]{2,1,0:T(8,128)(2,1)S(1)}, bf16[4,96,1152]{2,1,0:T(8,128)(2,1)S(1)}) custom-call(s32[8]{0:T(128)S(1)} %stack.35.place_ref, s32[1]{0:T(128)} %bitcast.9.column_ref, s32[8]{0:T(128)S(1)} %bitcast.47, s32[1]{0:T(128)S(6)} %copy.14.count_ref, bf16[2,1,96,4096]{3,2,1,0:T(8,128)(2,1)S(1)} %bitcast.29, ...), custom_call_target="tpu_custom_call" | custom-call | flops 3221225472 | bytes 1048576 | tf_op jit(solution)/shard_map/pallas_call | solution.py:276
  44.3 16.7 %shard_map.79 = (bf16[4,48,1152]{2,1,0:T(8,128)(2,1)S(1)}, bf16[4,48,1152]{2,1,0:T(8,128)(2,1)S(1)}) custom-call(s32[8]{0:T(128)S(1)} %stack.35.place_ref, s32[1]{0:T(128)} %bitcast.9.column_ref, bf16[2,2,48,4096]{3,2,1,0:T(8,128)(2,1)S(1)} %bitcast.30, bf16[2,2,48,1024]{3,2,1,0:T(8,128)(2,1)S(1)} %bitcast.32, bf16[1,2,48,1024]{3,2,1,0:T(8,128)(2,1)S(1)} %bitcast.35, ...), custom_call_target="tpu_custom_call" | custom-call | flops 12884901888 | bytes 8388608 | tf_op jit(solution)/shard_map/pallas_call | solution.py:276
  61.0 1.6 %collective-permute-start.12 = (bf16[4,48,1152]{2,1,0:T(8,128)(2,1)S(1)}, bf16[4,48,1152]{2,1,0:T(8,128)(2,1)S(1)}, u32[]{:S(2)}, u32[]{:S(2)}) collective-permute-start(bf16[4,48,1152]{2,1,0:T(8,128)(2,1)S(1)} %get-tuple-element.22._), channel_id=1, source_target_pairs={{0,4},{1,5},{2,6},{3,7},{4,0},{5,1},{6,2},{7,3},{8,12},{9,13},{10,... | collective-permute-start | bytes 1327112 | tf_op jit(solution)/shard_map/ppermute | solution.py:466
  62.6 3.7 %collective-permute-done.10.theirs_ref = bf16[4,96,1152]{2,1,0:T(8,128)(2,1)S(1)} collective-permute-done((bf16[4,96,1152]{2,1,0:T(8,128)(2,1)S(1)}, bf16[4,96,1152]{2,1,0:T(8,128)(2,1)S(1)}, u32[]{:S(2)}, u32[]{:S(2)}) %collective-permute-start.10) | collective-permute-done | bytes 884768 | tf_op jit(solution)/shard_map/ppermute | solution.py:466
  66.3 1.9 %shard_map.80 = (bf16[1,96,1152]{2,1,0:T(8,128)(2,1)S(1)}, bf16[1,96,1152]{2,1,0:T(8,128)(2,1)S(1)}, bf16[1,96,1152]{2,1,0:T(8,128)(2,1)S(1)}, bf16[1,96,1152]{2,1,0:T(8,128)(2,1)S(1)}) custom-call(s32[1]{0:T(128)} %bitcast.spot_ref, bf16[4,96,1152]{2,1,0:T(8,128)(2,1)S(1)} %get-tuple-element.20.mine_ref, ...), custom_call_target="tpu_custom_call" | custom-call | flops 3538944 | bytes 2654208 | tf_op jit(solution)/shard_map/pallas_call | solution.py:366
  68.2 16.5 %shard_map.81 = (bf16[4,48,1152]{2,1,0:T(8,128)(2,1)S(1)}, bf16[4,48,1152]{2,1,0:T(8,128)(2,1)S(1)}) custom-call(s32[8]{0:T(128)S(1)} %stack.35.place_ref, s32[1]{0:T(128)} %bitcast.9.column_ref, bf16[2,2,48,4096]{3,2,1,0:T(8,128)(2,1)S(1)} %bitcast.31, bf16[2,2,48,1024]{3,2,1,0:T(8,128)(2,1)S(1)} %bitcast.33, bf16[1,2,48,1024]{3,2,1,0:T(8,128)(2,1)S(1)} %bitcast.36, ...), custom_call_target="tpu_custom_call" | custom-call | flops 12884901888 | bytes 8388608 | tf_op jit(solution)/shard_map/pallas_call | solution.py:276
  85.2 1.2 shard_map.82
  86.4 1.7 %collective-permute-start.16 = (bf16[1,48,1152]{2,1,0:T(8,128)(2,1)S(1)}, bf16[1,48,1152]{2,1,0:T(8,128)(2,1)S(1)}, u32[]{:S(2)}, u32[]{:S(2)}) collective-permute-start(bf16[1,48,1152]{2,1,0:T(8,128)(2,1)S(1)} %get-tuple-element.32), channel_id=1, source_target_pairs={{0,8},{1,9},{2,10},{3,11},{4,12},{5,13},{6,14},{7,15},{8,0},{9,1},... | collective-permute-start | bytes 331784 | tf_op jit(solution)/shard_map/ppermute | solution.py:472
  88.5 9.9 %collective-permute-start.17 = (bf16[1,48,1152]{2,1,0:T(8,128)(2,1)S(1)}, bf16[1,48,1152]{2,1,0:T(8,128)(2,1)S(1)}, u32[]{:S(2)}, u32[]{:S(2)}) collective-permute-start(bf16[1,48,1152]{2,1,0:T(8,128)(2,1)S(1)} %get-tuple-element.33), channel_id=1, source_target_pairs={{0,16},{1,17},{2,18},{3,19},{4,20},{5,21},{6,22},{7,23},{8,24},{9,... | collective-permute-start | bytes 331784 | tf_op jit(solution)/shard_map/ppermute | solution.py:472
  98.5 4.5 %collective-permute-start.21 = (bf16[1,96,1152]{2,1,0:T(8,128)(2,1)S(1)}, bf16[1,96,1152]{2,1,0:T(8,128)(2,1)S(1)}, u32[]{:S(2)}, u32[]{:S(2)}) collective-permute-start(bf16[1,96,1152]{2,1,0:T(8,128)(2,1)S(1)} %get-tuple-element.37), channel_id=1, source_target_pairs={{0,24},{1,25},{2,26},{3,27},{4,28},{5,29},{6,30},{7,31},{8,16},{9,... | collective-permute-start | bytes 663560 | tf_op jit(solution)/shard_map/ppermute | solution.py:472
  103.0 1.2 shard_map.83
  104.2 11.0 %collective-permute-start.13 = (bf16[1,48,1152]{2,1,0:T(8,128)(2,1)S(1)}, bf16[1,48,1152]{2,1,0:T(8,128)(2,1)S(1)}, u32[]{:S(2)}, u32[]{:S(2)}) collective-permute-start(bf16[1,48,1152]{2,1,0:T(8,128)(2,1)S(1)} %get-tuple-element.29), channel_id=1, source_target_pairs={{0,8},{1,9},{2,10},{3,11},{4,12},{5,13},{6,14},{7,15},{8,0},{9,1},... | collective-permute-start | bytes 331784 | tf_op jit(solution)/shard_map/ppermute | solution.py:472
  115.2 4.8 %collective-permute-done.18.refs_3_ = bf16[1,48,1152]{2,1,0:T(8,128)(2,1)S(1)} collective-permute-done((bf16[1,48,1152]{2,1,0:T(8,128)(2,1)S(1)}, bf16[1,48,1152]{2,1,0:T(8,128)(2,1)S(1)}, u32[]{:S(2)}, u32[]{:S(2)}) %collective-permute-start.18) | collective-permute-done | bytes 110624 | tf_op jit(solution)/shard_map/ppermute | solution.py:472
  120.0 7.8 %collective-permute-start.14 = (bf16[1,48,1152]{2,1,0:T(8,128)(2,1)S(1)}, bf16[1,48,1152]{2,1,0:T(8,128)(2,1)S(1)}, u32[]{:S(2)}, u32[]{:S(2)}) collective-permute-start(bf16[1,48,1152]{2,1,0:T(8,128)(2,1)S(1)} %get-tuple-element.30), channel_id=1, source_target_pairs={{0,16},{1,17},{2,18},{3,19},{4,20},{5,21},{6,22},{7,23},{8,24},{9,... | collective-permute-start | bytes 331784 | tf_op jit(solution)/shard_map/ppermute | solution.py:472
  127.8 2.4 %collective-permute-start.15 = (bf16[1,48,1152]{2,1,0:T(8,128)(2,1)S(1)}, bf16[1,48,1152]{2,1,0:T(8,128)(2,1)S(1)}, u32[]{:S(2)}, u32[]{:S(2)}) collective-permute-start(bf16[1,48,1152]{2,1,0:T(8,128)(2,1)S(1)} %get-tuple-element.31), channel_id=1, source_target_pairs={{0,24},{1,25},{2,26},{3,27},{4,28},{5,29},{6,30},{7,31},{8,16},{9,... | collective-permute-start | bytes 331784 | tf_op jit(solution)/shard_map/ppermute | solution.py:472
  131.2 1.3 shard_map.86
  132.5 3.3 %collective-permute-done.14.refs_2_ = bf16[1,48,1152]{2,1,0:T(8,128)(2,1)S(1)} collective-permute-done((bf16[1,48,1152]{2,1,0:T(8,128)(2,1)S(1)}, bf16[1,48,1152]{2,1,0:T(8,128)(2,1)S(1)}, u32[]{:S(2)}, u32[]{:S(2)}) %collective-permute-start.14) | collective-permute-done | bytes 110624 | tf_op jit(solution)/shard_map/ppermute | solution.py:472
  (42 shorter events, 6.6 us)
Async XLA Ops:
  2.4 9.8 %collective-permute-start.1 = (bf16[96,1024]{1,0:T(8,128)(2,1)S(1)}, bf16[96,1024]{1,0:T(8,128)(2,1)S(1)}, u32[]{:S(2)}, u32[]{:S(2)}) collective-permute-start(bf16[96,1024]{1,0:T(8,128)(2,1)S(1)} %get-tuple-element.41), channel_id=1, source_target_pairs={{0,2},{1,3},{2,0},{3,1},{4,6},{5,7},{6,4},{7,5},{8,10},{9,11},{10,... | collective-permute-start | bytes 589832 | tf_op jit(solution)/shard_map/ppermute | solution.py:425
  6.4 8.9 %collective-permute-start.6 = (bf16[96,1024]{1,0:T(8,128)(2,1)S(1)}, bf16[96,1024]{1,0:T(8,128)(2,1)S(1)}, u32[]{:S(2)}, u32[]{:S(2)}) collective-permute-start(bf16[96,1024]{1,0:T(8,128)(2,1)S(1)} %get-tuple-element.39), channel_id=1, source_target_pairs={{0,2},{1,3},{2,0},{3,1},{4,6},{5,7},{6,4},{7,5},{8,10},{9,11},{10,... | collective-permute-start | bytes 589832 | tf_op jit(solution)/shard_map/ppermute | solution.py:425
  6.5 12.6 %collective-permute-start.7 = (bf16[96,1024]{1,0:T(8,128)(2,1)S(1)}, bf16[96,1024]{1,0:T(8,128)(2,1)S(1)}, u32[]{:S(2)}, u32[]{:S(2)}) collective-permute-start(bf16[96,1024]{1,0:T(8,128)(2,1)S(1)} %get-tuple-element.38), channel_id=1, source_target_pairs={{0,3},{1,2},{2,1},{3,0},{4,7},{5,6},{6,5},{7,4},{8,11},{9,10},{10,... | collective-permute-start | bytes 589832 | tf_op jit(solution)/shard_map/ppermute | solution.py:425
  9.2 35.1 %collective-permute-start = (bf16[192,1024]{1,0:T(8,128)(2,1)}, bf16[192,1024]{1,0:T(8,128)(2,1)S(1)}, u32[]{:S(2)}, u32[]{:S(2)}) collective-permute-start(bf16[192,1024]{1,0:T(8,128)(2,1)} %constant_dynamic-slice_fusion.1), channel_id=1, source_target_pairs={{0,1},{1,0},{2,3},{3,2},{4,5},{5,4},{6,7},{7,6},{8,9},{9,8},{10,11... | collective-permute-start | bytes 1179656 | tf_op jit(solution)/shard_map/ppermute | solution.py:425
  10.4 21.9 %collective-permute-start.2 = (bf16[96,1024]{1,0:T(8,128)(2,1)}, bf16[96,1024]{1,0:T(8,128)(2,1)S(1)}, u32[]{:S(2)}, u32[]{:S(2)}) collective-permute-start(bf16[96,1024]{1,0:T(8,128)(2,1)} %get-tuple-element.40), channel_id=1, source_target_pairs={{0,3},{1,2},{2,1},{3,0},{4,7},{5,6},{6,5},{7,4},{8,11},{9,10},{10,... | collective-permute-start | bytes 589832 | tf_op jit(solution)/shard_map/ppermute | solution.py:425
  12.2 20.7 %collective-permute-start.5 = (bf16[192,1024]{1,0:T(8,128)(2,1)}, bf16[192,1024]{1,0:T(8,128)(2,1)S(1)}, u32[]{:S(2)}, u32[]{:S(2)}) collective-permute-start(bf16[192,1024]{1,0:T(8,128)(2,1)} %constant_dynamic-slice_fusion), channel_id=1, source_target_pairs={{0,1},{1,0},{2,3},{3,2},{4,5},{5,4},{6,7},{7,6},{8,9},{9,8},{10,11... | collective-permute-start | bytes 1179656 | tf_op jit(solution)/shard_map/ppermute | solution.py:425
  15.3 19.1 %collective-permute-start.8 = (bf16[96,1024]{1,0:T(8,128)(2,1)S(1)}, bf16[96,1024]{1,0:T(8,128)(2,1)S(1)}, u32[]{:S(2)}, u32[]{:S(2)}) collective-permute-start(bf16[96,1024]{1,0:T(8,128)(2,1)S(1)} %collective-permute-done.6), channel_id=1, source_target_pairs={{0,4},{1,5},{2,6},{3,7},{4,0},{5,1},{6,2},{7,3},{8,12},{9,13},{10,... | collective-permute-start | bytes 589832 | tf_op jit(solution)/shard_map/ppermute | solution.py:433
  19.1 15.4 %collective-permute-start.9 = (bf16[96,1024]{1,0:T(8,128)(2,1)S(1)}, bf16[96,1024]{1,0:T(8,128)(2,1)S(1)}, u32[]{:S(2)}, u32[]{:S(2)}) collective-permute-start(bf16[96,1024]{1,0:T(8,128)(2,1)S(1)} %collective-permute-done.7), channel_id=1, source_target_pairs={{0,4},{1,5},{2,6},{3,7},{4,0},{5,1},{6,2},{7,3},{8,12},{9,13},{10,... | collective-permute-start | bytes 589832 | tf_op jit(solution)/shard_map/ppermute | solution.py:433
  27.9 2.2 %copy-start = (bf16[4,4096,128]{2,1,0:T(8,128)(2,1)S(1)}, bf16[4,4096,128]{2,1,0:T(8,128)(2,1)}, u32[]{:S(2)}) copy-start(bf16[4,4096,128]{2,1,0:T(8,128)(2,1)} %get-tuple-element.42.value_ref.refs_7_) | copy-start | bytes 12582916
  30.1 2.2 %copy-start.2 = (bf16[4,4096,128]{2,1,0:T(8,128)(2,1)S(1)}, bf16[4,4096,128]{2,1,0:T(8,128)(2,1)}, u32[]{:S(2)}) copy-start(bf16[4,4096,128]{2,1,0:T(8,128)(2,1)} %get-tuple-element.43.key_ref.refs_6_) | copy-start | bytes 12582916
  32.2 2.2 %copy-start.4 = (bf16[192,4096]{1,0:T(8,128)(2,1)S(1)}, bf16[192,4096]{1,0:T(8,128)(2,1)}, u32[]{:S(2)}) copy-start(bf16[192,4096]{1,0:T(8,128)(2,1)} %param.7) | copy-start | bytes 4718596
  32.2 2.2 %copy-start.6 = (s32[1,8]{1,0:T(1,128)S(1)}, s32[1,8]{1,0:T(1,128)}, u32[]{:S(2)}) copy-start(s32[1,8]{1,0:T(1,128)} %param.10) | copy-start | bytes 100
  32.3 12.0 %collective-permute-start.3 = (bf16[96,1024]{1,0:T(8,128)(2,1)S(1)}, bf16[96,1024]{1,0:T(8,128)(2,1)S(1)}, u32[]{:S(2)}, u32[]{:S(2)}) collective-permute-start(bf16[96,1024]{1,0:T(8,128)(2,1)S(1)} %collective-permute-done.1), channel_id=1, source_target_pairs={{0,4},{1,5},{2,6},{3,7},{4,0},{5,1},{6,2},{7,3},{8,12},{9,13},{10,... | collective-permute-start | bytes 589832 | tf_op jit(solution)/shard_map/ppermute | solution.py:433
  32.9 11.4 %collective-permute-start.4 = (bf16[96,1024]{1,0:T(8,128)(2,1)S(1)}, bf16[96,1024]{1,0:T(8,128)(2,1)S(1)}, u32[]{:S(2)}, u32[]{:S(2)}) collective-permute-start(bf16[96,1024]{1,0:T(8,128)(2,1)S(1)} %collective-permute-done.2), channel_id=1, source_target_pairs={{0,4},{1,5},{2,6},{3,7},{4,0},{5,1},{6,2},{7,3},{8,12},{9,13},{10,... | collective-permute-start | bytes 589832 | tf_op jit(solution)/shard_map/ppermute | solution.py:433
  34.5 2.2 %copy-start.1 = (bf16[4,4096,128]{2,1,0:T(8,128)(2,1)S(1)}, bf16[4,4096,128]{2,1,0:T(8,128)(2,1)}, u32[]{:S(2)}) copy-start(bf16[4,4096,128]{2,1,0:T(8,128)(2,1)} %get-tuple-element.42.value_ref.refs_7_) | copy-start | bytes 12582916
  36.6 2.2 %copy-start.3 = (bf16[4,4096,128]{2,1,0:T(8,128)(2,1)S(1)}, bf16[4,4096,128]{2,1,0:T(8,128)(2,1)}, u32[]{:S(2)}) copy-start(bf16[4,4096,128]{2,1,0:T(8,128)(2,1)} %get-tuple-element.43.key_ref.refs_6_) | copy-start | bytes 12582916
  38.8 5.5 %copy-start.5 = (bf16[192,4096]{1,0:T(8,128)(2,1)S(1)}, bf16[192,4096]{1,0:T(8,128)(2,1)}, u32[]{:S(2)}) copy-start(bf16[192,4096]{1,0:T(8,128)(2,1)} %param.6) | copy-start | bytes 4718596
  43.7 22.6 %collective-permute-start.10 = (bf16[4,96,1152]{2,1,0:T(8,128)(2,1)S(1)}, bf16[4,96,1152]{2,1,0:T(8,128)(2,1)S(1)}, u32[]{:S(2)}, u32[]{:S(2)}) collective-permute-start(bf16[4,96,1152]{2,1,0:T(8,128)(2,1)S(1)} %get-tuple-element.21.refs_8_), channel_id=1, source_target_pairs={{0,4},{1,5},{2,6},{3,7},{4,0},{5,1},{6,2},{7,3},{8,12},{9,13},{10,... | collective-permute-start | bytes 2654216 | tf_op jit(solution)/shard_map/ppermute | solution.py:466
  61.0 24.3 %collective-permute-start.12 = (bf16[4,48,1152]{2,1,0:T(8,128)(2,1)S(1)}, bf16[4,48,1152]{2,1,0:T(8,128)(2,1)S(1)}, u32[]{:S(2)}, u32[]{:S(2)}) collective-permute-start(bf16[4,48,1152]{2,1,0:T(8,128)(2,1)S(1)} %get-tuple-element.22._), channel_id=1, source_target_pairs={{0,4},{1,5},{2,6},{3,7},{4,0},{5,1},{6,2},{7,3},{8,12},{9,13},{10,... | collective-permute-start | bytes 1327112 | tf_op jit(solution)/shard_map/ppermute | solution.py:466
  84.7 18.2 %collective-permute-start.11 = (bf16[4,48,1152]{2,1,0:T(8,128)(2,1)S(1)}, bf16[4,48,1152]{2,1,0:T(8,128)(2,1)S(1)}, u32[]{:S(2)}, u32[]{:S(2)}) collective-permute-start(bf16[4,48,1152]{2,1,0:T(8,128)(2,1)S(1)} %get-tuple-element.25._), channel_id=1, source_target_pairs={{0,4},{1,5},{2,6},{3,7},{4,0},{5,1},{6,2},{7,3},{8,12},{9,13},{10,... | collective-permute-start | bytes 1327112 | tf_op jit(solution)/shard_map/ppermute | solution.py:466
  86.4 12.1 %collective-permute-start.16 = (bf16[1,48,1152]{2,1,0:T(8,128)(2,1)S(1)}, bf16[1,48,1152]{2,1,0:T(8,128)(2,1)S(1)}, u32[]{:S(2)}, u32[]{:S(2)}) collective-permute-start(bf16[1,48,1152]{2,1,0:T(8,128)(2,1)S(1)} %get-tuple-element.32), channel_id=1, source_target_pairs={{0,8},{1,9},{2,10},{3,11},{4,12},{5,13},{6,14},{7,15},{8,0},{9,1},... | collective-permute-start | bytes 331784 | tf_op jit(solution)/shard_map/ppermute | solution.py:472
  88.1 39.7 %collective-permute-start.19 = (bf16[1,96,1152]{2,1,0:T(8,128)(2,1)S(1)}, bf16[1,96,1152]{2,1,0:T(8,128)(2,1)S(1)}, u32[]{:S(2)}, u32[]{:S(2)}) collective-permute-start(bf16[1,96,1152]{2,1,0:T(8,128)(2,1)S(1)} %get-tuple-element.35), channel_id=1, source_target_pairs={{0,8},{1,9},{2,10},{3,11},{4,12},{5,13},{6,14},{7,15},{8,0},{9,1},... | collective-permute-start | bytes 663560 | tf_op jit(solution)/shard_map/ppermute | solution.py:472
  88.5 15.6 %collective-permute-start.17 = (bf16[1,48,1152]{2,1,0:T(8,128)(2,1)S(1)}, bf16[1,48,1152]{2,1,0:T(8,128)(2,1)S(1)}, u32[]{:S(2)}, u32[]{:S(2)}) collective-permute-start(bf16[1,48,1152]{2,1,0:T(8,128)(2,1)S(1)} %get-tuple-element.33), channel_id=1, source_target_pairs={{0,16},{1,17},{2,18},{3,19},{4,20},{5,21},{6,22},{7,23},{8,24},{9,... | collective-permute-start | bytes 331784 | tf_op jit(solution)/shard_map/ppermute | solution.py:472
  98.4 32.8 %collective-permute-start.20 = (bf16[1,96,1152]{2,1,0:T(8,128)(2,1)S(1)}, bf16[1,96,1152]{2,1,0:T(8,128)(2,1)S(1)}, u32[]{:S(2)}, u32[]{:S(2)}) collective-permute-start(bf16[1,96,1152]{2,1,0:T(8,128)(2,1)S(1)} %get-tuple-element.36), channel_id=1, source_target_pairs={{0,16},{1,17},{2,18},{3,19},{4,20},{5,21},{6,22},{7,23},{8,24},{9,... | collective-permute-start | bytes 663560 | tf_op jit(solution)/shard_map/ppermute | solution.py:472
  98.5 32.7 %collective-permute-start.21 = (bf16[1,96,1152]{2,1,0:T(8,128)(2,1)S(1)}, bf16[1,96,1152]{2,1,0:T(8,128)(2,1)S(1)}, u32[]{:S(2)}, u32[]{:S(2)}) collective-permute-start(bf16[1,96,1152]{2,1,0:T(8,128)(2,1)S(1)} %get-tuple-element.37), channel_id=1, source_target_pairs={{0,24},{1,25},{2,26},{3,27},{4,28},{5,29},{6,30},{7,31},{8,16},{9,... | collective-permute-start | bytes 663560 | tf_op jit(solution)/shard_map/ppermute | solution.py:472
  103.0 17.0 %collective-permute-start.18 = (bf16[1,48,1152]{2,1,0:T(8,128)(2,1)S(1)}, bf16[1,48,1152]{2,1,0:T(8,128)(2,1)S(1)}, u32[]{:S(2)}, u32[]{:S(2)}) collective-permute-start(bf16[1,48,1152]{2,1,0:T(8,128)(2,1)S(1)} %get-tuple-element.34), channel_id=1, source_target_pairs={{0,24},{1,25},{2,26},{3,27},{4,28},{5,29},{6,30},{7,31},{8,16},{9,... | collective-permute-start | bytes 331784 | tf_op jit(solution)/shard_map/ppermute | solution.py:472
  104.2 28.4 %collective-permute-start.13 = (bf16[1,48,1152]{2,1,0:T(8,128)(2,1)S(1)}, bf16[1,48,1152]{2,1,0:T(8,128)(2,1)S(1)}, u32[]{:S(2)}, u32[]{:S(2)}) collective-permute-start(bf16[1,48,1152]{2,1,0:T(8,128)(2,1)S(1)} %get-tuple-element.29), channel_id=1, source_target_pairs={{0,8},{1,9},{2,10},{3,11},{4,12},{5,13},{6,14},{7,15},{8,0},{9,1},... | collective-permute-start | bytes 331784 | tf_op jit(solution)/shard_map/ppermute | solution.py:472
  120.0 15.9 %collective-permute-start.14 = (bf16[1,48,1152]{2,1,0:T(8,128)(2,1)S(1)}, bf16[1,48,1152]{2,1,0:T(8,128)(2,1)S(1)}, u32[]{:S(2)}, u32[]{:S(2)}) collective-permute-start(bf16[1,48,1152]{2,1,0:T(8,128)(2,1)S(1)} %get-tuple-element.30), channel_id=1, source_target_pairs={{0,16},{1,17},{2,18},{3,19},{4,20},{5,21},{6,22},{7,23},{8,24},{9,... | collective-permute-start | bytes 331784 | tf_op jit(solution)/shard_map/ppermute | solution.py:472
  127.8 8.1 %collective-permute-start.15 = (bf16[1,48,1152]{2,1,0:T(8,128)(2,1)S(1)}, bf16[1,48,1152]{2,1,0:T(8,128)(2,1)S(1)}, u32[]{:S(2)}, u32[]{:S(2)}) collective-permute-start(bf16[1,48,1152]{2,1,0:T(8,128)(2,1)S(1)} %get-tuple-element.31), channel_id=1, source_target_pairs={{0,24},{1,25},{2,26},{3,27},{4,28},{5,29},{6,30},{7,31},{8,16},{9,... | collective-permute-start | bytes 331784 | tf_op jit(solution)/shard_map/ppermute | solution.py:472

commit v2 on v1

--- a/solution.py
+++ b/solution.py
@@ -17,18 +17,22 @@
 AXES = ("ctx", "head")
 ATTEND_BYTES = 24 << 20
 MERGE_BYTES = 8 << 20
+PICK_BYTES = 56 << 20
 
 
 def with_ones(values):
     return jnp.concatenate([values, jnp.ones_like(values)], axis=1)
 
 
-def stacked_queries(query_refs, group_size):
+def stacked_queries(query_refs, column_ref, heads, group_size, group, half):
     parts = []
     for head in range(group_size):
         for ref in query_refs:
-            for item in range(ref.shape[0]):
-                parts.append(ref[item, 0, :, head * HD : (head + 1) * HD])
+            column = group * group_size + head
+            if ref.shape[3] > heads * HD:
+                column += column_ref[0] * heads
+            start = pl.multiple_of(column * HD, HD)
+            parts += [ref[item, half, :, pl.ds(start, HD)] for item in range(ref.shape[0])]
     return jnp.concatenate(parts, axis=0)
 
 
@@ -89,25 +93,26 @@
             out_ref[item, :, heads * HD :] = term_lanes(stat_ref[at], heads)
 
 
-def dense_kernel(place_ref, column_ref, *refs, pieces, outs, group_size, block_keys):
+def dense_kernel(place_ref, column_ref, *refs, pieces, outs, group_size, half, block_keys):
     query_refs = refs[:pieces]
     key_ref, value_ref, _ = refs[pieces : pieces + 3]
     out_refs = refs[pieces + 3 : pieces + 3 + outs]
     held_ref, stat_ref = refs[pieces + 3 + outs :]
     group = pl.program_id(0)
     rows = query_refs[0].shape[2]
+    heads = (held_ref.shape[2] - LANES) // HD
 
     @pl.when(group == 0)
     def _():
         stat_ref[...] = jnp.zeros_like(stat_ref)
 
-    queries = stacked_queries(query_refs, group_size)
+    queries = stacked_queries(query_refs, column_ref, heads, group_size, group, half)
     size = chain_rows(queries.shape[0])
     starts = range(0, queries.shape[0], size)
     chains = [None for _ in starts]
     for step in range(key_ref.shape[1] // block_keys):
         span = pl.ds(step * block_keys, block_keys)
-        keys, values = key_ref[0, span, :], with_ones(value_ref[0, span, :])
+        keys, values = key_ref[group, span, :], with_ones(value_ref[group, span, :])
         for index, start in enumerate(starts):
             scores = raw_scores(queries[start : start + size], keys)
             newtop = jnp.max(scores, axis=1, keepdims=True)
@@ -126,52 +131,34 @@
         hand_out(out_refs, held_ref, stat_ref)
 
 
-def kept_kernel(place_ref, column_ref, list_ref, count_ref, *refs, pieces, outs, group_size):
+def kept_kernel(place_ref, column_ref, list_ref, count_ref, *refs, pieces, outs, group_size, half):
     query_refs = refs[:pieces]
     key_ref, value_ref, _ = refs[pieces : pieces + 3]
     out_refs = refs[pieces + 3 : pieces + 3 + outs]
-    held_ref, stat_ref, top_ref, sum_ref, keys_ref, values_ref, sems = refs[pieces + 3 + outs :]
+    held_ref, stat_ref, top_ref, sum_ref = refs[pieces + 3 + outs :]
     group = pl.program_id(0)
     rows = query_refs[0].shape[2]
+    heads = (held_ref.shape[2] - LANES) // HD
     kept = count_ref[0]
-    slots = keys_ref.shape[0]
+    slots = list_ref.shape[0]
     sizes = [size for size in (2, 4) if size < slots] + [min(8, slots)]
     most = sizes[-1]
-    loaded = pl.cdiv(kept, most) * most
-    for size in reversed(sizes[:-1]):
-        loaded = jnp.where(kept <= size, size, loaded)
-
-    def copies(slot):
-        block = list_ref[jnp.minimum(slot, kept - 1)]
-        span = pl.ds(pl.multiple_of(block * BLK, BLK), BLK)
-        return [
-            pltpu.make_async_copy(source.at[:, span, :], held.at[slot], sems.at[which, slot])
-            for which, (source, held) in enumerate(
-                ((key_ref, keys_ref), (value_ref, values_ref))
-            )
-        ]
 
     @pl.when(group == 0)
     def _():
         stat_ref[...] = jnp.zeros_like(stat_ref)
 
-        @pl.loop(0, loaded)
-        def _(slot):
-            for copy in copies(slot):
-                copy.start()
-
-        @pl.loop(0, loaded)
-        def _(slot):
-            for copy in copies(slot):
-                copy.wait()
-
-    queries = stacked_queries(query_refs, group_size)
+    def block_of(ref, slot):
+        block = list_ref[jnp.minimum(slot, kept - 1)]
+        return ref[group, pl.ds(pl.multiple_of(block * BLK, BLK), BLK), :]
+
+    queries = stacked_queries(query_refs, column_ref, heads, group_size, group, half)
     size = chain_rows(queries.shape[0])
     starts = range(0, queries.shape[0], size)
 
     def absorb(first, length, fresh):
-        keys = jnp.concatenate([keys_ref[first + i, group] for i in range(length)], axis=0)
-        values = jnp.concatenate([values_ref[first + i, group] for i in range(length)], axis=0)
+        keys = jnp.concatenate([block_of(key_ref, first + i) for i in range(length)], axis=0)
+        values = jnp.concatenate([block_of(value_ref, first + i) for i in range(length)], axis=0)
         values = with_ones(values)
         slot = lax.broadcasted_iota(jnp.int32, (1, length * BLK), 1) // BLK + first
         chains = []
@@ -214,7 +201,7 @@
         def _():
             hold(absorb(0, most, True))
 
-            @pl.loop(1, loaded // most)
+            @pl.loop(1, pl.cdiv(kept, most))
             def _(step):
                 hold(absorb(step * most, most, False))
 
@@ -224,16 +211,6 @@
     @pl.when(group == pl.num_programs(0) - 1)
     def _():
         hand_out(out_refs, held_ref, stat_ref)
-
-
-def query_spec(piece, own, group_size, kept, half):
-    block = (piece.shape[0], 1, piece.shape[2], group_size * HD)
-
-    def index(group, *rest):
-        column = group + rest[-3 if kept else -1][0] if own else group
-        return (0, half, 0, column)
-
-    return pl.BlockSpec(block, index)
 
 
 def partial_call(pieces, places, column, keys, values, half, outs, after, kept=None):
@@ -244,45 +221,31 @@
     count = sum(piece.shape[0] for piece in pieces)
     width = heads * HD + LANES
     stacked = count * rows * group_size
-    specs = [
-        query_spec(piece, piece.shape[3] > heads * HD, group_size, kept is not None, half)
-        for piece in pieces
-    ]
-    anywhere = pl.BlockSpec(memory_space=pl.ANY)
-    out_shape = [jax.ShapeDtypeStruct((count // outs, rows, width), jnp.bfloat16)] * outs
-    out_specs = [pl.BlockSpec(memory_space=pltpu.VMEM)] * outs
+    vmem = pl.BlockSpec(memory_space=pltpu.VMEM)
     scratch = [
         pltpu.VMEM((count, rows, width), jnp.bfloat16),
         pltpu.VMEM((count, rows, LANES), jnp.float32),
     ]
     if kept is None:
-        whole = pl.BlockSpec((1, length, HD), lambda group, *_: (group, 0, 0))
         kernel = functools.partial(dense_kernel, block_keys=math.gcd(length, 512))
-        operands, cache_specs, reads = (places, column), [whole, whole], length
+        operands, reads = (places, column), length
     else:
-        slots = kept[0].shape[0]
-        slots = slots if slots <= 8 else pl.cdiv(slots, 8) * 8
         kernel = kept_kernel
         operands, reads = (places, column, *kept), 4 * BLK
-        cache_specs = [anywhere] * 2
-        held = stacked if slots > 8 else 8
-        scratch += [
-            pltpu.VMEM((held, LANES), jnp.float32),
-            pltpu.VMEM((held, 2 * HD), jnp.float32),
-            pltpu.VMEM((slots, kv_local, BLK, HD), jnp.bfloat16),
-            pltpu.VMEM((slots, kv_local, BLK, HD), jnp.bfloat16),
-            pltpu.SemaphoreType.DMA((2, slots)),
-        ]
+        held = stacked if kept[0].shape[0] > 8 else 8
+        scratch += [pltpu.VMEM((held, LANES), jnp.float32), pltpu.VMEM((held, 2 * HD), jnp.float32)]
     return pl.pallas_call(
-        functools.partial(kernel, pieces=len(pieces), outs=outs, group_size=group_size),
+        functools.partial(
+            kernel, pieces=len(pieces), outs=outs, group_size=group_size, half=half
+        ),
         grid_spec=pltpu.PrefetchScalarGridSpec(
             num_scalar_prefetch=len(operands),
             grid=(kv_local,),
-            in_specs=specs + cache_specs + [anywhere],
-            out_specs=out_specs,
+            in_specs=[vmem] * (len(pieces) + 2) + [pl.BlockSpec(memory_space=pl.ANY)],
+            out_specs=[vmem] * outs,
             scratch_shapes=scratch,
         ),
-        out_shape=out_shape,
+        out_shape=[jax.ShapeDtypeStruct((count // outs, rows, width), jnp.bfloat16)] * outs,
         compiler_params=pltpu.CompilerParams(vmem_limit_bytes=ATTEND_BYTES),
         cost_estimate=pl.CostEstimate(
             flops=8 * stacked * reads * HD * kv_local,
@@ -382,19 +345,51 @@
     )(spot, mine, theirs, after)
 
 
-def settle_kernel(key_ref, value_ref, out_ref):
-    out_ref[...] = jnp.zeros_like(out_ref)
+def settle_kernel(keys_in, values_in, key_ref, value_ref):
+    pass
 
 
 def settle(keys, values):
-    anywhere = pl.BlockSpec(memory_space=pl.ANY)
+    vmem = pl.BlockSpec(memory_space=pltpu.VMEM)
     return pl.pallas_call(
         settle_kernel,
-        in_specs=[anywhere, anywhere],
-        out_specs=pl.BlockSpec(memory_space=pltpu.VMEM),
-        out_shape=jax.ShapeDtypeStruct((8, LANES), jnp.float32),
+        in_specs=[vmem, vmem],
+        out_specs=[vmem, vmem],
+        out_shape=[jax.ShapeDtypeStruct(x.shape, x.dtype) for x in (keys, values)],
+        input_output_aliases={0: 0, 1: 1},
         compiler_params=pltpu.CompilerParams(vmem_limit_bytes=MERGE_BYTES),
     )(keys, values)
+
+
+def pick_kernel(spot_ref, *refs, boxes):
+    count = len(boxes)
+    sems = refs[-1]
+    sources, outs = refs[: -1 - count], refs[-1 - count : -1]
+    copies = []
+    for index, (which, bit, shared) in enumerate(boxes):
+        rows, columns = outs[index].shape
+        row = pl.multiple_of(spot_ref[1] * rows, rows) if shared else 0
+        column = pl.multiple_of((spot_ref[0] ^ bit) * columns, columns)
+        window = sources[which].at[pl.ds(row, rows), pl.ds(column, columns)]
+        copies.append(pltpu.make_async_copy(window, outs[index], sems.at[index]))
+    for copy in copies:
+        copy.start()
+    for copy in copies:
+        copy.wait()
+
+
+def pick(blocks, spot, boxes, mine):
+    rows = blocks[0].shape[0]
+    shapes = [(rows // 2 if shared else rows, mine) for _, _, shared in boxes]
+    return pl.pallas_call(
+        functools.partial(pick_kernel, boxes=boxes),
+        in_specs=[pl.BlockSpec(memory_space=pltpu.SMEM)]
+        + [pl.BlockSpec(memory_space=pl.ANY)] * len(blocks),
+        out_specs=[pl.BlockSpec(memory_space=pltpu.VMEM)] * len(boxes),
+        out_shape=[jax.ShapeDtypeStruct(shape, jnp.bfloat16) for shape in shapes],
+        scratch_shapes=[pltpu.SemaphoreType.DMA((len(boxes),))],
+        compiler_params=pltpu.CompilerParams(vmem_limit_bytes=PICK_BYTES),
+    )(spot, *blocks)
 
 
 def to_owners(part):
@@ -407,7 +402,7 @@
     return [(c * head + h, (c ^ ctx_bit) * head + (h ^ head_bit)) for c, h in spots]
 
 
-def relayed(shape, q_first, q_second, k_cache):
+def relayed(shape, q_first, q_second):
     head = shape["head"]
     me = lax.axis_index("head")
     spot = lax.axis_index("ctx")
@@ -416,18 +411,20 @@
     mine = wide // head
     half = rows // 2
 
-    def columns_of(block, other, start, count):
-        return lax.dynamic_slice(block, (start, other * mine), (count, mine))
-
-    blocks = (q_second, q_first)
-
-    def sent(block, bit, start, count):
-        return lax.ppermute(columns_of(block, me ^ bit, start, count), AXES, swapped(shape, 0, bit))
-
-    got = [[sent(block, bit, low * half, half) for bit in (2, 3)] for block in blocks]
-    near = [sent(block, 1, 0, rows) for block in blocks]
+    here = jnp.stack([me, low]).astype(jnp.int32)
+
+    def sent(block, bit):
+        return lax.ppermute(block, AXES, swapped(shape, 0, bit))
+
+    boxes = [(0, 2, True), (0, 3, True)]
+    picked = pick([q_second], here, boxes, mine)
+    got = [[sent(x, bit) for x, bit in zip(picked, (2, 3))]]
+    boxes = [(0, 1, False), (1, 1, False), (1, 2, True), (1, 3, True)]
+    near_s, near_f, *picked = pick([q_second, q_first], here, boxes, mine)
+    got.append([sent(x, bit) for x, bit in zip(picked, (2, 3))])
+    near = [sent(near_s, 1), sent(near_f, 1)]
     pieces = []
-    for block, beside, remote in zip(blocks, near, got):
+    for block, beside, remote in zip((q_second, q_first), near, got):
         others = []
         for x in remote:
             others.append(lax.ppermute(x, AXES, swapped(shape, 1, 0)))
@@ -444,8 +441,7 @@
         owner // 2 + jnp.where(owner % 2 == low, len(owners) // 2, 0) for owner in owners
     ]
     places = jnp.stack(places).astype(jnp.int32)
-    column = jnp.reshape(me * k_cache.shape[1], (1,)).astype(jnp.int32)
-    return pieces[0], pieces[1], places, column
+    return pieces[0], pieces[1], places, jnp.reshape(me, (1,)).astype(jnp.int32), got[0][0]
 
 
 def in_halves(pieces, halves):
@@ -454,11 +450,13 @@
 
 def shards(shape, q_first, q_second, k_cache, v_cache, kept_blocks, kept_count):
     ctx, head = shape["ctx"], shape["head"]
-    keys, values = jnp.swapaxes(k_cache, 0, 1), jnp.swapaxes(v_cache, 0, 1)
     owned = q_first.shape[0] * head // ctx
     kept = (kept_blocks[0], kept_count)
     if head == 4 and ctx == 2 * head and owned % 32 == 0:
-        second, first, places, column = relayed(shape, q_first, q_second, k_cache)
+        second, first, places, column, arrived = relayed(shape, q_first, q_second)
+        keys = jnp.swapaxes(k_cache, 0, 1)
+        late, _ = lax.optimization_barrier((v_cache, arrived))
+        keys, values = settle(keys, jnp.swapaxes(late, 0, 1))
         first, second = in_halves(first, 2), in_halves(second, 1)
         spot = jnp.reshape(lax.axis_index("ctx") // 2, (1,)).astype(jnp.int32)
 
@@ -467,17 +465,14 @@
 
         def across_owners(parts):
             moved = []
-            for offset, part in enumerate(parts):
-                if offset:
-                    part = lax.ppermute(part, AXES, swapped(shape, 2 * offset, 0))
-                moved.append(part)
-            return moved
+            for offset in (3, 2, 1):
+                moved.append(lax.ppermute(parts[offset], AXES, swapped(shape, 2 * offset, 0)))
+            return [parts[0], *moved]
 
         def attend(pieces, half, after, kept=None):
             return partial_call(pieces, places, column, keys, values, half, 2, after, kept)
 
-        settled = settle(keys, values)
-        send_s, keep_s = attend(second, 0, settled, kept)
+        send_s, keep_s = attend(second, 0, spot, kept)
         got_s = across_pair(send_s)
         send_a, keep_a = attend(first, 0, send_s)
         got_a = across_pair(send_a)
@@ -492,6 +487,7 @@
         out_second = merge(final_s)[0]
         out_first = merge(final_b, 1, 2, merge(final_a, 0, 2))
         return (out_first.reshape(owned, -1), out_second)
+    keys, values = jnp.swapaxes(k_cache, 0, 1), jnp.swapaxes(v_cache, 0, 1)
     second, first = (
         [lax.all_to_all(block, "head", split_axis=1, concat_axis=0, tiled=True)[None, None]]
         for block in (q_second, q_first)

time: 137 us -> 121 us (0.88)
  local copies, waits for them, and re-layouts: 21.8 us -> 4.67 us
  starting transfers between devices: 51.5 us -> 38.7 us
  waiting for transfers between devices: 16.5 us -> 24.3 us
  Pallas kernels: 45.7 us -> 51.5 us
    ppermute x15, starting transfers between devices: 43.1 us -> 29.5 us  [the longest x9 24 us: across_owners(): lax.ppermute(parts[offset], AXES, swapped(shape, 2 * offset, 0))]
    unnamed x14 -> x6, local copies, waits for them, and re-layouts: 8.75 us -> 0.02 us
    ppermute x15, waiting for transfers between devices: 12.8 us -> 21.4 us  [the longest x9 14.6 us: across_owners(): lax.ppermute(parts[offset], AXES, swapped(shape, 2 * offset, 0))]
    dynamic_slice x4 -> x0, local copies, waits for them, and re-layouts: 6.37 us -> none  [columns_of(): return lax.dynamic_slice(block, (start, other * mine), (count, mine))]
    pallas_call x1 -> x3, Pallas kernels: 0.01 us -> 5.42 us  [the longest x2 5.41 us: pick(): pl.pallas_call(functools.partial(pick_kernel, boxes=boxes), in_specs=[pl....]
    ppermute x3, waiting for transfers between devices: 3.72 us -> 0.01 us  [across_pair(): return lax.ppermute(send, AXES, swapped(shape, 1, 0))]
    ppermute x4, waiting for transfers between devices: 0.01 us -> 2.93 us  [relayed(): others.append(lax.ppermute(x, AXES, swapped(shape, 1, 0)))]
    transpose x1, local copies, waits for them, and re-layouts: 6.57 us -> 4.56 us  [shards(): keys, values = settle(keys, jnp.swapaxes(late, 0, 1))]
  transfers between devices with their start and end apart: 22 -> 22, of which waited for: 5 -> 6; matrix products, arithmetic and copies ran while one was open for 8% -> 4% of each run, Pallas kernels for 33% -> 40%
where the time goes in v2:
time: 121 us
  Pallas kernels  51.5 us (43%)
  starting transfers between devices  38.7 us (32%)
  waiting for transfers between devices  24.3 us (20%)
  local copies, waits for them, and re-layouts  4.67 us (4%)
  between operations  1.49 us (1%)
    pallas_call x3, Pallas kernels, partial_call(): pl.pallas_call(functools.partial(kernel, pieces=len(pieces), outs=outs, g...  38.4 us
    ppermute x9, starting transfers between devices, across_owners(): lax.ppermute(parts[offset], AXES, swapped(shape, 2 * offset, 0))  24 us
    ppermute x9, waiting for transfers between devices, across_owners(): lax.ppermute(parts[offset], AXES, swapped(shape, 2 * offset, 0))  14.6 us
    ppermute x6, waiting for transfers between devices, sent(): return lax.ppermute(block, AXES, swapped(shape, 0, bit))  6.74 us
    ppermute x4, starting transfers between devices, relayed(): others.append(lax.ppermute(x, AXES, swapped(shape, 1, 0)))  5.64 us
    ppermute x6, starting transfers between devices, sent(): return lax.ppermute(block, AXES, swapped(shape, 0, bit))  5.46 us
    pallas_call x2, Pallas kernels, pick(): pl.pallas_call(functools.partial(pick_kernel, boxes=boxes), in_specs=[pl....  5.41 us
    transpose x1, local copies, waits for them, and re-layouts, shards(): keys, values = settle(keys, jnp.swapaxes(late, 0, 1))  4.56 us
  transfers between devices with their start and end apart: 22, of which 6 were waited for; matrix products, arithmetic and copies ran while one was open for 4% of the time, Pallas kernels for 40%

profile of v2, /device:TPU:0, one launch (start us, length us, event | category | flops | bytes accessed | tf_op | source)
XLA Modules:
  0.0 121.3 jit_solution(530505020870613804)
XLA Ops:
  1.3 2.5 %shard_map.78 = (bf16[96,1024]{1,0:T(8,128)(2,1)}, bf16[96,1024]{1,0:T(8,128)(2,1)}) custom-call(s32[2]{0:T(128)} %pad_add_fusion.spot_ref, bf16[192,4096]{1,0:T(8,128)(2,1)} %refs_0_.3), custom_call_target="tpu_custom_call" | custom-call | tf_op jit(solution)/shard_map/pallas_call | solution.py:384
  3.8 3.0 %collective-permute-start.5 = (bf16[96,1024]{1,0:T(8,128)(2,1)}, bf16[96,1024]{1,0:T(8,128)(2,1)S(1)}, u32[]{:S(2)}, u32[]{:S(2)}) collective-permute-start(bf16[96,1024]{1,0:T(8,128)(2,1)} %get-tuple-element.32), channel_id=1, source_target_pairs={{0,2},{1,3},{2,0},{3,1},{4,6},{5,7},{6,4},{7,5},{8,10},{9,11},{10,... | collective-permute-start | bytes 589832 | tf_op jit(solution)/shard_map/ppermute | solution.py:417
  6.8 2.9 %shard_map.77 = (bf16[192,1024]{1,0:T(8,128)(2,1)}, bf16[192,1024]{1,0:T(8,128)(2,1)}, bf16[96,1024]{1,0:T(8,128)(2,1)}, bf16[96,1024]{1,0:T(8,128)(2,1)}) custom-call(s32[2]{0:T(128)} %pad_add_fusion.spot_ref, bf16[192,4096]{1,0:T(8,128)(2,1)} %refs_0_.3, bf16[192,4096]{1,0:T(8,128)(2,1)} %refs_1_.1), custom_call_target="tpu_custom_call" | custom-call | tf_op jit(solution)/shard_map/pallas_call | solution.py:384
  9.7 1.2 %collective-permute-start.1 = (bf16[96,1024]{1,0:T(8,128)(2,1)}, bf16[96,1024]{1,0:T(8,128)(2,1)S(1)}, u32[]{:S(2)}, u32[]{:S(2)}) collective-permute-start(bf16[96,1024]{1,0:T(8,128)(2,1)} %get-tuple-element.30), channel_id=1, source_target_pairs={{0,2},{1,3},{2,0},{3,1},{4,6},{5,7},{6,4},{7,5},{8,10},{9,11},{10,... | collective-permute-start | bytes 589832 | tf_op jit(solution)/shard_map/ppermute | solution.py:417
  11.0 0.7 collective-permute-start.6
  13.0 3.6 %collective-permute-done.7 = bf16[96,1024]{1,0:T(8,128)(2,1)S(1)} collective-permute-done((bf16[96,1024]{1,0:T(8,128)(2,1)}, bf16[96,1024]{1,0:T(8,128)(2,1)S(1)}, u32[]{:S(2)}, u32[]{:S(2)}) %collective-permute-start.7) | collective-permute-done | bytes 196640 | tf_op jit(solution)/shard_map/ppermute | solution.py:417
  16.6 1.5 %collective-permute-start.8 = (bf16[96,1024]{1,0:T(8,128)(2,1)S(1)}, bf16[96,1024]{1,0:T(8,128)(2,1)S(1)}, u32[]{:S(2)}, u32[]{:S(2)}) collective-permute-start(bf16[96,1024]{1,0:T(8,128)(2,1)S(1)} %collective-permute-done.5), channel_id=1, source_target_pairs={{0,4},{1,5},{2,6},{3,7},{4,0},{5,1},{6,2},{7,3},{8,12},{9,13},{10,... | collective-permute-start | bytes 589832 | tf_op jit(solution)/shard_map/ppermute | solution.py:430
  18.1 3.0 %collective-permute-done.1 = bf16[96,1024]{1,0:T(8,128)(2,1)S(1)} collective-permute-done((bf16[96,1024]{1,0:T(8,128)(2,1)}, bf16[96,1024]{1,0:T(8,128)(2,1)S(1)}, u32[]{:S(2)}, u32[]{:S(2)}) %collective-permute-start.1) | collective-permute-done | bytes 196640 | tf_op jit(solution)/shard_map/ppermute | solution.py:417
  21.2 2.0 %collective-permute-start.9 = (bf16[96,1024]{1,0:T(8,128)(2,1)S(1)}, bf16[96,1024]{1,0:T(8,128)(2,1)S(1)}, u32[]{:S(2)}, u32[]{:S(2)}) collective-permute-start(bf16[96,1024]{1,0:T(8,128)(2,1)S(1)} %collective-permute-done.7), channel_id=1, source_target_pairs={{0,4},{1,5},{2,6},{3,7},{4,0},{5,1},{6,2},{7,3},{8,12},{9,13},{10,... | collective-permute-start | bytes 589832 | tf_op jit(solution)/shard_map/ppermute | solution.py:430
  23.2 4.6 %copy_bitcast_fusion = (bf16[4,4096,128]{2,1,0:T(8,128)(2,1)S(1)}, bf16[4,4096,128]{2,1,0:T(8,128)(2,1)S(1)}) fusion(bf16[4096,4,128]{2,1,0:T(4,128)(2,1)} %param.9, bf16[4096,4,128]{2,1,0:T(4,128)(2,1)} %param.8), kind=kLoop, calls=%fused_computation | loop fusion | bytes 16777216 | tf_op jit(solution)/shard_map/transpose | solution.py:459
  27.9 2.0 %collective-permute-start.4 = (bf16[96,1024]{1,0:T(8,128)(2,1)S(1)}, bf16[96,1024]{1,0:T(8,128)(2,1)S(1)}, u32[]{:S(2)}, u32[]{:S(2)}) collective-permute-start(bf16[96,1024]{1,0:T(8,128)(2,1)S(1)} %collective-permute-done.2), channel_id=1, source_target_pairs={{0,4},{1,5},{2,6},{3,7},{4,0},{5,1},{6,2},{7,3},{8,12},{9,13},{10,... | collective-permute-start | bytes 589832 | tf_op jit(solution)/shard_map/ppermute | solution.py:430
  30.0 4.5 %shard_map.80 = (bf16[4,96,1152]{2,1,0:T(8,128)(2,1)S(1)}, bf16[4,96,1152]{2,1,0:T(8,128)(2,1)S(1)}) custom-call(s32[8]{0:T(128)S(1)} %stack.42.place_ref, s32[1]{0:T(128)} %bitcast.9.column_ref, s32[8]{0:T(128)S(1)} %bitcast.48, s32[1]{0:T(128)S(6)} %copy.18.count_ref, bf16[2,1,96,4096]{3,2,1,0:T(8,128)(2,1)S(1)} %bitcast.30, ...), custom_call_target="tpu_custom_call" | custom-call | flops 3221225472 | bytes 1048576 | tf_op jit(solution)/shard_map/pallas_call | solution.py:237
  34.5 1.1 collective-permute-start.10
  35.6 2.9 %collective-permute-done.4 = bf16[96,1024]{1,0:T(8,128)(2,1)S(1)} collective-permute-done((bf16[96,1024]{1,0:T(8,128)(2,1)S(1)}, bf16[96,1024]{1,0:T(8,128)(2,1)S(1)}, u32[]{:S(2)}, u32[]{:S(2)}) %collective-permute-start.4) | collective-permute-done | bytes 196640 | tf_op jit(solution)/shard_map/ppermute | solution.py:430
  38.5 17.0 %shard_map.81 = (bf16[4,48,1152]{2,1,0:T(8,128)(2,1)S(1)}, bf16[4,48,1152]{2,1,0:T(8,128)(2,1)S(1)}) custom-call(s32[8]{0:T(128)S(1)} %stack.42.place_ref, s32[1]{0:T(128)} %bitcast.9.column_ref, bf16[2,2,48,4096]{3,2,1,0:T(8,128)(2,1)S(1)} %bitcast.31, bf16[2,2,48,1024]{3,2,1,0:T(8,128)(2,1)S(1)} %bitcast.34, bf16[1,2,48,1024]{3,2,1,0:T(8,128)(2,1)S(1)} %bitcast.36, ...), custom_call_target="tpu_custom_call" | custom-call | flops 12884901888 | bytes 8388608 | tf_op jit(solution)/shard_map/pallas_call | solution.py:237
  55.6 1.5 %collective-permute-start.12 = (bf16[4,48,1152]{2,1,0:T(8,128)(2,1)S(1)}, bf16[4,48,1152]{2,1,0:T(8,128)(2,1)S(1)}, u32[]{:S(2)}, u32[]{:S(2)}) collective-permute-start(bf16[4,48,1152]{2,1,0:T(8,128)(2,1)S(1)} %get-tuple-element.40._), channel_id=1, source_target_pairs={{0,4},{1,5},{2,6},{3,7},{4,0},{5,1},{6,2},{7,3},{8,12},{9,13},{10,... | collective-permute-start | bytes 1327112 | tf_op jit(solution)/shard_map/ppermute | solution.py:464
  57.0 1.9 %shard_map.82 = (bf16[1,96,1152]{2,1,0:T(8,128)(2,1)S(1)}, bf16[1,96,1152]{2,1,0:T(8,128)(2,1)S(1)}, bf16[1,96,1152]{2,1,0:T(8,128)(2,1)S(1)}, bf16[1,96,1152]{2,1,0:T(8,128)(2,1)S(1)}) custom-call(s32[1]{0:T(128)} %bitcast.refs_8_.spot_ref, bf16[4,96,1152]{2,1,0:T(8,128)(2,1)S(1)} %get-tuple-element.38.mine_ref, ...), custom_call_target="tpu_custom_call" | custom-call | flops 3538944 | bytes 2654208 | tf_op jit(solution)/shard_map/pallas_call | solution.py:329
  58.9 16.9 %shard_map.83 = (bf16[4,48,1152]{2,1,0:T(8,128)(2,1)S(1)}, bf16[4,48,1152]{2,1,0:T(8,128)(2,1)S(1)}) custom-call(s32[8]{0:T(128)S(1)} %stack.42.place_ref, s32[1]{0:T(128)} %bitcast.9.column_ref, bf16[2,2,48,4096]{3,2,1,0:T(8,128)(2,1)S(1)} %bitcast.32, bf16[2,2,48,1024]{3,2,1,0:T(8,128)(2,1)S(1)} %bitcast.35, bf16[1,2,48,1024]{3,2,1,0:T(8,128)(2,1)S(1)} %bitcast.37, ...), custom_call_target="tpu_custom_call" | custom-call | flops 12884901888 | bytes 8388608 | tf_op jit(solution)/shard_map/pallas_call | solution.py:237
  75.8 1.0 collective-permute-start.11
  76.8 1.2 shard_map.84
  78.0 4.2 %collective-permute-start.16 = (bf16[1,48,1152]{2,1,0:T(8,128)(2,1)S(1)}, bf16[1,48,1152]{2,1,0:T(8,128)(2,1)S(1)}, u32[]{:S(2)}, u32[]{:S(2)}) collective-permute-start(bf16[1,48,1152]{2,1,0:T(8,128)(2,1)S(1)} %get-tuple-element.50), channel_id=1, source_target_pairs={{0,24},{1,25},{2,26},{3,27},{4,28},{5,29},{6,30},{7,31},{8,16},{9,... | collective-permute-start | bytes 331784 | tf_op jit(solution)/shard_map/ppermute | solution.py:469
  82.3 5.1 %collective-permute-start.20 = (bf16[1,96,1152]{2,1,0:T(8,128)(2,1)S(1)}, bf16[1,96,1152]{2,1,0:T(8,128)(2,1)S(1)}, u32[]{:S(2)}, u32[]{:S(2)}) collective-permute-start(bf16[1,96,1152]{2,1,0:T(8,128)(2,1)S(1)} %get-tuple-element.54), channel_id=1, source_target_pairs={{0,16},{1,17},{2,18},{3,19},{4,20},{5,21},{6,22},{7,23},{8,24},{9,... | collective-permute-start | bytes 663560 | tf_op jit(solution)/shard_map/ppermute | solution.py:469
  87.3 9.1 %collective-permute-start.17 = (bf16[1,48,1152]{2,1,0:T(8,128)(2,1)S(1)}, bf16[1,48,1152]{2,1,0:T(8,128)(2,1)S(1)}, u32[]{:S(2)}, u32[]{:S(2)}) collective-permute-start(bf16[1,48,1152]{2,1,0:T(8,128)(2,1)S(1)} %get-tuple-element.51), channel_id=1, source_target_pairs={{0,16},{1,17},{2,18},{3,19},{4,20},{5,21},{6,22},{7,23},{8,24},{9,... | collective-permute-start | bytes 331784 | tf_op jit(solution)/shard_map/ppermute | solution.py:469
  96.4 1.2 %collective-permute-start.18 = (bf16[1,48,1152]{2,1,0:T(8,128)(2,1)S(1)}, bf16[1,48,1152]{2,1,0:T(8,128)(2,1)S(1)}, u32[]{:S(2)}, u32[]{:S(2)}) collective-permute-start(bf16[1,48,1152]{2,1,0:T(8,128)(2,1)S(1)} %get-tuple-element.52), channel_id=1, source_target_pairs={{0,8},{1,9},{2,10},{3,11},{4,12},{5,13},{6,14},{7,15},{8,0},{9,1},... | collective-permute-start | bytes 331784 | tf_op jit(solution)/shard_map/ppermute | solution.py:469
  97.7 1.2 shard_map.85
  98.8 10.0 %collective-permute-done.17.refs_2_ = bf16[1,48,1152]{2,1,0:T(8,128)(2,1)S(1)} collective-permute-done((bf16[1,48,1152]{2,1,0:T(8,128)(2,1)S(1)}, bf16[1,48,1152]{2,1,0:T(8,128)(2,1)S(1)}, u32[]{:S(2)}, u32[]{:S(2)}) %collective-permute-start.17) | collective-permute-done | bytes 110624 | tf_op jit(solution)/shard_map/ppermute | solution.py:469
  108.8 2.8 %collective-permute-start.13 = (bf16[1,48,1152]{2,1,0:T(8,128)(2,1)S(1)}, bf16[1,48,1152]{2,1,0:T(8,128)(2,1)S(1)}, u32[]{:S(2)}, u32[]{:S(2)}) collective-permute-start(bf16[1,48,1152]{2,1,0:T(8,128)(2,1)S(1)} %get-tuple-element.47), channel_id=1, source_target_pairs={{0,24},{1,25},{2,26},{3,27},{4,28},{5,29},{6,30},{7,31},{8,16},{9,... | collective-permute-start | bytes 331784 | tf_op jit(solution)/shard_map/ppermute | solution.py:469
  111.6 1.6 %collective-permute-start.15 = (bf16[1,48,1152]{2,1,0:T(8,128)(2,1)S(1)}, bf16[1,48,1152]{2,1,0:T(8,128)(2,1)S(1)}, u32[]{:S(2)}, u32[]{:S(2)}) collective-permute-start(bf16[1,48,1152]{2,1,0:T(8,128)(2,1)S(1)} %get-tuple-element.49), channel_id=1, source_target_pairs={{0,8},{1,9},{2,10},{3,11},{4,12},{5,13},{6,14},{7,15},{8,0},{9,1},... | collective-permute-start | bytes 331784 | tf_op jit(solution)/shard_map/ppermute | solution.py:469
  113.2 1.0 shard_map.86.refs_4_
  114.3 1.3 %shard_map.88 = bf16[1,96,1024]{2,1,0:T(8,128)(2,1)} custom-call(bf16[1,96,1152]{2,1,0:T(8,128)(2,1)S(1)} %get-tuple-element.41.refs_8_.refs_0_, bf16[1,96,1152]{2,1,0:T(8,128)(2,1)S(1)} %collective-permute-done.19.refs_1_, bf16[1,96,1152]{2,1,0:T(8,128)(2,1)S(1)} %collective-permute-done.20.refs_2_, bf16[1,96,1152]{2,1,0:T(8,128)(2,1)S(1)} %collective-permute-done.21.refs_3_), custom_call_target="tpu_custom_call" | custom-call | flops 1572864 | bytes 884736 | tf_op jit(solution)/shard_map/pallas_call | solution.py:299
  116.1 4.1 %collective-permute-done.14.refs_2_ = bf16[1,48,1152]{2,1,0:T(8,128)(2,1)S(1)} collective-permute-done((bf16[1,48,1152]{2,1,0:T(8,128)(2,1)S(1)}, bf16[1,48,1152]{2,1,0:T(8,128)(2,1)S(1)}, u32[]{:S(2)}, u32[]{:S(2)}) %collective-permute-start.14) | collective-permute-done | bytes 110624 | tf_op jit(solution)/shard_map/ppermute | solution.py:469
  120.2 1.0 shard_map.87
  (33 shorter events, 2.0 us)
Async XLA Ops:
  3.8 9.0 %collective-permute-start.5 = (bf16[96,1024]{1,0:T(8,128)(2,1)}, bf16[96,1024]{1,0:T(8,128)(2,1)S(1)}, u32[]{:S(2)}, u32[]{:S(2)}) collective-permute-start(bf16[96,1024]{1,0:T(8,128)(2,1)} %get-tuple-element.32), channel_id=1, source_target_pairs={{0,2},{1,3},{2,0},{3,1},{4,6},{5,7},{6,4},{7,5},{8,10},{9,11},{10,... | collective-permute-start | bytes 589832 | tf_op jit(solution)/shard_map/ppermute | solution.py:417
  6.8 9.8 %collective-permute-start.7 = (bf16[96,1024]{1,0:T(8,128)(2,1)}, bf16[96,1024]{1,0:T(8,128)(2,1)S(1)}, u32[]{:S(2)}, u32[]{:S(2)}) collective-permute-start(bf16[96,1024]{1,0:T(8,128)(2,1)} %get-tuple-element.37), channel_id=1, source_target_pairs={{0,3},{1,2},{2,1},{3,0},{4,7},{5,6},{6,5},{7,4},{8,11},{9,10},{10,... | collective-permute-start | bytes 589832 | tf_op jit(solution)/shard_map/ppermute | solution.py:417
  9.7 11.4 %collective-permute-start.1 = (bf16[96,1024]{1,0:T(8,128)(2,1)}, bf16[96,1024]{1,0:T(8,128)(2,1)S(1)}, u32[]{:S(2)}, u32[]{:S(2)}) collective-permute-start(bf16[96,1024]{1,0:T(8,128)(2,1)} %get-tuple-element.30), channel_id=1, source_target_pairs={{0,2},{1,3},{2,0},{3,1},{4,6},{5,7},{6,4},{7,5},{8,10},{9,11},{10,... | collective-permute-start | bytes 589832 | tf_op jit(solution)/shard_map/ppermute | solution.py:417
  11.0 16.9 %collective-permute-start.6 = (bf16[192,1024]{1,0:T(8,128)(2,1)}, bf16[192,1024]{1,0:T(8,128)(2,1)S(1)}, u32[]{:S(2)}, u32[]{:S(2)}) collective-permute-start(bf16[192,1024]{1,0:T(8,128)(2,1)} %get-tuple-element.36), channel_id=1, source_target_pairs={{0,1},{1,0},{2,3},{3,2},{4,5},{5,4},{6,7},{7,6},{8,9},{9,8},{10,11... | collective-permute-start | bytes 1179656 | tf_op jit(solution)/shard_map/ppermute | solution.py:417
  11.7 16.2 %collective-permute-start.2 = (bf16[96,1024]{1,0:T(8,128)(2,1)}, bf16[96,1024]{1,0:T(8,128)(2,1)S(1)}, u32[]{:S(2)}, u32[]{:S(2)}) collective-permute-start(bf16[96,1024]{1,0:T(8,128)(2,1)} %get-tuple-element.31), channel_id=1, source_target_pairs={{0,3},{1,2},{2,1},{3,0},{4,7},{5,6},{6,5},{7,4},{8,11},{9,10},{10,... | collective-permute-start | bytes 589832 | tf_op jit(solution)/shard_map/ppermute | solution.py:417
  12.8 25.8 %collective-permute-start = (bf16[192,1024]{1,0:T(8,128)(2,1)}, bf16[192,1024]{1,0:T(8,128)(2,1)S(1)}, u32[]{:S(2)}, u32[]{:S(2)}) collective-permute-start(bf16[192,1024]{1,0:T(8,128)(2,1)} %get-tuple-element.29), channel_id=1, source_target_pairs={{0,1},{1,0},{2,3},{3,2},{4,5},{5,4},{6,7},{7,6},{8,9},{9,8},{10,11... | collective-permute-start | bytes 1179656 | tf_op jit(solution)/shard_map/ppermute | solution.py:417
  16.6 13.3 %collective-permute-start.8 = (bf16[96,1024]{1,0:T(8,128)(2,1)S(1)}, bf16[96,1024]{1,0:T(8,128)(2,1)S(1)}, u32[]{:S(2)}, u32[]{:S(2)}) collective-permute-start(bf16[96,1024]{1,0:T(8,128)(2,1)S(1)} %collective-permute-done.5), channel_id=1, source_target_pairs={{0,4},{1,5},{2,6},{3,7},{4,0},{5,1},{6,2},{7,3},{8,12},{9,13},{10,... | collective-permute-start | bytes 589832 | tf_op jit(solution)/shard_map/ppermute | solution.py:430
  21.2 8.8 %collective-permute-start.9 = (bf16[96,1024]{1,0:T(8,128)(2,1)S(1)}, bf16[96,1024]{1,0:T(8,128)(2,1)S(1)}, u32[]{:S(2)}, u32[]{:S(2)}) collective-permute-start(bf16[96,1024]{1,0:T(8,128)(2,1)S(1)} %collective-permute-done.7), channel_id=1, source_target_pairs={{0,4},{1,5},{2,6},{3,7},{4,0},{5,1},{6,2},{7,3},{8,12},{9,13},{10,... | collective-permute-start | bytes 589832 | tf_op jit(solution)/shard_map/ppermute | solution.py:430
  27.8 2.1 %copy-start = (bf16[192,4096]{1,0:T(8,128)(2,1)S(1)}, bf16[192,4096]{1,0:T(8,128)(2,1)}, u32[]{:S(2)}) copy-start(bf16[192,4096]{1,0:T(8,128)(2,1)} %refs_0_.3) | copy-start | bytes 4718596
  27.8 2.1 %copy-start.2 = (s32[1,8]{1,0:T(1,128)S(1)}, s32[1,8]{1,0:T(1,128)}, u32[]{:S(2)}) copy-start(s32[1,8]{1,0:T(1,128)} %param.10) | copy-start | bytes 100
  27.8 7.8 %collective-permute-start.3 = (bf16[96,1024]{1,0:T(8,128)(2,1)S(1)}, bf16[96,1024]{1,0:T(8,128)(2,1)S(1)}, u32[]{:S(2)}, u32[]{:S(2)}) collective-permute-start(bf16[96,1024]{1,0:T(8,128)(2,1)S(1)} %collective-permute-done.1), channel_id=1, source_target_pairs={{0,4},{1,5},{2,6},{3,7},{4,0},{5,1},{6,2},{7,3},{8,12},{9,13},{10,... | collective-permute-start | bytes 589832 | tf_op jit(solution)/shard_map/ppermute | solution.py:430
  27.9 10.6 %collective-permute-start.4 = (bf16[96,1024]{1,0:T(8,128)(2,1)S(1)}, bf16[96,1024]{1,0:T(8,128)(2,1)S(1)}, u32[]{:S(2)}, u32[]{:S(2)}) collective-permute-start(bf16[96,1024]{1,0:T(8,128)(2,1)S(1)} %collective-permute-done.2), channel_id=1, source_target_pairs={{0,4},{1,5},{2,6},{3,7},{4,0},{5,1},{6,2},{7,3},{8,12},{9,13},{10,... | collective-permute-start | bytes 589832 | tf_op jit(solution)/shard_map/ppermute | solution.py:430
  30.0 8.6 %copy-start.1 = (bf16[192,4096]{1,0:T(8,128)(2,1)S(1)}, bf16[192,4096]{1,0:T(8,128)(2,1)}, u32[]{:S(2)}) copy-start(bf16[192,4096]{1,0:T(8,128)(2,1)} %refs_1_.1) | copy-start | bytes 4718596
  34.5 22.5 %collective-permute-start.10 = (bf16[4,96,1152]{2,1,0:T(8,128)(2,1)S(1)}, bf16[4,96,1152]{2,1,0:T(8,128)(2,1)S(1)}, u32[]{:S(2)}, u32[]{:S(2)}) collective-permute-start(bf16[4,96,1152]{2,1,0:T(8,128)(2,1)S(1)} %get-tuple-element.39.refs_8_), channel_id=1, source_target_pairs={{0,4},{1,5},{2,6},{3,7},{4,0},{5,1},{6,2},{7,3},{8,12},{9,13},{10,... | collective-permute-start | bytes 2654216 | tf_op jit(solution)/shard_map/ppermute | solution.py:464
  55.6 21.3 %collective-permute-start.12 = (bf16[4,48,1152]{2,1,0:T(8,128)(2,1)S(1)}, bf16[4,48,1152]{2,1,0:T(8,128)(2,1)S(1)}, u32[]{:S(2)}, u32[]{:S(2)}) collective-permute-start(bf16[4,48,1152]{2,1,0:T(8,128)(2,1)S(1)} %get-tuple-element.40._), channel_id=1, source_target_pairs={{0,4},{1,5},{2,6},{3,7},{4,0},{5,1},{6,2},{7,3},{8,12},{9,13},{10,... | collective-permute-start | bytes 1327112 | tf_op jit(solution)/shard_map/ppermute | solution.py:464
  75.8 20.6 %collective-permute-start.11 = (bf16[4,48,1152]{2,1,0:T(8,128)(2,1)S(1)}, bf16[4,48,1152]{2,1,0:T(8,128)(2,1)S(1)}, u32[]{:S(2)}, u32[]{:S(2)}) collective-permute-start(bf16[4,48,1152]{2,1,0:T(8,128)(2,1)S(1)} %get-tuple-element.43._), channel_id=1, source_target_pairs={{0,4},{1,5},{2,6},{3,7},{4,0},{5,1},{6,2},{7,3},{8,12},{9,13},{10,... | collective-permute-start | bytes 1327112 | tf_op jit(solution)/shard_map/ppermute | solution.py:464
  78.0 9.3 %collective-permute-start.16 = (bf16[1,48,1152]{2,1,0:T(8,128)(2,1)S(1)}, bf16[1,48,1152]{2,1,0:T(8,128)(2,1)S(1)}, u32[]{:S(2)}, u32[]{:S(2)}) collective-permute-start(bf16[1,48,1152]{2,1,0:T(8,128)(2,1)S(1)} %get-tuple-element.50), channel_id=1, source_target_pairs={{0,24},{1,25},{2,26},{3,27},{4,28},{5,29},{6,30},{7,31},{8,16},{9,... | collective-permute-start | bytes 331784 | tf_op jit(solution)/shard_map/ppermute | solution.py:469
  82.2 29.4 %collective-permute-start.19 = (bf16[1,96,1152]{2,1,0:T(8,128)(2,1)S(1)}, bf16[1,96,1152]{2,1,0:T(8,128)(2,1)S(1)}, u32[]{:S(2)}, u32[]{:S(2)}) collective-permute-start(bf16[1,96,1152]{2,1,0:T(8,128)(2,1)S(1)} %get-tuple-element.53), channel_id=1, source_target_pairs={{0,24},{1,25},{2,26},{3,27},{4,28},{5,29},{6,30},{7,31},{8,16},{9,... | collective-permute-start | bytes 663560 | tf_op jit(solution)/shard_map/ppermute | solution.py:469
  82.3 32.0 %collective-permute-start.20 = (bf16[1,96,1152]{2,1,0:T(8,128)(2,1)S(1)}, bf16[1,96,1152]{2,1,0:T(8,128)(2,1)S(1)}, u32[]{:S(2)}, u32[]{:S(2)}) collective-permute-start(bf16[1,96,1152]{2,1,0:T(8,128)(2,1)S(1)} %get-tuple-element.54), channel_id=1, source_target_pairs={{0,16},{1,17},{2,18},{3,19},{4,20},{5,21},{6,22},{7,23},{8,24},{9,... | collective-permute-start | bytes 663560 | tf_op jit(solution)/shard_map/ppermute | solution.py:469
  87.3 26.9 %collective-permute-start.21 = (bf16[1,96,1152]{2,1,0:T(8,128)(2,1)S(1)}, bf16[1,96,1152]{2,1,0:T(8,128)(2,1)S(1)}, u32[]{:S(2)}, u32[]{:S(2)}) collective-permute-start(bf16[1,96,1152]{2,1,0:T(8,128)(2,1)S(1)} %get-tuple-element.55), channel_id=1, source_target_pairs={{0,8},{1,9},{2,10},{3,11},{4,12},{5,13},{6,14},{7,15},{8,0},{9,1},... | collective-permute-start | bytes 663560 | tf_op jit(solution)/shard_map/ppermute | solution.py:469
  87.3 21.5 %collective-permute-start.17 = (bf16[1,48,1152]{2,1,0:T(8,128)(2,1)S(1)}, bf16[1,48,1152]{2,1,0:T(8,128)(2,1)S(1)}, u32[]{:S(2)}, u32[]{:S(2)}) collective-permute-start(bf16[1,48,1152]{2,1,0:T(8,128)(2,1)S(1)} %get-tuple-element.51), channel_id=1, source_target_pairs={{0,16},{1,17},{2,18},{3,19},{4,20},{5,21},{6,22},{7,23},{8,24},{9,... | collective-permute-start | bytes 331784 | tf_op jit(solution)/shard_map/ppermute | solution.py:469
  96.4 15.1 %collective-permute-start.18 = (bf16[1,48,1152]{2,1,0:T(8,128)(2,1)S(1)}, bf16[1,48,1152]{2,1,0:T(8,128)(2,1)S(1)}, u32[]{:S(2)}, u32[]{:S(2)}) collective-permute-start(bf16[1,48,1152]{2,1,0:T(8,128)(2,1)S(1)} %get-tuple-element.52), channel_id=1, source_target_pairs={{0,8},{1,9},{2,10},{3,11},{4,12},{5,13},{6,14},{7,15},{8,0},{9,1},... | collective-permute-start | bytes 331784 | tf_op jit(solution)/shard_map/ppermute | solution.py:469
  108.8 7.3 %collective-permute-start.13 = (bf16[1,48,1152]{2,1,0:T(8,128)(2,1)S(1)}, bf16[1,48,1152]{2,1,0:T(8,128)(2,1)S(1)}, u32[]{:S(2)}, u32[]{:S(2)}) collective-permute-start(bf16[1,48,1152]{2,1,0:T(8,128)(2,1)S(1)} %get-tuple-element.47), channel_id=1, source_target_pairs={{0,24},{1,25},{2,26},{3,27},{4,28},{5,29},{6,30},{7,31},{8,16},{9,... | collective-permute-start | bytes 331784 | tf_op jit(solution)/shard_map/ppermute | solution.py:469
  111.6 8.7 %collective-permute-start.14 = (bf16[1,48,1152]{2,1,0:T(8,128)(2,1)S(1)}, bf16[1,48,1152]{2,1,0:T(8,128)(2,1)S(1)}, u32[]{:S(2)}, u32[]{:S(2)}) collective-permute-start(bf16[1,48,1152]{2,1,0:T(8,128)(2,1)S(1)} %get-tuple-element.48), channel_id=1, source_target_pairs={{0,16},{1,17},{2,18},{3,19},{4,20},{5,21},{6,22},{7,23},{8,24},{9,... | collective-permute-start | bytes 331784 | tf_op jit(solution)/shard_map/ppermute | solution.py:469
  111.6 8.6 %collective-permute-start.15 = (bf16[1,48,1152]{2,1,0:T(8,128)(2,1)S(1)}, bf16[1,48,1152]{2,1,0:T(8,128)(2,1)S(1)}, u32[]{:S(2)}, u32[]{:S(2)}) collective-permute-start(bf16[1,48,1152]{2,1,0:T(8,128)(2,1)S(1)} %get-tuple-element.49), channel_id=1, source_target_pairs={{0,8},{1,9},{2,10},{3,11},{4,12},{5,13},{6,14},{7,15},{8,0},{9,1},... | collective-permute-start | bytes 331784 | tf_op jit(solution)/shard_map/ppermute | solution.py:469

commit v3 on v2

--- a/solution.py
+++ b/solution.py
@@ -24,15 +24,15 @@
     return jnp.concatenate([values, jnp.ones_like(values)], axis=1)
 
 
-def stacked_queries(query_refs, column_ref, heads, group_size, group, half):
+def stacked_queries(query_refs, column_ref, heads, group_size, group, span):
     parts = []
     for head in range(group_size):
         for ref in query_refs:
             column = group * group_size + head
-            if ref.shape[3] > heads * HD:
+            if ref.shape[2] > heads * HD:
                 column += column_ref[0] * heads
             start = pl.multiple_of(column * HD, HD)
-            parts += [ref[item, half, :, pl.ds(start, HD)] for item in range(ref.shape[0])]
+            parts += [ref[item, slice(*span), pl.ds(start, HD)] for item in range(ref.shape[0])]
     return jnp.concatenate(parts, axis=0)
 
 
@@ -43,7 +43,7 @@
 
 
 def chain_rows(total):
-    return math.gcd(total, 384)
+    return next(size for size in (384, 512, 256, 128, total) if total % size == 0)
 
 
 def in_terms(level):
@@ -93,26 +93,26 @@
             out_ref[item, :, heads * HD :] = term_lanes(stat_ref[at], heads)
 
 
-def dense_kernel(place_ref, column_ref, *refs, pieces, outs, group_size, half, block_keys):
+def dense_kernel(place_ref, column_ref, *refs, pieces, outs, group_size, span, block_keys):
     query_refs = refs[:pieces]
     key_ref, value_ref, _ = refs[pieces : pieces + 3]
     out_refs = refs[pieces + 3 : pieces + 3 + outs]
     held_ref, stat_ref = refs[pieces + 3 + outs :]
     group = pl.program_id(0)
-    rows = query_refs[0].shape[2]
+    rows = span[1] - span[0]
     heads = (held_ref.shape[2] - LANES) // HD
 
     @pl.when(group == 0)
     def _():
         stat_ref[...] = jnp.zeros_like(stat_ref)
 
-    queries = stacked_queries(query_refs, column_ref, heads, group_size, group, half)
+    queries = stacked_queries(query_refs, column_ref, heads, group_size, group, span)
     size = chain_rows(queries.shape[0])
     starts = range(0, queries.shape[0], size)
     chains = [None for _ in starts]
     for step in range(key_ref.shape[1] // block_keys):
-        span = pl.ds(step * block_keys, block_keys)
-        keys, values = key_ref[group, span, :], with_ones(value_ref[group, span, :])
+        here = pl.ds(step * block_keys, block_keys)
+        keys, values = key_ref[group, here, :], with_ones(value_ref[group, here, :])
         for index, start in enumerate(starts):
             scores = raw_scores(queries[start : start + size], keys)
             newtop = jnp.max(scores, axis=1, keepdims=True)
@@ -131,13 +131,13 @@
         hand_out(out_refs, held_ref, stat_ref)
 
 
-def kept_kernel(place_ref, column_ref, list_ref, count_ref, *refs, pieces, outs, group_size, half):
+def kept_kernel(place_ref, column_ref, list_ref, count_ref, *refs, pieces, outs, group_size, span):
     query_refs = refs[:pieces]
     key_ref, value_ref, _ = refs[pieces : pieces + 3]
     out_refs = refs[pieces + 3 : pieces + 3 + outs]
     held_ref, stat_ref, top_ref, sum_ref = refs[pieces + 3 + outs :]
     group = pl.program_id(0)
-    rows = query_refs[0].shape[2]
+    rows = span[1] - span[0]
     heads = (held_ref.shape[2] - LANES) // HD
     kept = count_ref[0]
     slots = list_ref.shape[0]
@@ -152,7 +152,7 @@
         block = list_ref[jnp.minimum(slot, kept - 1)]
         return ref[group, pl.ds(pl.multiple_of(block * BLK, BLK), BLK), :]
 
-    queries = stacked_queries(query_refs, column_ref, heads, group_size, group, half)
+    queries = stacked_queries(query_refs, column_ref, heads, group_size, group, span)
     size = chain_rows(queries.shape[0])
     starts = range(0, queries.shape[0], size)
 
@@ -163,17 +163,17 @@
         slot = lax.broadcasted_iota(jnp.int32, (1, length * BLK), 1) // BLK + first
         chains = []
         for start in starts:
-            span = pl.ds(start, size)
+            held = pl.ds(start, size)
             scores = raw_scores(queries[start : start + size], keys)
             scores = jnp.where(slot < kept, scores, -jnp.inf)
             newtop = jnp.max(scores, axis=1, keepdims=True)
             if not fresh:
-                top = top_ref[span, :1]
+                top = top_ref[held, :1]
                 newtop = jnp.maximum(top, newtop)
             weights = jnp.exp2(scores - newtop).astype(jnp.bfloat16)
             summed = jnp.dot(weights, values, preferred_element_type=jnp.float32)
             if not fresh:
-                summed = sum_ref[span, :] * jnp.exp2(top - newtop) + summed
+                summed = sum_ref[held, :] * jnp.exp2(top - newtop) + summed
             chains.append((newtop, summed))
         return chains
 
@@ -193,9 +193,9 @@
 
         def hold(chains):
             for start, (top, summed) in zip(starts, chains):
-                span = pl.ds(start, size)
-                sum_ref[span, :] = summed
-                top_ref[span, :] = jnp.broadcast_to(top, (size, LANES))
+                held = pl.ds(start, size)
+                sum_ref[held, :] = summed
+                top_ref[held, :] = jnp.broadcast_to(top, (size, LANES))
 
         @pl.when(kept > most)
         def _():
@@ -205,19 +205,19 @@
             def _(step):
                 hold(absorb(step * most, most, False))
 
-            spans = [pl.ds(start, size) for start in starts]
-            finish([(top_ref[span, :1], sum_ref[span, :]) for span in spans])
+            holds = [pl.ds(start, size) for start in starts]
+            finish([(top_ref[held, :1], sum_ref[held, :]) for held in holds])
 
     @pl.when(group == pl.num_programs(0) - 1)
     def _():
         hand_out(out_refs, held_ref, stat_ref)
 
 
-def partial_call(pieces, places, column, keys, values, half, outs, after, kept=None):
+def partial_call(pieces, places, column, keys, values, span, outs, after, kept=None):
     kv_local, length, _ = keys.shape
-    heads = pieces[-1].shape[3] // HD
+    heads = pieces[-1].shape[2] // HD
     group_size = heads // kv_local
-    rows = pieces[0].shape[2]
+    rows = span[1] - span[0]
     count = sum(piece.shape[0] for piece in pieces)
     width = heads * HD + LANES
     stacked = count * rows * group_size
@@ -236,7 +236,7 @@
         scratch += [pltpu.VMEM((held, LANES), jnp.float32), pltpu.VMEM((held, 2 * HD), jnp.float32)]
     return pl.pallas_call(
         functools.partial(
-            kernel, pieces=len(pieces), outs=outs, group_size=group_size, half=half
+            kernel, pieces=len(pieces), outs=outs, group_size=group_size, span=span
         ),
         grid_spec=pltpu.PrefetchScalarGridSpec(
             num_scalar_prefetch=len(operands),
@@ -283,12 +283,18 @@
         parts += [ref.at[index] for index in range(ref.shape[0])]
     heads = (parts[0].shape[1] - LANES) // HD
     shares, _ = shares_of(parts, heads)
+    unit = out_ref.shape[1]
     for head in range(heads):
-        out_ref[0, :, head * HD : (head + 1) * HD] = weighted(parts, shares, head)
-
-
-def merge(parts, half=0, halves=1, onto=None):
+        value = weighted(parts, shares, head)
+        for block in range(out_ref.shape[0]):
+            rows = value[block * unit : (block + 1) * unit]
+            out_ref[block, :, head * HD : (head + 1) * HD] = rows
+
+
+def merge(parts, at=0, whole=None, onto=None):
     _, rows, width = parts[0].shape
+    whole = whole or rows
+    unit = math.gcd(rows, whole - rows or rows)
     sources = sum(part.shape[0] for part in parts)
     columns = width - LANES
     in_specs = [pl.BlockSpec(memory_space=pltpu.VMEM) for part in parts]
@@ -300,8 +306,8 @@
         functools.partial(merge_kernel, onto=onto is not None),
         grid=(1,),
         in_specs=in_specs,
-        out_specs=pl.BlockSpec((1, rows, columns), lambda i: (half, 0, 0)),
-        out_shape=jax.ShapeDtypeStruct((halves, rows, columns), jnp.bfloat16),
+        out_specs=pl.BlockSpec((rows // unit, unit, columns), lambda i: (at // rows, 0, 0)),
+        out_shape=jax.ShapeDtypeStruct((whole // unit, unit, columns), jnp.bfloat16),
         input_output_aliases={} if onto is None else {len(parts): 0},
         compiler_params=pltpu.CompilerParams(vmem_limit_bytes=MERGE_BYTES),
         cost_estimate=pl.CostEstimate(
@@ -312,37 +318,34 @@
     )(*operands)
 
 
-def pair_kernel(spot_ref, mine_ref, theirs_ref, _, *out_refs):
-    heads = (mine_ref.shape[2] - LANES) // HD
+def quad_kernel(spot_ref, *refs, sources):
+    part_refs, out_refs = refs[:sources], refs[sources + 1 :]
+    heads = (part_refs[0].shape[2] - LANES) // HD
     for offset, out_ref in enumerate(out_refs):
-        spot = spot_ref[0] ^ offset
-        parts = [mine_ref.at[spot], theirs_ref.at[spot]]
+        parts = [ref.at[spot_ref[0] ^ offset] for ref in part_refs]
         shares, level = shares_of(parts, heads)
         for head in range(heads):
             out_ref[0, :, head * HD : (head + 1) * HD] = weighted(parts, shares, head)
         out_ref[0, :, heads * HD :] = term_lanes(level, heads)
 
 
-def merge_pair(mine, theirs, spot, after):
-    owners, rows, width = mine.shape
+def merge_quad(parts, spot, after):
+    owners, rows, width = parts[0].shape
     vmem = pl.BlockSpec(memory_space=pltpu.VMEM)
     return pl.pallas_call(
-        pair_kernel,
-        in_specs=[
-            pl.BlockSpec(memory_space=pltpu.SMEM),
-            vmem,
-            vmem,
-            pl.BlockSpec(memory_space=pl.ANY),
-        ],
+        functools.partial(quad_kernel, sources=len(parts)),
+        in_specs=[pl.BlockSpec(memory_space=pltpu.SMEM)]
+        + [vmem] * len(parts)
+        + [pl.BlockSpec(memory_space=pl.ANY)],
         out_specs=[vmem] * owners,
         out_shape=[jax.ShapeDtypeStruct((1, rows, width), jnp.bfloat16)] * owners,
         compiler_params=pltpu.CompilerParams(vmem_limit_bytes=MERGE_BYTES),
         cost_estimate=pl.CostEstimate(
-            flops=8 * owners * rows * width,
-            bytes_accessed=6 * owners * rows * width,
+            flops=4 * len(parts) * owners * rows * width,
+            bytes_accessed=2 * (len(parts) + 1) * owners * rows * width,
             transcendentals=0,
         ),
-    )(spot, mine, theirs, after)
+    )(spot, *parts, after)
 
 
 def settle_kernel(keys_in, values_in, key_ref, value_ref):
@@ -416,8 +419,10 @@
     def sent(block, bit):
         return lax.ppermute(block, AXES, swapped(shape, 0, bit))
 
-    boxes = [(0, 2, True), (0, 3, True)]
-    picked = pick([q_second], here, boxes, mine)
+    picked = [
+        lax.dynamic_slice(q_second, (low * half, (me ^ bit) * mine), (half, mine))
+        for bit in (2, 3)
+    ]
     got = [[sent(x, bit) for x, bit in zip(picked, (2, 3))]]
     boxes = [(0, 1, False), (1, 1, False), (1, 2, True), (1, 3, True)]
     near_s, near_f, *picked = pick([q_second, q_first], here, boxes, mine)
@@ -437,65 +442,56 @@
         owners += [2 * (me ^ bit), 2 * (me ^ bit) + 1]
     owners += [2 * (me ^ 2) + low, 2 * (me ^ 3) + low]
     owners += [2 * (me ^ 2) + 1 - low, 2 * (me ^ 3) + 1 - low]
-    places = [
-        owner // 2 + jnp.where(owner % 2 == low, len(owners) // 2, 0) for owner in owners
-    ]
+    places = [((owner ^ spot) % 4) * 2 + owner // 4 for owner in owners]
     places = jnp.stack(places).astype(jnp.int32)
     return pieces[0], pieces[1], places, jnp.reshape(me, (1,)).astype(jnp.int32), got[0][0]
-
-
-def in_halves(pieces, halves):
-    return [x.reshape(x.shape[0], halves, x.shape[1] // halves, x.shape[2]) for x in pieces]
 
 
 def shards(shape, q_first, q_second, k_cache, v_cache, kept_blocks, kept_count):
     ctx, head = shape["ctx"], shape["head"]
     owned = q_first.shape[0] * head // ctx
     kept = (kept_blocks[0], kept_count)
-    if head == 4 and ctx == 2 * head and owned % 32 == 0:
+    if head == 4 and ctx == 8 and owned % 48 == 0:
         second, first, places, column, arrived = relayed(shape, q_first, q_second)
         keys = jnp.swapaxes(k_cache, 0, 1)
         late, _ = lax.optimization_barrier((v_cache, arrived))
         keys, values = settle(keys, jnp.swapaxes(late, 0, 1))
-        first, second = in_halves(first, 2), in_halves(second, 1)
-        spot = jnp.reshape(lax.axis_index("ctx") // 2, (1,)).astype(jnp.int32)
-
-        def across_pair(send):
-            return lax.ppermute(send, AXES, swapped(shape, 1, 0))
-
-        def across_owners(parts):
-            moved = []
-            for offset in (3, 2, 1):
-                moved.append(lax.ppermute(parts[offset], AXES, swapped(shape, 2 * offset, 0)))
-            return [parts[0], *moved]
-
-        def attend(pieces, half, after, kept=None):
-            return partial_call(pieces, places, column, keys, values, half, 2, after, kept)
-
-        send_s, keep_s = attend(second, 0, spot, kept)
-        got_s = across_pair(send_s)
-        send_a, keep_a = attend(first, 0, send_s)
-        got_a = across_pair(send_a)
-        pair_s = merge_pair(keep_s, got_s, spot, send_a)
-        final_s = across_owners(pair_s)
-        send_b, keep_b = attend(first, 1, pair_s[0])
-        got_b = across_pair(send_b)
-        pair_a = merge_pair(keep_a, got_a, spot, send_b)
-        final_a = across_owners(pair_a)
-        pair_b = merge_pair(keep_b, got_b, spot, pair_a[0])
-        final_b = across_owners(pair_b)
-        out_second = merge(final_s)[0]
-        out_first = merge(final_b, 1, 2, merge(final_a, 0, 2))
-        return (out_first.reshape(owned, -1), out_second)
+        spot = jnp.reshape(lax.axis_index("ctx") // 4, (1,)).astype(jnp.int32)
+        cut = owned * 2 // 3
+
+        def moved(part, bits):
+            return lax.ppermute(part, AXES, swapped(shape, bits, 0))
+
+        def gathered(parts):
+            return [parts[0]] + [moved(parts[bits], bits) for bits in (3, 1, 2)]
+
+        def attend(pieces, span, after, kept=None):
+            parts = partial_call(pieces, places, column, keys, values, span, 4, after, kept)
+            return parts, gathered(parts)
+
+        def settled(parts, after):
+            mine, other = merge_quad(parts, spot, after)
+            return mine, moved(other, 4)
+
+        sent_s, quad_s = attend(second, (0, owned), spot, kept)
+        sent_a, quad_a = attend(first, (0, cut), sent_s[0])
+        last_s = settled(quad_s, sent_a[0])
+        sent_b, quad_b = attend(first, (cut, owned), last_s[0])
+        last_a = settled(quad_a, sent_b[0])
+        last_b = settled(quad_b, last_a[0])
+        out_second = merge(last_s)
+        out_first = merge(last_b, cut, owned, merge(last_a, 0, owned))
+        return (out_first.reshape(owned, -1), out_second.reshape(owned, -1))
     keys, values = jnp.swapaxes(k_cache, 0, 1), jnp.swapaxes(v_cache, 0, 1)
     second, first = (
-        [lax.all_to_all(block, "head", split_axis=1, concat_axis=0, tiled=True)[None, None]]
+        [lax.all_to_all(block, "head", split_axis=1, concat_axis=0, tiled=True)[None]]
         for block in (q_second, q_first)
     )
     nothing = jnp.zeros((1,), jnp.int32)
     outs = []
     for pieces, which in ((first, None), (second, kept)):
-        (part,) = partial_call(pieces, nothing, nothing, keys, values, 0, 1, nothing, which)
+        span = (0, pieces[0].shape[1])
+        (part,) = partial_call(pieces, nothing, nothing, keys, values, span, 1, nothing, which)
         outs.append(merge([to_owners(part.reshape(ctx, owned, part.shape[2]))])[0])
     return tuple(outs)
 

time: 121 us -> 107 us (0.88)
  starting transfers between devices: 38.7 us -> 27.4 us
  Pallas kernels: 51.5 us -> 49.2 us
  waiting for transfers between devices: 24.3 us -> 22.3 us
    ppermute x12, starting transfers between devices: 27.6 us -> 16.3 us  [moved(): return lax.ppermute(part, AXES, swapped(shape, bits, 0))]
    ppermute x12, waiting for transfers between devices: 14.6 us -> 9.12 us  [moved(): return lax.ppermute(part, AXES, swapped(shape, bits, 0))]
    ppermute x4, waiting for transfers between devices: 2.93 us -> 7.35 us  [relayed(): others.append(lax.ppermute(x, AXES, swapped(shape, 1, 0)))]
    pallas_call x2 -> x1, Pallas kernels: 5.41 us -> 2.93 us  [pick(): pl.pallas_call(functools.partial(pick_kernel, boxes=boxes), in_specs=[pl....]
    pallas_call x3, Pallas kernels: 38.4 us -> 40 us  [partial_call(): pl.pallas_call(functools.partial(kernel, pieces=len(pieces), outs=outs, g...]
  transfers between devices with their start and end apart: 22 -> 22, of which waited for: 6 -> 6; matrix products, arithmetic and copies ran while one was open for 4% -> 5% of each run, Pallas kernels for 40% -> 45%
where the time goes in v3:
time: 107 us
  Pallas kernels  49.2 us (46%)
  starting transfers between devices  27.4 us (26%)
  waiting for transfers between devices  22.3 us (21%)
  local copies, waits for them, and re-layouts  5.73 us (5%)
  between operations  1.53 us (1%)
    pallas_call x3, Pallas kernels, partial_call(): pl.pallas_call(functools.partial(kernel, pieces=len(pieces), outs=outs, g...  40 us
    ppermute x12, starting transfers between devices, moved(): return lax.ppermute(part, AXES, swapped(shape, bits, 0))  16.3 us
    ppermute x12, waiting for transfers between devices, moved(): return lax.ppermute(part, AXES, swapped(shape, bits, 0))  9.12 us
    ppermute x4, waiting for transfers between devices, relayed(): others.append(lax.ppermute(x, AXES, swapped(shape, 1, 0)))  7.35 us
    ppermute x6, waiting for transfers between devices, sent(): return lax.ppermute(block, AXES, swapped(shape, 0, bit))  5.81 us
    ppermute x4, starting transfers between devices, relayed(): others.append(lax.ppermute(x, AXES, swapped(shape, 1, 0)))  5.64 us
    ppermute x6, starting transfers between devices, sent(): return lax.ppermute(block, AXES, swapped(shape, 0, bit))  5.5 us
    transpose x1, local copies, waits for them, and re-layouts, shards(): keys, values = settle(keys, jnp.swapaxes(late, 0, 1))  4.56 us
  transfers between devices with their start and end apart: 22, of which 6 were waited for; matrix products, arithmetic and copies ran while one was open for 5% of the time, Pallas kernels for 45%

profile of v3, /device:TPU:0, one launch (start us, length us, event | category | flops | bytes accessed | tf_op | source)
XLA Modules:
  0.0 106.8 jit_solution(15628515805125825445)
XLA Ops:
  0.7 1.1 fusion
  1.7 3.0 %collective-permute-start.5 = (bf16[96,1024]{1,0:T(8,128)(2,1)S(1)}, bf16[96,1024]{1,0:T(8,128)(2,1)S(1)}, u32[]{:S(2)}, u32[]{:S(2)}) collective-permute-start(bf16[96,1024]{1,0:T(8,128)(2,1)S(1)} %get-tuple-element.53), channel_id=1, source_target_pairs={{0,2},{1,3},{2,0},{3,1},{4,6},{5,7},{6,4},{7,5},{8,10},{9,11},{10,... | collective-permute-start | bytes 589832 | tf_op jit(solution)/shard_map/ppermute | solution.py:420
  4.8 0.7 pad_add_fusion.spot_ref
  5.4 2.9 %shard_map.77 = (bf16[192,1024]{1,0:T(8,128)(2,1)}, bf16[192,1024]{1,0:T(8,128)(2,1)}, bf16[96,1024]{1,0:T(8,128)(2,1)}, bf16[96,1024]{1,0:T(8,128)(2,1)}) custom-call(s32[2]{0:T(128)} %pad_add_fusion.spot_ref, bf16[192,4096]{1,0:T(8,128)(2,1)} %refs_0_.1, bf16[192,4096]{1,0:T(8,128)(2,1)} %refs_1_.1), custom_call_target="tpu_custom_call" | custom-call | tf_op jit(solution)/shard_map/pallas_call | solution.py:387
  8.3 1.2 %collective-permute-start.1 = (bf16[96,1024]{1,0:T(8,128)(2,1)}, bf16[96,1024]{1,0:T(8,128)(2,1)S(1)}, u32[]{:S(2)}, u32[]{:S(2)}) collective-permute-start(bf16[96,1024]{1,0:T(8,128)(2,1)} %get-tuple-element.28), channel_id=1, source_target_pairs={{0,2},{1,3},{2,0},{3,1},{4,6},{5,7},{6,4},{7,5},{8,10},{9,11},{10,... | collective-permute-start | bytes 589832 | tf_op jit(solution)/shard_map/ppermute | solution.py:420
  9.6 0.7 collective-permute-start.6
  11.6 2.6 %collective-permute-done.7 = bf16[96,1024]{1,0:T(8,128)(2,1)S(1)} collective-permute-done((bf16[96,1024]{1,0:T(8,128)(2,1)S(1)}, bf16[96,1024]{1,0:T(8,128)(2,1)S(1)}, u32[]{:S(2)}, u32[]{:S(2)}) %collective-permute-start.7) | collective-permute-done | bytes 196640 | tf_op jit(solution)/shard_map/ppermute | solution.py:420
  14.3 1.5 %collective-permute-start.8 = (bf16[96,1024]{1,0:T(8,128)(2,1)S(1)}, bf16[96,1024]{1,0:T(8,128)(2,1)S(1)}, u32[]{:S(2)}, u32[]{:S(2)}) collective-permute-start(bf16[96,1024]{1,0:T(8,128)(2,1)S(1)} %collective-permute-done.5), channel_id=1, source_target_pairs={{0,4},{1,5},{2,6},{3,7},{4,0},{5,1},{6,2},{7,3},{8,12},{9,13},{10,... | collective-permute-start | bytes 589832 | tf_op jit(solution)/shard_map/ppermute | solution.py:435
  15.8 3.2 %collective-permute-done.1 = bf16[96,1024]{1,0:T(8,128)(2,1)S(1)} collective-permute-done((bf16[96,1024]{1,0:T(8,128)(2,1)}, bf16[96,1024]{1,0:T(8,128)(2,1)S(1)}, u32[]{:S(2)}, u32[]{:S(2)}) %collective-permute-start.1) | collective-permute-done | bytes 196640 | tf_op jit(solution)/shard_map/ppermute | solution.py:420
  18.9 2.0 %collective-permute-start.9 = (bf16[96,1024]{1,0:T(8,128)(2,1)S(1)}, bf16[96,1024]{1,0:T(8,128)(2,1)S(1)}, u32[]{:S(2)}, u32[]{:S(2)}) collective-permute-start(bf16[96,1024]{1,0:T(8,128)(2,1)S(1)} %collective-permute-done.7), channel_id=1, source_target_pairs={{0,4},{1,5},{2,6},{3,7},{4,0},{5,1},{6,2},{7,3},{8,12},{9,13},{10,... | collective-permute-start | bytes 589832 | tf_op jit(solution)/shard_map/ppermute | solution.py:435
  21.0 4.6 %copy_bitcast_fusion = (bf16[4,4096,128]{2,1,0:T(8,128)(2,1)S(1)}, bf16[4,4096,128]{2,1,0:T(8,128)(2,1)S(1)}) fusion(bf16[4096,4,128]{2,1,0:T(4,128)(2,1)} %param.9, bf16[4096,4,128]{2,1,0:T(4,128)(2,1)} %param.8), kind=kLoop, calls=%fused_computation | loop fusion | bytes 16777216 | tf_op jit(solution)/shard_map/transpose | solution.py:458
  25.7 2.0 %collective-permute-start.4 = (bf16[96,1024]{1,0:T(8,128)(2,1)S(1)}, bf16[96,1024]{1,0:T(8,128)(2,1)S(1)}, u32[]{:S(2)}, u32[]{:S(2)}) collective-permute-start(bf16[96,1024]{1,0:T(8,128)(2,1)S(1)} %collective-permute-done.2), channel_id=1, source_target_pairs={{0,4},{1,5},{2,6},{3,7},{4,0},{5,1},{6,2},{7,3},{8,12},{9,13},{10,... | collective-permute-start | bytes 589832 | tf_op jit(solution)/shard_map/ppermute | solution.py:435
  27.7 4.5 %shard_map.79 = (bf16[2,96,1152]{2,1,0:T(8,128)(2,1)S(1)}, bf16[2,96,1152]{2,1,0:T(8,128)(2,1)S(1)}, bf16[2,96,1152]{2,1,0:T(8,128)(2,1)S(1)}, bf16[2,96,1152]{2,1,0:T(8,128)(2,1)S(1)}) custom-call(s32[8]{0:T(128)S(1)} %stack.42.place_ref, s32[1]{0:T(128)} %bitcast.9.column_ref, s32[8]{0:T(128)S(1)} %bitcast.48, s32[1]{0:T(128)S(6)} %copy.18.count_ref, ...), custom_call_target="tpu_custom_call" | custom-call | flops 3221225472 | bytes 1048576 | tf_op jit(solution)/shard_map/pallas_call | solution.py:237
  32.3 2.1 %collective-permute-start.10 = (bf16[2,96,1152]{2,1,0:T(8,128)(2,1)S(1)}, bf16[2,96,1152]{2,1,0:T(8,128)(2,1)S(1)}, u32[]{:S(2)}, u32[]{:S(2)}) collective-permute-start(bf16[2,96,1152]{2,1,0:T(8,128)(2,1)S(1)} %get-tuple-element.35), channel_id=1, source_target_pairs={{0,12},{1,13},{2,14},{3,15},{4,8},{5,9},{6,10},{7,11},{8,4},{9,5},... | collective-permute-start | bytes 1327112 | tf_op jit(solution)/shard_map/ppermute | solution.py:463
  34.4 1.0 collective-permute-start.11
  35.8 7.3 %collective-permute-done.4 = bf16[96,1024]{1,0:T(8,128)(2,1)S(1)} collective-permute-done((bf16[96,1024]{1,0:T(8,128)(2,1)S(1)}, bf16[96,1024]{1,0:T(8,128)(2,1)S(1)}, u32[]{:S(2)}, u32[]{:S(2)}) %collective-permute-start.4) | collective-permute-done | bytes 196640 | tf_op jit(solution)/shard_map/ppermute | solution.py:435
  43.2 22.8 %shard_map.80 = (bf16[2,64,1152]{2,1,0:T(8,128)(2,1)S(1)}, bf16[2,64,1152]{2,1,0:T(8,128)(2,1)S(1)}, bf16[2,64,1152]{2,1,0:T(8,128)(2,1)S(1)}, bf16[2,64,1152]{2,1,0:T(8,128)(2,1)S(1)}) custom-call(s32[8]{0:T(128)S(1)} %stack.42.place_ref, s32[1]{0:T(128)} %bitcast.9.column_ref, bf16[2,96,4096]{2,1,0:T(8,128)(2,1)S(1)} %bitcast.31, ...), custom_call_target="tpu_custom_call" | custom-call | flops 17179869184 | bytes 8388608 | tf_op jit(solution)/shard_map/pallas_call | solution.py:237
  66.0 5.5 %collective-permute-start.16 = (bf16[2,64,1152]{2,1,0:T(8,128)(2,1)S(1)}, bf16[2,64,1152]{2,1,0:T(8,128)(2,1)S(1)}, u32[]{:S(2)}, u32[]{:S(2)}) collective-permute-start(bf16[2,64,1152]{2,1,0:T(8,128)(2,1)S(1)} %get-tuple-element.44), channel_id=1, source_target_pairs={{0,12},{1,13},{2,14},{3,15},{4,8},{5,9},{6,10},{7,11},{8,4},{9,5},... | collective-permute-start | bytes 884744 | tf_op jit(solution)/shard_map/ppermute | solution.py:463
  71.5 0.6 collective-permute-start.18
  72.1 1.6 %shard_map.81 = (bf16[1,96,1152]{2,1,0:T(8,128)(2,1)S(1)}, bf16[1,96,1152]{2,1,0:T(8,128)(2,1)S(1)}) custom-call(s32[1]{0:T(128)} %bitcast.refs_8_.spot_ref, bf16[2,96,1152]{2,1,0:T(8,128)(2,1)S(1)} %get-tuple-element.34.refs_8_.refs_0_, bf16[2,96,1152]{2,1,0:T(8,128)(2,1)S(1)} %collective-permute-done.10.refs_1_, ...), custom_call_target="tpu_custom_call" | custom-call | flops 3538944 | bytes 2211840 | tf_op jit(solution)/shard_map/pallas_call | solution.py:335
  73.7 12.7 %shard_map.82 = (bf16[2,32,1152]{2,1,0:T(8,128)(2,1)S(1)}, bf16[2,32,1152]{2,1,0:T(8,128)(2,1)S(1)}, bf16[2,32,1152]{2,1,0:T(8,128)(2,1)S(1)}, bf16[2,32,1152]{2,1,0:T(8,128)(2,1)S(1)}) custom-call(s32[8]{0:T(128)S(1)} %stack.42.place_ref, s32[1]{0:T(128)} %bitcast.9.column_ref, bf16[2,96,4096]{2,1,0:T(8,128)(2,1)S(1)} %bitcast.32, ...), custom_call_target="tpu_custom_call" | custom-call | flops 8589934592 | bytes 8388608 | tf_op jit(solution)/shard_map/pallas_call | solution.py:237
  86.4 2.9 %collective-permute-start.13 = (bf16[2,32,1152]{2,1,0:T(8,128)(2,1)S(1)}, bf16[2,32,1152]{2,1,0:T(8,128)(2,1)S(1)}, u32[]{:S(2)}, u32[]{:S(2)}) collective-permute-start(bf16[2,32,1152]{2,1,0:T(8,128)(2,1)S(1)} %get-tuple-element.41), channel_id=1, source_target_pairs={{0,12},{1,13},{2,14},{3,15},{4,8},{5,9},{6,10},{7,11},{8,4},{9,5},... | collective-permute-start | bytes 442376 | tf_op jit(solution)/shard_map/ppermute | solution.py:463
  89.3 0.6 collective-permute-start.15
  89.9 1.7 %collective-permute-start.21 = (bf16[1,96,1152]{2,1,0:T(8,128)(2,1)S(1)}, bf16[1,96,1152]{2,1,0:T(8,128)(2,1)S(1)}, u32[]{:S(2)}, u32[]{:S(2)}) collective-permute-start(bf16[1,96,1152]{2,1,0:T(8,128)(2,1)S(1)} %get-tuple-element.51), channel_id=1, source_target_pairs={{0,16},{1,17},{2,18},{3,19},{4,20},{5,21},{6,22},{7,23},{8,24},{9,... | collective-permute-start | bytes 663560 | tf_op jit(solution)/shard_map/ppermute | solution.py:463
  91.6 1.1 %shard_map.83 = (bf16[1,64,1152]{2,1,0:T(8,128)(2,1)S(1)}, bf16[1,64,1152]{2,1,0:T(8,128)(2,1)S(1)}) custom-call(s32[1]{0:T(128)} %bitcast.refs_8_.spot_ref, bf16[2,64,1152]{2,1,0:T(8,128)(2,1)S(1)} %get-tuple-element.38.refs_4_.refs_0_, bf16[2,64,1152]{2,1,0:T(8,128)(2,1)S(1)} %collective-permute-done.16.refs_1_, ...), custom_call_target="tpu_custom_call" | custom-call | flops 2359296 | bytes 1474560 | tf_op jit(solution)/shard_map/pallas_call | solution.py:335
  92.7 1.3 %collective-permute-start.20 = (bf16[1,64,1152]{2,1,0:T(8,128)(2,1)S(1)}, bf16[1,64,1152]{2,1,0:T(8,128)(2,1)S(1)}, u32[]{:S(2)}, u32[]{:S(2)}) collective-permute-start(bf16[1,64,1152]{2,1,0:T(8,128)(2,1)S(1)} %get-tuple-element.50), channel_id=1, source_target_pairs={{0,16},{1,17},{2,18},{3,19},{4,20},{5,21},{6,22},{7,23},{8,24},{9,... | collective-permute-start | bytes 442376 | tf_op jit(solution)/shard_map/ppermute | solution.py:463
  94.4 3.8 %collective-permute-done.15.refs_3_ = bf16[2,32,1152]{2,1,0:T(8,128)(2,1)S(1)} collective-permute-done((bf16[2,32,1152]{2,1,0:T(8,128)(2,1)S(1)}, bf16[2,32,1152]{2,1,0:T(8,128)(2,1)S(1)}, u32[]{:S(2)}, u32[]{:S(2)}) %collective-permute-start.15) | collective-permute-done | bytes 147488 | tf_op jit(solution)/shard_map/ppermute | solution.py:463
  98.2 0.7 shard_map.84
  99.0 4.9 %collective-permute-done.20.refs_1_ = bf16[1,64,1152]{2,1,0:T(8,128)(2,1)S(1)} collective-permute-done((bf16[1,64,1152]{2,1,0:T(8,128)(2,1)S(1)}, bf16[1,64,1152]{2,1,0:T(8,128)(2,1)S(1)}, u32[]{:S(2)}, u32[]{:S(2)}) %collective-permute-start.20) | collective-permute-done | bytes 147488 | tf_op jit(solution)/shard_map/ppermute | solution.py:463
  103.9 1.0 shard_map.85.refs_2_
  104.9 1.1 %shard_map.87 = bf16[1,96,1024]{2,1,0:T(8,128)(2,1)} custom-call(bf16[1,96,1152]{2,1,0:T(8,128)(2,1)S(1)} %get-tuple-element.39.refs_8_.refs_0_, bf16[1,96,1152]{2,1,0:T(8,128)(2,1)S(1)} %collective-permute-done.21.refs_1_), custom_call_target="tpu_custom_call" | custom-call | flops 786432 | bytes 442368 | tf_op jit(solution)/shard_map/pallas_call | solution.py:305
  105.9 0.9 shard_map.86
  (33 shorter events, 1.7 us)
Async XLA Ops:
  1.7 9.6 %collective-permute-start.5 = (bf16[96,1024]{1,0:T(8,128)(2,1)S(1)}, bf16[96,1024]{1,0:T(8,128)(2,1)S(1)}, u32[]{:S(2)}, u32[]{:S(2)}) collective-permute-start(bf16[96,1024]{1,0:T(8,128)(2,1)S(1)} %get-tuple-element.53), channel_id=1, source_target_pairs={{0,2},{1,3},{2,0},{3,1},{4,6},{5,7},{6,4},{7,5},{8,10},{9,11},{10,... | collective-permute-start | bytes 589832 | tf_op jit(solution)/shard_map/ppermute | solution.py:420
  4.8 9.5 %collective-permute-start.7 = (bf16[96,1024]{1,0:T(8,128)(2,1)S(1)}, bf16[96,1024]{1,0:T(8,128)(2,1)S(1)}, u32[]{:S(2)}, u32[]{:S(2)}) collective-permute-start(bf16[96,1024]{1,0:T(8,128)(2,1)S(1)} %get-tuple-element.52), channel_id=1, source_target_pairs={{0,3},{1,2},{2,1},{3,0},{4,7},{5,6},{6,5},{7,4},{8,11},{9,10},{10,... | collective-permute-start | bytes 589832 | tf_op jit(solution)/shard_map/ppermute | solution.py:420
  8.3 10.6 %collective-permute-start.1 = (bf16[96,1024]{1,0:T(8,128)(2,1)}, bf16[96,1024]{1,0:T(8,128)(2,1)S(1)}, u32[]{:S(2)}, u32[]{:S(2)}) collective-permute-start(bf16[96,1024]{1,0:T(8,128)(2,1)} %get-tuple-element.28), channel_id=1, source_target_pairs={{0,2},{1,3},{2,0},{3,1},{4,6},{5,7},{6,4},{7,5},{8,10},{9,11},{10,... | collective-permute-start | bytes 589832 | tf_op jit(solution)/shard_map/ppermute | solution.py:420
  9.6 18.1 %collective-permute-start.6 = (bf16[192,1024]{1,0:T(8,128)(2,1)}, bf16[192,1024]{1,0:T(8,128)(2,1)S(1)}, u32[]{:S(2)}, u32[]{:S(2)}) collective-permute-start(bf16[192,1024]{1,0:T(8,128)(2,1)} %get-tuple-element.33), channel_id=1, source_target_pairs={{0,1},{1,0},{2,3},{3,2},{4,5},{5,4},{6,7},{7,6},{8,9},{9,8},{10,11... | collective-permute-start | bytes 1179656 | tf_op jit(solution)/shard_map/ppermute | solution.py:420
  10.3 15.3 %collective-permute-start.2 = (bf16[96,1024]{1,0:T(8,128)(2,1)}, bf16[96,1024]{1,0:T(8,128)(2,1)S(1)}, u32[]{:S(2)}, u32[]{:S(2)}) collective-permute-start(bf16[96,1024]{1,0:T(8,128)(2,1)} %get-tuple-element.29), channel_id=1, source_target_pairs={{0,3},{1,2},{2,1},{3,0},{4,7},{5,6},{6,5},{7,4},{8,11},{9,10},{10,... | collective-permute-start | bytes 589832 | tf_op jit(solution)/shard_map/ppermute | solution.py:420
  11.4 31.8 %collective-permute-start = (bf16[192,1024]{1,0:T(8,128)(2,1)}, bf16[192,1024]{1,0:T(8,128)(2,1)S(1)}, u32[]{:S(2)}, u32[]{:S(2)}) collective-permute-start(bf16[192,1024]{1,0:T(8,128)(2,1)} %get-tuple-element.27), channel_id=1, source_target_pairs={{0,1},{1,0},{2,3},{3,2},{4,5},{5,4},{6,7},{7,6},{8,9},{9,8},{10,11... | collective-permute-start | bytes 1179656 | tf_op jit(solution)/shard_map/ppermute | solution.py:420
  14.3 11.4 %collective-permute-start.8 = (bf16[96,1024]{1,0:T(8,128)(2,1)S(1)}, bf16[96,1024]{1,0:T(8,128)(2,1)S(1)}, u32[]{:S(2)}, u32[]{:S(2)}) collective-permute-start(bf16[96,1024]{1,0:T(8,128)(2,1)S(1)} %collective-permute-done.5), channel_id=1, source_target_pairs={{0,4},{1,5},{2,6},{3,7},{4,0},{5,1},{6,2},{7,3},{8,12},{9,13},{10,... | collective-permute-start | bytes 589832 | tf_op jit(solution)/shard_map/ppermute | solution.py:435
  18.9 8.8 %collective-permute-start.9 = (bf16[96,1024]{1,0:T(8,128)(2,1)S(1)}, bf16[96,1024]{1,0:T(8,128)(2,1)S(1)}, u32[]{:S(2)}, u32[]{:S(2)}) collective-permute-start(bf16[96,1024]{1,0:T(8,128)(2,1)S(1)} %collective-permute-done.7), channel_id=1, source_target_pairs={{0,4},{1,5},{2,6},{3,7},{4,0},{5,1},{6,2},{7,3},{8,12},{9,13},{10,... | collective-permute-start | bytes 589832 | tf_op jit(solution)/shard_map/ppermute | solution.py:435
  25.5 2.1 %copy-start = (bf16[192,4096]{1,0:T(8,128)(2,1)S(1)}, bf16[192,4096]{1,0:T(8,128)(2,1)}, u32[]{:S(2)}) copy-start(bf16[192,4096]{1,0:T(8,128)(2,1)} %refs_0_.1) | copy-start | bytes 4718596
  25.6 2.1 %copy-start.2 = (s32[1,8]{1,0:T(1,128)S(1)}, s32[1,8]{1,0:T(1,128)}, u32[]{:S(2)}) copy-start(s32[1,8]{1,0:T(1,128)} %param.10) | copy-start | bytes 100
  25.6 9.8 %collective-permute-start.3 = (bf16[96,1024]{1,0:T(8,128)(2,1)S(1)}, bf16[96,1024]{1,0:T(8,128)(2,1)S(1)}, u32[]{:S(2)}, u32[]{:S(2)}) collective-permute-start(bf16[96,1024]{1,0:T(8,128)(2,1)S(1)} %collective-permute-done.1), channel_id=1, source_target_pairs={{0,4},{1,5},{2,6},{3,7},{4,0},{5,1},{6,2},{7,3},{8,12},{9,13},{10,... | collective-permute-start | bytes 589832 | tf_op jit(solution)/shard_map/ppermute | solution.py:435
  25.7 17.5 %collective-permute-start.4 = (bf16[96,1024]{1,0:T(8,128)(2,1)S(1)}, bf16[96,1024]{1,0:T(8,128)(2,1)S(1)}, u32[]{:S(2)}, u32[]{:S(2)}) collective-permute-start(bf16[96,1024]{1,0:T(8,128)(2,1)S(1)} %collective-permute-done.2), channel_id=1, source_target_pairs={{0,4},{1,5},{2,6},{3,7},{4,0},{5,1},{6,2},{7,3},{8,12},{9,13},{10,... | collective-permute-start | bytes 589832 | tf_op jit(solution)/shard_map/ppermute | solution.py:435
  27.7 15.5 %copy-start.1 = (bf16[192,4096]{1,0:T(8,128)(2,1)S(1)}, bf16[192,4096]{1,0:T(8,128)(2,1)}, u32[]{:S(2)}) copy-start(bf16[192,4096]{1,0:T(8,128)(2,1)} %refs_1_.1) | copy-start | bytes 4718596
  32.3 39.2 %collective-permute-start.10 = (bf16[2,96,1152]{2,1,0:T(8,128)(2,1)S(1)}, bf16[2,96,1152]{2,1,0:T(8,128)(2,1)S(1)}, u32[]{:S(2)}, u32[]{:S(2)}) collective-permute-start(bf16[2,96,1152]{2,1,0:T(8,128)(2,1)S(1)} %get-tuple-element.35), channel_id=1, source_target_pairs={{0,12},{1,13},{2,14},{3,15},{4,8},{5,9},{6,10},{7,11},{8,4},{9,5},... | collective-permute-start | bytes 1327112 | tf_op jit(solution)/shard_map/ppermute | solution.py:463
  34.4 37.7 %collective-permute-start.11 = (bf16[2,96,1152]{2,1,0:T(8,128)(2,1)S(1)}, bf16[2,96,1152]{2,1,0:T(8,128)(2,1)S(1)}, u32[]{:S(2)}, u32[]{:S(2)}) collective-permute-start(bf16[2,96,1152]{2,1,0:T(8,128)(2,1)S(1)} %get-tuple-element.36), channel_id=1, source_target_pairs={{0,4},{1,5},{2,6},{3,7},{4,0},{5,1},{6,2},{7,3},{8,12},{9,13},{10,... | collective-permute-start | bytes 1327112 | tf_op jit(solution)/shard_map/ppermute | solution.py:463
  35.4 36.7 %collective-permute-start.12 = (bf16[2,96,1152]{2,1,0:T(8,128)(2,1)S(1)}, bf16[2,96,1152]{2,1,0:T(8,128)(2,1)S(1)}, u32[]{:S(2)}, u32[]{:S(2)}) collective-permute-start(bf16[2,96,1152]{2,1,0:T(8,128)(2,1)S(1)} %get-tuple-element.37), channel_id=1, source_target_pairs={{0,8},{1,9},{2,10},{3,11},{4,12},{5,13},{6,14},{7,15},{8,0},{9,1},... | collective-permute-start | bytes 1327112 | tf_op jit(solution)/shard_map/ppermute | solution.py:463
  66.0 23.3 %collective-permute-start.16 = (bf16[2,64,1152]{2,1,0:T(8,128)(2,1)S(1)}, bf16[2,64,1152]{2,1,0:T(8,128)(2,1)S(1)}, u32[]{:S(2)}, u32[]{:S(2)}) collective-permute-start(bf16[2,64,1152]{2,1,0:T(8,128)(2,1)S(1)} %get-tuple-element.44), channel_id=1, source_target_pairs={{0,12},{1,13},{2,14},{3,15},{4,8},{5,9},{6,10},{7,11},{8,4},{9,5},... | collective-permute-start | bytes 884744 | tf_op jit(solution)/shard_map/ppermute | solution.py:463
  71.5 18.5 %collective-permute-start.17 = (bf16[2,64,1152]{2,1,0:T(8,128)(2,1)S(1)}, bf16[2,64,1152]{2,1,0:T(8,128)(2,1)S(1)}, u32[]{:S(2)}, u32[]{:S(2)}) collective-permute-start(bf16[2,64,1152]{2,1,0:T(8,128)(2,1)S(1)} %get-tuple-element.45), channel_id=1, source_target_pairs={{0,4},{1,5},{2,6},{3,7},{4,0},{5,1},{6,2},{7,3},{8,12},{9,13},{10,... | collective-permute-start | bytes 884744 | tf_op jit(solution)/shard_map/ppermute | solution.py:463
  71.5 20.2 %collective-permute-start.18 = (bf16[2,64,1152]{2,1,0:T(8,128)(2,1)S(1)}, bf16[2,64,1152]{2,1,0:T(8,128)(2,1)S(1)}, u32[]{:S(2)}, u32[]{:S(2)}) collective-permute-start(bf16[2,64,1152]{2,1,0:T(8,128)(2,1)S(1)} %get-tuple-element.46), channel_id=1, source_target_pairs={{0,8},{1,9},{2,10},{3,11},{4,12},{5,13},{6,14},{7,15},{8,0},{9,1},... | collective-permute-start | bytes 884744 | tf_op jit(solution)/shard_map/ppermute | solution.py:463
  86.4 7.7 %collective-permute-start.13 = (bf16[2,32,1152]{2,1,0:T(8,128)(2,1)S(1)}, bf16[2,32,1152]{2,1,0:T(8,128)(2,1)S(1)}, u32[]{:S(2)}, u32[]{:S(2)}) collective-permute-start(bf16[2,32,1152]{2,1,0:T(8,128)(2,1)S(1)} %get-tuple-element.41), channel_id=1, source_target_pairs={{0,12},{1,13},{2,14},{3,15},{4,8},{5,9},{6,10},{7,11},{8,4},{9,5},... | collective-permute-start | bytes 442376 | tf_op jit(solution)/shard_map/ppermute | solution.py:463
  89.3 5.2 %collective-permute-start.14 = (bf16[2,32,1152]{2,1,0:T(8,128)(2,1)S(1)}, bf16[2,32,1152]{2,1,0:T(8,128)(2,1)S(1)}, u32[]{:S(2)}, u32[]{:S(2)}) collective-permute-start(bf16[2,32,1152]{2,1,0:T(8,128)(2,1)S(1)} %get-tuple-element.42), channel_id=1, source_target_pairs={{0,4},{1,5},{2,6},{3,7},{4,0},{5,1},{6,2},{7,3},{8,12},{9,13},{10,... | collective-permute-start | bytes 442376 | tf_op jit(solution)/shard_map/ppermute | solution.py:463
  89.3 9.0 %collective-permute-start.15 = (bf16[2,32,1152]{2,1,0:T(8,128)(2,1)S(1)}, bf16[2,32,1152]{2,1,0:T(8,128)(2,1)S(1)}, u32[]{:S(2)}, u32[]{:S(2)}) collective-permute-start(bf16[2,32,1152]{2,1,0:T(8,128)(2,1)S(1)} %get-tuple-element.43), channel_id=1, source_target_pairs={{0,8},{1,9},{2,10},{3,11},{4,12},{5,13},{6,14},{7,15},{8,0},{9,1},... | collective-permute-start | bytes 442376 | tf_op jit(solution)/shard_map/ppermute | solution.py:463
  89.9 14.9 %collective-permute-start.21 = (bf16[1,96,1152]{2,1,0:T(8,128)(2,1)S(1)}, bf16[1,96,1152]{2,1,0:T(8,128)(2,1)S(1)}, u32[]{:S(2)}, u32[]{:S(2)}) collective-permute-start(bf16[1,96,1152]{2,1,0:T(8,128)(2,1)S(1)} %get-tuple-element.51), channel_id=1, source_target_pairs={{0,16},{1,17},{2,18},{3,19},{4,20},{5,21},{6,22},{7,23},{8,24},{9,... | collective-permute-start | bytes 663560 | tf_op jit(solution)/shard_map/ppermute | solution.py:463
  92.7 11.2 %collective-permute-start.20 = (bf16[1,64,1152]{2,1,0:T(8,128)(2,1)S(1)}, bf16[1,64,1152]{2,1,0:T(8,128)(2,1)S(1)}, u32[]{:S(2)}, u32[]{:S(2)}) collective-permute-start(bf16[1,64,1152]{2,1,0:T(8,128)(2,1)S(1)} %get-tuple-element.50), channel_id=1, source_target_pairs={{0,16},{1,17},{2,18},{3,19},{4,20},{5,21},{6,22},{7,23},{8,24},{9,... | collective-permute-start | bytes 442376 | tf_op jit(solution)/shard_map/ppermute | solution.py:463
  98.9 7.0 %collective-permute-start.19 = (bf16[1,32,1152]{2,1,0:T(8,128)(2,1)S(1)}, bf16[1,32,1152]{2,1,0:T(8,128)(2,1)S(1)}, u32[]{:S(2)}, u32[]{:S(2)}) collective-permute-start(bf16[1,32,1152]{2,1,0:T(8,128)(2,1)S(1)} %get-tuple-element.49), channel_id=1, source_target_pairs={{0,16},{1,17},{2,18},{3,19},{4,20},{5,21},{6,22},{7,23},{8,24},{9,... | collective-permute-start | bytes 221192 | tf_op jit(solution)/shard_map/ppermute | solution.py:463

commit v4 on v3

--- a/solution.py
+++ b/solution.py
@@ -43,7 +43,35 @@
 
 
 def chain_rows(total):
-    return next(size for size in (384, 512, 256, 128, total) if total % size == 0)
+    return next(size for size in (256, 384, 128, total) if total % size == 0)
+
+
+def flash(queries, steps, chains=None):
+    size = chain_rows(queries.shape[0])
+    count = queries.shape[0] // size
+    chains = list(chains or [None] * count)
+    items = [(step, chain) for step in range(len(steps)) for chain in range(count)]
+
+    def scores_of(item):
+        step, chain = item
+        keys, _, mask = steps[step]
+        scores = raw_scores(queries[chain * size : (chain + 1) * size], keys())
+        return scores if mask is None else jnp.where(mask, scores, -jnp.inf)
+
+    scores = scores_of(items[0])
+    for at, (step, chain) in enumerate(items):
+        following = scores_of(items[at + 1]) if at + 1 < len(items) else None
+        newtop = jnp.max(scores, axis=1, keepdims=True)
+        if chains[chain] is not None:
+            newtop = jnp.maximum(chains[chain][0], newtop)
+        weights = jnp.exp2(scores - newtop).astype(jnp.bfloat16)
+        summed = jnp.dot(weights, steps[step][1](), preferred_element_type=jnp.float32)
+        if chains[chain] is not None:
+            top, before = chains[chain]
+            summed = before * jnp.exp2(top - newtop) + summed
+        chains[chain] = (newtop, summed)
+        scores = following
+    return chains
 
 
 def in_terms(level):
@@ -107,23 +135,14 @@
         stat_ref[...] = jnp.zeros_like(stat_ref)
 
     queries = stacked_queries(query_refs, column_ref, heads, group_size, group, span)
-    size = chain_rows(queries.shape[0])
-    starts = range(0, queries.shape[0], size)
-    chains = [None for _ in starts]
+    steps = []
     for step in range(key_ref.shape[1] // block_keys):
         here = pl.ds(step * block_keys, block_keys)
-        keys, values = key_ref[group, here, :], with_ones(value_ref[group, here, :])
-        for index, start in enumerate(starts):
-            scores = raw_scores(queries[start : start + size], keys)
-            newtop = jnp.max(scores, axis=1, keepdims=True)
-            if chains[index] is not None:
-                newtop = jnp.maximum(chains[index][0], newtop)
-            weights = jnp.exp2(scores - newtop).astype(jnp.bfloat16)
-            summed = jnp.dot(weights, values, preferred_element_type=jnp.float32)
-            if chains[index] is not None:
-                top, before = chains[index]
-                summed = before * jnp.exp2(top - newtop) + summed
-            chains[index] = (newtop, summed)
+        steps.append(
+            (lambda here=here: key_ref[group, here, :],
+             lambda here=here: with_ones(value_ref[group, here, :]), None)
+        )
+    chains = flash(queries, steps)
     write_partial(held_ref, stat_ref, place_ref, chains, group_size, group, rows)
 
     @pl.when(group == pl.num_programs(0) - 1)
@@ -156,26 +175,20 @@
     size = chain_rows(queries.shape[0])
     starts = range(0, queries.shape[0], size)
 
-    def absorb(first, length, fresh):
-        keys = jnp.concatenate([block_of(key_ref, first + i) for i in range(length)], axis=0)
-        values = jnp.concatenate([block_of(value_ref, first + i) for i in range(length)], axis=0)
-        values = with_ones(values)
-        slot = lax.broadcasted_iota(jnp.int32, (1, length * BLK), 1) // BLK + first
-        chains = []
-        for start in starts:
-            held = pl.ds(start, size)
-            scores = raw_scores(queries[start : start + size], keys)
-            scores = jnp.where(slot < kept, scores, -jnp.inf)
-            newtop = jnp.max(scores, axis=1, keepdims=True)
-            if not fresh:
-                top = top_ref[held, :1]
-                newtop = jnp.maximum(top, newtop)
-            weights = jnp.exp2(scores - newtop).astype(jnp.bfloat16)
-            summed = jnp.dot(weights, values, preferred_element_type=jnp.float32)
-            if not fresh:
-                summed = sum_ref[held, :] * jnp.exp2(top - newtop) + summed
-            chains.append((newtop, summed))
-        return chains
+    def blocks_of(ref, first, length):
+        return jnp.concatenate([block_of(ref, first + i) for i in range(length)], axis=0)
+
+    def absorb(first, length, chains=None):
+        steps = []
+        for begin in range(0, length, 4):
+            some = min(4, length - begin)
+            start = first + begin
+            mask = lax.broadcasted_iota(jnp.int32, (1, some * BLK), 1) // BLK + start < kept
+            steps.append(
+                (lambda start=start, some=some: blocks_of(key_ref, start, some),
+                 lambda start=start, some=some: with_ones(blocks_of(value_ref, start, some)), mask)
+            )
+        return flash(queries, steps, chains)
 
     def finish(chains):
         write_partial(held_ref, stat_ref, place_ref, chains, group_size, group, rows)
@@ -185,7 +198,7 @@
 
         @pl.when((kept > least) & (kept <= length))
         def _(length=length):
-            finish(absorb(0, length, True))
+            finish(absorb(0, length))
 
         least = length
 
@@ -197,16 +210,19 @@
                 sum_ref[held, :] = summed
                 top_ref[held, :] = jnp.broadcast_to(top, (size, LANES))
 
+        def fetch():
+            holds = [pl.ds(start, size) for start in starts]
+            return [(top_ref[held, :1], sum_ref[held, :]) for held in holds]
+
         @pl.when(kept > most)
         def _():
-            hold(absorb(0, most, True))
+            hold(absorb(0, most))
 
             @pl.loop(1, pl.cdiv(kept, most))
             def _(step):
-                hold(absorb(step * most, most, False))
-
-            holds = [pl.ds(start, size) for start in starts]
-            finish([(top_ref[held, :1], sum_ref[held, :]) for held in holds])
+                hold(absorb(step * most, most, fetch()))
+
+            finish(fetch())
 
     @pl.when(group == pl.num_programs(0) - 1)
     def _():

time: 107 us -> 105 us (0.981)
  Pallas kernels: 49.2 us -> 47.8 us
  waiting for transfers between devices: 22.3 us -> 20.9 us
    pallas_call x3, Pallas kernels: 40 us -> 38.6 us  [partial_call(): pl.pallas_call(functools.partial(kernel, pieces=len(pieces), outs=outs, g...]
    ppermute x12, waiting for transfers between devices: 9.12 us -> 7.88 us  [moved(): return lax.ppermute(part, AXES, swapped(shape, bits, 0))]
  transfers between devices with their start and end apart: 22 -> 22, of which waited for: 6 -> 7; matrix products, arithmetic and copies ran while one was open for 5% -> 5% of each run, Pallas kernels for 45% -> 45%
where the time goes in v4:
time: 105 us; the launch traced here: 104 us
  Pallas kernels  47.8 us (46%)
  starting transfers between devices  28 us (27%)
  waiting for transfers between devices  20.9 us (20%)
  local copies, waits for them, and re-layouts  5.73 us (5%)
  between operations  1.52 us (1%)
    pallas_call x3, Pallas kernels, partial_call(): pl.pallas_call(functools.partial(kernel, pieces=len(pieces), outs=outs, g...  38.6 us
    ppermute x12, starting transfers between devices, moved(): return lax.ppermute(part, AXES, swapped(shape, bits, 0))  16.8 us
    ppermute x12, waiting for transfers between devices, moved(): return lax.ppermute(part, AXES, swapped(shape, bits, 0))  7.88 us
    ppermute x4, waiting for transfers between devices, relayed(): others.append(lax.ppermute(x, AXES, swapped(shape, 1, 0)))  7.19 us
    ppermute x6, waiting for transfers between devices, sent(): return lax.ppermute(block, AXES, swapped(shape, 0, bit))  5.81 us
    ppermute x4, starting transfers between devices, relayed(): others.append(lax.ppermute(x, AXES, swapped(shape, 1, 0)))  5.64 us
    ppermute x6, starting transfers between devices, sent(): return lax.ppermute(block, AXES, swapped(shape, 0, bit))  5.5 us
    transpose x1, local copies, waits for them, and re-layouts, shards(): keys, values = settle(keys, jnp.swapaxes(late, 0, 1))  4.56 us
  transfers between devices with their start and end apart: 22, of which 7 were waited for; matrix products, arithmetic and copies ran while one was open for 5% of the time, Pallas kernels for 45%

profile of v4, /device:TPU:0, one launch (start us, length us, event | category | flops | bytes accessed | tf_op | source)
XLA Modules:
  0.0 104.5 jit_solution(13880919027113917256)
XLA Ops:
  0.7 1.1 %fusion = (bf16[96,1024]{1,0:T(8,128)(2,1)S(1)}, bf16[96,1024]{1,0:T(8,128)(2,1)S(1)}) fusion(bf16[192,4096]{1,0:T(8,128)(2,1)} %refs_0_.1, s32[]{:T(128)S(6)} %select_n.95, s32[]{:T(128)S(6)} %select_n.97, s32[]{:T(128)S(6)} %select_n.96), kind=kLoop, calls=%fused_computation.3 | loop fusion | bytes 786444 | tf_op jit(solution)/shard_map/dynamic_slice | solution.py:439
  1.7 3.0 %collective-permute-start.5 = (bf16[96,1024]{1,0:T(8,128)(2,1)S(1)}, bf16[96,1024]{1,0:T(8,128)(2,1)S(1)}, u32[]{:S(2)}, u32[]{:S(2)}) collective-permute-start(bf16[96,1024]{1,0:T(8,128)(2,1)S(1)} %get-tuple-element.53), channel_id=1, source_target_pairs={{0,2},{1,3},{2,0},{3,1},{4,6},{5,7},{6,4},{7,5},{8,10},{9,11},{10,... | collective-permute-start | bytes 589832 | tf_op jit(solution)/shard_map/ppermute | solution.py:436
  4.8 0.7 pad_add_fusion.spot_ref
  5.4 2.9 %shard_map.77 = (bf16[192,1024]{1,0:T(8,128)(2,1)}, bf16[192,1024]{1,0:T(8,128)(2,1)}, bf16[96,1024]{1,0:T(8,128)(2,1)}, bf16[96,1024]{1,0:T(8,128)(2,1)}) custom-call(s32[2]{0:T(128)} %pad_add_fusion.spot_ref, bf16[192,4096]{1,0:T(8,128)(2,1)} %refs_0_.1, bf16[192,4096]{1,0:T(8,128)(2,1)} %refs_1_.1), custom_call_target="tpu_custom_call" | custom-call | tf_op jit(solution)/shard_map/pallas_call | solution.py:403
  8.3 1.2 %collective-permute-start.1 = (bf16[96,1024]{1,0:T(8,128)(2,1)}, bf16[96,1024]{1,0:T(8,128)(2,1)S(1)}, u32[]{:S(2)}, u32[]{:S(2)}) collective-permute-start(bf16[96,1024]{1,0:T(8,128)(2,1)} %get-tuple-element.28), channel_id=1, source_target_pairs={{0,2},{1,3},{2,0},{3,1},{4,6},{5,7},{6,4},{7,5},{8,10},{9,11},{10,... | collective-permute-start | bytes 589832 | tf_op jit(solution)/shard_map/ppermute | solution.py:436
  9.6 0.7 collective-permute-start.6
  11.6 2.6 %collective-permute-done.7 = bf16[96,1024]{1,0:T(8,128)(2,1)S(1)} collective-permute-done((bf16[96,1024]{1,0:T(8,128)(2,1)S(1)}, bf16[96,1024]{1,0:T(8,128)(2,1)S(1)}, u32[]{:S(2)}, u32[]{:S(2)}) %collective-permute-start.7) | collective-permute-done | bytes 196640 | tf_op jit(solution)/shard_map/ppermute | solution.py:436
  14.3 1.5 %collective-permute-start.8 = (bf16[96,1024]{1,0:T(8,128)(2,1)S(1)}, bf16[96,1024]{1,0:T(8,128)(2,1)S(1)}, u32[]{:S(2)}, u32[]{:S(2)}) collective-permute-start(bf16[96,1024]{1,0:T(8,128)(2,1)S(1)} %collective-permute-done.5), channel_id=1, source_target_pairs={{0,4},{1,5},{2,6},{3,7},{4,0},{5,1},{6,2},{7,3},{8,12},{9,13},{10,... | collective-permute-start | bytes 589832 | tf_op jit(solution)/shard_map/ppermute | solution.py:451
  15.8 3.2 %collective-permute-done.1 = bf16[96,1024]{1,0:T(8,128)(2,1)S(1)} collective-permute-done((bf16[96,1024]{1,0:T(8,128)(2,1)}, bf16[96,1024]{1,0:T(8,128)(2,1)S(1)}, u32[]{:S(2)}, u32[]{:S(2)}) %collective-permute-start.1) | collective-permute-done | bytes 196640 | tf_op jit(solution)/shard_map/ppermute | solution.py:436
  18.9 2.0 %collective-permute-start.9 = (bf16[96,1024]{1,0:T(8,128)(2,1)S(1)}, bf16[96,1024]{1,0:T(8,128)(2,1)S(1)}, u32[]{:S(2)}, u32[]{:S(2)}) collective-permute-start(bf16[96,1024]{1,0:T(8,128)(2,1)S(1)} %collective-permute-done.7), channel_id=1, source_target_pairs={{0,4},{1,5},{2,6},{3,7},{4,0},{5,1},{6,2},{7,3},{8,12},{9,13},{10,... | collective-permute-start | bytes 589832 | tf_op jit(solution)/shard_map/ppermute | solution.py:451
  21.0 4.6 %copy_bitcast_fusion = (bf16[4,4096,128]{2,1,0:T(8,128)(2,1)S(1)}, bf16[4,4096,128]{2,1,0:T(8,128)(2,1)S(1)}) fusion(bf16[4096,4,128]{2,1,0:T(4,128)(2,1)} %param.9, bf16[4096,4,128]{2,1,0:T(4,128)(2,1)} %param.8), kind=kLoop, calls=%fused_computation | loop fusion | bytes 16777216 | tf_op jit(solution)/shard_map/transpose | solution.py:474
  25.7 2.0 %collective-permute-start.4 = (bf16[96,1024]{1,0:T(8,128)(2,1)S(1)}, bf16[96,1024]{1,0:T(8,128)(2,1)S(1)}, u32[]{:S(2)}, u32[]{:S(2)}) collective-permute-start(bf16[96,1024]{1,0:T(8,128)(2,1)S(1)} %collective-permute-done.2), channel_id=1, source_target_pairs={{0,4},{1,5},{2,6},{3,7},{4,0},{5,1},{6,2},{7,3},{8,12},{9,13},{10,... | collective-permute-start | bytes 589832 | tf_op jit(solution)/shard_map/ppermute | solution.py:451
  27.7 4.6 %shard_map.79 = (bf16[2,96,1152]{2,1,0:T(8,128)(2,1)S(1)}, bf16[2,96,1152]{2,1,0:T(8,128)(2,1)S(1)}, bf16[2,96,1152]{2,1,0:T(8,128)(2,1)S(1)}, bf16[2,96,1152]{2,1,0:T(8,128)(2,1)S(1)}) custom-call(s32[8]{0:T(128)S(1)} %stack.42.place_ref, s32[1]{0:T(128)} %bitcast.9.column_ref, s32[8]{0:T(128)S(1)} %bitcast.48, s32[1]{0:T(128)S(6)} %copy.18.count_ref, ...), custom_call_target="tpu_custom_call" | custom-call | flops 3221225472 | bytes 1048576 | tf_op jit(solution)/shard_map/pallas_call | solution.py:253
  32.3 2.1 %collective-permute-start.10 = (bf16[2,96,1152]{2,1,0:T(8,128)(2,1)S(1)}, bf16[2,96,1152]{2,1,0:T(8,128)(2,1)S(1)}, u32[]{:S(2)}, u32[]{:S(2)}) collective-permute-start(bf16[2,96,1152]{2,1,0:T(8,128)(2,1)S(1)} %get-tuple-element.35), channel_id=1, source_target_pairs={{0,12},{1,13},{2,14},{3,15},{4,8},{5,9},{6,10},{7,11},{8,4},{9,5},... | collective-permute-start | bytes 1327112 | tf_op jit(solution)/shard_map/ppermute | solution.py:479
  34.4 1.0 collective-permute-start.11
  35.9 7.2 %collective-permute-done.4 = bf16[96,1024]{1,0:T(8,128)(2,1)S(1)} collective-permute-done((bf16[96,1024]{1,0:T(8,128)(2,1)S(1)}, bf16[96,1024]{1,0:T(8,128)(2,1)S(1)}, u32[]{:S(2)}, u32[]{:S(2)}) %collective-permute-start.4) | collective-permute-done | bytes 196640 | tf_op jit(solution)/shard_map/ppermute | solution.py:451
  43.1 22.2 %shard_map.80 = (bf16[2,64,1152]{2,1,0:T(8,128)(2,1)S(1)}, bf16[2,64,1152]{2,1,0:T(8,128)(2,1)S(1)}, bf16[2,64,1152]{2,1,0:T(8,128)(2,1)S(1)}, bf16[2,64,1152]{2,1,0:T(8,128)(2,1)S(1)}) custom-call(s32[8]{0:T(128)S(1)} %stack.42.place_ref, s32[1]{0:T(128)} %bitcast.9.column_ref, bf16[2,96,4096]{2,1,0:T(8,128)(2,1)S(1)} %bitcast.31, ...), custom_call_target="tpu_custom_call" | custom-call | flops 17179869184 | bytes 8388608 | tf_op jit(solution)/shard_map/pallas_call | solution.py:253
  65.2 5.6 %collective-permute-start.16 = (bf16[2,64,1152]{2,1,0:T(8,128)(2,1)S(1)}, bf16[2,64,1152]{2,1,0:T(8,128)(2,1)S(1)}, u32[]{:S(2)}, u32[]{:S(2)}) collective-permute-start(bf16[2,64,1152]{2,1,0:T(8,128)(2,1)S(1)} %get-tuple-element.44), channel_id=1, source_target_pairs={{0,12},{1,13},{2,14},{3,15},{4,8},{5,9},{6,10},{7,11},{8,4},{9,5},... | collective-permute-start | bytes 884744 | tf_op jit(solution)/shard_map/ppermute | solution.py:479
  70.8 0.6 collective-permute-start.18
  71.4 1.6 %shard_map.81 = (bf16[1,96,1152]{2,1,0:T(8,128)(2,1)S(1)}, bf16[1,96,1152]{2,1,0:T(8,128)(2,1)S(1)}) custom-call(s32[1]{0:T(128)} %bitcast.refs_8_.spot_ref, bf16[2,96,1152]{2,1,0:T(8,128)(2,1)S(1)} %get-tuple-element.34.refs_8_.refs_0_, bf16[2,96,1152]{2,1,0:T(8,128)(2,1)S(1)} %collective-permute-done.10.refs_1_, ...), custom_call_target="tpu_custom_call" | custom-call | flops 3538944 | bytes 2211840 | tf_op jit(solution)/shard_map/pallas_call | solution.py:351
  73.0 11.8 %shard_map.82 = (bf16[2,32,1152]{2,1,0:T(8,128)(2,1)S(1)}, bf16[2,32,1152]{2,1,0:T(8,128)(2,1)S(1)}, bf16[2,32,1152]{2,1,0:T(8,128)(2,1)S(1)}, bf16[2,32,1152]{2,1,0:T(8,128)(2,1)S(1)}) custom-call(s32[8]{0:T(128)S(1)} %stack.42.place_ref, s32[1]{0:T(128)} %bitcast.9.column_ref, bf16[2,96,4096]{2,1,0:T(8,128)(2,1)S(1)} %bitcast.32, ...), custom_call_target="tpu_custom_call" | custom-call | flops 8589934592 | bytes 8388608 | tf_op jit(solution)/shard_map/pallas_call | solution.py:253
  84.8 2.9 %collective-permute-start.13 = (bf16[2,32,1152]{2,1,0:T(8,128)(2,1)S(1)}, bf16[2,32,1152]{2,1,0:T(8,128)(2,1)S(1)}, u32[]{:S(2)}, u32[]{:S(2)}) collective-permute-start(bf16[2,32,1152]{2,1,0:T(8,128)(2,1)S(1)} %get-tuple-element.41), channel_id=1, source_target_pairs={{0,12},{1,13},{2,14},{3,15},{4,8},{5,9},{6,10},{7,11},{8,4},{9,5},... | collective-permute-start | bytes 442376 | tf_op jit(solution)/shard_map/ppermute | solution.py:479
  88.4 0.9 collective-permute-start.21
  89.3 1.1 %shard_map.83 = (bf16[1,64,1152]{2,1,0:T(8,128)(2,1)S(1)}, bf16[1,64,1152]{2,1,0:T(8,128)(2,1)S(1)}) custom-call(s32[1]{0:T(128)} %bitcast.refs_8_.spot_ref, bf16[2,64,1152]{2,1,0:T(8,128)(2,1)S(1)} %get-tuple-element.38.refs_4_.refs_0_, bf16[2,64,1152]{2,1,0:T(8,128)(2,1)S(1)} %collective-permute-done.16.refs_1_, ...), custom_call_target="tpu_custom_call" | custom-call | flops 2359296 | bytes 1474560 | tf_op jit(solution)/shard_map/pallas_call | solution.py:351
  90.4 2.1 %collective-permute-start.20 = (bf16[1,64,1152]{2,1,0:T(8,128)(2,1)S(1)}, bf16[1,64,1152]{2,1,0:T(8,128)(2,1)S(1)}, u32[]{:S(2)}, u32[]{:S(2)}) collective-permute-start(bf16[1,64,1152]{2,1,0:T(8,128)(2,1)S(1)} %get-tuple-element.50), channel_id=1, source_target_pairs={{0,16},{1,17},{2,18},{3,19},{4,20},{5,21},{6,22},{7,23},{8,24},{9,... | collective-permute-start | bytes 442376 | tf_op jit(solution)/shard_map/ppermute | solution.py:479
  92.5 0.8 collective-permute-done.13.refs_1_
  93.8 2.2 %collective-permute-done.15.refs_3_ = bf16[2,32,1152]{2,1,0:T(8,128)(2,1)S(1)} collective-permute-done((bf16[2,32,1152]{2,1,0:T(8,128)(2,1)S(1)}, bf16[2,32,1152]{2,1,0:T(8,128)(2,1)S(1)}, u32[]{:S(2)}, u32[]{:S(2)}) %collective-permute-start.15) | collective-permute-done | bytes 147488 | tf_op jit(solution)/shard_map/ppermute | solution.py:479
  96.0 0.7 shard_map.84
  97.2 4.4 %collective-permute-done.20.refs_1_ = bf16[1,64,1152]{2,1,0:T(8,128)(2,1)S(1)} collective-permute-done((bf16[1,64,1152]{2,1,0:T(8,128)(2,1)S(1)}, bf16[1,64,1152]{2,1,0:T(8,128)(2,1)S(1)}, u32[]{:S(2)}, u32[]{:S(2)}) %collective-permute-start.20) | collective-permute-done | bytes 147488 | tf_op jit(solution)/shard_map/ppermute | solution.py:479
  101.6 1.0 shard_map.85.refs_2_
  102.5 1.1 %shard_map.87 = bf16[1,96,1024]{2,1,0:T(8,128)(2,1)} custom-call(bf16[1,96,1152]{2,1,0:T(8,128)(2,1)S(1)} %get-tuple-element.39.refs_8_.refs_0_, bf16[1,96,1152]{2,1,0:T(8,128)(2,1)S(1)} %collective-permute-done.21.refs_1_), custom_call_target="tpu_custom_call" | custom-call | flops 786432 | bytes 442368 | tf_op jit(solution)/shard_map/pallas_call | solution.py:321
  103.6 0.9 shard_map.86
  (33 shorter events, 2.9 us)
Async XLA Ops:
  1.7 9.6 %collective-permute-start.5 = (bf16[96,1024]{1,0:T(8,128)(2,1)S(1)}, bf16[96,1024]{1,0:T(8,128)(2,1)S(1)}, u32[]{:S(2)}, u32[]{:S(2)}) collective-permute-start(bf16[96,1024]{1,0:T(8,128)(2,1)S(1)} %get-tuple-element.53), channel_id=1, source_target_pairs={{0,2},{1,3},{2,0},{3,1},{4,6},{5,7},{6,4},{7,5},{8,10},{9,11},{10,... | collective-permute-start | bytes 589832 | tf_op jit(solution)/shard_map/ppermute | solution.py:436
  4.8 9.5 %collective-permute-start.7 = (bf16[96,1024]{1,0:T(8,128)(2,1)S(1)}, bf16[96,1024]{1,0:T(8,128)(2,1)S(1)}, u32[]{:S(2)}, u32[]{:S(2)}) collective-permute-start(bf16[96,1024]{1,0:T(8,128)(2,1)S(1)} %get-tuple-element.52), channel_id=1, source_target_pairs={{0,3},{1,2},{2,1},{3,0},{4,7},{5,6},{6,5},{7,4},{8,11},{9,10},{10,... | collective-permute-start | bytes 589832 | tf_op jit(solution)/shard_map/ppermute | solution.py:436
  8.3 10.6 %collective-permute-start.1 = (bf16[96,1024]{1,0:T(8,128)(2,1)}, bf16[96,1024]{1,0:T(8,128)(2,1)S(1)}, u32[]{:S(2)}, u32[]{:S(2)}) collective-permute-start(bf16[96,1024]{1,0:T(8,128)(2,1)} %get-tuple-element.28), channel_id=1, source_target_pairs={{0,2},{1,3},{2,0},{3,1},{4,6},{5,7},{6,4},{7,5},{8,10},{9,11},{10,... | collective-permute-start | bytes 589832 | tf_op jit(solution)/shard_map/ppermute | solution.py:436
  9.6 18.1 %collective-permute-start.6 = (bf16[192,1024]{1,0:T(8,128)(2,1)}, bf16[192,1024]{1,0:T(8,128)(2,1)S(1)}, u32[]{:S(2)}, u32[]{:S(2)}) collective-permute-start(bf16[192,1024]{1,0:T(8,128)(2,1)} %get-tuple-element.33), channel_id=1, source_target_pairs={{0,1},{1,0},{2,3},{3,2},{4,5},{5,4},{6,7},{7,6},{8,9},{9,8},{10,11... | collective-permute-start | bytes 1179656 | tf_op jit(solution)/shard_map/ppermute | solution.py:436
  10.3 15.3 %collective-permute-start.2 = (bf16[96,1024]{1,0:T(8,128)(2,1)}, bf16[96,1024]{1,0:T(8,128)(2,1)S(1)}, u32[]{:S(2)}, u32[]{:S(2)}) collective-permute-start(bf16[96,1024]{1,0:T(8,128)(2,1)} %get-tuple-element.29), channel_id=1, source_target_pairs={{0,3},{1,2},{2,1},{3,0},{4,7},{5,6},{6,5},{7,4},{8,11},{9,10},{10,... | collective-permute-start | bytes 589832 | tf_op jit(solution)/shard_map/ppermute | solution.py:436
  11.4 31.7 %collective-permute-start = (bf16[192,1024]{1,0:T(8,128)(2,1)}, bf16[192,1024]{1,0:T(8,128)(2,1)S(1)}, u32[]{:S(2)}, u32[]{:S(2)}) collective-permute-start(bf16[192,1024]{1,0:T(8,128)(2,1)} %get-tuple-element.27), channel_id=1, source_target_pairs={{0,1},{1,0},{2,3},{3,2},{4,5},{5,4},{6,7},{7,6},{8,9},{9,8},{10,11... | collective-permute-start | bytes 1179656 | tf_op jit(solution)/shard_map/ppermute | solution.py:436
  14.3 11.4 %collective-permute-start.8 = (bf16[96,1024]{1,0:T(8,128)(2,1)S(1)}, bf16[96,1024]{1,0:T(8,128)(2,1)S(1)}, u32[]{:S(2)}, u32[]{:S(2)}) collective-permute-start(bf16[96,1024]{1,0:T(8,128)(2,1)S(1)} %collective-permute-done.5), channel_id=1, source_target_pairs={{0,4},{1,5},{2,6},{3,7},{4,0},{5,1},{6,2},{7,3},{8,12},{9,13},{10,... | collective-permute-start | bytes 589832 | tf_op jit(solution)/shard_map/ppermute | solution.py:451
  18.9 8.8 %collective-permute-start.9 = (bf16[96,1024]{1,0:T(8,128)(2,1)S(1)}, bf16[96,1024]{1,0:T(8,128)(2,1)S(1)}, u32[]{:S(2)}, u32[]{:S(2)}) collective-permute-start(bf16[96,1024]{1,0:T(8,128)(2,1)S(1)} %collective-permute-done.7), channel_id=1, source_target_pairs={{0,4},{1,5},{2,6},{3,7},{4,0},{5,1},{6,2},{7,3},{8,12},{9,13},{10,... | collective-permute-start | bytes 589832 | tf_op jit(solution)/shard_map/ppermute | solution.py:451
  25.5 2.1 %copy-start = (bf16[192,4096]{1,0:T(8,128)(2,1)S(1)}, bf16[192,4096]{1,0:T(8,128)(2,1)}, u32[]{:S(2)}) copy-start(bf16[192,4096]{1,0:T(8,128)(2,1)} %refs_0_.1) | copy-start | bytes 4718596
  25.6 2.1 %copy-start.2 = (s32[1,8]{1,0:T(1,128)S(1)}, s32[1,8]{1,0:T(1,128)}, u32[]{:S(2)}) copy-start(s32[1,8]{1,0:T(1,128)} %param.10) | copy-start | bytes 100
  25.6 9.8 %collective-permute-start.3 = (bf16[96,1024]{1,0:T(8,128)(2,1)S(1)}, bf16[96,1024]{1,0:T(8,128)(2,1)S(1)}, u32[]{:S(2)}, u32[]{:S(2)}) collective-permute-start(bf16[96,1024]{1,0:T(8,128)(2,1)S(1)} %collective-permute-done.1), channel_id=1, source_target_pairs={{0,4},{1,5},{2,6},{3,7},{4,0},{5,1},{6,2},{7,3},{8,12},{9,13},{10,... | collective-permute-start | bytes 589832 | tf_op jit(solution)/shard_map/ppermute | solution.py:451
  25.7 17.4 %collective-permute-start.4 = (bf16[96,1024]{1,0:T(8,128)(2,1)S(1)}, bf16[96,1024]{1,0:T(8,128)(2,1)S(1)}, u32[]{:S(2)}, u32[]{:S(2)}) collective-permute-start(bf16[96,1024]{1,0:T(8,128)(2,1)S(1)} %collective-permute-done.2), channel_id=1, source_target_pairs={{0,4},{1,5},{2,6},{3,7},{4,0},{5,1},{6,2},{7,3},{8,12},{9,13},{10,... | collective-permute-start | bytes 589832 | tf_op jit(solution)/shard_map/ppermute | solution.py:451
  27.7 15.4 %copy-start.1 = (bf16[192,4096]{1,0:T(8,128)(2,1)S(1)}, bf16[192,4096]{1,0:T(8,128)(2,1)}, u32[]{:S(2)}) copy-start(bf16[192,4096]{1,0:T(8,128)(2,1)} %refs_1_.1) | copy-start | bytes 4718596
  32.3 38.5 %collective-permute-start.10 = (bf16[2,96,1152]{2,1,0:T(8,128)(2,1)S(1)}, bf16[2,96,1152]{2,1,0:T(8,128)(2,1)S(1)}, u32[]{:S(2)}, u32[]{:S(2)}) collective-permute-start(bf16[2,96,1152]{2,1,0:T(8,128)(2,1)S(1)} %get-tuple-element.35), channel_id=1, source_target_pairs={{0,12},{1,13},{2,14},{3,15},{4,8},{5,9},{6,10},{7,11},{8,4},{9,5},... | collective-permute-start | bytes 1327112 | tf_op jit(solution)/shard_map/ppermute | solution.py:479
  34.4 37.0 %collective-permute-start.11 = (bf16[2,96,1152]{2,1,0:T(8,128)(2,1)S(1)}, bf16[2,96,1152]{2,1,0:T(8,128)(2,1)S(1)}, u32[]{:S(2)}, u32[]{:S(2)}) collective-permute-start(bf16[2,96,1152]{2,1,0:T(8,128)(2,1)S(1)} %get-tuple-element.36), channel_id=1, source_target_pairs={{0,4},{1,5},{2,6},{3,7},{4,0},{5,1},{6,2},{7,3},{8,12},{9,13},{10,... | collective-permute-start | bytes 1327112 | tf_op jit(solution)/shard_map/ppermute | solution.py:479
  35.4 36.0 %collective-permute-start.12 = (bf16[2,96,1152]{2,1,0:T(8,128)(2,1)S(1)}, bf16[2,96,1152]{2,1,0:T(8,128)(2,1)S(1)}, u32[]{:S(2)}, u32[]{:S(2)}) collective-permute-start(bf16[2,96,1152]{2,1,0:T(8,128)(2,1)S(1)} %get-tuple-element.37), channel_id=1, source_target_pairs={{0,8},{1,9},{2,10},{3,11},{4,12},{5,13},{6,14},{7,15},{8,0},{9,1},... | collective-permute-start | bytes 1327112 | tf_op jit(solution)/shard_map/ppermute | solution.py:479
  65.2 22.5 %collective-permute-start.16 = (bf16[2,64,1152]{2,1,0:T(8,128)(2,1)S(1)}, bf16[2,64,1152]{2,1,0:T(8,128)(2,1)S(1)}, u32[]{:S(2)}, u32[]{:S(2)}) collective-permute-start(bf16[2,64,1152]{2,1,0:T(8,128)(2,1)S(1)} %get-tuple-element.44), channel_id=1, source_target_pairs={{0,12},{1,13},{2,14},{3,15},{4,8},{5,9},{6,10},{7,11},{8,4},{9,5},... | collective-permute-start | bytes 884744 | tf_op jit(solution)/shard_map/ppermute | solution.py:479
  70.8 17.6 %collective-permute-start.17 = (bf16[2,64,1152]{2,1,0:T(8,128)(2,1)S(1)}, bf16[2,64,1152]{2,1,0:T(8,128)(2,1)S(1)}, u32[]{:S(2)}, u32[]{:S(2)}) collective-permute-start(bf16[2,64,1152]{2,1,0:T(8,128)(2,1)S(1)} %get-tuple-element.45), channel_id=1, source_target_pairs={{0,4},{1,5},{2,6},{3,7},{4,0},{5,1},{6,2},{7,3},{8,12},{9,13},{10,... | collective-permute-start | bytes 884744 | tf_op jit(solution)/shard_map/ppermute | solution.py:479
  70.8 18.5 %collective-permute-start.18 = (bf16[2,64,1152]{2,1,0:T(8,128)(2,1)S(1)}, bf16[2,64,1152]{2,1,0:T(8,128)(2,1)S(1)}, u32[]{:S(2)}, u32[]{:S(2)}) collective-permute-start(bf16[2,64,1152]{2,1,0:T(8,128)(2,1)S(1)} %get-tuple-element.46), channel_id=1, source_target_pairs={{0,8},{1,9},{2,10},{3,11},{4,12},{5,13},{6,14},{7,15},{8,0},{9,1},... | collective-permute-start | bytes 884744 | tf_op jit(solution)/shard_map/ppermute | solution.py:479
  84.8 8.5 %collective-permute-start.13 = (bf16[2,32,1152]{2,1,0:T(8,128)(2,1)S(1)}, bf16[2,32,1152]{2,1,0:T(8,128)(2,1)S(1)}, u32[]{:S(2)}, u32[]{:S(2)}) collective-permute-start(bf16[2,32,1152]{2,1,0:T(8,128)(2,1)S(1)} %get-tuple-element.41), channel_id=1, source_target_pairs={{0,12},{1,13},{2,14},{3,15},{4,8},{5,9},{6,10},{7,11},{8,4},{9,5},... | collective-permute-start | bytes 442376 | tf_op jit(solution)/shard_map/ppermute | solution.py:479
  87.8 6.1 %collective-permute-start.14 = (bf16[2,32,1152]{2,1,0:T(8,128)(2,1)S(1)}, bf16[2,32,1152]{2,1,0:T(8,128)(2,1)S(1)}, u32[]{:S(2)}, u32[]{:S(2)}) collective-permute-start(bf16[2,32,1152]{2,1,0:T(8,128)(2,1)S(1)} %get-tuple-element.42), channel_id=1, source_target_pairs={{0,4},{1,5},{2,6},{3,7},{4,0},{5,1},{6,2},{7,3},{8,12},{9,13},{10,... | collective-permute-start | bytes 442376 | tf_op jit(solution)/shard_map/ppermute | solution.py:479
  87.8 8.2 %collective-permute-start.15 = (bf16[2,32,1152]{2,1,0:T(8,128)(2,1)S(1)}, bf16[2,32,1152]{2,1,0:T(8,128)(2,1)S(1)}, u32[]{:S(2)}, u32[]{:S(2)}) collective-permute-start(bf16[2,32,1152]{2,1,0:T(8,128)(2,1)S(1)} %get-tuple-element.43), channel_id=1, source_target_pairs={{0,8},{1,9},{2,10},{3,11},{4,12},{5,13},{6,14},{7,15},{8,0},{9,1},... | collective-permute-start | bytes 442376 | tf_op jit(solution)/shard_map/ppermute | solution.py:479
  88.4 14.1 %collective-permute-start.21 = (bf16[1,96,1152]{2,1,0:T(8,128)(2,1)S(1)}, bf16[1,96,1152]{2,1,0:T(8,128)(2,1)S(1)}, u32[]{:S(2)}, u32[]{:S(2)}) collective-permute-start(bf16[1,96,1152]{2,1,0:T(8,128)(2,1)S(1)} %get-tuple-element.51), channel_id=1, source_target_pairs={{0,16},{1,17},{2,18},{3,19},{4,20},{5,21},{6,22},{7,23},{8,24},{9,... | collective-permute-start | bytes 663560 | tf_op jit(solution)/shard_map/ppermute | solution.py:479
  90.4 11.1 %collective-permute-start.20 = (bf16[1,64,1152]{2,1,0:T(8,128)(2,1)S(1)}, bf16[1,64,1152]{2,1,0:T(8,128)(2,1)S(1)}, u32[]{:S(2)}, u32[]{:S(2)}) collective-permute-start(bf16[1,64,1152]{2,1,0:T(8,128)(2,1)S(1)} %get-tuple-element.50), channel_id=1, source_target_pairs={{0,16},{1,17},{2,18},{3,19},{4,20},{5,21},{6,22},{7,23},{8,24},{9,... | collective-permute-start | bytes 442376 | tf_op jit(solution)/shard_map/ppermute | solution.py:479
  96.7 6.9 %collective-permute-start.19 = (bf16[1,32,1152]{2,1,0:T(8,128)(2,1)S(1)}, bf16[1,32,1152]{2,1,0:T(8,128)(2,1)S(1)}, u32[]{:S(2)}, u32[]{:S(2)}) collective-permute-start(bf16[1,32,1152]{2,1,0:T(8,128)(2,1)S(1)} %get-tuple-element.49), channel_id=1, source_target_pairs={{0,16},{1,17},{2,18},{3,19},{4,20},{5,21},{6,22},{7,23},{8,24},{9,... | collective-permute-start | bytes 221192 | tf_op jit(solution)/shard_map/ppermute | solution.py:479

commit v5 on v4

--- a/solution.py
+++ b/solution.py
@@ -439,28 +439,25 @@
         lax.dynamic_slice(q_second, (low * half, (me ^ bit) * mine), (half, mine))
         for bit in (2, 3)
     ]
-    got = [[sent(x, bit) for x, bit in zip(picked, (2, 3))]]
-    boxes = [(0, 1, False), (1, 1, False), (1, 2, True), (1, 3, True)]
-    near_s, near_f, *picked = pick([q_second, q_first], here, boxes, mine)
-    got.append([sent(x, bit) for x, bit in zip(picked, (2, 3))])
-    near = [sent(near_s, 1), sent(near_f, 1)]
-    pieces = []
-    for block, beside, remote in zip((q_second, q_first), near, got):
-        others = []
-        for x in remote:
-            others.append(lax.ppermute(x, AXES, swapped(shape, 1, 0)))
-        pieces.append(
-            [block.reshape(2, half, wide), beside.reshape(2, half, mine)]
-            + [x.reshape(1, half, mine) for x in remote + others]
-        )
-    owners = []
-    for bit in (0, 1):
-        owners += [2 * (me ^ bit), 2 * (me ^ bit) + 1]
-    owners += [2 * (me ^ 2) + low, 2 * (me ^ 3) + low]
-    owners += [2 * (me ^ 2) + 1 - low, 2 * (me ^ 3) + 1 - low]
-    places = [((owner ^ spot) % 4) * 2 + owner // 4 for owner in owners]
-    places = jnp.stack(places).astype(jnp.int32)
-    return pieces[0], pieces[1], places, jnp.reshape(me, (1,)).astype(jnp.int32), got[0][0]
+    got = [sent(x, bit) for x, bit in zip(picked, (2, 3))]
+    boxes = [(0, 1, False)] + [(1, bit, False) for bit in (1, 2, 3)]
+    near_s, *picked_f = pick([q_second, q_first], here, boxes, mine)
+    near_s = sent(near_s, 1)
+    beside = [sent(x, bit) for x, bit in zip(picked_f, (1, 2, 3))]
+    others = []
+    for x in got:
+        others.append(lax.ppermute(x, AXES, swapped(shape, 1, 0)))
+    second = [q_second.reshape(2, half, wide), near_s.reshape(2, half, mine)]
+    second += [x.reshape(1, half, mine) for x in got + others]
+    first = [q_first.reshape(2, half, wide)] + [x.reshape(2, half, mine) for x in beside]
+
+    def places_of(owners):
+        return jnp.stack([((o ^ spot) % 4) * 2 + o // 4 for o in owners]).astype(jnp.int32)
+
+    straight = [2 * (me ^ bit) + side for bit in range(4) for side in (0, 1)]
+    shared = [2 * (me ^ bit) + side for side in (low, 1 - low) for bit in (2, 3)]
+    places = places_of(straight[:4] + shared), places_of(straight)
+    return second, first, places, jnp.reshape(me, (1,)).astype(jnp.int32)
 
 
 def shards(shape, q_first, q_second, k_cache, v_cache, kept_blocks, kept_count):
@@ -468,10 +465,8 @@
     owned = q_first.shape[0] * head // ctx
     kept = (kept_blocks[0], kept_count)
     if head == 4 and ctx == 8 and owned % 48 == 0:
-        second, first, places, column, arrived = relayed(shape, q_first, q_second)
-        keys = jnp.swapaxes(k_cache, 0, 1)
-        late, _ = lax.optimization_barrier((v_cache, arrived))
-        keys, values = settle(keys, jnp.swapaxes(late, 0, 1))
+        second, first, places, column = relayed(shape, q_first, q_second)
+        keys, values = settle(jnp.swapaxes(k_cache, 0, 1), jnp.swapaxes(v_cache, 0, 1))
         spot = jnp.reshape(lax.axis_index("ctx") // 4, (1,)).astype(jnp.int32)
         cut = owned * 2 // 3
 
@@ -482,7 +477,8 @@
             return [parts[0]] + [moved(parts[bits], bits) for bits in (3, 1, 2)]
 
         def attend(pieces, span, after, kept=None):
-            parts = partial_call(pieces, places, column, keys, values, span, 4, after, kept)
+            at = places[0 if kept else 1]
+            parts = partial_call(pieces, at, column, keys, values, span, 4, after, kept)
             return parts, gathered(parts)
 
         def settled(parts, after):

time: 105 us -> 119 us (1.13)
  local copies, waits for them, and re-layouts: 5.73 us -> 20.5 us
  waiting for transfers between devices: 20.9 us -> 17.2 us
  starting transfers between devices: 28 us -> 31.3 us
    unnamed x6 -> x18, local copies, waits for them, and re-layouts: 0.02 us -> 12.7 us
    ppermute x4 -> x2, waiting for transfers between devices: 7.19 us -> 0.01 us  [relayed(): others.append(lax.ppermute(x, AXES, swapped(shape, 1, 0)))]
    ppermute x12, starting transfers between devices: 16.8 us -> 23.3 us  [moved(): return lax.ppermute(part, AXES, swapped(shape, bits, 0))]
    ppermute x4 -> x2, starting transfers between devices: 5.64 us -> 2.03 us  [relayed(): others.append(lax.ppermute(x, AXES, swapped(shape, 1, 0)))]
    ppermute x12, waiting for transfers between devices: 7.88 us -> 10.6 us  [moved(): return lax.ppermute(part, AXES, swapped(shape, bits, 0))]
    transpose x1, local copies, waits for them, and re-layouts: 4.56 us -> 6.6 us  [shards(): jnp.swapaxes(v_cache, 0, 1)]
  transfers between devices with their start and end apart: 22 -> 20, of which waited for: 7 -> 3; matrix products, arithmetic and copies ran while one was open for 5% -> 7% of each run, Pallas kernels for 45% -> 37%
where the time goes in v5:
time: 119 us
  Pallas kernels  47.4 us (40%)
  starting transfers between devices  31.3 us (26%)
  local copies, waits for them, and re-layouts  20.5 us (17%)
  waiting for transfers between devices  17.2 us (14%)
  between operations  1.54 us (1%)
    pallas_call x3, Pallas kernels, partial_call(): pl.pallas_call(functools.partial(kernel, pieces=len(pieces), outs=outs, g...  37.9 us
    ppermute x12, starting transfers between devices, moved(): return lax.ppermute(part, AXES, swapped(shape, bits, 0))  23.3 us
    unnamed x18, local copies, waits for them, and re-layouts  12.7 us
    ppermute x12, waiting for transfers between devices, moved(): return lax.ppermute(part, AXES, swapped(shape, bits, 0))  10.6 us
    ppermute x6, waiting for transfers between devices, sent(): return lax.ppermute(block, AXES, swapped(shape, 0, bit))  6.65 us
    transpose x1, local copies, waits for them, and re-layouts, shards(): jnp.swapaxes(v_cache, 0, 1)  6.6 us
    ppermute x6, starting transfers between devices, sent(): return lax.ppermute(block, AXES, swapped(shape, 0, bit))  6.02 us
    pallas_call x3, Pallas kernels, merge_quad(): pl.pallas_call(functools.partial(quad_kernel, sources=len(parts)), in_spe...  3.35 us
  transfers between devices with their start and end apart: 20, of which 3 were waited for; matrix products, arithmetic and copies ran while one was open for 7% of the time, Pallas kernels for 37%

profile of v5, /device:TPU:0, one launch (start us, length us, event | category | flops | bytes accessed | tf_op | source)
XLA Modules:
  0.0 118.7 jit_solution(2851096819389752148)
XLA Ops:
  0.6 0.7 pad_add_fusion.spot_ref
  1.3 3.2 %shard_map.77 = (bf16[192,1024]{1,0:T(8,128)(2,1)}, bf16[192,1024]{1,0:T(8,128)(2,1)}, bf16[192,1024]{1,0:T(8,128)(2,1)}, bf16[192,1024]{1,0:T(8,128)(2,1)}) custom-call(s32[2]{0:T(128)} %pad_add_fusion.spot_ref, bf16[192,4096]{1,0:T(8,128)(2,1)} %refs_0_.1, bf16[192,4096]{1,0:T(8,128)(2,1)} %refs_1_.1), custom_call_target="tpu_custom_call" | custom-call | tf_op jit(solution)/shard_map/pallas_call | solution.py:403
  4.5 0.6 collective-permute-start.3
  5.1 1.0 fusion
  6.1 2.6 %collective-permute-start.4 = (bf16[96,1024]{1,0:T(8,128)(2,1)S(1)}, bf16[96,1024]{1,0:T(8,128)(2,1)S(1)}, u32[]{:S(2)}, u32[]{:S(2)}) collective-permute-start(bf16[96,1024]{1,0:T(8,128)(2,1)S(1)} %get-tuple-element.51), channel_id=1, source_target_pairs={{0,2},{1,3},{2,0},{3,1},{4,6},{5,7},{6,4},{7,5},{8,10},{9,11},{10,... | collective-permute-start | bytes 589832 | tf_op jit(solution)/shard_map/ppermute | solution.py:436
  8.9 1.9 %collective-permute-start.1 = (bf16[192,1024]{1,0:T(8,128)(2,1)}, bf16[192,1024]{1,0:T(8,128)(2,1)S(1)}, u32[]{:S(2)}, u32[]{:S(2)}) collective-permute-start(bf16[192,1024]{1,0:T(8,128)(2,1)} %get-tuple-element.27), channel_id=1, source_target_pairs={{0,2},{1,3},{2,0},{3,1},{4,6},{5,7},{6,4},{7,5},{8,10},{9,11},{10,... | collective-permute-start | bytes 1179656 | tf_op jit(solution)/shard_map/ppermute | solution.py:436
  10.9 3.6 %collective-permute-done.4 = bf16[96,1024]{1,0:T(8,128)(2,1)S(1)} collective-permute-done((bf16[96,1024]{1,0:T(8,128)(2,1)S(1)}, bf16[96,1024]{1,0:T(8,128)(2,1)S(1)}, u32[]{:S(2)}, u32[]{:S(2)}) %collective-permute-start.4) | collective-permute-done | bytes 196640 | tf_op jit(solution)/shard_map/ppermute | solution.py:436
  14.5 0.7 collective-permute-start.2
  15.2 3.0 %collective-permute-done.5 = bf16[96,1024]{1,0:T(8,128)(2,1)S(1)} collective-permute-done((bf16[96,1024]{1,0:T(8,128)(2,1)S(1)}, bf16[96,1024]{1,0:T(8,128)(2,1)S(1)}, u32[]{:S(2)}, u32[]{:S(2)}) %collective-permute-start.5) | collective-permute-done | bytes 196640 | tf_op jit(solution)/shard_map/ppermute | solution.py:436
  18.2 1.5 %collective-permute-start.6 = (bf16[96,1024]{1,0:T(8,128)(2,1)S(1)}, bf16[96,1024]{1,0:T(8,128)(2,1)}, u32[]{:S(2)}, u32[]{:S(2)}) collective-permute-start(bf16[96,1024]{1,0:T(8,128)(2,1)S(1)} %collective-permute-done.4), channel_id=1, source_target_pairs={{0,4},{1,5},{2,6},{3,7},{4,0},{5,1},{6,2},{7,3},{8,12},{9,13},{10,... | collective-permute-start | bytes 589832 | tf_op jit(solution)/shard_map/ppermute | solution.py:449
  20.3 6.6 %copy_bitcast_fusion = (bf16[4,4096,128]{2,1,0:T(8,128)(2,1)}, bf16[4,4096,128]{2,1,0:T(8,128)(2,1)}) fusion(bf16[4096,4,128]{2,1,0:T(4,128)(2,1)} %param.9, bf16[4096,4,128]{2,1,0:T(4,128)(2,1)} %param.8), kind=kLoop, calls=%fused_computation | loop fusion | bytes 16777216 | tf_op jit(solution)/shard_map/transpose | solution.py:469
  27.6 2.2 %copy-done = bf16[4,4096,128]{2,1,0:T(8,128)(2,1)S(1)} copy-done((bf16[4,4096,128]{2,1,0:T(8,128)(2,1)S(1)}, bf16[4,4096,128]{2,1,0:T(8,128)(2,1)}, u32[]{:S(2)}) %copy-start) | copy-done | bytes 4194328
  29.8 2.2 %copy-done.3 = bf16[4,4096,128]{2,1,0:T(8,128)(2,1)S(1)} copy-done((bf16[4,4096,128]{2,1,0:T(8,128)(2,1)S(1)}, bf16[4,4096,128]{2,1,0:T(8,128)(2,1)}, u32[]{:S(2)}) %copy-start.3) | copy-done | bytes 4194328
  32.0 2.0 %copy-done.1 = bf16[4,4096,128]{2,1,0:T(8,128)(2,1)} copy-done((bf16[4,4096,128]{2,1,0:T(8,128)(2,1)}, bf16[4,4096,128]{2,1,0:T(8,128)(2,1)S(1)}, u32[]{:S(2)}) %copy-start.1) | copy-done | bytes 4194328
  34.0 2.0 %copy-done.4 = bf16[4,4096,128]{2,1,0:T(8,128)(2,1)} copy-done((bf16[4,4096,128]{2,1,0:T(8,128)(2,1)}, bf16[4,4096,128]{2,1,0:T(8,128)(2,1)S(1)}, u32[]{:S(2)}) %copy-start.4) | copy-done | bytes 4194328
  36.2 2.2 %copy-done.2 = bf16[4,4096,128]{2,1,0:T(8,128)(2,1)S(1)} copy-done((bf16[4,4096,128]{2,1,0:T(8,128)(2,1)S(1)}, bf16[4,4096,128]{2,1,0:T(8,128)(2,1)}, u32[]{:S(2)}) %copy-start.2) | copy-done | bytes 4194328
  38.4 2.2 %copy-done.5 = bf16[4,4096,128]{2,1,0:T(8,128)(2,1)S(1)} copy-done((bf16[4,4096,128]{2,1,0:T(8,128)(2,1)S(1)}, bf16[4,4096,128]{2,1,0:T(8,128)(2,1)}, u32[]{:S(2)}) %copy-start.5) | copy-done | bytes 4194328
  40.6 5.6 %shard_map.79 = (bf16[2,96,1152]{2,1,0:T(8,128)(2,1)S(1)}, bf16[2,96,1152]{2,1,0:T(8,128)(2,1)S(1)}, bf16[2,96,1152]{2,1,0:T(8,128)(2,1)S(1)}, bf16[2,96,1152]{2,1,0:T(8,128)(2,1)S(1)}) custom-call(s32[8]{0:T(128)S(1)} %stack.68.place_ref, s32[1]{0:T(128)} %bitcast.9.column_ref, s32[8]{0:T(128)S(1)} %bitcast.44, s32[1]{0:T(128)S(6)} %copy.18.count_ref, ...), custom_call_target="tpu_custom_call" | custom-call | flops 3221225472 | bytes 1048576 | tf_op jit(solution)/shard_map/pallas_call | solution.py:253
  46.2 2.6 %collective-permute-start.8 = (bf16[2,96,1152]{2,1,0:T(8,128)(2,1)S(1)}, bf16[2,96,1152]{2,1,0:T(8,128)(2,1)S(1)}, u32[]{:S(2)}, u32[]{:S(2)}) collective-permute-start(bf16[2,96,1152]{2,1,0:T(8,128)(2,1)S(1)} %get-tuple-element.33), channel_id=1, source_target_pairs={{0,12},{1,13},{2,14},{3,15},{4,8},{5,9},{6,10},{7,11},{8,4},{9,5},... | collective-permute-start | bytes 1327112 | tf_op jit(solution)/shard_map/ppermute | solution.py:474
  49.7 21.0 %shard_map.80 = (bf16[2,64,1152]{2,1,0:T(8,128)(2,1)S(1)}, bf16[2,64,1152]{2,1,0:T(8,128)(2,1)S(1)}, bf16[2,64,1152]{2,1,0:T(8,128)(2,1)S(1)}, bf16[2,64,1152]{2,1,0:T(8,128)(2,1)S(1)}) custom-call(s32[8]{0:T(128)S(1)} %stack.61.place_ref, s32[1]{0:T(128)} %bitcast.9.column_ref, bf16[2,96,4096]{2,1,0:T(8,128)(2,1)S(1)} %bitcast.33, ...), custom_call_target="tpu_custom_call" | custom-call | flops 17179869184 | bytes 8388608 | tf_op jit(solution)/shard_map/pallas_call | solution.py:253
  70.8 2.6 %collective-permute-start.14 = (bf16[2,64,1152]{2,1,0:T(8,128)(2,1)S(1)}, bf16[2,64,1152]{2,1,0:T(8,128)(2,1)S(1)}, u32[]{:S(2)}, u32[]{:S(2)}) collective-permute-start(bf16[2,64,1152]{2,1,0:T(8,128)(2,1)S(1)} %get-tuple-element.42), channel_id=1, source_target_pairs={{0,12},{1,13},{2,14},{3,15},{4,8},{5,9},{6,10},{7,11},{8,4},{9,5},... | collective-permute-start | bytes 884744 | tf_op jit(solution)/shard_map/ppermute | solution.py:474
  74.3 1.6 %shard_map.81 = (bf16[1,96,1152]{2,1,0:T(8,128)(2,1)S(1)}, bf16[1,96,1152]{2,1,0:T(8,128)(2,1)S(1)}) custom-call(s32[1]{0:T(128)} %bitcast.refs_8_.spot_ref, bf16[2,96,1152]{2,1,0:T(8,128)(2,1)S(1)} %get-tuple-element.32.refs_6_.refs_0_, bf16[2,96,1152]{2,1,0:T(8,128)(2,1)S(1)} %collective-permute-done.8.refs_1_, ...), custom_call_target="tpu_custom_call" | custom-call | flops 3538944 | bytes 2211840 | tf_op jit(solution)/shard_map/pallas_call | solution.py:351
  75.9 11.3 %shard_map.82 = (bf16[2,32,1152]{2,1,0:T(8,128)(2,1)S(1)}, bf16[2,32,1152]{2,1,0:T(8,128)(2,1)S(1)}, bf16[2,32,1152]{2,1,0:T(8,128)(2,1)S(1)}, bf16[2,32,1152]{2,1,0:T(8,128)(2,1)S(1)}) custom-call(s32[8]{0:T(128)S(1)} %stack.61.place_ref, s32[1]{0:T(128)} %bitcast.9.column_ref, bf16[2,96,4096]{2,1,0:T(8,128)(2,1)S(1)} %bitcast.34, ...), custom_call_target="tpu_custom_call" | custom-call | flops 8589934592 | bytes 8388608 | tf_op jit(solution)/shard_map/pallas_call | solution.py:253
  87.2 2.6 %collective-permute-start.11 = (bf16[2,32,1152]{2,1,0:T(8,128)(2,1)S(1)}, bf16[2,32,1152]{2,1,0:T(8,128)(2,1)S(1)}, u32[]{:S(2)}, u32[]{:S(2)}) collective-permute-start(bf16[2,32,1152]{2,1,0:T(8,128)(2,1)S(1)} %get-tuple-element.39), channel_id=1, source_target_pairs={{0,12},{1,13},{2,14},{3,15},{4,8},{5,9},{6,10},{7,11},{8,4},{9,5},... | collective-permute-start | bytes 442376 | tf_op jit(solution)/shard_map/ppermute | solution.py:474
  90.8 7.9 %collective-permute-start.19 = (bf16[1,96,1152]{2,1,0:T(8,128)(2,1)S(1)}, bf16[1,96,1152]{2,1,0:T(8,128)(2,1)S(1)}, u32[]{:S(2)}, u32[]{:S(2)}) collective-permute-start(bf16[1,96,1152]{2,1,0:T(8,128)(2,1)S(1)} %get-tuple-element.49), channel_id=1, source_target_pairs={{0,16},{1,17},{2,18},{3,19},{4,20},{5,21},{6,22},{7,23},{8,24},{9,... | collective-permute-start | bytes 663560 | tf_op jit(solution)/shard_map/ppermute | solution.py:474
  98.7 1.1 shard_map.83
  99.9 0.7 shard_map.84
  100.6 4.7 %collective-permute-start.17 = (bf16[1,32,1152]{2,1,0:T(8,128)(2,1)S(1)}, bf16[1,32,1152]{2,1,0:T(8,128)(2,1)S(1)}, u32[]{:S(2)}, u32[]{:S(2)}) collective-permute-start(bf16[1,32,1152]{2,1,0:T(8,128)(2,1)S(1)} %get-tuple-element.47), channel_id=1, source_target_pairs={{0,16},{1,17},{2,18},{3,19},{4,20},{5,21},{6,22},{7,23},{8,24},{9,... | collective-permute-start | bytes 221192 | tf_op jit(solution)/shard_map/ppermute | solution.py:474
  105.3 10.5 %collective-permute-done.18.refs_1_ = bf16[1,64,1152]{2,1,0:T(8,128)(2,1)S(1)} collective-permute-done((bf16[1,64,1152]{2,1,0:T(8,128)(2,1)S(1)}, bf16[1,64,1152]{2,1,0:T(8,128)(2,1)S(1)}, u32[]{:S(2)}, u32[]{:S(2)}) %collective-permute-start.18) | collective-permute-done | bytes 147488 | tf_op jit(solution)/shard_map/ppermute | solution.py:474
  115.8 1.0 shard_map.85.refs_2_
  116.8 1.1 shard_map.87
  117.8 0.9 shard_map.86
  (42 shorter events, 3.9 us)
Async XLA Ops:
  4.5 15.2 %collective-permute-start.3 = (bf16[192,1024]{1,0:T(8,128)(2,1)}, bf16[192,1024]{1,0:T(8,128)(2,1)S(1)}, u32[]{:S(2)}, u32[]{:S(2)}) collective-permute-start(bf16[192,1024]{1,0:T(8,128)(2,1)} %get-tuple-element.31), channel_id=1, source_target_pairs={{0,1},{1,0},{2,3},{3,2},{4,5},{5,4},{6,7},{7,6},{8,9},{9,8},{10,11... | collective-permute-start | bytes 1179656 | tf_op jit(solution)/shard_map/ppermute | solution.py:436
  6.1 8.3 %collective-permute-start.4 = (bf16[96,1024]{1,0:T(8,128)(2,1)S(1)}, bf16[96,1024]{1,0:T(8,128)(2,1)S(1)}, u32[]{:S(2)}, u32[]{:S(2)}) collective-permute-start(bf16[96,1024]{1,0:T(8,128)(2,1)S(1)} %get-tuple-element.51), channel_id=1, source_target_pairs={{0,2},{1,3},{2,0},{3,1},{4,6},{5,7},{6,4},{7,5},{8,10},{9,11},{10,... | collective-permute-start | bytes 589832 | tf_op jit(solution)/shard_map/ppermute | solution.py:436
  8.7 9.5 %collective-permute-start.5 = (bf16[96,1024]{1,0:T(8,128)(2,1)S(1)}, bf16[96,1024]{1,0:T(8,128)(2,1)S(1)}, u32[]{:S(2)}, u32[]{:S(2)}) collective-permute-start(bf16[96,1024]{1,0:T(8,128)(2,1)S(1)} %get-tuple-element.50), channel_id=1, source_target_pairs={{0,3},{1,2},{2,1},{3,0},{4,7},{5,6},{6,5},{7,4},{8,11},{9,10},{10,... | collective-permute-start | bytes 589832 | tf_op jit(solution)/shard_map/ppermute | solution.py:436
  8.9 40.4 %collective-permute-start = (bf16[192,1024]{1,0:T(8,128)(2,1)}, bf16[192,1024]{1,0:T(8,128)(2,1)S(1)}, u32[]{:S(2)}, u32[]{:S(2)}) collective-permute-start(bf16[192,1024]{1,0:T(8,128)(2,1)} %get-tuple-element.26), channel_id=1, source_target_pairs={{0,1},{1,0},{2,3},{3,2},{4,5},{5,4},{6,7},{7,6},{8,9},{9,8},{10,11... | collective-permute-start | bytes 1179656 | tf_op jit(solution)/shard_map/ppermute | solution.py:436
  8.9 40.8 %collective-permute-start.1 = (bf16[192,1024]{1,0:T(8,128)(2,1)}, bf16[192,1024]{1,0:T(8,128)(2,1)S(1)}, u32[]{:S(2)}, u32[]{:S(2)}) collective-permute-start(bf16[192,1024]{1,0:T(8,128)(2,1)} %get-tuple-element.27), channel_id=1, source_target_pairs={{0,2},{1,3},{2,0},{3,1},{4,6},{5,7},{6,4},{7,5},{8,10},{9,11},{10,... | collective-permute-start | bytes 1179656 | tf_op jit(solution)/shard_map/ppermute | solution.py:436
  14.5 35.3 %collective-permute-start.2 = (bf16[192,1024]{1,0:T(8,128)(2,1)}, bf16[192,1024]{1,0:T(8,128)(2,1)S(1)}, u32[]{:S(2)}, u32[]{:S(2)}) collective-permute-start(bf16[192,1024]{1,0:T(8,128)(2,1)} %get-tuple-element.28), channel_id=1, source_target_pairs={{0,3},{1,2},{2,1},{3,0},{4,7},{5,6},{6,5},{7,4},{8,11},{9,10},{10,... | collective-permute-start | bytes 1179656 | tf_op jit(solution)/shard_map/ppermute | solution.py:436
  18.2 17.9 %collective-permute-start.6 = (bf16[96,1024]{1,0:T(8,128)(2,1)S(1)}, bf16[96,1024]{1,0:T(8,128)(2,1)}, u32[]{:S(2)}, u32[]{:S(2)}) collective-permute-start(bf16[96,1024]{1,0:T(8,128)(2,1)S(1)} %collective-permute-done.4), channel_id=1, source_target_pairs={{0,4},{1,5},{2,6},{3,7},{4,0},{5,1},{6,2},{7,3},{8,12},{9,13},{10,... | collective-permute-start | bytes 589832 | tf_op jit(solution)/shard_map/ppermute | solution.py:449
  19.7 16.4 %collective-permute-start.7 = (bf16[96,1024]{1,0:T(8,128)(2,1)S(1)}, bf16[96,1024]{1,0:T(8,128)(2,1)}, u32[]{:S(2)}, u32[]{:S(2)}) collective-permute-start(bf16[96,1024]{1,0:T(8,128)(2,1)S(1)} %collective-permute-done.5), channel_id=1, source_target_pairs={{0,4},{1,5},{2,6},{3,7},{4,0},{5,1},{6,2},{7,3},{8,12},{9,13},{10,... | collective-permute-start | bytes 589832 | tf_op jit(solution)/shard_map/ppermute | solution.py:449
  27.6 2.2 %copy-start = (bf16[4,4096,128]{2,1,0:T(8,128)(2,1)S(1)}, bf16[4,4096,128]{2,1,0:T(8,128)(2,1)}, u32[]{:S(2)}) copy-start(bf16[4,4096,128]{2,1,0:T(8,128)(2,1)} %get-tuple-element.52.values_in) | copy-start | bytes 12582916
  29.8 2.2 %copy-start.3 = (bf16[4,4096,128]{2,1,0:T(8,128)(2,1)S(1)}, bf16[4,4096,128]{2,1,0:T(8,128)(2,1)}, u32[]{:S(2)}) copy-start(bf16[4,4096,128]{2,1,0:T(8,128)(2,1)} %get-tuple-element.53.keys_in) | copy-start | bytes 12582916
  32.0 4.2 %copy-start.6 = (bf16[192,4096]{1,0:T(8,128)(2,1)S(1)}, bf16[192,4096]{1,0:T(8,128)(2,1)}, u32[]{:S(2)}) copy-start(bf16[192,4096]{1,0:T(8,128)(2,1)} %refs_0_.1) | copy-start | bytes 4718596
  32.0 4.2 %copy-start.8 = (s32[1,8]{1,0:T(1,128)S(1)}, s32[1,8]{1,0:T(1,128)}, u32[]{:S(2)}) copy-start(s32[1,8]{1,0:T(1,128)} %param.10) | copy-start | bytes 100
  32.0 2.0 %copy-start.1 = (bf16[4,4096,128]{2,1,0:T(8,128)(2,1)}, bf16[4,4096,128]{2,1,0:T(8,128)(2,1)S(1)}, u32[]{:S(2)}) copy-start(bf16[4,4096,128]{2,1,0:T(8,128)(2,1)S(1)} %get-tuple-element.30.refs_7_.refs_5_) | copy-start | bytes 12582916
  34.0 2.0 %copy-start.4 = (bf16[4,4096,128]{2,1,0:T(8,128)(2,1)}, bf16[4,4096,128]{2,1,0:T(8,128)(2,1)S(1)}, u32[]{:S(2)}) copy-start(bf16[4,4096,128]{2,1,0:T(8,128)(2,1)S(1)} %get-tuple-element.29.refs_6_.refs_4_) | copy-start | bytes 12582916
  36.2 2.2 %copy-start.2 = (bf16[4,4096,128]{2,1,0:T(8,128)(2,1)S(1)}, bf16[4,4096,128]{2,1,0:T(8,128)(2,1)}, u32[]{:S(2)}) copy-start(bf16[4,4096,128]{2,1,0:T(8,128)(2,1)} %copy-done.1) | copy-start | bytes 12582916
  38.4 2.2 %copy-start.5 = (bf16[4,4096,128]{2,1,0:T(8,128)(2,1)S(1)}, bf16[4,4096,128]{2,1,0:T(8,128)(2,1)}, u32[]{:S(2)}) copy-start(bf16[4,4096,128]{2,1,0:T(8,128)(2,1)} %copy-done.4) | copy-start | bytes 12582916
  40.6 9.2 %copy-start.7 = (bf16[192,4096]{1,0:T(8,128)(2,1)S(1)}, bf16[192,4096]{1,0:T(8,128)(2,1)}, u32[]{:S(2)}) copy-start(bf16[192,4096]{1,0:T(8,128)(2,1)} %refs_1_.1) | copy-start | bytes 4718596
  46.2 27.7 %collective-permute-start.8 = (bf16[2,96,1152]{2,1,0:T(8,128)(2,1)S(1)}, bf16[2,96,1152]{2,1,0:T(8,128)(2,1)S(1)}, u32[]{:S(2)}, u32[]{:S(2)}) collective-permute-start(bf16[2,96,1152]{2,1,0:T(8,128)(2,1)S(1)} %get-tuple-element.33), channel_id=1, source_target_pairs={{0,12},{1,13},{2,14},{3,15},{4,8},{5,9},{6,10},{7,11},{8,4},{9,5},... | collective-permute-start | bytes 1327112 | tf_op jit(solution)/shard_map/ppermute | solution.py:474
  48.7 25.6 %collective-permute-start.9 = (bf16[2,96,1152]{2,1,0:T(8,128)(2,1)S(1)}, bf16[2,96,1152]{2,1,0:T(8,128)(2,1)S(1)}, u32[]{:S(2)}, u32[]{:S(2)}) collective-permute-start(bf16[2,96,1152]{2,1,0:T(8,128)(2,1)S(1)} %get-tuple-element.34), channel_id=1, source_target_pairs={{0,4},{1,5},{2,6},{3,7},{4,0},{5,1},{6,2},{7,3},{8,12},{9,13},{10,... | collective-permute-start | bytes 1327112 | tf_op jit(solution)/shard_map/ppermute | solution.py:474
  49.2 25.1 %collective-permute-start.10 = (bf16[2,96,1152]{2,1,0:T(8,128)(2,1)S(1)}, bf16[2,96,1152]{2,1,0:T(8,128)(2,1)S(1)}, u32[]{:S(2)}, u32[]{:S(2)}) collective-permute-start(bf16[2,96,1152]{2,1,0:T(8,128)(2,1)S(1)} %get-tuple-element.35), channel_id=1, source_target_pairs={{0,8},{1,9},{2,10},{3,11},{4,12},{5,13},{6,14},{7,15},{8,0},{9,1},... | collective-permute-start | bytes 1327112 | tf_op jit(solution)/shard_map/ppermute | solution.py:474
  70.8 19.5 %collective-permute-start.14 = (bf16[2,64,1152]{2,1,0:T(8,128)(2,1)S(1)}, bf16[2,64,1152]{2,1,0:T(8,128)(2,1)S(1)}, u32[]{:S(2)}, u32[]{:S(2)}) collective-permute-start(bf16[2,64,1152]{2,1,0:T(8,128)(2,1)S(1)} %get-tuple-element.42), channel_id=1, source_target_pairs={{0,12},{1,13},{2,14},{3,15},{4,8},{5,9},{6,10},{7,11},{8,4},{9,5},... | collective-permute-start | bytes 884744 | tf_op jit(solution)/shard_map/ppermute | solution.py:474
  73.4 17.4 %collective-permute-start.15 = (bf16[2,64,1152]{2,1,0:T(8,128)(2,1)S(1)}, bf16[2,64,1152]{2,1,0:T(8,128)(2,1)S(1)}, u32[]{:S(2)}, u32[]{:S(2)}) collective-permute-start(bf16[2,64,1152]{2,1,0:T(8,128)(2,1)S(1)} %get-tuple-element.43), channel_id=1, source_target_pairs={{0,4},{1,5},{2,6},{3,7},{4,0},{5,1},{6,2},{7,3},{8,12},{9,13},{10,... | collective-permute-start | bytes 884744 | tf_op jit(solution)/shard_map/ppermute | solution.py:474
  73.9 24.8 %collective-permute-start.16 = (bf16[2,64,1152]{2,1,0:T(8,128)(2,1)S(1)}, bf16[2,64,1152]{2,1,0:T(8,128)(2,1)S(1)}, u32[]{:S(2)}, u32[]{:S(2)}) collective-permute-start(bf16[2,64,1152]{2,1,0:T(8,128)(2,1)S(1)} %get-tuple-element.44), channel_id=1, source_target_pairs={{0,8},{1,9},{2,10},{3,11},{4,12},{5,13},{6,14},{7,15},{8,0},{9,1},... | collective-permute-start | bytes 884744 | tf_op jit(solution)/shard_map/ppermute | solution.py:474
  87.2 12.7 %collective-permute-start.11 = (bf16[2,32,1152]{2,1,0:T(8,128)(2,1)S(1)}, bf16[2,32,1152]{2,1,0:T(8,128)(2,1)S(1)}, u32[]{:S(2)}, u32[]{:S(2)}) collective-permute-start(bf16[2,32,1152]{2,1,0:T(8,128)(2,1)S(1)} %get-tuple-element.39), channel_id=1, source_target_pairs={{0,12},{1,13},{2,14},{3,15},{4,8},{5,9},{6,10},{7,11},{8,4},{9,5},... | collective-permute-start | bytes 442376 | tf_op jit(solution)/shard_map/ppermute | solution.py:474
  89.8 10.1 %collective-permute-start.12 = (bf16[2,32,1152]{2,1,0:T(8,128)(2,1)S(1)}, bf16[2,32,1152]{2,1,0:T(8,128)(2,1)S(1)}, u32[]{:S(2)}, u32[]{:S(2)}) collective-permute-start(bf16[2,32,1152]{2,1,0:T(8,128)(2,1)S(1)} %get-tuple-element.40), channel_id=1, source_target_pairs={{0,4},{1,5},{2,6},{3,7},{4,0},{5,1},{6,2},{7,3},{8,12},{9,13},{10,... | collective-permute-start | bytes 442376 | tf_op jit(solution)/shard_map/ppermute | solution.py:474
  90.3 9.6 %collective-permute-start.13 = (bf16[2,32,1152]{2,1,0:T(8,128)(2,1)S(1)}, bf16[2,32,1152]{2,1,0:T(8,128)(2,1)S(1)}, u32[]{:S(2)}, u32[]{:S(2)}) collective-permute-start(bf16[2,32,1152]{2,1,0:T(8,128)(2,1)S(1)} %get-tuple-element.41), channel_id=1, source_target_pairs={{0,8},{1,9},{2,10},{3,11},{4,12},{5,13},{6,14},{7,15},{8,0},{9,1},... | collective-permute-start | bytes 442376 | tf_op jit(solution)/shard_map/ppermute | solution.py:474
  90.8 26.0 %collective-permute-start.19 = (bf16[1,96,1152]{2,1,0:T(8,128)(2,1)S(1)}, bf16[1,96,1152]{2,1,0:T(8,128)(2,1)S(1)}, u32[]{:S(2)}, u32[]{:S(2)}) collective-permute-start(bf16[1,96,1152]{2,1,0:T(8,128)(2,1)S(1)} %get-tuple-element.49), channel_id=1, source_target_pairs={{0,16},{1,17},{2,18},{3,19},{4,20},{5,21},{6,22},{7,23},{8,24},{9,... | collective-permute-start | bytes 663560 | tf_op jit(solution)/shard_map/ppermute | solution.py:474
  99.8 16.0 %collective-permute-start.18 = (bf16[1,64,1152]{2,1,0:T(8,128)(2,1)S(1)}, bf16[1,64,1152]{2,1,0:T(8,128)(2,1)S(1)}, u32[]{:S(2)}, u32[]{:S(2)}) collective-permute-start(bf16[1,64,1152]{2,1,0:T(8,128)(2,1)S(1)} %get-tuple-element.48), channel_id=1, source_target_pairs={{0,16},{1,17},{2,18},{3,19},{4,20},{5,21},{6,22},{7,23},{8,24},{9,... | collective-permute-start | bytes 442376 | tf_op jit(solution)/shard_map/ppermute | solution.py:474
  100.6 17.2 %collective-permute-start.17 = (bf16[1,32,1152]{2,1,0:T(8,128)(2,1)S(1)}, bf16[1,32,1152]{2,1,0:T(8,128)(2,1)S(1)}, u32[]{:S(2)}, u32[]{:S(2)}) collective-permute-start(bf16[1,32,1152]{2,1,0:T(8,128)(2,1)S(1)} %get-tuple-element.47), channel_id=1, source_target_pairs={{0,16},{1,17},{2,18},{3,19},{4,20},{5,21},{6,22},{7,23},{8,24},{9,... | collective-permute-start | bytes 221192 | tf_op jit(solution)/shard_map/ppermute | solution.py:474

commit v6 on v5

--- a/solution.py
+++ b/solution.py
@@ -457,7 +457,7 @@
     straight = [2 * (me ^ bit) + side for bit in range(4) for side in (0, 1)]
     shared = [2 * (me ^ bit) + side for side in (low, 1 - low) for bit in (2, 3)]
     places = places_of(straight[:4] + shared), places_of(straight)
-    return second, first, places, jnp.reshape(me, (1,)).astype(jnp.int32)
+    return second, first, places, jnp.reshape(me, (1,)).astype(jnp.int32), got[0]
 
 
 def shards(shape, q_first, q_second, k_cache, v_cache, kept_blocks, kept_count):
@@ -465,8 +465,10 @@
     owned = q_first.shape[0] * head // ctx
     kept = (kept_blocks[0], kept_count)
     if head == 4 and ctx == 8 and owned % 48 == 0:
-        second, first, places, column = relayed(shape, q_first, q_second)
-        keys, values = settle(jnp.swapaxes(k_cache, 0, 1), jnp.swapaxes(v_cache, 0, 1))
+        second, first, places, column, arrived = relayed(shape, q_first, q_second)
+        keys = jnp.swapaxes(k_cache, 0, 1)
+        late, _ = lax.optimization_barrier((v_cache, arrived))
+        keys, values = settle(keys, jnp.swapaxes(late, 0, 1))
         spot = jnp.reshape(lax.axis_index("ctx") // 4, (1,)).astype(jnp.int32)
         cut = owned * 2 // 3
 
@@ -474,7 +476,7 @@
             return lax.ppermute(part, AXES, swapped(shape, bits, 0))
 
         def gathered(parts):
-            return [parts[0]] + [moved(parts[bits], bits) for bits in (3, 1, 2)]
+            return [parts[0]] + [moved(parts[bits], bits) for bits in (1, 2, 3)]
 
         def attend(pieces, span, after, kept=None):
             at = places[0 if kept else 1]

time: 119 us -> 106 us (0.89)
  local copies, waits for them, and re-layouts: 20.5 us -> 5.81 us
    unnamed x18 -> x6, local copies, waits for them, and re-layouts: 12.7 us -> 0.02 us
    ppermute x2, waiting for transfers between devices: 0.01 us -> 2.26 us  [relayed(): others.append(lax.ppermute(x, AXES, swapped(shape, 1, 0)))]
    transpose x1, local copies, waits for them, and re-layouts: 6.6 us -> 4.56 us  [shards(): keys, values = settle(keys, jnp.swapaxes(late, 0, 1))]
    ppermute x12, waiting for transfers between devices: 10.6 us -> 8.88 us  [moved(): return lax.ppermute(part, AXES, swapped(shape, bits, 0))]
  transfers between devices with their start and end apart: 20 -> 20, of which waited for: 3 -> 5; matrix products, arithmetic and copies ran while one was open for 7% -> 5% of each run, Pallas kernels for 37% -> 45%
where the time goes in v6:
time: 106 us
  Pallas kernels  48.1 us (45%)
  starting transfers between devices  32 us (30%)
  waiting for transfers between devices  17.5 us (17%)
  local copies, waits for them, and re-layouts  5.81 us (5%)
  between operations  1.7 us (2%)
    pallas_call x3, Pallas kernels, partial_call(): pl.pallas_call(functools.partial(kernel, pieces=len(pieces), outs=outs, g...  38.6 us
    ppermute x12, starting transfers between devices, moved(): return lax.ppermute(part, AXES, swapped(shape, bits, 0))  24.2 us
    ppermute x12, waiting for transfers between devices, moved(): return lax.ppermute(part, AXES, swapped(shape, bits, 0))  8.88 us
    ppermute x6, waiting for transfers between devices, sent(): return lax.ppermute(block, AXES, swapped(shape, 0, bit))  6.35 us
    ppermute x6, starting transfers between devices, sent(): return lax.ppermute(block, AXES, swapped(shape, 0, bit))  5.16 us
    transpose x1, local copies, waits for them, and re-layouts, shards(): keys, values = settle(keys, jnp.swapaxes(late, 0, 1))  4.56 us
    pallas_call x3, Pallas kernels, merge_quad(): pl.pallas_call(functools.partial(quad_kernel, sources=len(parts)), in_spe...  3.34 us
    pallas_call x1, Pallas kernels, pick(): pl.pallas_call(functools.partial(pick_kernel, boxes=boxes), in_specs=[pl....  3.23 us
  transfers between devices with their start and end apart: 20, of which 5 were waited for; matrix products, arithmetic and copies ran while one was open for 5% of the time, Pallas kernels for 45%

profile of v6, /device:TPU:0, one launch (start us, length us, event | category | flops | bytes accessed | tf_op | source)
XLA Modules:
  0.0 105.7 jit_solution(17179981207722163118)
XLA Ops:
  0.7 1.1 fusion
  1.7 3.0 %collective-permute-start.3 = (bf16[96,1024]{1,0:T(8,128)(2,1)S(1)}, bf16[96,1024]{1,0:T(8,128)(2,1)S(1)}, u32[]{:S(2)}, u32[]{:S(2)}) collective-permute-start(bf16[96,1024]{1,0:T(8,128)(2,1)S(1)} %get-tuple-element.53), channel_id=1, source_target_pairs={{0,2},{1,3},{2,0},{3,1},{4,6},{5,7},{6,4},{7,5},{8,10},{9,11},{10,... | collective-permute-start | bytes 589832 | tf_op jit(solution)/shard_map/ppermute | solution.py:436
  4.8 5.7 %collective-permute-done.3 = bf16[96,1024]{1,0:T(8,128)(2,1)S(1)} collective-permute-done((bf16[96,1024]{1,0:T(8,128)(2,1)S(1)}, bf16[96,1024]{1,0:T(8,128)(2,1)S(1)}, u32[]{:S(2)}, u32[]{:S(2)}) %collective-permute-start.3) | collective-permute-done | bytes 196640 | tf_op jit(solution)/shard_map/ppermute | solution.py:436
  10.5 2.0 %collective-permute-start.6 = (bf16[96,1024]{1,0:T(8,128)(2,1)S(1)}, bf16[96,1024]{1,0:T(8,128)(2,1)S(1)}, u32[]{:S(2)}, u32[]{:S(2)}) collective-permute-start(bf16[96,1024]{1,0:T(8,128)(2,1)S(1)} %collective-permute-done.3), channel_id=1, source_target_pairs={{0,4},{1,5},{2,6},{3,7},{4,0},{5,1},{6,2},{7,3},{8,12},{9,13},{10,... | collective-permute-start | bytes 589832 | tf_op jit(solution)/shard_map/ppermute | solution.py:449
  12.6 0.6 pad_add_fusion.spot_ref
  13.2 3.2 %shard_map.77 = (bf16[192,1024]{1,0:T(8,128)(2,1)}, bf16[192,1024]{1,0:T(8,128)(2,1)}, bf16[192,1024]{1,0:T(8,128)(2,1)}, bf16[192,1024]{1,0:T(8,128)(2,1)}) custom-call(s32[2]{0:T(128)} %pad_add_fusion.spot_ref, bf16[192,4096]{1,0:T(8,128)(2,1)} %refs_0_.1, bf16[192,4096]{1,0:T(8,128)(2,1)} %refs_1_.1), custom_call_target="tpu_custom_call" | custom-call | tf_op jit(solution)/shard_map/pallas_call | solution.py:403
  17.0 1.5 %collective-permute-start.1 = (bf16[192,1024]{1,0:T(8,128)(2,1)}, bf16[192,1024]{1,0:T(8,128)(2,1)S(1)}, u32[]{:S(2)}, u32[]{:S(2)}) collective-permute-start(bf16[192,1024]{1,0:T(8,128)(2,1)} %get-tuple-element.28), channel_id=1, source_target_pairs={{0,2},{1,3},{2,0},{3,1},{4,6},{5,7},{6,4},{7,5},{8,10},{9,11},{10,... | collective-permute-start | bytes 1179656 | tf_op jit(solution)/shard_map/ppermute | solution.py:436
  19.6 0.6 collective-permute-start.7
  20.2 4.6 %copy_bitcast_fusion = (bf16[4,4096,128]{2,1,0:T(8,128)(2,1)S(1)}, bf16[4,4096,128]{2,1,0:T(8,128)(2,1)S(1)}) fusion(bf16[4096,4,128]{2,1,0:T(4,128)(2,1)} %param.9, bf16[4096,4,128]{2,1,0:T(4,128)(2,1)} %param.8), kind=kLoop, calls=%fused_computation | loop fusion | bytes 16777216 | tf_op jit(solution)/shard_map/transpose | solution.py:471
  24.8 2.3 %collective-permute-done.7 = bf16[96,1024]{1,0:T(8,128)(2,1)S(1)} collective-permute-done((bf16[96,1024]{1,0:T(8,128)(2,1)S(1)}, bf16[96,1024]{1,0:T(8,128)(2,1)S(1)}, u32[]{:S(2)}, u32[]{:S(2)}) %collective-permute-start.7) | collective-permute-done | bytes 196640 | tf_op jit(solution)/shard_map/ppermute | solution.py:449
  27.1 4.6 %shard_map.79 = (bf16[2,96,1152]{2,1,0:T(8,128)(2,1)S(1)}, bf16[2,96,1152]{2,1,0:T(8,128)(2,1)S(1)}, bf16[2,96,1152]{2,1,0:T(8,128)(2,1)S(1)}, bf16[2,96,1152]{2,1,0:T(8,128)(2,1)S(1)}) custom-call(s32[8]{0:T(128)S(1)} %stack.68.place_ref, s32[1]{0:T(128)} %bitcast.9.column_ref, s32[8]{0:T(128)S(1)} %bitcast.46, s32[1]{0:T(128)S(6)} %copy.18.count_ref, ...), custom_call_target="tpu_custom_call" | custom-call | flops 3221225472 | bytes 1048576 | tf_op jit(solution)/shard_map/pallas_call | solution.py:253
  31.7 1.7 %collective-permute-start.10 = (bf16[2,96,1152]{2,1,0:T(8,128)(2,1)S(1)}, bf16[2,96,1152]{2,1,0:T(8,128)(2,1)S(1)}, u32[]{:S(2)}, u32[]{:S(2)}) collective-permute-start(bf16[2,96,1152]{2,1,0:T(8,128)(2,1)S(1)} %get-tuple-element.37), channel_id=1, source_target_pairs={{0,12},{1,13},{2,14},{3,15},{4,8},{5,9},{6,10},{7,11},{8,4},{9,5},... | collective-permute-start | bytes 1327112 | tf_op jit(solution)/shard_map/ppermute | solution.py:476
  33.4 1.4 %collective-permute-start.8 = (bf16[2,96,1152]{2,1,0:T(8,128)(2,1)S(1)}, bf16[2,96,1152]{2,1,0:T(8,128)(2,1)S(1)}, u32[]{:S(2)}, u32[]{:S(2)}) collective-permute-start(bf16[2,96,1152]{2,1,0:T(8,128)(2,1)S(1)} %get-tuple-element.35), channel_id=1, source_target_pairs={{0,4},{1,5},{2,6},{3,7},{4,0},{5,1},{6,2},{7,3},{8,12},{9,13},{10,... | collective-permute-start | bytes 1327112 | tf_op jit(solution)/shard_map/ppermute | solution.py:476
  35.2 0.6 collective-permute-done.2
  35.8 22.1 %shard_map.80 = (bf16[2,64,1152]{2,1,0:T(8,128)(2,1)S(1)}, bf16[2,64,1152]{2,1,0:T(8,128)(2,1)S(1)}, bf16[2,64,1152]{2,1,0:T(8,128)(2,1)S(1)}, bf16[2,64,1152]{2,1,0:T(8,128)(2,1)S(1)}) custom-call(s32[8]{0:T(128)S(1)} %stack.61.place_ref, s32[1]{0:T(128)} %bitcast.9.column_ref, bf16[2,96,4096]{2,1,0:T(8,128)(2,1)S(1)} %bitcast.33, ...), custom_call_target="tpu_custom_call" | custom-call | flops 17179869184 | bytes 8388608 | tf_op jit(solution)/shard_map/pallas_call | solution.py:253
  58.0 0.6 collective-permute-start.14
  58.6 1.6 %collective-permute-start.15 = (bf16[2,64,1152]{2,1,0:T(8,128)(2,1)S(1)}, bf16[2,64,1152]{2,1,0:T(8,128)(2,1)S(1)}, u32[]{:S(2)}, u32[]{:S(2)}) collective-permute-start(bf16[2,64,1152]{2,1,0:T(8,128)(2,1)S(1)} %get-tuple-element.45), channel_id=1, source_target_pairs={{0,8},{1,9},{2,10},{3,11},{4,12},{5,13},{6,14},{7,15},{8,0},{9,1},... | collective-permute-start | bytes 884744 | tf_op jit(solution)/shard_map/ppermute | solution.py:476
  60.2 1.4 %collective-permute-start.16 = (bf16[2,64,1152]{2,1,0:T(8,128)(2,1)S(1)}, bf16[2,64,1152]{2,1,0:T(8,128)(2,1)S(1)}, u32[]{:S(2)}, u32[]{:S(2)}) collective-permute-start(bf16[2,64,1152]{2,1,0:T(8,128)(2,1)S(1)} %get-tuple-element.46), channel_id=1, source_target_pairs={{0,12},{1,13},{2,14},{3,15},{4,8},{5,9},{6,10},{7,11},{8,4},{9,5},... | collective-permute-start | bytes 884744 | tf_op jit(solution)/shard_map/ppermute | solution.py:476
  61.6 1.6 %shard_map.81 = (bf16[1,96,1152]{2,1,0:T(8,128)(2,1)S(1)}, bf16[1,96,1152]{2,1,0:T(8,128)(2,1)S(1)}) custom-call(s32[1]{0:T(128)} %bitcast.refs_8_.spot_ref, bf16[2,96,1152]{2,1,0:T(8,128)(2,1)S(1)} %get-tuple-element.34.refs_6_.refs_0_, bf16[2,96,1152]{2,1,0:T(8,128)(2,1)S(1)} %collective-permute-done.8.refs_1_, ...), custom_call_target="tpu_custom_call" | custom-call | flops 3538944 | bytes 2211840 | tf_op jit(solution)/shard_map/pallas_call | solution.py:351
  63.1 11.8 %shard_map.82 = (bf16[2,32,1152]{2,1,0:T(8,128)(2,1)S(1)}, bf16[2,32,1152]{2,1,0:T(8,128)(2,1)S(1)}, bf16[2,32,1152]{2,1,0:T(8,128)(2,1)S(1)}, bf16[2,32,1152]{2,1,0:T(8,128)(2,1)S(1)}) custom-call(s32[8]{0:T(128)S(1)} %stack.61.place_ref, s32[1]{0:T(128)} %bitcast.9.column_ref, bf16[2,96,4096]{2,1,0:T(8,128)(2,1)S(1)} %bitcast.34, ...), custom_call_target="tpu_custom_call" | custom-call | flops 8589934592 | bytes 8388608 | tf_op jit(solution)/shard_map/pallas_call | solution.py:253
  75.0 0.6 collective-permute-start.11
  75.6 1.6 %collective-permute-start.12 = (bf16[2,32,1152]{2,1,0:T(8,128)(2,1)S(1)}, bf16[2,32,1152]{2,1,0:T(8,128)(2,1)S(1)}, u32[]{:S(2)}, u32[]{:S(2)}) collective-permute-start(bf16[2,32,1152]{2,1,0:T(8,128)(2,1)S(1)} %get-tuple-element.42), channel_id=1, source_target_pairs={{0,8},{1,9},{2,10},{3,11},{4,12},{5,13},{6,14},{7,15},{8,0},{9,1},... | collective-permute-start | bytes 442376 | tf_op jit(solution)/shard_map/ppermute | solution.py:476
  77.1 1.4 %collective-permute-start.13 = (bf16[2,32,1152]{2,1,0:T(8,128)(2,1)S(1)}, bf16[2,32,1152]{2,1,0:T(8,128)(2,1)S(1)}, u32[]{:S(2)}, u32[]{:S(2)}) collective-permute-start(bf16[2,32,1152]{2,1,0:T(8,128)(2,1)S(1)} %get-tuple-element.43), channel_id=1, source_target_pairs={{0,12},{1,13},{2,14},{3,15},{4,8},{5,9},{6,10},{7,11},{8,4},{9,5},... | collective-permute-start | bytes 442376 | tf_op jit(solution)/shard_map/ppermute | solution.py:476
  78.5 7.6 %collective-permute-start.19 = (bf16[1,96,1152]{2,1,0:T(8,128)(2,1)S(1)}, bf16[1,96,1152]{2,1,0:T(8,128)(2,1)S(1)}, u32[]{:S(2)}, u32[]{:S(2)}) collective-permute-start(bf16[1,96,1152]{2,1,0:T(8,128)(2,1)S(1)} %get-tuple-element.51), channel_id=1, source_target_pairs={{0,16},{1,17},{2,18},{3,19},{4,20},{5,21},{6,22},{7,23},{8,24},{9,... | collective-permute-start | bytes 663560 | tf_op jit(solution)/shard_map/ppermute | solution.py:476
  86.1 1.1 %shard_map.83 = (bf16[1,64,1152]{2,1,0:T(8,128)(2,1)S(1)}, bf16[1,64,1152]{2,1,0:T(8,128)(2,1)S(1)}) custom-call(s32[1]{0:T(128)} %bitcast.refs_8_.spot_ref, bf16[2,64,1152]{2,1,0:T(8,128)(2,1)S(1)} %get-tuple-element.38.refs_4_.refs_0_, bf16[2,64,1152]{2,1,0:T(8,128)(2,1)S(1)} %collective-permute-done.14.refs_1_, ...), custom_call_target="tpu_custom_call" | custom-call | flops 2359296 | bytes 1474560 | tf_op jit(solution)/shard_map/pallas_call | solution.py:351
  87.3 0.8 collective-permute-done.13.refs_3_
  88.1 0.7 shard_map.84
  88.8 5.9 %collective-permute-start.17 = (bf16[1,32,1152]{2,1,0:T(8,128)(2,1)S(1)}, bf16[1,32,1152]{2,1,0:T(8,128)(2,1)S(1)}, u32[]{:S(2)}, u32[]{:S(2)}) collective-permute-start(bf16[1,32,1152]{2,1,0:T(8,128)(2,1)S(1)} %get-tuple-element.49), channel_id=1, source_target_pairs={{0,16},{1,17},{2,18},{3,19},{4,20},{5,21},{6,22},{7,23},{8,24},{9,... | collective-permute-start | bytes 221192 | tf_op jit(solution)/shard_map/ppermute | solution.py:476
  94.7 8.0 %collective-permute-done.18.refs_1_ = bf16[1,64,1152]{2,1,0:T(8,128)(2,1)S(1)} collective-permute-done((bf16[1,64,1152]{2,1,0:T(8,128)(2,1)S(1)}, bf16[1,64,1152]{2,1,0:T(8,128)(2,1)S(1)}, u32[]{:S(2)}, u32[]{:S(2)}) %collective-permute-start.18) | collective-permute-done | bytes 147488 | tf_op jit(solution)/shard_map/ppermute | solution.py:476
  102.8 1.0 shard_map.85.refs_2_
  103.7 1.1 %shard_map.87 = bf16[1,96,1024]{2,1,0:T(8,128)(2,1)} custom-call(bf16[1,96,1152]{2,1,0:T(8,128)(2,1)S(1)} %get-tuple-element.39.refs_6_.refs_0_, bf16[1,96,1152]{2,1,0:T(8,128)(2,1)S(1)} %collective-permute-done.19.refs_1_), custom_call_target="tpu_custom_call" | custom-call | flops 786432 | bytes 442368 | tf_op jit(solution)/shard_map/pallas_call | solution.py:321
  104.8 0.9 shard_map.86
  (30 shorter events, 1.4 us)
Async XLA Ops:
  1.7 8.8 %collective-permute-start.3 = (bf16[96,1024]{1,0:T(8,128)(2,1)S(1)}, bf16[96,1024]{1,0:T(8,128)(2,1)S(1)}, u32[]{:S(2)}, u32[]{:S(2)}) collective-permute-start(bf16[96,1024]{1,0:T(8,128)(2,1)S(1)} %get-tuple-element.53), channel_id=1, source_target_pairs={{0,2},{1,3},{2,0},{3,1},{4,6},{5,7},{6,4},{7,5},{8,10},{9,11},{10,... | collective-permute-start | bytes 589832 | tf_op jit(solution)/shard_map/ppermute | solution.py:436
  4.8 14.8 %collective-permute-start.5 = (bf16[96,1024]{1,0:T(8,128)(2,1)S(1)}, bf16[96,1024]{1,0:T(8,128)(2,1)S(1)}, u32[]{:S(2)}, u32[]{:S(2)}) collective-permute-start(bf16[96,1024]{1,0:T(8,128)(2,1)S(1)} %get-tuple-element.52), channel_id=1, source_target_pairs={{0,3},{1,2},{2,1},{3,0},{4,7},{5,6},{6,5},{7,4},{8,11},{9,10},{10,... | collective-permute-start | bytes 589832 | tf_op jit(solution)/shard_map/ppermute | solution.py:436
  10.5 9.1 %collective-permute-start.6 = (bf16[96,1024]{1,0:T(8,128)(2,1)S(1)}, bf16[96,1024]{1,0:T(8,128)(2,1)S(1)}, u32[]{:S(2)}, u32[]{:S(2)}) collective-permute-start(bf16[96,1024]{1,0:T(8,128)(2,1)S(1)} %collective-permute-done.3), channel_id=1, source_target_pairs={{0,4},{1,5},{2,6},{3,7},{4,0},{5,1},{6,2},{7,3},{8,12},{9,13},{10,... | collective-permute-start | bytes 589832 | tf_op jit(solution)/shard_map/ppermute | solution.py:449
  16.4 10.7 %collective-permute-start.4 = (bf16[192,1024]{1,0:T(8,128)(2,1)}, bf16[192,1024]{1,0:T(8,128)(2,1)S(1)}, u32[]{:S(2)}, u32[]{:S(2)}) collective-permute-start(bf16[192,1024]{1,0:T(8,128)(2,1)} %get-tuple-element.33), channel_id=1, source_target_pairs={{0,1},{1,0},{2,3},{3,2},{4,5},{5,4},{6,7},{7,6},{8,9},{9,8},{10,11... | collective-permute-start | bytes 1179656 | tf_op jit(solution)/shard_map/ppermute | solution.py:436
  16.5 18.3 %collective-permute-start = (bf16[192,1024]{1,0:T(8,128)(2,1)}, bf16[192,1024]{1,0:T(8,128)(2,1)S(1)}, u32[]{:S(2)}, u32[]{:S(2)}) collective-permute-start(bf16[192,1024]{1,0:T(8,128)(2,1)} %get-tuple-element.27), channel_id=1, source_target_pairs={{0,1},{1,0},{2,3},{3,2},{4,5},{5,4},{6,7},{7,6},{8,9},{9,8},{10,11... | collective-permute-start | bytes 1179656 | tf_op jit(solution)/shard_map/ppermute | solution.py:436
  17.0 18.3 %collective-permute-start.1 = (bf16[192,1024]{1,0:T(8,128)(2,1)}, bf16[192,1024]{1,0:T(8,128)(2,1)S(1)}, u32[]{:S(2)}, u32[]{:S(2)}) collective-permute-start(bf16[192,1024]{1,0:T(8,128)(2,1)} %get-tuple-element.28), channel_id=1, source_target_pairs={{0,2},{1,3},{2,0},{3,1},{4,6},{5,7},{6,4},{7,5},{8,10},{9,11},{10,... | collective-permute-start | bytes 1179656 | tf_op jit(solution)/shard_map/ppermute | solution.py:436
  19.5 16.3 %collective-permute-start.2 = (bf16[192,1024]{1,0:T(8,128)(2,1)}, bf16[192,1024]{1,0:T(8,128)(2,1)S(1)}, u32[]{:S(2)}, u32[]{:S(2)}) collective-permute-start(bf16[192,1024]{1,0:T(8,128)(2,1)} %get-tuple-element.29), channel_id=1, source_target_pairs={{0,3},{1,2},{2,1},{3,0},{4,7},{5,6},{6,5},{7,4},{8,11},{9,10},{10,... | collective-permute-start | bytes 1179656 | tf_op jit(solution)/shard_map/ppermute | solution.py:436
  19.6 7.4 %collective-permute-start.7 = (bf16[96,1024]{1,0:T(8,128)(2,1)S(1)}, bf16[96,1024]{1,0:T(8,128)(2,1)S(1)}, u32[]{:S(2)}, u32[]{:S(2)}) collective-permute-start(bf16[96,1024]{1,0:T(8,128)(2,1)S(1)} %collective-permute-done.5), channel_id=1, source_target_pairs={{0,4},{1,5},{2,6},{3,7},{4,0},{5,1},{6,2},{7,3},{8,12},{9,13},{10,... | collective-permute-start | bytes 589832 | tf_op jit(solution)/shard_map/ppermute | solution.py:449
  24.8 2.3 %copy-start = (bf16[192,4096]{1,0:T(8,128)(2,1)S(1)}, bf16[192,4096]{1,0:T(8,128)(2,1)}, u32[]{:S(2)}) copy-start(bf16[192,4096]{1,0:T(8,128)(2,1)} %refs_0_.1) | copy-start | bytes 4718596
  24.8 2.3 %copy-start.2 = (s32[1,8]{1,0:T(1,128)S(1)}, s32[1,8]{1,0:T(1,128)}, u32[]{:S(2)}) copy-start(s32[1,8]{1,0:T(1,128)} %param.10) | copy-start | bytes 100
  27.1 8.8 %copy-start.1 = (bf16[192,4096]{1,0:T(8,128)(2,1)S(1)}, bf16[192,4096]{1,0:T(8,128)(2,1)}, u32[]{:S(2)}) copy-start(bf16[192,4096]{1,0:T(8,128)(2,1)} %refs_1_.1) | copy-start | bytes 4718596
  31.7 28.5 %collective-permute-start.10 = (bf16[2,96,1152]{2,1,0:T(8,128)(2,1)S(1)}, bf16[2,96,1152]{2,1,0:T(8,128)(2,1)S(1)}, u32[]{:S(2)}, u32[]{:S(2)}) collective-permute-start(bf16[2,96,1152]{2,1,0:T(8,128)(2,1)S(1)} %get-tuple-element.37), channel_id=1, source_target_pairs={{0,12},{1,13},{2,14},{3,15},{4,8},{5,9},{6,10},{7,11},{8,4},{9,5},... | collective-permute-start | bytes 1327112 | tf_op jit(solution)/shard_map/ppermute | solution.py:476
  33.4 28.2 %collective-permute-start.8 = (bf16[2,96,1152]{2,1,0:T(8,128)(2,1)S(1)}, bf16[2,96,1152]{2,1,0:T(8,128)(2,1)S(1)}, u32[]{:S(2)}, u32[]{:S(2)}) collective-permute-start(bf16[2,96,1152]{2,1,0:T(8,128)(2,1)S(1)} %get-tuple-element.35), channel_id=1, source_target_pairs={{0,4},{1,5},{2,6},{3,7},{4,0},{5,1},{6,2},{7,3},{8,12},{9,13},{10,... | collective-permute-start | bytes 1327112 | tf_op jit(solution)/shard_map/ppermute | solution.py:476
  34.8 26.8 %collective-permute-start.9 = (bf16[2,96,1152]{2,1,0:T(8,128)(2,1)S(1)}, bf16[2,96,1152]{2,1,0:T(8,128)(2,1)S(1)}, u32[]{:S(2)}, u32[]{:S(2)}) collective-permute-start(bf16[2,96,1152]{2,1,0:T(8,128)(2,1)S(1)} %get-tuple-element.36), channel_id=1, source_target_pairs={{0,8},{1,9},{2,10},{3,11},{4,12},{5,13},{6,14},{7,15},{8,0},{9,1},... | collective-permute-start | bytes 1327112 | tf_op jit(solution)/shard_map/ppermute | solution.py:476
  58.0 19.1 %collective-permute-start.14 = (bf16[2,64,1152]{2,1,0:T(8,128)(2,1)S(1)}, bf16[2,64,1152]{2,1,0:T(8,128)(2,1)S(1)}, u32[]{:S(2)}, u32[]{:S(2)}) collective-permute-start(bf16[2,64,1152]{2,1,0:T(8,128)(2,1)S(1)} %get-tuple-element.44), channel_id=1, source_target_pairs={{0,4},{1,5},{2,6},{3,7},{4,0},{5,1},{6,2},{7,3},{8,12},{9,13},{10,... | collective-permute-start | bytes 884744 | tf_op jit(solution)/shard_map/ppermute | solution.py:476
  58.6 20.0 %collective-permute-start.15 = (bf16[2,64,1152]{2,1,0:T(8,128)(2,1)S(1)}, bf16[2,64,1152]{2,1,0:T(8,128)(2,1)S(1)}, u32[]{:S(2)}, u32[]{:S(2)}) collective-permute-start(bf16[2,64,1152]{2,1,0:T(8,128)(2,1)S(1)} %get-tuple-element.45), channel_id=1, source_target_pairs={{0,8},{1,9},{2,10},{3,11},{4,12},{5,13},{6,14},{7,15},{8,0},{9,1},... | collective-permute-start | bytes 884744 | tf_op jit(solution)/shard_map/ppermute | solution.py:476
  60.2 26.0 %collective-permute-start.16 = (bf16[2,64,1152]{2,1,0:T(8,128)(2,1)S(1)}, bf16[2,64,1152]{2,1,0:T(8,128)(2,1)S(1)}, u32[]{:S(2)}, u32[]{:S(2)}) collective-permute-start(bf16[2,64,1152]{2,1,0:T(8,128)(2,1)S(1)} %get-tuple-element.46), channel_id=1, source_target_pairs={{0,12},{1,13},{2,14},{3,15},{4,8},{5,9},{6,10},{7,11},{8,4},{9,5},... | collective-permute-start | bytes 884744 | tf_op jit(solution)/shard_map/ppermute | solution.py:476
  75.0 12.4 %collective-permute-start.11 = (bf16[2,32,1152]{2,1,0:T(8,128)(2,1)S(1)}, bf16[2,32,1152]{2,1,0:T(8,128)(2,1)S(1)}, u32[]{:S(2)}, u32[]{:S(2)}) collective-permute-start(bf16[2,32,1152]{2,1,0:T(8,128)(2,1)S(1)} %get-tuple-element.41), channel_id=1, source_target_pairs={{0,4},{1,5},{2,6},{3,7},{4,0},{5,1},{6,2},{7,3},{8,12},{9,13},{10,... | collective-permute-start | bytes 442376 | tf_op jit(solution)/shard_map/ppermute | solution.py:476
  75.6 11.8 %collective-permute-start.12 = (bf16[2,32,1152]{2,1,0:T(8,128)(2,1)S(1)}, bf16[2,32,1152]{2,1,0:T(8,128)(2,1)S(1)}, u32[]{:S(2)}, u32[]{:S(2)}) collective-permute-start(bf16[2,32,1152]{2,1,0:T(8,128)(2,1)S(1)} %get-tuple-element.42), channel_id=1, source_target_pairs={{0,8},{1,9},{2,10},{3,11},{4,12},{5,13},{6,14},{7,15},{8,0},{9,1},... | collective-permute-start | bytes 442376 | tf_op jit(solution)/shard_map/ppermute | solution.py:476
  77.1 11.0 %collective-permute-start.13 = (bf16[2,32,1152]{2,1,0:T(8,128)(2,1)S(1)}, bf16[2,32,1152]{2,1,0:T(8,128)(2,1)S(1)}, u32[]{:S(2)}, u32[]{:S(2)}) collective-permute-start(bf16[2,32,1152]{2,1,0:T(8,128)(2,1)S(1)} %get-tuple-element.43), channel_id=1, source_target_pairs={{0,12},{1,13},{2,14},{3,15},{4,8},{5,9},{6,10},{7,11},{8,4},{9,5},... | collective-permute-start | bytes 442376 | tf_op jit(solution)/shard_map/ppermute | solution.py:476
  78.5 25.2 %collective-permute-start.19 = (bf16[1,96,1152]{2,1,0:T(8,128)(2,1)S(1)}, bf16[1,96,1152]{2,1,0:T(8,128)(2,1)S(1)}, u32[]{:S(2)}, u32[]{:S(2)}) collective-permute-start(bf16[1,96,1152]{2,1,0:T(8,128)(2,1)S(1)} %get-tuple-element.51), channel_id=1, source_target_pairs={{0,16},{1,17},{2,18},{3,19},{4,20},{5,21},{6,22},{7,23},{8,24},{9,... | collective-permute-start | bytes 663560 | tf_op jit(solution)/shard_map/ppermute | solution.py:476
  87.2 15.5 %collective-permute-start.18 = (bf16[1,64,1152]{2,1,0:T(8,128)(2,1)S(1)}, bf16[1,64,1152]{2,1,0:T(8,128)(2,1)S(1)}, u32[]{:S(2)}, u32[]{:S(2)}) collective-permute-start(bf16[1,64,1152]{2,1,0:T(8,128)(2,1)S(1)} %get-tuple-element.50), channel_id=1, source_target_pairs={{0,16},{1,17},{2,18},{3,19},{4,20},{5,21},{6,22},{7,23},{8,24},{9,... | collective-permute-start | bytes 442376 | tf_op jit(solution)/shard_map/ppermute | solution.py:476
  88.8 16.0 %collective-permute-start.17 = (bf16[1,32,1152]{2,1,0:T(8,128)(2,1)S(1)}, bf16[1,32,1152]{2,1,0:T(8,128)(2,1)S(1)}, u32[]{:S(2)}, u32[]{:S(2)}) collective-permute-start(bf16[1,32,1152]{2,1,0:T(8,128)(2,1)S(1)} %get-tuple-element.49), channel_id=1, source_target_pairs={{0,16},{1,17},{2,18},{3,19},{4,20},{5,21},{6,22},{7,23},{8,24},{9,... | collective-permute-start | bytes 221192 | tf_op jit(solution)/shard_map/ppermute | solution.py:476

commit v7 on v6

--- a/solution.py
+++ b/solution.py
@@ -89,25 +89,27 @@
 
 
 def write_partial(held_ref, stat_ref, place_ref, chains, group_size, group, rows):
-    values, levels = [], []
+    values, tops, totals = [], [], []
     for top, summed in chains:
         total = summed[:, HD:]
         values.append((summed[:, :HD] / total).astype(jnp.bfloat16))
-        levels.append(top + jnp.log2(total))
-    value = jnp.concatenate(values, axis=0)
-    level = jnp.concatenate(levels, axis=0)
+        tops.append(jnp.broadcast_to(top, total.shape))
+        totals.append(total)
+    value, top, total = (jnp.concatenate(x, axis=0) for x in (values, tops, totals))
     count = held_ref.shape[0]
     lane = lax.broadcasted_iota(jnp.int32, (rows, LANES), 1)
     for item in range(count):
         place = place_ref[item]
-        stat = stat_ref[place]
+        kept_top, kept_total = stat_ref[0, place], stat_ref[1, place]
         for head in range(group_size):
             column = group * group_size + head
             at = (head * count + item) * rows
             start = pl.multiple_of(column * HD, HD)
             held_ref[place, :, pl.ds(start, HD)] = value[at : at + rows]
-            stat = jnp.where(lane == column, level[at : at + rows], stat)
-        stat_ref[place] = stat
+            kept_top = jnp.where(lane == column, top[at : at + rows], kept_top)
+            kept_total = jnp.where(lane == column, total[at : at + rows], kept_total)
+        stat_ref[0, place] = kept_top
+        stat_ref[1, place] = kept_total
 
 
 def hand_out(out_refs, held_ref, stat_ref):
@@ -117,8 +119,9 @@
     for index, out_ref in enumerate(out_refs):
         for item in range(share):
             at = index * share + item
+            level = stat_ref[0, at] + jnp.log2(stat_ref[1, at])
             out_ref[item, :, : heads * HD] = held_ref[at, :, : heads * HD]
-            out_ref[item, :, heads * HD :] = term_lanes(stat_ref[at], heads)
+            out_ref[item, :, heads * HD :] = term_lanes(level, heads)
 
 
 def dense_kernel(place_ref, column_ref, *refs, pieces, outs, group_size, span, block_keys):
@@ -132,7 +135,8 @@
 
     @pl.when(group == 0)
     def _():
-        stat_ref[...] = jnp.zeros_like(stat_ref)
+        stat_ref[0] = jnp.zeros_like(stat_ref[0])
+        stat_ref[1] = jnp.ones_like(stat_ref[1])
 
     queries = stacked_queries(query_refs, column_ref, heads, group_size, group, span)
     steps = []
@@ -165,7 +169,8 @@
 
     @pl.when(group == 0)
     def _():
-        stat_ref[...] = jnp.zeros_like(stat_ref)
+        stat_ref[0] = jnp.zeros_like(stat_ref[0])
+        stat_ref[1] = jnp.ones_like(stat_ref[1])
 
     def block_of(ref, slot):
         block = list_ref[jnp.minimum(slot, kept - 1)]
@@ -240,7 +245,7 @@
     vmem = pl.BlockSpec(memory_space=pltpu.VMEM)
     scratch = [
         pltpu.VMEM((count, rows, width), jnp.bfloat16),
-        pltpu.VMEM((count, rows, LANES), jnp.float32),
+        pltpu.VMEM((2, count, rows, LANES), jnp.float32),
     ]
     if kept is None:
         kernel = functools.partial(dense_kernel, block_keys=math.gcd(length, 512))
@@ -476,7 +481,8 @@
             return lax.ppermute(part, AXES, swapped(shape, bits, 0))
 
         def gathered(parts):
-            return [parts[0]] + [moved(parts[bits], bits) for bits in (1, 2, 3)]
+            got = {bits: moved(parts[bits], bits) for bits in (1, 2, 3)}
+            return [parts[0], got[1], got[2], got[3]]
 
         def attend(pieces, span, after, kept=None):
             at = places[0 if kept else 1]

time: 106 us -> 106 us (level)
  no operation moved by 1% of the time
where the time goes in v7:
time: 106 us
  Pallas kernels  48.3 us (46%)
  starting transfers between devices  32.6 us (31%)
  waiting for transfers between devices  17 us (16%)
  local copies, waits for them, and re-layouts  5.81 us (5%)
  between operations  1.7 us (2%)
    pallas_call x3, Pallas kernels, partial_call(): pl.pallas_call(functools.partial(kernel, pieces=len(pieces), outs=outs, g...  38.8 us
    ppermute x12, starting transfers between devices, moved(): return lax.ppermute(part, AXES, swapped(shape, bits, 0))  24.8 us
    ppermute x12, waiting for transfers between devices, moved(): return lax.ppermute(part, AXES, swapped(shape, bits, 0))  8.46 us
    ppermute x6, waiting for transfers between devices, sent(): return lax.ppermute(block, AXES, swapped(shape, 0, bit))  6.31 us
    ppermute x6, starting transfers between devices, sent(): return lax.ppermute(block, AXES, swapped(shape, 0, bit))  5.16 us
    transpose x1, local copies, waits for them, and re-layouts, shards(): keys, values = settle(keys, jnp.swapaxes(late, 0, 1))  4.56 us
    pallas_call x3, Pallas kernels, merge_quad(): pl.pallas_call(functools.partial(quad_kernel, sources=len(parts)), in_spe...  3.34 us
    pallas_call x1, Pallas kernels, pick(): pl.pallas_call(functools.partial(pick_kernel, boxes=boxes), in_specs=[pl....  3.23 us
  transfers between devices with their start and end apart: 20, of which 5 were waited for; matrix products, arithmetic and copies ran while one was open for 5% of the time, Pallas kernels for 45%

profile of v7, /device:TPU:0, one launch (start us, length us, event | category | flops | bytes accessed | tf_op | source)
XLA Modules:
  0.0 106.1 jit_solution(5298452735900590362)
XLA Ops:
  0.7 1.1 fusion
  1.7 3.0 %collective-permute-start.3 = (bf16[96,1024]{1,0:T(8,128)(2,1)S(1)}, bf16[96,1024]{1,0:T(8,128)(2,1)S(1)}, u32[]{:S(2)}, u32[]{:S(2)}) collective-permute-start(bf16[96,1024]{1,0:T(8,128)(2,1)S(1)} %get-tuple-element.53), channel_id=1, source_target_pairs={{0,2},{1,3},{2,0},{3,1},{4,6},{5,7},{6,4},{7,5},{8,10},{9,11},{10,... | collective-permute-start | bytes 589832 | tf_op jit(solution)/shard_map/ppermute | solution.py:441
  4.8 5.7 %collective-permute-done.3 = bf16[96,1024]{1,0:T(8,128)(2,1)S(1)} collective-permute-done((bf16[96,1024]{1,0:T(8,128)(2,1)S(1)}, bf16[96,1024]{1,0:T(8,128)(2,1)S(1)}, u32[]{:S(2)}, u32[]{:S(2)}) %collective-permute-start.3) | collective-permute-done | bytes 196640 | tf_op jit(solution)/shard_map/ppermute | solution.py:441
  10.5 2.0 %collective-permute-start.6 = (bf16[96,1024]{1,0:T(8,128)(2,1)S(1)}, bf16[96,1024]{1,0:T(8,128)(2,1)S(1)}, u32[]{:S(2)}, u32[]{:S(2)}) collective-permute-start(bf16[96,1024]{1,0:T(8,128)(2,1)S(1)} %collective-permute-done.3), channel_id=1, source_target_pairs={{0,4},{1,5},{2,6},{3,7},{4,0},{5,1},{6,2},{7,3},{8,12},{9,13},{10,... | collective-permute-start | bytes 589832 | tf_op jit(solution)/shard_map/ppermute | solution.py:454
  12.6 0.6 pad_add_fusion.spot_ref
  13.2 3.2 %shard_map.77 = (bf16[192,1024]{1,0:T(8,128)(2,1)}, bf16[192,1024]{1,0:T(8,128)(2,1)}, bf16[192,1024]{1,0:T(8,128)(2,1)}, bf16[192,1024]{1,0:T(8,128)(2,1)}) custom-call(s32[2]{0:T(128)} %pad_add_fusion.spot_ref, bf16[192,4096]{1,0:T(8,128)(2,1)} %refs_0_.1, bf16[192,4096]{1,0:T(8,128)(2,1)} %refs_1_.1), custom_call_target="tpu_custom_call" | custom-call | tf_op jit(solution)/shard_map/pallas_call | solution.py:408
  16.5 0.5 collective-permute-start
  17.0 1.5 %collective-permute-start.1 = (bf16[192,1024]{1,0:T(8,128)(2,1)}, bf16[192,1024]{1,0:T(8,128)(2,1)S(1)}, u32[]{:S(2)}, u32[]{:S(2)}) collective-permute-start(bf16[192,1024]{1,0:T(8,128)(2,1)} %get-tuple-element.28), channel_id=1, source_target_pairs={{0,2},{1,3},{2,0},{3,1},{4,6},{5,7},{6,4},{7,5},{8,10},{9,11},{10,... | collective-permute-start | bytes 1179656 | tf_op jit(solution)/shard_map/ppermute | solution.py:441
  19.6 0.6 collective-permute-start.7
  20.2 4.6 %copy_bitcast_fusion = (bf16[4,4096,128]{2,1,0:T(8,128)(2,1)S(1)}, bf16[4,4096,128]{2,1,0:T(8,128)(2,1)S(1)}) fusion(bf16[4096,4,128]{2,1,0:T(4,128)(2,1)} %param.9, bf16[4096,4,128]{2,1,0:T(4,128)(2,1)} %param.8), kind=kLoop, calls=%fused_computation | loop fusion | bytes 16777216 | tf_op jit(solution)/shard_map/transpose | solution.py:476
  24.8 2.3 %collective-permute-done.7 = bf16[96,1024]{1,0:T(8,128)(2,1)S(1)} collective-permute-done((bf16[96,1024]{1,0:T(8,128)(2,1)S(1)}, bf16[96,1024]{1,0:T(8,128)(2,1)S(1)}, u32[]{:S(2)}, u32[]{:S(2)}) %collective-permute-start.7) | collective-permute-done | bytes 196640 | tf_op jit(solution)/shard_map/ppermute | solution.py:454
  27.1 4.6 %shard_map.79 = (bf16[2,96,1152]{2,1,0:T(8,128)(2,1)S(1)}, bf16[2,96,1152]{2,1,0:T(8,128)(2,1)S(1)}, bf16[2,96,1152]{2,1,0:T(8,128)(2,1)S(1)}, bf16[2,96,1152]{2,1,0:T(8,128)(2,1)S(1)}) custom-call(s32[8]{0:T(128)S(1)} %stack.68.place_ref, s32[1]{0:T(128)} %bitcast.9.column_ref, s32[8]{0:T(128)S(1)} %bitcast.46, s32[1]{0:T(128)S(6)} %copy.18.count_ref, ...), custom_call_target="tpu_custom_call" | custom-call | flops 3221225472 | bytes 1048576 | tf_op jit(solution)/shard_map/pallas_call | solution.py:258
  31.7 1.7 %collective-permute-start.10 = (bf16[2,96,1152]{2,1,0:T(8,128)(2,1)S(1)}, bf16[2,96,1152]{2,1,0:T(8,128)(2,1)S(1)}, u32[]{:S(2)}, u32[]{:S(2)}) collective-permute-start(bf16[2,96,1152]{2,1,0:T(8,128)(2,1)S(1)} %get-tuple-element.37), channel_id=1, source_target_pairs={{0,12},{1,13},{2,14},{3,15},{4,8},{5,9},{6,10},{7,11},{8,4},{9,5},... | collective-permute-start | bytes 1327112 | tf_op jit(solution)/shard_map/ppermute | solution.py:481
  33.4 1.4 %collective-permute-start.8 = (bf16[2,96,1152]{2,1,0:T(8,128)(2,1)S(1)}, bf16[2,96,1152]{2,1,0:T(8,128)(2,1)S(1)}, u32[]{:S(2)}, u32[]{:S(2)}) collective-permute-start(bf16[2,96,1152]{2,1,0:T(8,128)(2,1)S(1)} %get-tuple-element.35), channel_id=1, source_target_pairs={{0,4},{1,5},{2,6},{3,7},{4,0},{5,1},{6,2},{7,3},{8,12},{9,13},{10,... | collective-permute-start | bytes 1327112 | tf_op jit(solution)/shard_map/ppermute | solution.py:481
  35.3 0.6 collective-permute-done.2
  35.8 22.3 %shard_map.80 = (bf16[2,64,1152]{2,1,0:T(8,128)(2,1)S(1)}, bf16[2,64,1152]{2,1,0:T(8,128)(2,1)S(1)}, bf16[2,64,1152]{2,1,0:T(8,128)(2,1)S(1)}, bf16[2,64,1152]{2,1,0:T(8,128)(2,1)S(1)}) custom-call(s32[8]{0:T(128)S(1)} %stack.61.place_ref, s32[1]{0:T(128)} %bitcast.9.column_ref, bf16[2,96,4096]{2,1,0:T(8,128)(2,1)S(1)} %bitcast.33, ...), custom_call_target="tpu_custom_call" | custom-call | flops 17179869184 | bytes 8388608 | tf_op jit(solution)/shard_map/pallas_call | solution.py:258
  58.1 0.6 collective-permute-start.14
  58.7 1.6 %collective-permute-start.15 = (bf16[2,64,1152]{2,1,0:T(8,128)(2,1)S(1)}, bf16[2,64,1152]{2,1,0:T(8,128)(2,1)S(1)}, u32[]{:S(2)}, u32[]{:S(2)}) collective-permute-start(bf16[2,64,1152]{2,1,0:T(8,128)(2,1)S(1)} %get-tuple-element.45), channel_id=1, source_target_pairs={{0,8},{1,9},{2,10},{3,11},{4,12},{5,13},{6,14},{7,15},{8,0},{9,1},... | collective-permute-start | bytes 884744 | tf_op jit(solution)/shard_map/ppermute | solution.py:481
  60.2 1.4 %collective-permute-start.16 = (bf16[2,64,1152]{2,1,0:T(8,128)(2,1)S(1)}, bf16[2,64,1152]{2,1,0:T(8,128)(2,1)S(1)}, u32[]{:S(2)}, u32[]{:S(2)}) collective-permute-start(bf16[2,64,1152]{2,1,0:T(8,128)(2,1)S(1)} %get-tuple-element.46), channel_id=1, source_target_pairs={{0,12},{1,13},{2,14},{3,15},{4,8},{5,9},{6,10},{7,11},{8,4},{9,5},... | collective-permute-start | bytes 884744 | tf_op jit(solution)/shard_map/ppermute | solution.py:481
  61.7 1.6 %shard_map.81 = (bf16[1,96,1152]{2,1,0:T(8,128)(2,1)S(1)}, bf16[1,96,1152]{2,1,0:T(8,128)(2,1)S(1)}) custom-call(s32[1]{0:T(128)} %bitcast.refs_8_.spot_ref, bf16[2,96,1152]{2,1,0:T(8,128)(2,1)S(1)} %get-tuple-element.34.refs_6_.refs_0_, bf16[2,96,1152]{2,1,0:T(8,128)(2,1)S(1)} %collective-permute-done.8.refs_1_, ...), custom_call_target="tpu_custom_call" | custom-call | flops 3538944 | bytes 2211840 | tf_op jit(solution)/shard_map/pallas_call | solution.py:356
  63.2 11.9 %shard_map.82 = (bf16[2,32,1152]{2,1,0:T(8,128)(2,1)S(1)}, bf16[2,32,1152]{2,1,0:T(8,128)(2,1)S(1)}, bf16[2,32,1152]{2,1,0:T(8,128)(2,1)S(1)}, bf16[2,32,1152]{2,1,0:T(8,128)(2,1)S(1)}) custom-call(s32[8]{0:T(128)S(1)} %stack.61.place_ref, s32[1]{0:T(128)} %bitcast.9.column_ref, bf16[2,96,4096]{2,1,0:T(8,128)(2,1)S(1)} %bitcast.34, ...), custom_call_target="tpu_custom_call" | custom-call | flops 8589934592 | bytes 8388608 | tf_op jit(solution)/shard_map/pallas_call | solution.py:258
  75.1 0.6 collective-permute-start.11
  75.7 1.6 %collective-permute-start.12 = (bf16[2,32,1152]{2,1,0:T(8,128)(2,1)S(1)}, bf16[2,32,1152]{2,1,0:T(8,128)(2,1)S(1)}, u32[]{:S(2)}, u32[]{:S(2)}) collective-permute-start(bf16[2,32,1152]{2,1,0:T(8,128)(2,1)S(1)} %get-tuple-element.42), channel_id=1, source_target_pairs={{0,8},{1,9},{2,10},{3,11},{4,12},{5,13},{6,14},{7,15},{8,0},{9,1},... | collective-permute-start | bytes 442376 | tf_op jit(solution)/shard_map/ppermute | solution.py:481
  77.3 1.4 %collective-permute-start.13 = (bf16[2,32,1152]{2,1,0:T(8,128)(2,1)S(1)}, bf16[2,32,1152]{2,1,0:T(8,128)(2,1)S(1)}, u32[]{:S(2)}, u32[]{:S(2)}) collective-permute-start(bf16[2,32,1152]{2,1,0:T(8,128)(2,1)S(1)} %get-tuple-element.43), channel_id=1, source_target_pairs={{0,12},{1,13},{2,14},{3,15},{4,8},{5,9},{6,10},{7,11},{8,4},{9,5},... | collective-permute-start | bytes 442376 | tf_op jit(solution)/shard_map/ppermute | solution.py:481
  78.7 7.8 %collective-permute-start.19 = (bf16[1,96,1152]{2,1,0:T(8,128)(2,1)S(1)}, bf16[1,96,1152]{2,1,0:T(8,128)(2,1)S(1)}, u32[]{:S(2)}, u32[]{:S(2)}) collective-permute-start(bf16[1,96,1152]{2,1,0:T(8,128)(2,1)S(1)} %get-tuple-element.51), channel_id=1, source_target_pairs={{0,16},{1,17},{2,18},{3,19},{4,20},{5,21},{6,22},{7,23},{8,24},{9,... | collective-permute-start | bytes 663560 | tf_op jit(solution)/shard_map/ppermute | solution.py:481
  86.5 1.1 %shard_map.83 = (bf16[1,64,1152]{2,1,0:T(8,128)(2,1)S(1)}, bf16[1,64,1152]{2,1,0:T(8,128)(2,1)S(1)}) custom-call(s32[1]{0:T(128)} %bitcast.refs_8_.spot_ref, bf16[2,64,1152]{2,1,0:T(8,128)(2,1)S(1)} %get-tuple-element.38.refs_4_.refs_0_, bf16[2,64,1152]{2,1,0:T(8,128)(2,1)S(1)} %collective-permute-done.14.refs_1_, ...), custom_call_target="tpu_custom_call" | custom-call | flops 2359296 | bytes 1474560 | tf_op jit(solution)/shard_map/pallas_call | solution.py:356
  88.1 0.7 shard_map.84
  88.8 6.3 %collective-permute-start.17 = (bf16[1,32,1152]{2,1,0:T(8,128)(2,1)S(1)}, bf16[1,32,1152]{2,1,0:T(8,128)(2,1)S(1)}, u32[]{:S(2)}, u32[]{:S(2)}) collective-permute-start(bf16[1,32,1152]{2,1,0:T(8,128)(2,1)S(1)} %get-tuple-element.49), channel_id=1, source_target_pairs={{0,16},{1,17},{2,18},{3,19},{4,20},{5,21},{6,22},{7,23},{8,24},{9,... | collective-permute-start | bytes 221192 | tf_op jit(solution)/shard_map/ppermute | solution.py:481
  95.1 8.0 %collective-permute-done.18.refs_1_ = bf16[1,64,1152]{2,1,0:T(8,128)(2,1)S(1)} collective-permute-done((bf16[1,64,1152]{2,1,0:T(8,128)(2,1)S(1)}, bf16[1,64,1152]{2,1,0:T(8,128)(2,1)S(1)}, u32[]{:S(2)}, u32[]{:S(2)}) %collective-permute-start.18) | collective-permute-done | bytes 147488 | tf_op jit(solution)/shard_map/ppermute | solution.py:481
  103.1 1.0 shard_map.85.refs_2_
  104.1 1.1 %shard_map.87 = bf16[1,96,1024]{2,1,0:T(8,128)(2,1)} custom-call(bf16[1,96,1152]{2,1,0:T(8,128)(2,1)S(1)} %get-tuple-element.39.refs_6_.refs_0_, bf16[1,96,1152]{2,1,0:T(8,128)(2,1)S(1)} %collective-permute-done.19.refs_1_), custom_call_target="tpu_custom_call" | custom-call | flops 786432 | bytes 442368 | tf_op jit(solution)/shard_map/pallas_call | solution.py:326
  105.2 0.9 shard_map.86
  (30 shorter events, 1.3 us)
Async XLA Ops:
  1.7 8.8 %collective-permute-start.3 = (bf16[96,1024]{1,0:T(8,128)(2,1)S(1)}, bf16[96,1024]{1,0:T(8,128)(2,1)S(1)}, u32[]{:S(2)}, u32[]{:S(2)}) collective-permute-start(bf16[96,1024]{1,0:T(8,128)(2,1)S(1)} %get-tuple-element.53), channel_id=1, source_target_pairs={{0,2},{1,3},{2,0},{3,1},{4,6},{5,7},{6,4},{7,5},{8,10},{9,11},{10,... | collective-permute-start | bytes 589832 | tf_op jit(solution)/shard_map/ppermute | solution.py:441
  4.8 14.8 %collective-permute-start.5 = (bf16[96,1024]{1,0:T(8,128)(2,1)S(1)}, bf16[96,1024]{1,0:T(8,128)(2,1)S(1)}, u32[]{:S(2)}, u32[]{:S(2)}) collective-permute-start(bf16[96,1024]{1,0:T(8,128)(2,1)S(1)} %get-tuple-element.52), channel_id=1, source_target_pairs={{0,3},{1,2},{2,1},{3,0},{4,7},{5,6},{6,5},{7,4},{8,11},{9,10},{10,... | collective-permute-start | bytes 589832 | tf_op jit(solution)/shard_map/ppermute | solution.py:441
  10.5 9.1 %collective-permute-start.6 = (bf16[96,1024]{1,0:T(8,128)(2,1)S(1)}, bf16[96,1024]{1,0:T(8,128)(2,1)S(1)}, u32[]{:S(2)}, u32[]{:S(2)}) collective-permute-start(bf16[96,1024]{1,0:T(8,128)(2,1)S(1)} %collective-permute-done.3), channel_id=1, source_target_pairs={{0,4},{1,5},{2,6},{3,7},{4,0},{5,1},{6,2},{7,3},{8,12},{9,13},{10,... | collective-permute-start | bytes 589832 | tf_op jit(solution)/shard_map/ppermute | solution.py:454
  16.4 10.7 %collective-permute-start.4 = (bf16[192,1024]{1,0:T(8,128)(2,1)}, bf16[192,1024]{1,0:T(8,128)(2,1)S(1)}, u32[]{:S(2)}, u32[]{:S(2)}) collective-permute-start(bf16[192,1024]{1,0:T(8,128)(2,1)} %get-tuple-element.33), channel_id=1, source_target_pairs={{0,1},{1,0},{2,3},{3,2},{4,5},{5,4},{6,7},{7,6},{8,9},{9,8},{10,11... | collective-permute-start | bytes 1179656 | tf_op jit(solution)/shard_map/ppermute | solution.py:441
  16.5 18.3 %collective-permute-start = (bf16[192,1024]{1,0:T(8,128)(2,1)}, bf16[192,1024]{1,0:T(8,128)(2,1)S(1)}, u32[]{:S(2)}, u32[]{:S(2)}) collective-permute-start(bf16[192,1024]{1,0:T(8,128)(2,1)} %get-tuple-element.27), channel_id=1, source_target_pairs={{0,1},{1,0},{2,3},{3,2},{4,5},{5,4},{6,7},{7,6},{8,9},{9,8},{10,11... | collective-permute-start | bytes 1179656 | tf_op jit(solution)/shard_map/ppermute | solution.py:441
  17.0 18.3 %collective-permute-start.1 = (bf16[192,1024]{1,0:T(8,128)(2,1)}, bf16[192,1024]{1,0:T(8,128)(2,1)S(1)}, u32[]{:S(2)}, u32[]{:S(2)}) collective-permute-start(bf16[192,1024]{1,0:T(8,128)(2,1)} %get-tuple-element.28), channel_id=1, source_target_pairs={{0,2},{1,3},{2,0},{3,1},{4,6},{5,7},{6,4},{7,5},{8,10},{9,11},{10,... | collective-permute-start | bytes 1179656 | tf_op jit(solution)/shard_map/ppermute | solution.py:441
  19.5 16.3 %collective-permute-start.2 = (bf16[192,1024]{1,0:T(8,128)(2,1)}, bf16[192,1024]{1,0:T(8,128)(2,1)S(1)}, u32[]{:S(2)}, u32[]{:S(2)}) collective-permute-start(bf16[192,1024]{1,0:T(8,128)(2,1)} %get-tuple-element.29), channel_id=1, source_target_pairs={{0,3},{1,2},{2,1},{3,0},{4,7},{5,6},{6,5},{7,4},{8,11},{9,10},{10,... | collective-permute-start | bytes 1179656 | tf_op jit(solution)/shard_map/ppermute | solution.py:441
  19.6 7.4 %collective-permute-start.7 = (bf16[96,1024]{1,0:T(8,128)(2,1)S(1)}, bf16[96,1024]{1,0:T(8,128)(2,1)S(1)}, u32[]{:S(2)}, u32[]{:S(2)}) collective-permute-start(bf16[96,1024]{1,0:T(8,128)(2,1)S(1)} %collective-permute-done.5), channel_id=1, source_target_pairs={{0,4},{1,5},{2,6},{3,7},{4,0},{5,1},{6,2},{7,3},{8,12},{9,13},{10,... | collective-permute-start | bytes 589832 | tf_op jit(solution)/shard_map/ppermute | solution.py:454
  24.8 2.3 %copy-start = (bf16[192,4096]{1,0:T(8,128)(2,1)S(1)}, bf16[192,4096]{1,0:T(8,128)(2,1)}, u32[]{:S(2)}) copy-start(bf16[192,4096]{1,0:T(8,128)(2,1)} %refs_0_.1) | copy-start | bytes 4718596
  24.8 2.3 %copy-start.2 = (s32[1,8]{1,0:T(1,128)S(1)}, s32[1,8]{1,0:T(1,128)}, u32[]{:S(2)}) copy-start(s32[1,8]{1,0:T(1,128)} %param.10) | copy-start | bytes 100
  27.1 8.8 %copy-start.1 = (bf16[192,4096]{1,0:T(8,128)(2,1)S(1)}, bf16[192,4096]{1,0:T(8,128)(2,1)}, u32[]{:S(2)}) copy-start(bf16[192,4096]{1,0:T(8,128)(2,1)} %refs_1_.1) | copy-start | bytes 4718596
  31.7 28.5 %collective-permute-start.10 = (bf16[2,96,1152]{2,1,0:T(8,128)(2,1)S(1)}, bf16[2,96,1152]{2,1,0:T(8,128)(2,1)S(1)}, u32[]{:S(2)}, u32[]{:S(2)}) collective-permute-start(bf16[2,96,1152]{2,1,0:T(8,128)(2,1)S(1)} %get-tuple-element.37), channel_id=1, source_target_pairs={{0,12},{1,13},{2,14},{3,15},{4,8},{5,9},{6,10},{7,11},{8,4},{9,5},... | collective-permute-start | bytes 1327112 | tf_op jit(solution)/shard_map/ppermute | solution.py:481
  33.4 28.3 %collective-permute-start.8 = (bf16[2,96,1152]{2,1,0:T(8,128)(2,1)S(1)}, bf16[2,96,1152]{2,1,0:T(8,128)(2,1)S(1)}, u32[]{:S(2)}, u32[]{:S(2)}) collective-permute-start(bf16[2,96,1152]{2,1,0:T(8,128)(2,1)S(1)} %get-tuple-element.35), channel_id=1, source_target_pairs={{0,4},{1,5},{2,6},{3,7},{4,0},{5,1},{6,2},{7,3},{8,12},{9,13},{10,... | collective-permute-start | bytes 1327112 | tf_op jit(solution)/shard_map/ppermute | solution.py:481
  34.8 26.8 %collective-permute-start.9 = (bf16[2,96,1152]{2,1,0:T(8,128)(2,1)S(1)}, bf16[2,96,1152]{2,1,0:T(8,128)(2,1)S(1)}, u32[]{:S(2)}, u32[]{:S(2)}) collective-permute-start(bf16[2,96,1152]{2,1,0:T(8,128)(2,1)S(1)} %get-tuple-element.36), channel_id=1, source_target_pairs={{0,8},{1,9},{2,10},{3,11},{4,12},{5,13},{6,14},{7,15},{8,0},{9,1},... | collective-permute-start | bytes 1327112 | tf_op jit(solution)/shard_map/ppermute | solution.py:481
  58.1 19.2 %collective-permute-start.14 = (bf16[2,64,1152]{2,1,0:T(8,128)(2,1)S(1)}, bf16[2,64,1152]{2,1,0:T(8,128)(2,1)S(1)}, u32[]{:S(2)}, u32[]{:S(2)}) collective-permute-start(bf16[2,64,1152]{2,1,0:T(8,128)(2,1)S(1)} %get-tuple-element.44), channel_id=1, source_target_pairs={{0,4},{1,5},{2,6},{3,7},{4,0},{5,1},{6,2},{7,3},{8,12},{9,13},{10,... | collective-permute-start | bytes 884744 | tf_op jit(solution)/shard_map/ppermute | solution.py:481
  58.7 20.0 %collective-permute-start.15 = (bf16[2,64,1152]{2,1,0:T(8,128)(2,1)S(1)}, bf16[2,64,1152]{2,1,0:T(8,128)(2,1)S(1)}, u32[]{:S(2)}, u32[]{:S(2)}) collective-permute-start(bf16[2,64,1152]{2,1,0:T(8,128)(2,1)S(1)} %get-tuple-element.45), channel_id=1, source_target_pairs={{0,8},{1,9},{2,10},{3,11},{4,12},{5,13},{6,14},{7,15},{8,0},{9,1},... | collective-permute-start | bytes 884744 | tf_op jit(solution)/shard_map/ppermute | solution.py:481
  60.2 26.3 %collective-permute-start.16 = (bf16[2,64,1152]{2,1,0:T(8,128)(2,1)S(1)}, bf16[2,64,1152]{2,1,0:T(8,128)(2,1)S(1)}, u32[]{:S(2)}, u32[]{:S(2)}) collective-permute-start(bf16[2,64,1152]{2,1,0:T(8,128)(2,1)S(1)} %get-tuple-element.46), channel_id=1, source_target_pairs={{0,12},{1,13},{2,14},{3,15},{4,8},{5,9},{6,10},{7,11},{8,4},{9,5},... | collective-permute-start | bytes 884744 | tf_op jit(solution)/shard_map/ppermute | solution.py:481
  75.1 12.6 %collective-permute-start.11 = (bf16[2,32,1152]{2,1,0:T(8,128)(2,1)S(1)}, bf16[2,32,1152]{2,1,0:T(8,128)(2,1)S(1)}, u32[]{:S(2)}, u32[]{:S(2)}) collective-permute-start(bf16[2,32,1152]{2,1,0:T(8,128)(2,1)S(1)} %get-tuple-element.41), channel_id=1, source_target_pairs={{0,4},{1,5},{2,6},{3,7},{4,0},{5,1},{6,2},{7,3},{8,12},{9,13},{10,... | collective-permute-start | bytes 442376 | tf_op jit(solution)/shard_map/ppermute | solution.py:481
  75.7 12.0 %collective-permute-start.12 = (bf16[2,32,1152]{2,1,0:T(8,128)(2,1)S(1)}, bf16[2,32,1152]{2,1,0:T(8,128)(2,1)S(1)}, u32[]{:S(2)}, u32[]{:S(2)}) collective-permute-start(bf16[2,32,1152]{2,1,0:T(8,128)(2,1)S(1)} %get-tuple-element.42), channel_id=1, source_target_pairs={{0,8},{1,9},{2,10},{3,11},{4,12},{5,13},{6,14},{7,15},{8,0},{9,1},... | collective-permute-start | bytes 442376 | tf_op jit(solution)/shard_map/ppermute | solution.py:481
  77.3 10.8 %collective-permute-start.13 = (bf16[2,32,1152]{2,1,0:T(8,128)(2,1)S(1)}, bf16[2,32,1152]{2,1,0:T(8,128)(2,1)S(1)}, u32[]{:S(2)}, u32[]{:S(2)}) collective-permute-start(bf16[2,32,1152]{2,1,0:T(8,128)(2,1)S(1)} %get-tuple-element.43), channel_id=1, source_target_pairs={{0,12},{1,13},{2,14},{3,15},{4,8},{5,9},{6,10},{7,11},{8,4},{9,5},... | collective-permute-start | bytes 442376 | tf_op jit(solution)/shard_map/ppermute | solution.py:481
  78.7 25.4 %collective-permute-start.19 = (bf16[1,96,1152]{2,1,0:T(8,128)(2,1)S(1)}, bf16[1,96,1152]{2,1,0:T(8,128)(2,1)S(1)}, u32[]{:S(2)}, u32[]{:S(2)}) collective-permute-start(bf16[1,96,1152]{2,1,0:T(8,128)(2,1)S(1)} %get-tuple-element.51), channel_id=1, source_target_pairs={{0,16},{1,17},{2,18},{3,19},{4,20},{5,21},{6,22},{7,23},{8,24},{9,... | collective-permute-start | bytes 663560 | tf_op jit(solution)/shard_map/ppermute | solution.py:481
  87.6 15.5 %collective-permute-start.18 = (bf16[1,64,1152]{2,1,0:T(8,128)(2,1)S(1)}, bf16[1,64,1152]{2,1,0:T(8,128)(2,1)S(1)}, u32[]{:S(2)}, u32[]{:S(2)}) collective-permute-start(bf16[1,64,1152]{2,1,0:T(8,128)(2,1)S(1)} %get-tuple-element.50), channel_id=1, source_target_pairs={{0,16},{1,17},{2,18},{3,19},{4,20},{5,21},{6,22},{7,23},{8,24},{9,... | collective-permute-start | bytes 442376 | tf_op jit(solution)/shard_map/ppermute | solution.py:481
  88.8 16.4 %collective-permute-start.17 = (bf16[1,32,1152]{2,1,0:T(8,128)(2,1)S(1)}, bf16[1,32,1152]{2,1,0:T(8,128)(2,1)S(1)}, u32[]{:S(2)}, u32[]{:S(2)}) collective-permute-start(bf16[1,32,1152]{2,1,0:T(8,128)(2,1)S(1)} %get-tuple-element.49), channel_id=1, source_target_pairs={{0,16},{1,17},{2,18},{3,19},{4,20},{5,21},{6,22},{7,23},{8,24},{9,... | collective-permute-start | bytes 221192 | tf_op jit(solution)/shard_map/ppermute | solution.py:481

commit v8 on v7

--- a/solution.py
+++ b/solution.py
@@ -183,12 +183,14 @@
     def blocks_of(ref, first, length):
         return jnp.concatenate([block_of(ref, first + i) for i in range(length)], axis=0)
 
-    def absorb(first, length, chains=None):
+    def absorb(first, length, sure, chains=None):
         steps = []
         for begin in range(0, length, 4):
             some = min(4, length - begin)
             start = first + begin
-            mask = lax.broadcasted_iota(jnp.int32, (1, some * BLK), 1) // BLK + start < kept
+            mask = None
+            if begin + some > sure:
+                mask = lax.broadcasted_iota(jnp.int32, (1, some * BLK), 1) // BLK + start < kept
             steps.append(
                 (lambda start=start, some=some: blocks_of(key_ref, start, some),
                  lambda start=start, some=some: with_ones(blocks_of(value_ref, start, some)), mask)
@@ -202,8 +204,8 @@
     for length in sizes:
 
         @pl.when((kept > least) & (kept <= length))
-        def _(length=length):
-            finish(absorb(0, length))
+        def _(length=length, sure=least + 1):
+            finish(absorb(0, length, sure))
 
         least = length
 
@@ -221,11 +223,11 @@
 
         @pl.when(kept > most)
         def _():
-            hold(absorb(0, most))
+            hold(absorb(0, most, most))
 
             @pl.loop(1, pl.cdiv(kept, most))
             def _(step):
-                hold(absorb(step * most, most, fetch()))
+                hold(absorb(step * most, most, 1, fetch()))
 
             finish(fetch())
 
@@ -440,9 +442,10 @@
     def sent(block, bit):
         return lax.ppermute(block, AXES, swapped(shape, 0, bit))
 
+    sides = low, spot // 2 % 2
     picked = [
-        lax.dynamic_slice(q_second, (low * half, (me ^ bit) * mine), (half, mine))
-        for bit in (2, 3)
+        lax.dynamic_slice(q_second, (side * half, (me ^ bit) * mine), (half, mine))
+        for side, bit in zip(sides, (2, 3))
     ]
     got = [sent(x, bit) for x, bit in zip(picked, (2, 3))]
     boxes = [(0, 1, False)] + [(1, bit, False) for bit in (1, 2, 3)]
@@ -450,8 +453,8 @@
     near_s = sent(near_s, 1)
     beside = [sent(x, bit) for x, bit in zip(picked_f, (1, 2, 3))]
     others = []
-    for x in got:
-        others.append(lax.ppermute(x, AXES, swapped(shape, 1, 0)))
+    for order, x in enumerate(got):
+        others.append(lax.ppermute(x, AXES, swapped(shape, 1 + order, 0)))
     second = [q_second.reshape(2, half, wide), near_s.reshape(2, half, mine)]
     second += [x.reshape(1, half, mine) for x in got + others]
     first = [q_first.reshape(2, half, wide)] + [x.reshape(2, half, mine) for x in beside]
@@ -460,7 +463,8 @@
         return jnp.stack([((o ^ spot) % 4) * 2 + o // 4 for o in owners]).astype(jnp.int32)
 
     straight = [2 * (me ^ bit) + side for bit in range(4) for side in (0, 1)]
-    shared = [2 * (me ^ bit) + side for side in (low, 1 - low) for bit in (2, 3)]
+    shared = [2 * (me ^ bit) + side for side, bit in zip(sides, (2, 3))]
+    shared += [2 * (me ^ bit) + 1 - side for side, bit in zip(sides, (2, 3))]
     places = places_of(straight[:4] + shared), places_of(straight)
     return second, first, places, jnp.reshape(me, (1,)).astype(jnp.int32), got[0]
 

time: 106 us -> 107 us (level)
    ppermute x12, waiting for transfers between devices: 8.46 us -> 9.64 us  [moved(): return lax.ppermute(part, AXES, swapped(shape, bits, 0))]
    ppermute x2, waiting for transfers between devices: 2.26 us -> 1.19 us  [relayed(): others.append(lax.ppermute(x, AXES, swapped(shape, 1 + order, 0)))]
  transfers between devices with their start and end apart: 20 -> 20, of which waited for: 5 -> 5; matrix products, arithmetic and copies ran while one was open for 5% -> 5% of each run, Pallas kernels for 45% -> 44%
where the time goes in v8:
time: 107 us
  Pallas kernels  48.3 us (45%)
  starting transfers between devices  33.2 us (31%)
  waiting for transfers between devices  16.9 us (16%)
  local copies, waits for them, and re-layouts  5.99 us (6%)
  between operations  1.73 us (2%)
    pallas_call x3, Pallas kernels, partial_call(): pl.pallas_call(functools.partial(kernel, pieces=len(pieces), outs=outs, g...  38.8 us
    ppermute x12, starting transfers between devices, moved(): return lax.ppermute(part, AXES, swapped(shape, bits, 0))  24.3 us
    ppermute x12, waiting for transfers between devices, moved(): return lax.ppermute(part, AXES, swapped(shape, bits, 0))  9.64 us
    ppermute x6, waiting for transfers between devices, sent(): return lax.ppermute(block, AXES, swapped(shape, 0, bit))  6.11 us
    ppermute x6, starting transfers between devices, sent(): return lax.ppermute(block, AXES, swapped(shape, 0, bit))  5.16 us
    transpose x1, local copies, waits for them, and re-layouts, shards(): keys, values = settle(keys, jnp.swapaxes(late, 0, 1))  4.56 us
    ppermute x2, starting transfers between devices, relayed(): others.append(lax.ppermute(x, AXES, swapped(shape, 1 + order, 0)))  3.69 us
    pallas_call x3, Pallas kernels, merge_quad(): pl.pallas_call(functools.partial(quad_kernel, sources=len(parts)), in_spe...  3.34 us
  transfers between devices with their start and end apart: 20, of which 5 were waited for; matrix products, arithmetic and copies ran while one was open for 5% of the time, Pallas kernels for 44%

profile of v8, /device:TPU:0, one launch (start us, length us, event | category | flops | bytes accessed | tf_op | source)
XLA Modules:
  0.0 106.8 jit_solution(5165889405932787576)
XLA Ops:
  0.7 1.1 fusion
  1.8 3.0 %collective-permute-start.3 = (bf16[96,1024]{1,0:T(8,128)(2,1)S(1)}, bf16[96,1024]{1,0:T(8,128)(2,1)S(1)}, u32[]{:S(2)}, u32[]{:S(2)}) collective-permute-start(bf16[96,1024]{1,0:T(8,128)(2,1)S(1)} %get-tuple-element.53), channel_id=1, source_target_pairs={{0,2},{1,3},{2,0},{3,1},{4,6},{5,7},{6,4},{7,5},{8,10},{9,11},{10,... | collective-permute-start | bytes 589832 | tf_op jit(solution)/shard_map/ppermute | solution.py:443
  4.8 5.7 %collective-permute-done.3 = bf16[96,1024]{1,0:T(8,128)(2,1)S(1)} collective-permute-done((bf16[96,1024]{1,0:T(8,128)(2,1)S(1)}, bf16[96,1024]{1,0:T(8,128)(2,1)S(1)}, u32[]{:S(2)}, u32[]{:S(2)}) %collective-permute-start.3) | collective-permute-done | bytes 196640 | tf_op jit(solution)/shard_map/ppermute | solution.py:443
  10.5 2.0 %collective-permute-start.6 = (bf16[96,1024]{1,0:T(8,128)(2,1)S(1)}, bf16[96,1024]{1,0:T(8,128)(2,1)S(1)}, u32[]{:S(2)}, u32[]{:S(2)}) collective-permute-start(bf16[96,1024]{1,0:T(8,128)(2,1)S(1)} %collective-permute-done.3), channel_id=1, source_target_pairs={{0,4},{1,5},{2,6},{3,7},{4,0},{5,1},{6,2},{7,3},{8,12},{9,13},{10,... | collective-permute-start | bytes 589832 | tf_op jit(solution)/shard_map/ppermute | solution.py:457
  12.6 0.6 pad_add_fusion.spot_ref
  13.2 3.2 %shard_map.77 = (bf16[192,1024]{1,0:T(8,128)(2,1)}, bf16[192,1024]{1,0:T(8,128)(2,1)}, bf16[192,1024]{1,0:T(8,128)(2,1)}, bf16[192,1024]{1,0:T(8,128)(2,1)}) custom-call(s32[2]{0:T(128)} %pad_add_fusion.spot_ref, bf16[192,4096]{1,0:T(8,128)(2,1)} %refs_0_.1, bf16[192,4096]{1,0:T(8,128)(2,1)} %refs_1_.1), custom_call_target="tpu_custom_call" | custom-call | tf_op jit(solution)/shard_map/pallas_call | solution.py:410
  17.0 1.5 %collective-permute-start.1 = (bf16[192,1024]{1,0:T(8,128)(2,1)}, bf16[192,1024]{1,0:T(8,128)(2,1)S(1)}, u32[]{:S(2)}, u32[]{:S(2)}) collective-permute-start(bf16[192,1024]{1,0:T(8,128)(2,1)} %get-tuple-element.28), channel_id=1, source_target_pairs={{0,2},{1,3},{2,0},{3,1},{4,6},{5,7},{6,4},{7,5},{8,10},{9,11},{10,... | collective-permute-start | bytes 1179656 | tf_op jit(solution)/shard_map/ppermute | solution.py:443
  19.7 1.6 %collective-permute-start.7 = (bf16[96,1024]{1,0:T(8,128)(2,1)S(1)}, bf16[96,1024]{1,0:T(8,128)(2,1)S(1)}, u32[]{:S(2)}, u32[]{:S(2)}) collective-permute-start(bf16[96,1024]{1,0:T(8,128)(2,1)S(1)} %collective-permute-done.5), channel_id=1, source_target_pairs={{0,8},{1,9},{2,10},{3,11},{4,12},{5,13},{6,14},{7,15},{8,0},{9,1},... | collective-permute-start | bytes 589832 | tf_op jit(solution)/shard_map/ppermute | solution.py:457
  21.3 4.6 %copy_bitcast_fusion = (bf16[4,4096,128]{2,1,0:T(8,128)(2,1)S(1)}, bf16[4,4096,128]{2,1,0:T(8,128)(2,1)S(1)}) fusion(bf16[4096,4,128]{2,1,0:T(4,128)(2,1)} %param.9, bf16[4096,4,128]{2,1,0:T(4,128)(2,1)} %param.8), kind=kLoop, calls=%fused_computation | loop fusion | bytes 16777216 | tf_op jit(solution)/shard_map/transpose | solution.py:480
  25.9 1.2 %collective-permute-done.7 = bf16[96,1024]{1,0:T(8,128)(2,1)S(1)} collective-permute-done((bf16[96,1024]{1,0:T(8,128)(2,1)S(1)}, bf16[96,1024]{1,0:T(8,128)(2,1)S(1)}, u32[]{:S(2)}, u32[]{:S(2)}) %collective-permute-start.7) | collective-permute-done | bytes 196640 | tf_op jit(solution)/shard_map/ppermute | solution.py:457
  27.3 4.6 %shard_map.79 = (bf16[2,96,1152]{2,1,0:T(8,128)(2,1)S(1)}, bf16[2,96,1152]{2,1,0:T(8,128)(2,1)S(1)}, bf16[2,96,1152]{2,1,0:T(8,128)(2,1)S(1)}, bf16[2,96,1152]{2,1,0:T(8,128)(2,1)S(1)}) custom-call(s32[8]{0:T(128)S(1)} %stack.68.place_ref, s32[1]{0:T(128)} %bitcast.9.column_ref, s32[8]{0:T(128)S(1)} %bitcast.46, s32[1]{0:T(128)S(6)} %copy.18.count_ref, ...), custom_call_target="tpu_custom_call" | custom-call | flops 3221225472 | bytes 1048576 | tf_op jit(solution)/shard_map/pallas_call | solution.py:260
  32.0 1.4 %collective-permute-start.10 = (bf16[2,96,1152]{2,1,0:T(8,128)(2,1)S(1)}, bf16[2,96,1152]{2,1,0:T(8,128)(2,1)S(1)}, u32[]{:S(2)}, u32[]{:S(2)}) collective-permute-start(bf16[2,96,1152]{2,1,0:T(8,128)(2,1)S(1)} %get-tuple-element.37), channel_id=1, source_target_pairs={{0,12},{1,13},{2,14},{3,15},{4,8},{5,9},{6,10},{7,11},{8,4},{9,5},... | collective-permute-start | bytes 1327112 | tf_op jit(solution)/shard_map/ppermute | solution.py:485
  33.3 1.5 %collective-permute-start.8 = (bf16[2,96,1152]{2,1,0:T(8,128)(2,1)S(1)}, bf16[2,96,1152]{2,1,0:T(8,128)(2,1)S(1)}, u32[]{:S(2)}, u32[]{:S(2)}) collective-permute-start(bf16[2,96,1152]{2,1,0:T(8,128)(2,1)S(1)} %get-tuple-element.35), channel_id=1, source_target_pairs={{0,4},{1,5},{2,6},{3,7},{4,0},{5,1},{6,2},{7,3},{8,12},{9,13},{10,... | collective-permute-start | bytes 1327112 | tf_op jit(solution)/shard_map/ppermute | solution.py:485
  34.9 0.7 collective-permute-start.9
  35.9 22.3 %shard_map.80 = (bf16[2,64,1152]{2,1,0:T(8,128)(2,1)S(1)}, bf16[2,64,1152]{2,1,0:T(8,128)(2,1)S(1)}, bf16[2,64,1152]{2,1,0:T(8,128)(2,1)S(1)}, bf16[2,64,1152]{2,1,0:T(8,128)(2,1)S(1)}) custom-call(s32[8]{0:T(128)S(1)} %stack.61.place_ref, s32[1]{0:T(128)} %bitcast.9.column_ref, bf16[2,96,4096]{2,1,0:T(8,128)(2,1)S(1)} %bitcast.33, ...), custom_call_target="tpu_custom_call" | custom-call | flops 17179869184 | bytes 8388608 | tf_op jit(solution)/shard_map/pallas_call | solution.py:260
  58.1 0.6 collective-permute-start.14
  58.7 1.6 %collective-permute-start.15 = (bf16[2,64,1152]{2,1,0:T(8,128)(2,1)S(1)}, bf16[2,64,1152]{2,1,0:T(8,128)(2,1)S(1)}, u32[]{:S(2)}, u32[]{:S(2)}) collective-permute-start(bf16[2,64,1152]{2,1,0:T(8,128)(2,1)S(1)} %get-tuple-element.45), channel_id=1, source_target_pairs={{0,8},{1,9},{2,10},{3,11},{4,12},{5,13},{6,14},{7,15},{8,0},{9,1},... | collective-permute-start | bytes 884744 | tf_op jit(solution)/shard_map/ppermute | solution.py:485
  60.3 1.4 %collective-permute-start.16 = (bf16[2,64,1152]{2,1,0:T(8,128)(2,1)S(1)}, bf16[2,64,1152]{2,1,0:T(8,128)(2,1)S(1)}, u32[]{:S(2)}, u32[]{:S(2)}) collective-permute-start(bf16[2,64,1152]{2,1,0:T(8,128)(2,1)S(1)} %get-tuple-element.46), channel_id=1, source_target_pairs={{0,12},{1,13},{2,14},{3,15},{4,8},{5,9},{6,10},{7,11},{8,4},{9,5},... | collective-permute-start | bytes 884744 | tf_op jit(solution)/shard_map/ppermute | solution.py:485
  61.7 1.6 %shard_map.81 = (bf16[1,96,1152]{2,1,0:T(8,128)(2,1)S(1)}, bf16[1,96,1152]{2,1,0:T(8,128)(2,1)S(1)}) custom-call(s32[1]{0:T(128)} %bitcast.refs_8_.spot_ref, bf16[2,96,1152]{2,1,0:T(8,128)(2,1)S(1)} %get-tuple-element.34.refs_6_.refs_0_, bf16[2,96,1152]{2,1,0:T(8,128)(2,1)S(1)} %collective-permute-done.8.refs_1_, ...), custom_call_target="tpu_custom_call" | custom-call | flops 3538944 | bytes 2211840 | tf_op jit(solution)/shard_map/pallas_call | solution.py:358
  63.3 11.9 %shard_map.82 = (bf16[2,32,1152]{2,1,0:T(8,128)(2,1)S(1)}, bf16[2,32,1152]{2,1,0:T(8,128)(2,1)S(1)}, bf16[2,32,1152]{2,1,0:T(8,128)(2,1)S(1)}, bf16[2,32,1152]{2,1,0:T(8,128)(2,1)S(1)}) custom-call(s32[8]{0:T(128)S(1)} %stack.61.place_ref, s32[1]{0:T(128)} %bitcast.9.column_ref, bf16[2,96,4096]{2,1,0:T(8,128)(2,1)S(1)} %bitcast.34, ...), custom_call_target="tpu_custom_call" | custom-call | flops 8589934592 | bytes 8388608 | tf_op jit(solution)/shard_map/pallas_call | solution.py:260
  75.2 0.6 collective-permute-start.11
  75.7 1.6 %collective-permute-start.12 = (bf16[2,32,1152]{2,1,0:T(8,128)(2,1)S(1)}, bf16[2,32,1152]{2,1,0:T(8,128)(2,1)S(1)}, u32[]{:S(2)}, u32[]{:S(2)}) collective-permute-start(bf16[2,32,1152]{2,1,0:T(8,128)(2,1)S(1)} %get-tuple-element.42), channel_id=1, source_target_pairs={{0,8},{1,9},{2,10},{3,11},{4,12},{5,13},{6,14},{7,15},{8,0},{9,1},... | collective-permute-start | bytes 442376 | tf_op jit(solution)/shard_map/ppermute | solution.py:485
  77.3 1.4 %collective-permute-start.13 = (bf16[2,32,1152]{2,1,0:T(8,128)(2,1)S(1)}, bf16[2,32,1152]{2,1,0:T(8,128)(2,1)S(1)}, u32[]{:S(2)}, u32[]{:S(2)}) collective-permute-start(bf16[2,32,1152]{2,1,0:T(8,128)(2,1)S(1)} %get-tuple-element.43), channel_id=1, source_target_pairs={{0,12},{1,13},{2,14},{3,15},{4,8},{5,9},{6,10},{7,11},{8,4},{9,5},... | collective-permute-start | bytes 442376 | tf_op jit(solution)/shard_map/ppermute | solution.py:485
  78.7 8.0 %collective-permute-start.19 = (bf16[1,96,1152]{2,1,0:T(8,128)(2,1)S(1)}, bf16[1,96,1152]{2,1,0:T(8,128)(2,1)S(1)}, u32[]{:S(2)}, u32[]{:S(2)}) collective-permute-start(bf16[1,96,1152]{2,1,0:T(8,128)(2,1)S(1)} %get-tuple-element.51), channel_id=1, source_target_pairs={{0,16},{1,17},{2,18},{3,19},{4,20},{5,21},{6,22},{7,23},{8,24},{9,... | collective-permute-start | bytes 663560 | tf_op jit(solution)/shard_map/ppermute | solution.py:485
  86.7 1.1 %shard_map.83 = (bf16[1,64,1152]{2,1,0:T(8,128)(2,1)S(1)}, bf16[1,64,1152]{2,1,0:T(8,128)(2,1)S(1)}) custom-call(s32[1]{0:T(128)} %bitcast.refs_8_.spot_ref, bf16[2,64,1152]{2,1,0:T(8,128)(2,1)S(1)} %get-tuple-element.38.refs_4_.refs_0_, bf16[2,64,1152]{2,1,0:T(8,128)(2,1)S(1)} %collective-permute-done.14.refs_1_, ...), custom_call_target="tpu_custom_call" | custom-call | flops 2359296 | bytes 1474560 | tf_op jit(solution)/shard_map/pallas_call | solution.py:358
  87.9 1.1 collective-permute-done.13.refs_3_
  89.0 0.7 shard_map.84
  89.6 5.6 %collective-permute-start.17 = (bf16[1,32,1152]{2,1,0:T(8,128)(2,1)S(1)}, bf16[1,32,1152]{2,1,0:T(8,128)(2,1)S(1)}, u32[]{:S(2)}, u32[]{:S(2)}) collective-permute-start(bf16[1,32,1152]{2,1,0:T(8,128)(2,1)S(1)} %get-tuple-element.49), channel_id=1, source_target_pairs={{0,16},{1,17},{2,18},{3,19},{4,20},{5,21},{6,22},{7,23},{8,24},{9,... | collective-permute-start | bytes 221192 | tf_op jit(solution)/shard_map/ppermute | solution.py:485
  95.3 8.6 %collective-permute-done.18.refs_1_ = bf16[1,64,1152]{2,1,0:T(8,128)(2,1)S(1)} collective-permute-done((bf16[1,64,1152]{2,1,0:T(8,128)(2,1)S(1)}, bf16[1,64,1152]{2,1,0:T(8,128)(2,1)S(1)}, u32[]{:S(2)}, u32[]{:S(2)}) %collective-permute-start.18) | collective-permute-done | bytes 147488 | tf_op jit(solution)/shard_map/ppermute | solution.py:485
  103.8 1.0 shard_map.85.refs_2_
  104.8 1.1 %shard_map.87 = bf16[1,96,1024]{2,1,0:T(8,128)(2,1)} custom-call(bf16[1,96,1152]{2,1,0:T(8,128)(2,1)S(1)} %get-tuple-element.39.refs_6_.refs_0_, bf16[1,96,1152]{2,1,0:T(8,128)(2,1)S(1)} %collective-permute-done.19.refs_1_), custom_call_target="tpu_custom_call" | custom-call | flops 786432 | bytes 442368 | tf_op jit(solution)/shard_map/pallas_call | solution.py:328
  105.9 0.9 shard_map.86
  (30 shorter events, 1.5 us)
Async XLA Ops:
  1.8 8.8 %collective-permute-start.3 = (bf16[96,1024]{1,0:T(8,128)(2,1)S(1)}, bf16[96,1024]{1,0:T(8,128)(2,1)S(1)}, u32[]{:S(2)}, u32[]{:S(2)}) collective-permute-start(bf16[96,1024]{1,0:T(8,128)(2,1)S(1)} %get-tuple-element.53), channel_id=1, source_target_pairs={{0,2},{1,3},{2,0},{3,1},{4,6},{5,7},{6,4},{7,5},{8,10},{9,11},{10,... | collective-permute-start | bytes 589832 | tf_op jit(solution)/shard_map/ppermute | solution.py:443
  4.8 14.8 %collective-permute-start.5 = (bf16[96,1024]{1,0:T(8,128)(2,1)S(1)}, bf16[96,1024]{1,0:T(8,128)(2,1)S(1)}, u32[]{:S(2)}, u32[]{:S(2)}) collective-permute-start(bf16[96,1024]{1,0:T(8,128)(2,1)S(1)} %get-tuple-element.52), channel_id=1, source_target_pairs={{0,3},{1,2},{2,1},{3,0},{4,7},{5,6},{6,5},{7,4},{8,11},{9,10},{10,... | collective-permute-start | bytes 589832 | tf_op jit(solution)/shard_map/ppermute | solution.py:443
  10.5 9.1 %collective-permute-start.6 = (bf16[96,1024]{1,0:T(8,128)(2,1)S(1)}, bf16[96,1024]{1,0:T(8,128)(2,1)S(1)}, u32[]{:S(2)}, u32[]{:S(2)}) collective-permute-start(bf16[96,1024]{1,0:T(8,128)(2,1)S(1)} %collective-permute-done.3), channel_id=1, source_target_pairs={{0,4},{1,5},{2,6},{3,7},{4,0},{5,1},{6,2},{7,3},{8,12},{9,13},{10,... | collective-permute-start | bytes 589832 | tf_op jit(solution)/shard_map/ppermute | solution.py:457
  16.4 10.7 %collective-permute-start.4 = (bf16[192,1024]{1,0:T(8,128)(2,1)}, bf16[192,1024]{1,0:T(8,128)(2,1)S(1)}, u32[]{:S(2)}, u32[]{:S(2)}) collective-permute-start(bf16[192,1024]{1,0:T(8,128)(2,1)} %get-tuple-element.33), channel_id=1, source_target_pairs={{0,1},{1,0},{2,3},{3,2},{4,5},{5,4},{6,7},{7,6},{8,9},{9,8},{10,11... | collective-permute-start | bytes 1179656 | tf_op jit(solution)/shard_map/ppermute | solution.py:443
  16.5 18.3 %collective-permute-start = (bf16[192,1024]{1,0:T(8,128)(2,1)}, bf16[192,1024]{1,0:T(8,128)(2,1)S(1)}, u32[]{:S(2)}, u32[]{:S(2)}) collective-permute-start(bf16[192,1024]{1,0:T(8,128)(2,1)} %get-tuple-element.27), channel_id=1, source_target_pairs={{0,1},{1,0},{2,3},{3,2},{4,5},{5,4},{6,7},{7,6},{8,9},{9,8},{10,11... | collective-permute-start | bytes 1179656 | tf_op jit(solution)/shard_map/ppermute | solution.py:443
  17.0 18.5 %collective-permute-start.1 = (bf16[192,1024]{1,0:T(8,128)(2,1)}, bf16[192,1024]{1,0:T(8,128)(2,1)S(1)}, u32[]{:S(2)}, u32[]{:S(2)}) collective-permute-start(bf16[192,1024]{1,0:T(8,128)(2,1)} %get-tuple-element.28), channel_id=1, source_target_pairs={{0,2},{1,3},{2,0},{3,1},{4,6},{5,7},{6,4},{7,5},{8,10},{9,11},{10,... | collective-permute-start | bytes 1179656 | tf_op jit(solution)/shard_map/ppermute | solution.py:443
  19.6 16.3 %collective-permute-start.2 = (bf16[192,1024]{1,0:T(8,128)(2,1)}, bf16[192,1024]{1,0:T(8,128)(2,1)S(1)}, u32[]{:S(2)}, u32[]{:S(2)}) collective-permute-start(bf16[192,1024]{1,0:T(8,128)(2,1)} %get-tuple-element.29), channel_id=1, source_target_pairs={{0,3},{1,2},{2,1},{3,0},{4,7},{5,6},{6,5},{7,4},{8,11},{9,10},{10,... | collective-permute-start | bytes 1179656 | tf_op jit(solution)/shard_map/ppermute | solution.py:443
  19.7 7.4 %collective-permute-start.7 = (bf16[96,1024]{1,0:T(8,128)(2,1)S(1)}, bf16[96,1024]{1,0:T(8,128)(2,1)S(1)}, u32[]{:S(2)}, u32[]{:S(2)}) collective-permute-start(bf16[96,1024]{1,0:T(8,128)(2,1)S(1)} %collective-permute-done.5), channel_id=1, source_target_pairs={{0,8},{1,9},{2,10},{3,11},{4,12},{5,13},{6,14},{7,15},{8,0},{9,1},... | collective-permute-start | bytes 589832 | tf_op jit(solution)/shard_map/ppermute | solution.py:457
  25.9 1.4 %copy-start = (bf16[192,4096]{1,0:T(8,128)(2,1)S(1)}, bf16[192,4096]{1,0:T(8,128)(2,1)}, u32[]{:S(2)}) copy-start(bf16[192,4096]{1,0:T(8,128)(2,1)} %refs_0_.1) | copy-start | bytes 4718596
  25.9 1.4 %copy-start.2 = (s32[1,8]{1,0:T(1,128)S(1)}, s32[1,8]{1,0:T(1,128)}, u32[]{:S(2)}) copy-start(s32[1,8]{1,0:T(1,128)} %param.10) | copy-start | bytes 100
  27.3 8.6 %copy-start.1 = (bf16[192,4096]{1,0:T(8,128)(2,1)S(1)}, bf16[192,4096]{1,0:T(8,128)(2,1)}, u32[]{:S(2)}) copy-start(bf16[192,4096]{1,0:T(8,128)(2,1)} %refs_1_.1) | copy-start | bytes 4718596
  32.0 28.3 %collective-permute-start.10 = (bf16[2,96,1152]{2,1,0:T(8,128)(2,1)S(1)}, bf16[2,96,1152]{2,1,0:T(8,128)(2,1)S(1)}, u32[]{:S(2)}, u32[]{:S(2)}) collective-permute-start(bf16[2,96,1152]{2,1,0:T(8,128)(2,1)S(1)} %get-tuple-element.37), channel_id=1, source_target_pairs={{0,12},{1,13},{2,14},{3,15},{4,8},{5,9},{6,10},{7,11},{8,4},{9,5},... | collective-permute-start | bytes 1327112 | tf_op jit(solution)/shard_map/ppermute | solution.py:485
  33.3 28.4 %collective-permute-start.8 = (bf16[2,96,1152]{2,1,0:T(8,128)(2,1)S(1)}, bf16[2,96,1152]{2,1,0:T(8,128)(2,1)S(1)}, u32[]{:S(2)}, u32[]{:S(2)}) collective-permute-start(bf16[2,96,1152]{2,1,0:T(8,128)(2,1)S(1)} %get-tuple-element.35), channel_id=1, source_target_pairs={{0,4},{1,5},{2,6},{3,7},{4,0},{5,1},{6,2},{7,3},{8,12},{9,13},{10,... | collective-permute-start | bytes 1327112 | tf_op jit(solution)/shard_map/ppermute | solution.py:485
  34.9 26.8 %collective-permute-start.9 = (bf16[2,96,1152]{2,1,0:T(8,128)(2,1)S(1)}, bf16[2,96,1152]{2,1,0:T(8,128)(2,1)S(1)}, u32[]{:S(2)}, u32[]{:S(2)}) collective-permute-start(bf16[2,96,1152]{2,1,0:T(8,128)(2,1)S(1)} %get-tuple-element.36), channel_id=1, source_target_pairs={{0,8},{1,9},{2,10},{3,11},{4,12},{5,13},{6,14},{7,15},{8,0},{9,1},... | collective-permute-start | bytes 1327112 | tf_op jit(solution)/shard_map/ppermute | solution.py:485
  58.1 19.2 %collective-permute-start.14 = (bf16[2,64,1152]{2,1,0:T(8,128)(2,1)S(1)}, bf16[2,64,1152]{2,1,0:T(8,128)(2,1)S(1)}, u32[]{:S(2)}, u32[]{:S(2)}) collective-permute-start(bf16[2,64,1152]{2,1,0:T(8,128)(2,1)S(1)} %get-tuple-element.44), channel_id=1, source_target_pairs={{0,4},{1,5},{2,6},{3,7},{4,0},{5,1},{6,2},{7,3},{8,12},{9,13},{10,... | collective-permute-start | bytes 884744 | tf_op jit(solution)/shard_map/ppermute | solution.py:485
  58.7 20.0 %collective-permute-start.15 = (bf16[2,64,1152]{2,1,0:T(8,128)(2,1)S(1)}, bf16[2,64,1152]{2,1,0:T(8,128)(2,1)S(1)}, u32[]{:S(2)}, u32[]{:S(2)}) collective-permute-start(bf16[2,64,1152]{2,1,0:T(8,128)(2,1)S(1)} %get-tuple-element.45), channel_id=1, source_target_pairs={{0,8},{1,9},{2,10},{3,11},{4,12},{5,13},{6,14},{7,15},{8,0},{9,1},... | collective-permute-start | bytes 884744 | tf_op jit(solution)/shard_map/ppermute | solution.py:485
  60.3 26.4 %collective-permute-start.16 = (bf16[2,64,1152]{2,1,0:T(8,128)(2,1)S(1)}, bf16[2,64,1152]{2,1,0:T(8,128)(2,1)S(1)}, u32[]{:S(2)}, u32[]{:S(2)}) collective-permute-start(bf16[2,64,1152]{2,1,0:T(8,128)(2,1)S(1)} %get-tuple-element.46), channel_id=1, source_target_pairs={{0,12},{1,13},{2,14},{3,15},{4,8},{5,9},{6,10},{7,11},{8,4},{9,5},... | collective-permute-start | bytes 884744 | tf_op jit(solution)/shard_map/ppermute | solution.py:485
  75.2 12.7 %collective-permute-start.11 = (bf16[2,32,1152]{2,1,0:T(8,128)(2,1)S(1)}, bf16[2,32,1152]{2,1,0:T(8,128)(2,1)S(1)}, u32[]{:S(2)}, u32[]{:S(2)}) collective-permute-start(bf16[2,32,1152]{2,1,0:T(8,128)(2,1)S(1)} %get-tuple-element.41), channel_id=1, source_target_pairs={{0,4},{1,5},{2,6},{3,7},{4,0},{5,1},{6,2},{7,3},{8,12},{9,13},{10,... | collective-permute-start | bytes 442376 | tf_op jit(solution)/shard_map/ppermute | solution.py:485
  75.7 12.1 %collective-permute-start.12 = (bf16[2,32,1152]{2,1,0:T(8,128)(2,1)S(1)}, bf16[2,32,1152]{2,1,0:T(8,128)(2,1)S(1)}, u32[]{:S(2)}, u32[]{:S(2)}) collective-permute-start(bf16[2,32,1152]{2,1,0:T(8,128)(2,1)S(1)} %get-tuple-element.42), channel_id=1, source_target_pairs={{0,8},{1,9},{2,10},{3,11},{4,12},{5,13},{6,14},{7,15},{8,0},{9,1},... | collective-permute-start | bytes 442376 | tf_op jit(solution)/shard_map/ppermute | solution.py:485
  77.3 11.6 %collective-permute-start.13 = (bf16[2,32,1152]{2,1,0:T(8,128)(2,1)S(1)}, bf16[2,32,1152]{2,1,0:T(8,128)(2,1)S(1)}, u32[]{:S(2)}, u32[]{:S(2)}) collective-permute-start(bf16[2,32,1152]{2,1,0:T(8,128)(2,1)S(1)} %get-tuple-element.43), channel_id=1, source_target_pairs={{0,12},{1,13},{2,14},{3,15},{4,8},{5,9},{6,10},{7,11},{8,4},{9,5},... | collective-permute-start | bytes 442376 | tf_op jit(solution)/shard_map/ppermute | solution.py:485
  78.7 26.1 %collective-permute-start.19 = (bf16[1,96,1152]{2,1,0:T(8,128)(2,1)S(1)}, bf16[1,96,1152]{2,1,0:T(8,128)(2,1)S(1)}, u32[]{:S(2)}, u32[]{:S(2)}) collective-permute-start(bf16[1,96,1152]{2,1,0:T(8,128)(2,1)S(1)} %get-tuple-element.51), channel_id=1, source_target_pairs={{0,16},{1,17},{2,18},{3,19},{4,20},{5,21},{6,22},{7,23},{8,24},{9,... | collective-permute-start | bytes 663560 | tf_op jit(solution)/shard_map/ppermute | solution.py:485
  87.8 16.0 %collective-permute-start.18 = (bf16[1,64,1152]{2,1,0:T(8,128)(2,1)S(1)}, bf16[1,64,1152]{2,1,0:T(8,128)(2,1)S(1)}, u32[]{:S(2)}, u32[]{:S(2)}) collective-permute-start(bf16[1,64,1152]{2,1,0:T(8,128)(2,1)S(1)} %get-tuple-element.50), channel_id=1, source_target_pairs={{0,16},{1,17},{2,18},{3,19},{4,20},{5,21},{6,22},{7,23},{8,24},{9,... | collective-permute-start | bytes 442376 | tf_op jit(solution)/shard_map/ppermute | solution.py:485
  89.6 16.2 %collective-permute-start.17 = (bf16[1,32,1152]{2,1,0:T(8,128)(2,1)S(1)}, bf16[1,32,1152]{2,1,0:T(8,128)(2,1)S(1)}, u32[]{:S(2)}, u32[]{:S(2)}) collective-permute-start(bf16[1,32,1152]{2,1,0:T(8,128)(2,1)S(1)} %get-tuple-element.49), channel_id=1, source_target_pairs={{0,16},{1,17},{2,18},{3,19},{4,20},{5,21},{6,22},{7,23},{8,24},{9,... | collective-permute-start | bytes 221192 | tf_op jit(solution)/shard_map/ppermute | solution.py:485

commit v9 on v8

--- a/solution.py
+++ b/solution.py
@@ -448,16 +448,16 @@
         for side, bit in zip(sides, (2, 3))
     ]
     got = [sent(x, bit) for x, bit in zip(picked, (2, 3))]
-    boxes = [(0, 1, False)] + [(1, bit, False) for bit in (1, 2, 3)]
-    near_s, *picked_f = pick([q_second, q_first], here, boxes, mine)
+    boxes = [(0, 0, False), (0, 1, False)] + [(1, bit, False) for bit in range(4)]
+    own_s, near_s, own_f, *picked_f = pick([q_second, q_first], here, boxes, mine)
     near_s = sent(near_s, 1)
     beside = [sent(x, bit) for x, bit in zip(picked_f, (1, 2, 3))]
     others = []
     for order, x in enumerate(got):
         others.append(lax.ppermute(x, AXES, swapped(shape, 1 + order, 0)))
-    second = [q_second.reshape(2, half, wide), near_s.reshape(2, half, mine)]
+    second = [x.reshape(2, half, mine) for x in (own_s, near_s)]
     second += [x.reshape(1, half, mine) for x in got + others]
-    first = [q_first.reshape(2, half, wide)] + [x.reshape(2, half, mine) for x in beside]
+    first = [x.reshape(2, half, mine) for x in [own_f] + beside]
 
     def places_of(owners):
         return jnp.stack([((o ^ spot) % 4) * 2 + o // 4 for o in owners]).astype(jnp.int32)

time: 107 us -> 107 us (level)
  transfers between devices with their start and end apart: 20 -> 20, of which waited for: 5 -> 5; matrix products, arithmetic and copies ran while one was open for 5% -> 5% of each run, Pallas kernels for 44% -> 45%
where the time goes in v9:
time: 107 us
  Pallas kernels  48.7 us (46%)
  starting transfers between devices  33.2 us (31%)
  waiting for transfers between devices  16.8 us (16%)
  local copies, waits for them, and re-layouts  5.81 us (5%)
  between operations  1.74 us (2%)
    pallas_call x3, Pallas kernels, partial_call(): pl.pallas_call(functools.partial(kernel, pieces=len(pieces), outs=outs, g...  38.7 us
    ppermute x12, starting transfers between devices, moved(): return lax.ppermute(part, AXES, swapped(shape, bits, 0))  24.3 us
    ppermute x12, waiting for transfers between devices, moved(): return lax.ppermute(part, AXES, swapped(shape, bits, 0))  9.31 us
    ppermute x6, waiting for transfers between devices, sent(): return lax.ppermute(block, AXES, swapped(shape, 0, bit))  6.32 us
    ppermute x6, starting transfers between devices, sent(): return lax.ppermute(block, AXES, swapped(shape, 0, bit))  5.16 us
    transpose x1, local copies, waits for them, and re-layouts, shards(): keys, values = settle(keys, jnp.swapaxes(late, 0, 1))  4.56 us
    pallas_call x1, Pallas kernels, pick(): pl.pallas_call(functools.partial(pick_kernel, boxes=boxes), in_specs=[pl....  3.73 us
    ppermute x2, starting transfers between devices, relayed(): others.append(lax.ppermute(x, AXES, swapped(shape, 1 + order, 0)))  3.69 us
  transfers between devices with their start and end apart: 20, of which 5 were waited for; matrix products, arithmetic and copies ran while one was open for 5% of the time, Pallas kernels for 45%

profile of v9, /device:TPU:0, one launch (start us, length us, event | category | flops | bytes accessed | tf_op | source)
XLA Modules:
  0.0 106.8 jit_solution(1287108094726349591)
XLA Ops:
  0.7 1.1 fusion
  1.8 3.0 %collective-permute-start.3 = (bf16[96,1024]{1,0:T(8,128)(2,1)S(1)}, bf16[96,1024]{1,0:T(8,128)(2,1)S(1)}, u32[]{:S(2)}, u32[]{:S(2)}) collective-permute-start(bf16[96,1024]{1,0:T(8,128)(2,1)S(1)} %get-tuple-element.57), channel_id=1, source_target_pairs={{0,2},{1,3},{2,0},{3,1},{4,6},{5,7},{6,4},{7,5},{8,10},{9,11},{10,... | collective-permute-start | bytes 589832 | tf_op jit(solution)/shard_map/ppermute | solution.py:443
  4.8 5.7 %collective-permute-done.3 = bf16[96,1024]{1,0:T(8,128)(2,1)S(1)} collective-permute-done((bf16[96,1024]{1,0:T(8,128)(2,1)S(1)}, bf16[96,1024]{1,0:T(8,128)(2,1)S(1)}, u32[]{:S(2)}, u32[]{:S(2)}) %collective-permute-start.3) | collective-permute-done | bytes 196640 | tf_op jit(solution)/shard_map/ppermute | solution.py:443
  10.5 2.0 %collective-permute-start.6 = (bf16[96,1024]{1,0:T(8,128)(2,1)S(1)}, bf16[96,1024]{1,0:T(8,128)(2,1)S(1)}, u32[]{:S(2)}, u32[]{:S(2)}) collective-permute-start(bf16[96,1024]{1,0:T(8,128)(2,1)S(1)} %collective-permute-done.3), channel_id=1, source_target_pairs={{0,4},{1,5},{2,6},{3,7},{4,0},{5,1},{6,2},{7,3},{8,12},{9,13},{10,... | collective-permute-start | bytes 589832 | tf_op jit(solution)/shard_map/ppermute | solution.py:457
  12.6 0.6 pad_add_fusion.spot_ref
  13.2 3.7 %shard_map.77 = (bf16[192,1024]{1,0:T(8,128)(2,1)}, bf16[192,1024]{1,0:T(8,128)(2,1)}, bf16[192,1024]{1,0:T(8,128)(2,1)}, bf16[192,1024]{1,0:T(8,128)(2,1)}, bf1...) custom-call(s32[2]{0:T(128)} %pad_add_fusion.spot_ref, bf16[192,4096]{1,0:T(8,128)(2,1)} %refs_0_.1, ...), custom_call_target="tpu_custom_call" | custom-call | tf_op jit(solution)/shard_map/pallas_call | solution.py:410
  17.5 1.5 %collective-permute-start.1 = (bf16[192,1024]{1,0:T(8,128)(2,1)}, bf16[192,1024]{1,0:T(8,128)(2,1)S(1)}, u32[]{:S(2)}, u32[]{:S(2)}) collective-permute-start(bf16[192,1024]{1,0:T(8,128)(2,1)} %get-tuple-element.31), channel_id=1, source_target_pairs={{0,2},{1,3},{2,0},{3,1},{4,6},{5,7},{6,4},{7,5},{8,10},{9,11},{10,... | collective-permute-start | bytes 1179656 | tf_op jit(solution)/shard_map/ppermute | solution.py:443
  20.1 1.6 %collective-permute-start.7 = (bf16[96,1024]{1,0:T(8,128)(2,1)S(1)}, bf16[96,1024]{1,0:T(8,128)(2,1)S(1)}, u32[]{:S(2)}, u32[]{:S(2)}) collective-permute-start(bf16[96,1024]{1,0:T(8,128)(2,1)S(1)} %collective-permute-done.5), channel_id=1, source_target_pairs={{0,8},{1,9},{2,10},{3,11},{4,12},{5,13},{6,14},{7,15},{8,0},{9,1},... | collective-permute-start | bytes 589832 | tf_op jit(solution)/shard_map/ppermute | solution.py:457
  21.8 4.6 %copy_bitcast_fusion = (bf16[4,4096,128]{2,1,0:T(8,128)(2,1)S(1)}, bf16[4,4096,128]{2,1,0:T(8,128)(2,1)S(1)}) fusion(bf16[4096,4,128]{2,1,0:T(4,128)(2,1)} %param.9, bf16[4096,4,128]{2,1,0:T(4,128)(2,1)} %param.8), kind=kLoop, calls=%fused_computation | loop fusion | bytes 16777216 | tf_op jit(solution)/shard_map/transpose | solution.py:480
  26.4 1.2 %collective-permute-done.7 = bf16[96,1024]{1,0:T(8,128)(2,1)S(1)} collective-permute-done((bf16[96,1024]{1,0:T(8,128)(2,1)S(1)}, bf16[96,1024]{1,0:T(8,128)(2,1)S(1)}, u32[]{:S(2)}, u32[]{:S(2)}) %collective-permute-start.7) | collective-permute-done | bytes 196640 | tf_op jit(solution)/shard_map/ppermute | solution.py:457
  27.6 4.6 %shard_map.79 = (bf16[2,96,1152]{2,1,0:T(8,128)(2,1)S(1)}, bf16[2,96,1152]{2,1,0:T(8,128)(2,1)S(1)}, bf16[2,96,1152]{2,1,0:T(8,128)(2,1)S(1)}, bf16[2,96,1152]{2,1,0:T(8,128)(2,1)S(1)}) custom-call(s32[8]{0:T(128)S(1)} %stack.68.place_ref, s32[1]{0:T(128)} %bitcast.9.column_ref, s32[8]{0:T(128)S(1)} %bitcast.46, s32[1]{0:T(128)S(6)} %copy.18.count_ref, ...), custom_call_target="tpu_custom_call" | custom-call | flops 3221225472 | bytes 1048576 | tf_op jit(solution)/shard_map/pallas_call | solution.py:260
  32.2 1.6 %collective-permute-start.10 = (bf16[2,96,1152]{2,1,0:T(8,128)(2,1)S(1)}, bf16[2,96,1152]{2,1,0:T(8,128)(2,1)S(1)}, u32[]{:S(2)}, u32[]{:S(2)}) collective-permute-start(bf16[2,96,1152]{2,1,0:T(8,128)(2,1)S(1)} %get-tuple-element.41), channel_id=1, source_target_pairs={{0,12},{1,13},{2,14},{3,15},{4,8},{5,9},{6,10},{7,11},{8,4},{9,5},... | collective-permute-start | bytes 1327112 | tf_op jit(solution)/shard_map/ppermute | solution.py:485
  33.8 1.5 %collective-permute-start.8 = (bf16[2,96,1152]{2,1,0:T(8,128)(2,1)S(1)}, bf16[2,96,1152]{2,1,0:T(8,128)(2,1)S(1)}, u32[]{:S(2)}, u32[]{:S(2)}) collective-permute-start(bf16[2,96,1152]{2,1,0:T(8,128)(2,1)S(1)} %get-tuple-element.39), channel_id=1, source_target_pairs={{0,4},{1,5},{2,6},{3,7},{4,0},{5,1},{6,2},{7,3},{8,12},{9,13},{10,... | collective-permute-start | bytes 1327112 | tf_op jit(solution)/shard_map/ppermute | solution.py:485
  35.8 0.6 collective-permute-done.2
  36.3 22.2 %shard_map.80 = (bf16[2,64,1152]{2,1,0:T(8,128)(2,1)S(1)}, bf16[2,64,1152]{2,1,0:T(8,128)(2,1)S(1)}, bf16[2,64,1152]{2,1,0:T(8,128)(2,1)S(1)}, bf16[2,64,1152]{2,1,0:T(8,128)(2,1)S(1)}) custom-call(s32[8]{0:T(128)S(1)} %stack.61.place_ref, s32[1]{0:T(128)} %bitcast.9.column_ref, bf16[2,96,1024]{2,1,0:T(8,128)(2,1)S(1)} %bitcast.32, ...), custom_call_target="tpu_custom_call" | custom-call | flops 17179869184 | bytes 8388608 | tf_op jit(solution)/shard_map/pallas_call | solution.py:260
  58.6 0.6 collective-permute-start.14
  59.1 1.6 %collective-permute-start.15 = (bf16[2,64,1152]{2,1,0:T(8,128)(2,1)S(1)}, bf16[2,64,1152]{2,1,0:T(8,128)(2,1)S(1)}, u32[]{:S(2)}, u32[]{:S(2)}) collective-permute-start(bf16[2,64,1152]{2,1,0:T(8,128)(2,1)S(1)} %get-tuple-element.49), channel_id=1, source_target_pairs={{0,8},{1,9},{2,10},{3,11},{4,12},{5,13},{6,14},{7,15},{8,0},{9,1},... | collective-permute-start | bytes 884744 | tf_op jit(solution)/shard_map/ppermute | solution.py:485
  60.7 1.4 %collective-permute-start.16 = (bf16[2,64,1152]{2,1,0:T(8,128)(2,1)S(1)}, bf16[2,64,1152]{2,1,0:T(8,128)(2,1)S(1)}, u32[]{:S(2)}, u32[]{:S(2)}) collective-permute-start(bf16[2,64,1152]{2,1,0:T(8,128)(2,1)S(1)} %get-tuple-element.50), channel_id=1, source_target_pairs={{0,12},{1,13},{2,14},{3,15},{4,8},{5,9},{6,10},{7,11},{8,4},{9,5},... | collective-permute-start | bytes 884744 | tf_op jit(solution)/shard_map/ppermute | solution.py:485
  62.1 1.6 %shard_map.81 = (bf16[1,96,1152]{2,1,0:T(8,128)(2,1)S(1)}, bf16[1,96,1152]{2,1,0:T(8,128)(2,1)S(1)}) custom-call(s32[1]{0:T(128)} %bitcast.refs_8_.spot_ref, bf16[2,96,1152]{2,1,0:T(8,128)(2,1)S(1)} %get-tuple-element.38.refs_6_.refs_0_, bf16[2,96,1152]{2,1,0:T(8,128)(2,1)S(1)} %collective-permute-done.8.refs_1_, ...), custom_call_target="tpu_custom_call" | custom-call | flops 3538944 | bytes 2211840 | tf_op jit(solution)/shard_map/pallas_call | solution.py:358
  63.7 11.9 %shard_map.82 = (bf16[2,32,1152]{2,1,0:T(8,128)(2,1)S(1)}, bf16[2,32,1152]{2,1,0:T(8,128)(2,1)S(1)}, bf16[2,32,1152]{2,1,0:T(8,128)(2,1)S(1)}, bf16[2,32,1152]{2,1,0:T(8,128)(2,1)S(1)}) custom-call(s32[8]{0:T(128)S(1)} %stack.61.place_ref, s32[1]{0:T(128)} %bitcast.9.column_ref, bf16[2,96,1024]{2,1,0:T(8,128)(2,1)S(1)} %bitcast.33, ...), custom_call_target="tpu_custom_call" | custom-call | flops 8589934592 | bytes 8388608 | tf_op jit(solution)/shard_map/pallas_call | solution.py:260
  75.6 0.6 collective-permute-start.11
  76.2 1.6 %collective-permute-start.12 = (bf16[2,32,1152]{2,1,0:T(8,128)(2,1)S(1)}, bf16[2,32,1152]{2,1,0:T(8,128)(2,1)S(1)}, u32[]{:S(2)}, u32[]{:S(2)}) collective-permute-start(bf16[2,32,1152]{2,1,0:T(8,128)(2,1)S(1)} %get-tuple-element.46), channel_id=1, source_target_pairs={{0,8},{1,9},{2,10},{3,11},{4,12},{5,13},{6,14},{7,15},{8,0},{9,1},... | collective-permute-start | bytes 442376 | tf_op jit(solution)/shard_map/ppermute | solution.py:485
  77.7 1.4 %collective-permute-start.13 = (bf16[2,32,1152]{2,1,0:T(8,128)(2,1)S(1)}, bf16[2,32,1152]{2,1,0:T(8,128)(2,1)S(1)}, u32[]{:S(2)}, u32[]{:S(2)}) collective-permute-start(bf16[2,32,1152]{2,1,0:T(8,128)(2,1)S(1)} %get-tuple-element.47), channel_id=1, source_target_pairs={{0,12},{1,13},{2,14},{3,15},{4,8},{5,9},{6,10},{7,11},{8,4},{9,5},... | collective-permute-start | bytes 442376 | tf_op jit(solution)/shard_map/ppermute | solution.py:485
  79.2 7.8 %collective-permute-start.19 = (bf16[1,96,1152]{2,1,0:T(8,128)(2,1)S(1)}, bf16[1,96,1152]{2,1,0:T(8,128)(2,1)S(1)}, u32[]{:S(2)}, u32[]{:S(2)}) collective-permute-start(bf16[1,96,1152]{2,1,0:T(8,128)(2,1)S(1)} %get-tuple-element.55), channel_id=1, source_target_pairs={{0,16},{1,17},{2,18},{3,19},{4,20},{5,21},{6,22},{7,23},{8,24},{9,... | collective-permute-start | bytes 663560 | tf_op jit(solution)/shard_map/ppermute | solution.py:485
  87.0 1.1 %shard_map.83 = (bf16[1,64,1152]{2,1,0:T(8,128)(2,1)S(1)}, bf16[1,64,1152]{2,1,0:T(8,128)(2,1)S(1)}) custom-call(s32[1]{0:T(128)} %bitcast.refs_8_.spot_ref, bf16[2,64,1152]{2,1,0:T(8,128)(2,1)S(1)} %get-tuple-element.42.refs_4_.refs_0_, bf16[2,64,1152]{2,1,0:T(8,128)(2,1)S(1)} %collective-permute-done.14.refs_1_, ...), custom_call_target="tpu_custom_call" | custom-call | flops 2359296 | bytes 1474560 | tf_op jit(solution)/shard_map/pallas_call | solution.py:358
  88.2 0.9 collective-permute-done.13.refs_3_
  89.1 0.7 shard_map.84
  89.8 5.8 %collective-permute-start.17 = (bf16[1,32,1152]{2,1,0:T(8,128)(2,1)S(1)}, bf16[1,32,1152]{2,1,0:T(8,128)(2,1)S(1)}, u32[]{:S(2)}, u32[]{:S(2)}) collective-permute-start(bf16[1,32,1152]{2,1,0:T(8,128)(2,1)S(1)} %get-tuple-element.53), channel_id=1, source_target_pairs={{0,16},{1,17},{2,18},{3,19},{4,20},{5,21},{6,22},{7,23},{8,24},{9,... | collective-permute-start | bytes 221192 | tf_op jit(solution)/shard_map/ppermute | solution.py:485
  95.5 8.4 %collective-permute-done.18.refs_1_ = bf16[1,64,1152]{2,1,0:T(8,128)(2,1)S(1)} collective-permute-done((bf16[1,64,1152]{2,1,0:T(8,128)(2,1)S(1)}, bf16[1,64,1152]{2,1,0:T(8,128)(2,1)S(1)}, u32[]{:S(2)}, u32[]{:S(2)}) %collective-permute-start.18) | collective-permute-done | bytes 147488 | tf_op jit(solution)/shard_map/ppermute | solution.py:485
  103.9 1.0 shard_map.85.refs_2_
  104.9 1.1 %shard_map.87 = bf16[1,96,1024]{2,1,0:T(8,128)(2,1)} custom-call(bf16[1,96,1152]{2,1,0:T(8,128)(2,1)S(1)} %get-tuple-element.43.refs_6_.refs_0_, bf16[1,96,1152]{2,1,0:T(8,128)(2,1)S(1)} %collective-permute-done.19.refs_1_), custom_call_target="tpu_custom_call" | custom-call | flops 786432 | bytes 442368 | tf_op jit(solution)/shard_map/pallas_call | solution.py:328
  106.0 0.9 shard_map.86
  (30 shorter events, 1.4 us)
Async XLA Ops:
  1.8 8.8 %collective-permute-start.3 = (bf16[96,1024]{1,0:T(8,128)(2,1)S(1)}, bf16[96,1024]{1,0:T(8,128)(2,1)S(1)}, u32[]{:S(2)}, u32[]{:S(2)}) collective-permute-start(bf16[96,1024]{1,0:T(8,128)(2,1)S(1)} %get-tuple-element.57), channel_id=1, source_target_pairs={{0,2},{1,3},{2,0},{3,1},{4,6},{5,7},{6,4},{7,5},{8,10},{9,11},{10,... | collective-permute-start | bytes 589832 | tf_op jit(solution)/shard_map/ppermute | solution.py:443
  4.8 15.3 %collective-permute-start.5 = (bf16[96,1024]{1,0:T(8,128)(2,1)S(1)}, bf16[96,1024]{1,0:T(8,128)(2,1)S(1)}, u32[]{:S(2)}, u32[]{:S(2)}) collective-permute-start(bf16[96,1024]{1,0:T(8,128)(2,1)S(1)} %get-tuple-element.56), channel_id=1, source_target_pairs={{0,3},{1,2},{2,1},{3,0},{4,7},{5,6},{6,5},{7,4},{8,11},{9,10},{10,... | collective-permute-start | bytes 589832 | tf_op jit(solution)/shard_map/ppermute | solution.py:443
  10.5 9.6 %collective-permute-start.6 = (bf16[96,1024]{1,0:T(8,128)(2,1)S(1)}, bf16[96,1024]{1,0:T(8,128)(2,1)S(1)}, u32[]{:S(2)}, u32[]{:S(2)}) collective-permute-start(bf16[96,1024]{1,0:T(8,128)(2,1)S(1)} %collective-permute-done.3), channel_id=1, source_target_pairs={{0,4},{1,5},{2,6},{3,7},{4,0},{5,1},{6,2},{7,3},{8,12},{9,13},{10,... | collective-permute-start | bytes 589832 | tf_op jit(solution)/shard_map/ppermute | solution.py:457
  16.9 10.7 %collective-permute-start.4 = (bf16[192,1024]{1,0:T(8,128)(2,1)}, bf16[192,1024]{1,0:T(8,128)(2,1)S(1)}, u32[]{:S(2)}, u32[]{:S(2)}) collective-permute-start(bf16[192,1024]{1,0:T(8,128)(2,1)} %get-tuple-element.37), channel_id=1, source_target_pairs={{0,1},{1,0},{2,3},{3,2},{4,5},{5,4},{6,7},{7,6},{8,9},{9,8},{10,11... | collective-permute-start | bytes 1179656 | tf_op jit(solution)/shard_map/ppermute | solution.py:443
  17.0 18.3 %collective-permute-start = (bf16[192,1024]{1,0:T(8,128)(2,1)}, bf16[192,1024]{1,0:T(8,128)(2,1)S(1)}, u32[]{:S(2)}, u32[]{:S(2)}) collective-permute-start(bf16[192,1024]{1,0:T(8,128)(2,1)} %get-tuple-element.30), channel_id=1, source_target_pairs={{0,1},{1,0},{2,3},{3,2},{4,5},{5,4},{6,7},{7,6},{8,9},{9,8},{10,11... | collective-permute-start | bytes 1179656 | tf_op jit(solution)/shard_map/ppermute | solution.py:443
  17.5 18.3 %collective-permute-start.1 = (bf16[192,1024]{1,0:T(8,128)(2,1)}, bf16[192,1024]{1,0:T(8,128)(2,1)S(1)}, u32[]{:S(2)}, u32[]{:S(2)}) collective-permute-start(bf16[192,1024]{1,0:T(8,128)(2,1)} %get-tuple-element.31), channel_id=1, source_target_pairs={{0,2},{1,3},{2,0},{3,1},{4,6},{5,7},{6,4},{7,5},{8,10},{9,11},{10,... | collective-permute-start | bytes 1179656 | tf_op jit(solution)/shard_map/ppermute | solution.py:443
  20.0 16.3 %collective-permute-start.2 = (bf16[192,1024]{1,0:T(8,128)(2,1)}, bf16[192,1024]{1,0:T(8,128)(2,1)S(1)}, u32[]{:S(2)}, u32[]{:S(2)}) collective-permute-start(bf16[192,1024]{1,0:T(8,128)(2,1)} %get-tuple-element.32), channel_id=1, source_target_pairs={{0,3},{1,2},{2,1},{3,0},{4,7},{5,6},{6,5},{7,4},{8,11},{9,10},{10,... | collective-permute-start | bytes 1179656 | tf_op jit(solution)/shard_map/ppermute | solution.py:443
  20.1 7.4 %collective-permute-start.7 = (bf16[96,1024]{1,0:T(8,128)(2,1)S(1)}, bf16[96,1024]{1,0:T(8,128)(2,1)S(1)}, u32[]{:S(2)}, u32[]{:S(2)}) collective-permute-start(bf16[96,1024]{1,0:T(8,128)(2,1)S(1)} %collective-permute-done.5), channel_id=1, source_target_pairs={{0,8},{1,9},{2,10},{3,11},{4,12},{5,13},{6,14},{7,15},{8,0},{9,1},... | collective-permute-start | bytes 589832 | tf_op jit(solution)/shard_map/ppermute | solution.py:457
  26.3 1.2 %copy-start.1 = (bf16[192,1024]{1,0:T(8,128)(2,1)S(1)}, bf16[192,1024]{1,0:T(8,128)(2,1)}, u32[]{:S(2)}) copy-start(bf16[192,1024]{1,0:T(8,128)(2,1)} %get-tuple-element.36) | copy-start | bytes 1179652
  26.4 1.2 %copy-start.2 = (s32[1,8]{1,0:T(1,128)S(1)}, s32[1,8]{1,0:T(1,128)}, u32[]{:S(2)}) copy-start(s32[1,8]{1,0:T(1,128)} %param.10) | copy-start | bytes 100
  27.6 8.8 %copy-start = (bf16[192,1024]{1,0:T(8,128)(2,1)S(1)}, bf16[192,1024]{1,0:T(8,128)(2,1)}, u32[]{:S(2)}) copy-start(bf16[192,1024]{1,0:T(8,128)(2,1)} %get-tuple-element.29) | copy-start | bytes 1179652
  32.2 28.5 %collective-permute-start.10 = (bf16[2,96,1152]{2,1,0:T(8,128)(2,1)S(1)}, bf16[2,96,1152]{2,1,0:T(8,128)(2,1)S(1)}, u32[]{:S(2)}, u32[]{:S(2)}) collective-permute-start(bf16[2,96,1152]{2,1,0:T(8,128)(2,1)S(1)} %get-tuple-element.41), channel_id=1, source_target_pairs={{0,12},{1,13},{2,14},{3,15},{4,8},{5,9},{6,10},{7,11},{8,4},{9,5},... | collective-permute-start | bytes 1327112 | tf_op jit(solution)/shard_map/ppermute | solution.py:485
  33.8 28.3 %collective-permute-start.8 = (bf16[2,96,1152]{2,1,0:T(8,128)(2,1)S(1)}, bf16[2,96,1152]{2,1,0:T(8,128)(2,1)S(1)}, u32[]{:S(2)}, u32[]{:S(2)}) collective-permute-start(bf16[2,96,1152]{2,1,0:T(8,128)(2,1)S(1)} %get-tuple-element.39), channel_id=1, source_target_pairs={{0,4},{1,5},{2,6},{3,7},{4,0},{5,1},{6,2},{7,3},{8,12},{9,13},{10,... | collective-permute-start | bytes 1327112 | tf_op jit(solution)/shard_map/ppermute | solution.py:485
  35.3 26.8 %collective-permute-start.9 = (bf16[2,96,1152]{2,1,0:T(8,128)(2,1)S(1)}, bf16[2,96,1152]{2,1,0:T(8,128)(2,1)S(1)}, u32[]{:S(2)}, u32[]{:S(2)}) collective-permute-start(bf16[2,96,1152]{2,1,0:T(8,128)(2,1)S(1)} %get-tuple-element.40), channel_id=1, source_target_pairs={{0,8},{1,9},{2,10},{3,11},{4,12},{5,13},{6,14},{7,15},{8,0},{9,1},... | collective-permute-start | bytes 1327112 | tf_op jit(solution)/shard_map/ppermute | solution.py:485
  58.6 19.2 %collective-permute-start.14 = (bf16[2,64,1152]{2,1,0:T(8,128)(2,1)S(1)}, bf16[2,64,1152]{2,1,0:T(8,128)(2,1)S(1)}, u32[]{:S(2)}, u32[]{:S(2)}) collective-permute-start(bf16[2,64,1152]{2,1,0:T(8,128)(2,1)S(1)} %get-tuple-element.48), channel_id=1, source_target_pairs={{0,4},{1,5},{2,6},{3,7},{4,0},{5,1},{6,2},{7,3},{8,12},{9,13},{10,... | collective-permute-start | bytes 884744 | tf_op jit(solution)/shard_map/ppermute | solution.py:485
  59.1 20.0 %collective-permute-start.15 = (bf16[2,64,1152]{2,1,0:T(8,128)(2,1)S(1)}, bf16[2,64,1152]{2,1,0:T(8,128)(2,1)S(1)}, u32[]{:S(2)}, u32[]{:S(2)}) collective-permute-start(bf16[2,64,1152]{2,1,0:T(8,128)(2,1)S(1)} %get-tuple-element.49), channel_id=1, source_target_pairs={{0,8},{1,9},{2,10},{3,11},{4,12},{5,13},{6,14},{7,15},{8,0},{9,1},... | collective-permute-start | bytes 884744 | tf_op jit(solution)/shard_map/ppermute | solution.py:485
  60.7 26.2 %collective-permute-start.16 = (bf16[2,64,1152]{2,1,0:T(8,128)(2,1)S(1)}, bf16[2,64,1152]{2,1,0:T(8,128)(2,1)S(1)}, u32[]{:S(2)}, u32[]{:S(2)}) collective-permute-start(bf16[2,64,1152]{2,1,0:T(8,128)(2,1)S(1)} %get-tuple-element.50), channel_id=1, source_target_pairs={{0,12},{1,13},{2,14},{3,15},{4,8},{5,9},{6,10},{7,11},{8,4},{9,5},... | collective-permute-start | bytes 884744 | tf_op jit(solution)/shard_map/ppermute | solution.py:485
  75.6 12.5 %collective-permute-start.11 = (bf16[2,32,1152]{2,1,0:T(8,128)(2,1)S(1)}, bf16[2,32,1152]{2,1,0:T(8,128)(2,1)S(1)}, u32[]{:S(2)}, u32[]{:S(2)}) collective-permute-start(bf16[2,32,1152]{2,1,0:T(8,128)(2,1)S(1)} %get-tuple-element.45), channel_id=1, source_target_pairs={{0,4},{1,5},{2,6},{3,7},{4,0},{5,1},{6,2},{7,3},{8,12},{9,13},{10,... | collective-permute-start | bytes 442376 | tf_op jit(solution)/shard_map/ppermute | solution.py:485
  76.2 12.0 %collective-permute-start.12 = (bf16[2,32,1152]{2,1,0:T(8,128)(2,1)S(1)}, bf16[2,32,1152]{2,1,0:T(8,128)(2,1)S(1)}, u32[]{:S(2)}, u32[]{:S(2)}) collective-permute-start(bf16[2,32,1152]{2,1,0:T(8,128)(2,1)S(1)} %get-tuple-element.46), channel_id=1, source_target_pairs={{0,8},{1,9},{2,10},{3,11},{4,12},{5,13},{6,14},{7,15},{8,0},{9,1},... | collective-permute-start | bytes 442376 | tf_op jit(solution)/shard_map/ppermute | solution.py:485
  77.7 11.3 %collective-permute-start.13 = (bf16[2,32,1152]{2,1,0:T(8,128)(2,1)S(1)}, bf16[2,32,1152]{2,1,0:T(8,128)(2,1)S(1)}, u32[]{:S(2)}, u32[]{:S(2)}) collective-permute-start(bf16[2,32,1152]{2,1,0:T(8,128)(2,1)S(1)} %get-tuple-element.47), channel_id=1, source_target_pairs={{0,12},{1,13},{2,14},{3,15},{4,8},{5,9},{6,10},{7,11},{8,4},{9,5},... | collective-permute-start | bytes 442376 | tf_op jit(solution)/shard_map/ppermute | solution.py:485
  79.2 25.7 %collective-permute-start.19 = (bf16[1,96,1152]{2,1,0:T(8,128)(2,1)S(1)}, bf16[1,96,1152]{2,1,0:T(8,128)(2,1)S(1)}, u32[]{:S(2)}, u32[]{:S(2)}) collective-permute-start(bf16[1,96,1152]{2,1,0:T(8,128)(2,1)S(1)} %get-tuple-element.55), channel_id=1, source_target_pairs={{0,16},{1,17},{2,18},{3,19},{4,20},{5,21},{6,22},{7,23},{8,24},{9,... | collective-permute-start | bytes 663560 | tf_op jit(solution)/shard_map/ppermute | solution.py:485
  88.1 15.8 %collective-permute-start.18 = (bf16[1,64,1152]{2,1,0:T(8,128)(2,1)S(1)}, bf16[1,64,1152]{2,1,0:T(8,128)(2,1)S(1)}, u32[]{:S(2)}, u32[]{:S(2)}) collective-permute-start(bf16[1,64,1152]{2,1,0:T(8,128)(2,1)S(1)} %get-tuple-element.54), channel_id=1, source_target_pairs={{0,16},{1,17},{2,18},{3,19},{4,20},{5,21},{6,22},{7,23},{8,24},{9,... | collective-permute-start | bytes 442376 | tf_op jit(solution)/shard_map/ppermute | solution.py:485
  89.8 16.2 %collective-permute-start.17 = (bf16[1,32,1152]{2,1,0:T(8,128)(2,1)S(1)}, bf16[1,32,1152]{2,1,0:T(8,128)(2,1)S(1)}, u32[]{:S(2)}, u32[]{:S(2)}) collective-permute-start(bf16[1,32,1152]{2,1,0:T(8,128)(2,1)S(1)} %get-tuple-element.53), channel_id=1, source_target_pairs={{0,16},{1,17},{2,18},{3,19},{4,20},{5,21},{6,22},{7,23},{8,24},{9,... | collective-permute-start | bytes 221192 | tf_op jit(solution)/shard_map/ppermute | solution.py:485
